TPU v7x, 32 devices: a whole 2x2x4 slice. The times are simulated.
32 devices in a mesh: dp: 8 (over y, x, core), blk: 4 (over z).
Axes of the slice: x: 2, y: 2, z: 4, core: 2. Of those that a mesh axis runs over, the one named last changes fastest.
Arguments:
- block_input: bfloat16 [8, 1024, 2048], P('dp', 'blk'), may hold values from -8 to 8
- out_cotangent: bfloat16 [8, 1024, 2048], P('dp', 'blk'), may hold values from -6 to 6
- row_lengths: int32 [8], P('dp'), may hold values from 256 to 1024, as said below
- rope_positions: int32 [8, 1024], P('dp', 'blk'), may hold values from 0 to 2046, as said below
- gain_attention: float32 [2048], replicated, may hold values from 0.25 to 1.75
- gain_feedforward: float32 [2048], replicated, may hold values from 0.25 to 1.75
- base_attention: bfloat16 [6, 2048, 512], P(None, None, 'dp'), may hold values from -0.125 to 0.125
- base_output: bfloat16 [4, 2048, 512], P(None, None, 'dp'), may hold values from -0.125 to 0.125
- base_feedforward: bfloat16 [2, 2048, 5632], P(None, None, 'dp'), may hold values from -0.125 to 0.125
- base_down: bfloat16 [5632, 2048], P(None, 'dp'), may hold values from -0.078125 to 0.078125
- rank_in_attention: bfloat16 [3, 2048, 16], replicated, may hold values from -0.125 to 0.125
- rank_out_attention: bfloat16 [6, 16, 512], replicated, may hold values from -0.75 to 0.75
- magnitude_attention: float32 [6, 512], replicated, may hold values from 0.8 to 2
- rank_in_output: bfloat16 [2048, 16], replicated, may hold values from -0.125 to 0.125
- rank_out_output: bfloat16 [4, 16, 512], replicated, may hold values from -0.75 to 0.75
- magnitude_output: float32 [4, 512], replicated, may hold values from 3 to 12
- rank_in_feedforward: bfloat16 [2, 2048, 16], replicated, may hold values from -0.125 to 0.125
- rank_out_feedforward: bfloat16 [2, 16, 5632], replicated, may hold values from -0.75 to 0.75
- magnitude_feedforward: float32 [2, 5632], replicated, may hold values from 0.7 to 2
- rank_in_down: bfloat16 [5632, 16], replicated, may hold values from -0.078125 to 0.078125
- rank_out_down: bfloat16 [16, 2048], replicated, may hold values from -0.75 to 0.75
- magnitude_down: float32 [2048], replicated, may hold values from 0.8 to 2.5
Outputs:
- block_output: bfloat16 [8, 1024, 2048], P('dp', 'blk')
- input_grad: bfloat16 [8, 1024, 2048], P('dp', 'blk')
- grad_rank_in_attention: float32 [3, 2048, 16], replicated
- grad_rank_out_attention: float32 [6, 16, 512], replicated
- grad_magnitude_attention: float32 [6, 512], replicated
- grad_rank_in_output: float32 [2048, 16], replicated
- grad_rank_out_output: float32 [4, 16, 512], replicated
- grad_magnitude_output: float32 [4, 512], replicated
- grad_rank_in_feedforward: float32 [2, 2048, 16], replicated
- grad_rank_out_feedforward: float32 [2, 16, 5632], replicated
- grad_magnitude_feedforward: float32 [2, 5632], replicated
- grad_rank_in_down: float32 [5632, 16], replicated
- grad_rank_out_down: float32 [16, 2048], replicated
- grad_magnitude_down: float32 [2048], replicated
Inputs may be any that keep to these rules, and one draw needn't show every extreme that they name: Row r holds row_lengths[r] real tokens followed by padding; some row is 1024 tokens long. `rope_positions`: each row's positions start at 0 and rise by 1 or 2 from one token to the next; some row rises by 2 at every token.
All inputs are finite; a program needn't handle non-finite values.
Results may differ from a plain program's by a relative error of at most 0.019.
Values may be sent and summed in bfloat16 or wider, within the bound.
No kernel may reach another device: no remote copies, remote signals or barrier semaphores. Data moves between devices by JAX's collectives and lax.ppermute only.
A program may use at most 704 MiB of HBM per device.

v0:
```python
import jax
import jax.numpy as jnp
from jax import lax
from jax.sharding import PartitionSpec as P

D = 2048
KV_HEADS = 4
HEAD = 128
FF = 5632
RANK = 16


alpha_value = 32.0
rms_eps = 1e-05
rope_base = 10000.0
masked_score = -1e30
highest = lax.Precision.HIGHEST
float_type = jnp.float32
low_type = jnp.bfloat16
contract_last = (((1,), (1,)), ((), ()))
contract_first = (((0,), (0,)), ((), ()))


def rms_scaled(values, gain_row):
    return (
        values * lax.rsqrt(jnp.mean(values * values, axis=-1, keepdims=True) + rms_eps) * gain_row
    )


def rotate(values, cosine_table, sine_table):
    half_size = values.shape[-1] // 2
    turned = jnp.concatenate([-values[..., half_size:], values[..., :half_size]], axis=-1)
    return values * cosine_table + turned * sine_table


def rope_tables(positions_row, head_size):
    frequency = rope_base ** (-(jnp.arange(head_size // 2, dtype=float_type) * 2.0) / head_size)
    angles = positions_row.astype(float_type)[:, None] * frequency[None, :]
    angles = jnp.concatenate([angles, angles], axis=-1)
    return (jnp.cos(angles), jnp.sin(angles))


def merge_norm(weights_part, rank_in, rank_out):
    merged = weights_part.astype(float_type) + alpha_value / RANK * jnp.dot(
        rank_in, rank_out, preferred_element_type=float_type
    )
    return (merged, jnp.sqrt(jnp.sum(merged * merged, axis=0)))


def dora_front(inputs, small_part, weights_part, rank_out):
    base_value = jnp.dot(inputs, weights_part, preferred_element_type=float_type)
    return base_value + alpha_value / RANK * jnp.dot(
        small_part, rank_out.astype(float_type), precision=highest
    )


def dora_back(
    small_part,
    grad_output,
    weights_part,
    rank_in,
    rank_out,
    magnitude,
    raw_value,
    merged,
    column_norm,
):
    factor = alpha_value / RANK
    grad_value = grad_output * (magnitude / column_norm)
    grad_inputs = lax.dot_general(
        grad_value.astype(low_type), weights_part, contract_last, preferred_element_type=float_type
    )
    rank_out_wide = rank_out.astype(float_type)
    grad_small = factor * lax.dot_general(
        grad_value, rank_out_wide, contract_last, precision=highest
    )
    grad_magnitude = jnp.sum(grad_output * raw_value, axis=0) / column_norm
    norm_coeff = -grad_magnitude * magnitude / (column_norm * column_norm)
    rank_in_wide = rank_in.astype(float_type)
    grad_rank_out = factor * (
        lax.dot_general(small_part, grad_value, contract_first, precision=highest)
        + norm_coeff[None, :]
        * lax.dot_general(rank_in_wide, merged, contract_first, precision=highest)
    )
    grad_rank_in = factor * lax.dot_general(
        merged * norm_coeff[None, :], rank_out_wide, contract_last, precision=highest
    )
    return (grad_inputs, grad_small, grad_rank_in, grad_rank_out, grad_magnitude)


def finish_adapter(inputs, grad_small, rank_in, grad_inputs, grad_rank_norm):
    rounded = grad_small.astype(low_type)
    grad_rank_in = (
        lax.dot_general(inputs, rounded, contract_first, preferred_element_type=float_type)
        + grad_rank_norm
    )
    grad_inputs = grad_inputs + lax.dot_general(
        rounded, rank_in, contract_last, preferred_element_type=float_type
    )
    return (grad_rank_in, grad_inputs)


def project_blocks(inputs, small_part, weights, rank_in, rank_out, magnitude):
    outputs = []
    kept_values = []
    for member in range(weights.shape[0]):
        merged, column_norm = merge_norm(weights[member], rank_in, rank_out[member])
        raw_value = dora_front(inputs, small_part, weights[member], rank_out[member])
        outputs.append(raw_value * (magnitude[member] / column_norm))
        kept_values.append(raw_value)
    return (jnp.concatenate(outputs, axis=1), kept_values)


def back_blocks(inputs, small_part, grads, weights, rank_in, rank_out, magnitude, kept_values):
    width_cols = weights.shape[2]
    grad_inputs = jnp.zeros((inputs.shape[0], weights.shape[1]), float_type)
    grad_small = jnp.zeros(small_part.shape, float_type)
    grad_rank_in = jnp.zeros(rank_in.shape, float_type)
    rank_out_grads = []
    magnitude_grads = []
    for member in range(weights.shape[0]):
        merged, column_norm = merge_norm(weights[member], rank_in, rank_out[member])
        grad_part = grads[:, member * width_cols : (member + 1) * width_cols]
        pieces = dora_back(
            small_part,
            grad_part,
            weights[member],
            rank_in,
            rank_out[member],
            magnitude[member],
            kept_values[member],
            merged,
            column_norm,
        )
        grad_inputs = grad_inputs + pieces[0]
        grad_small = grad_small + pieces[1]
        grad_rank_in = grad_rank_in + pieces[2]
        rank_out_grads.append(pieces[3])
        magnitude_grads.append(pieces[4])
    return (
        grad_inputs,
        grad_small,
        grad_rank_in,
        jnp.stack(rank_out_grads),
        jnp.stack(magnitude_grads),
    )


def fetch_attention(base_attention, base_output):
    gathered = (
        lax.all_gather(base_attention, "dp", axis=2, tiled=True),
        lax.all_gather(base_output, "dp", axis=2, tiled=True),
    )
    return gathered


def score_block(queries, keys_all, block_index, block_size, query_pos, seq_length):
    key_first = block_index * block_size
    key_part = lax.dynamic_slice_in_dim(keys_all, key_first, block_size, 0)
    scores = jnp.einsum(
        "tajd,sjd->ajts", queries, key_part, preferred_element_type=float_type
    ) * queries.shape[-1] ** (-0.5)
    key_pos = key_first + jnp.arange(block_size, dtype=jnp.int32)
    allowed = (key_pos[None, :] <= query_pos[:, None]) & (key_pos[None, :] < seq_length)
    return (scores, allowed[None, None])


def guarded(compute, carry):
    updated = compute(carry)
    return updated


def attention_forward(queries, keys_all, values_all, query_pos, seq_length):
    block_size = min(512, keys_all.shape[0])
    block_count = keys_all.shape[0] // block_size
    head_shape = (queries.shape[1], queries.shape[2], queries.shape[0])

    def stats_step(block_index, carry):

        def compute(state):
            running_max, running_sum = state
            scores, allowed = score_block(
                queries, keys_all, block_index, block_size, query_pos, seq_length
            )
            block_max = jnp.max(jnp.where(allowed, scores, masked_score), axis=-1)
            new_max = jnp.maximum(running_max, block_max)
            exp_terms = jnp.where(allowed, jnp.exp(scores - new_max[..., None]), 0.0)
            return (
                new_max,
                running_sum * jnp.exp(running_max - new_max) + jnp.sum(exp_terms, axis=-1),
            )

        return guarded(compute, carry)

    start_state = (
        jnp.full(head_shape, masked_score, float_type),
        jnp.zeros(head_shape, float_type),
    )
    running_max, running_sum = lax.fori_loop(0, block_count, stats_step, start_state)
    log_total = running_max + jnp.log(running_sum)

    def value_step(block_index, carry):

        def compute(accum):
            scores, allowed = score_block(
                queries, keys_all, block_index, block_size, query_pos, seq_length
            )
            weights = jnp.where(allowed, jnp.exp(scores - log_total[..., None]), 0.0).astype(
                low_type
            )
            value_part = lax.dynamic_slice_in_dim(
                values_all, block_index * block_size, block_size, 0
            )
            return accum + jnp.einsum(
                "ajts,sjd->tajd", weights, value_part, preferred_element_type=float_type
            )

        return guarded(compute, carry)

    mixed_heads = lax.fori_loop(0, block_count, value_step, jnp.zeros(queries.shape, float_type))
    return (mixed_heads, log_total)


def attention_backward(
    queries, keys_all, values_all, query_pos, seq_length, log_total, grad_mixed, row_delta
):
    block_size = min(512, keys_all.shape[0])
    block_count = keys_all.shape[0] // block_size
    score_scale = queries.shape[-1] ** (-0.5)

    def grad_step(block_index, carry):

        def compute(state):
            grad_queries, grad_keys, grad_values = state
            key_first = block_index * block_size
            scores, allowed = score_block(
                queries, keys_all, block_index, block_size, query_pos, seq_length
            )
            softmax_probs = jnp.where(allowed, jnp.exp(scores - log_total[..., None]), 0.0)
            key_part = lax.dynamic_slice_in_dim(keys_all, key_first, block_size, 0)
            value_part = lax.dynamic_slice_in_dim(values_all, key_first, block_size, 0)
            value_grad = jnp.einsum(
                "ajts,tajd->sjd",
                softmax_probs.astype(low_type),
                grad_mixed,
                preferred_element_type=float_type,
            )
            prob_grads = jnp.einsum(
                "tajd,sjd->ajts", grad_mixed, value_part, preferred_element_type=float_type
            )
            score_grads = (softmax_probs * (prob_grads - row_delta[..., None])).astype(low_type)
            grad_queries = (
                grad_queries
                + jnp.einsum(
                    "ajts,sjd->tajd", score_grads, key_part, preferred_element_type=float_type
                )
                * score_scale
            )
            key_grad = (
                jnp.einsum(
                    "ajts,tajd->sjd", score_grads, queries, preferred_element_type=float_type
                )
                * score_scale
            )
            grad_keys = lax.dynamic_update_slice_in_dim(
                grad_keys,
                lax.dynamic_slice_in_dim(grad_keys, key_first, block_size, 0) + key_grad,
                key_first,
                0,
            )
            grad_values = lax.dynamic_update_slice_in_dim(
                grad_values,
                lax.dynamic_slice_in_dim(grad_values, key_first, block_size, 0) + value_grad,
                key_first,
                0,
            )
            return (grad_queries, grad_keys, grad_values)

        return guarded(compute, carry)

    start_state = (
        jnp.zeros(queries.shape, float_type),
        jnp.zeros(keys_all.shape, float_type),
        jnp.zeros(values_all.shape, float_type),
    )
    return lax.fori_loop(0, block_count, grad_step, start_state)


def shards(
    block_input,
    out_cotangent,
    row_lengths,
    rope_positions,
    gain_attention,
    gain_feedforward,
    base_attention,
    base_output,
    base_feedforward,
    base_down,
    rank_in_attention,
    rank_out_attention,
    magnitude_attention,
    rank_in_output,
    rank_out_output,
    magnitude_output,
    rank_in_feedforward,
    rank_out_feedforward,
    magnitude_feedforward,
    rank_in_down,
    rank_out_down,
    magnitude_down,
):
    rows_in = block_input[0].astype(float_type)
    tokens = rows_in.shape[0]
    groups = rank_out_attention.shape[0] - 2
    key_width = rank_out_attention.shape[2]
    seq_length = row_lengths[0]
    query_pos = lax.axis_index("blk") * tokens + jnp.arange(tokens, dtype=jnp.int32)
    valid_rows = (query_pos < seq_length).astype(float_type)[:, None]
    cosine_table, sine_table = rope_tables(rope_positions[0], HEAD)
    cosine_query = cosine_table[:, None, None, :]
    sine_query = sine_table[:, None, None, :]
    cosine_key = cosine_table[:, None, :]
    sine_key = sine_table[:, None, :]
    query_shape = (tokens, groups, KV_HEADS, HEAD)
    key_shape = (tokens, KV_HEADS, HEAD)
    attention_full, output_full = fetch_attention(base_attention, base_output)
    normed = rms_scaled(rows_in, gain_attention).astype(low_type)
    smalls_attention = [
        jnp.dot(normed, rank_in_attention[member], preferred_element_type=float_type)
        for member in range(3)
    ]
    query_raw, query_kept = project_blocks(
        normed,
        smalls_attention[0],
        attention_full[:groups],
        rank_in_attention[0],
        rank_out_attention[:groups],
        magnitude_attention[:groups],
    )
    key_raw, key_kept = project_blocks(
        normed,
        smalls_attention[1],
        attention_full[groups : groups + 1],
        rank_in_attention[1],
        rank_out_attention[groups : groups + 1],
        magnitude_attention[groups : groups + 1],
    )
    value_raw, value_kept = project_blocks(
        normed,
        smalls_attention[2],
        attention_full[groups + 1 :],
        rank_in_attention[2],
        rank_out_attention[groups + 1 :],
        magnitude_attention[groups + 1 :],
    )
    queries = rotate(query_raw.reshape(query_shape), cosine_query, sine_query).astype(low_type)
    keys_rotated = rotate(key_raw.reshape(key_shape), cosine_key, sine_key).astype(low_type)
    values = value_raw.reshape(key_shape).astype(low_type)
    keys_all, values_all = (
        lax.all_gather(keys_rotated.reshape(tokens, key_width), "blk", axis=0, tiled=True),
        lax.all_gather(values.reshape(tokens, key_width), "blk", axis=0, tiled=True),
    )
    keys_all = keys_all.reshape((-1, KV_HEADS, HEAD))
    values_all = values_all.reshape((-1, KV_HEADS, HEAD))
    mixed_heads, log_total = attention_forward(queries, keys_all, values_all, query_pos, seq_length)
    mixed_low = mixed_heads.reshape(tokens, -1).astype(low_type)
    small_output = jnp.dot(mixed_low, rank_in_output, preferred_element_type=float_type)
    output_raw, output_kept = project_blocks(
        mixed_low, small_output, output_full, rank_in_output, rank_out_output, magnitude_output
    )
    residual = rows_in + output_raw
    normed_feed = rms_scaled(residual, gain_feedforward).astype(low_type)
    smalls_feed = [
        jnp.dot(normed_feed, rank_in_feedforward[member], preferred_element_type=float_type)
        for member in range(2)
    ]
    weights_part = lax.all_gather(base_feedforward, "dp", axis=2, tiled=True)
    projected = []
    for feed_member in range(2):
        merged, column_norm = merge_norm(
            weights_part[feed_member],
            rank_in_feedforward[feed_member],
            rank_out_feedforward[feed_member],
        )
        raw_value = dora_front(
            normed_feed,
            smalls_feed[feed_member],
            weights_part[feed_member],
            rank_out_feedforward[feed_member],
        )
        projected.append(raw_value * (magnitude_feedforward[feed_member] / column_norm))
    hidden = (jax.nn.silu(projected[0]) * projected[1]).astype(low_type)
    small_down = jnp.dot(hidden, rank_in_down, preferred_element_type=float_type)
    weights_part = lax.all_gather(base_down, "dp", axis=1, tiled=True)
    out_part = rank_out_down
    mag_part = magnitude_down
    merged, column_norm = merge_norm(weights_part, rank_in_down, out_part)
    down_value = dora_front(hidden, small_down, weights_part, out_part) * (mag_part / column_norm)
    block_out = (residual + down_value).astype(low_type)[None]
    grad_result = out_cotangent[0].astype(float_type) * valid_rows
    weights_part = lax.all_gather(base_down, "dp", axis=1, tiled=True)
    grad_inputs = jnp.zeros((tokens, FF), float_type)
    out_part = rank_out_down
    mag_part = magnitude_down
    merged, column_norm = merge_norm(weights_part, rank_in_down, out_part)
    raw_value = dora_front(hidden, small_down, weights_part, out_part)
    pieces = dora_back(
        small_down,
        grad_result,
        weights_part,
        rank_in_down,
        out_part,
        mag_part,
        raw_value,
        merged,
        column_norm,
    )
    down_carry = (pieces[0], pieces[1], pieces[2], pieces[3], pieces[4])
    grad_rank_in_down, grad_hidden = finish_adapter(
        hidden, down_carry[1], rank_in_down, down_carry[0], down_carry[2]
    )

    def feed_fold(carry, weights_part):
        grad_inputs, grad_small, grad_rank_in, grad_rank_out, grad_magnitude = carry
        merged_list = []
        norm_list = []
        raw_list = []
        for member in range(2):
            merged, column_norm = merge_norm(
                weights_part[member], rank_in_feedforward[member], rank_out_feedforward[member]
            )
            merged_list.append(merged)
            norm_list.append(column_norm)
            raw_list.append(
                dora_front(
                    normed_feed,
                    smalls_feed[member],
                    weights_part[member],
                    rank_out_feedforward[member],
                )
            )
        gate_value = raw_list[0] * (magnitude_feedforward[0] / norm_list[0])
        up_value = raw_list[1] * (magnitude_feedforward[1] / norm_list[1])
        sigma_value = jax.nn.sigmoid(gate_value)
        grad_list = [
            grad_hidden * up_value * sigma_value * (1.0 + gate_value * (1.0 - sigma_value)),
            grad_hidden * gate_value * sigma_value,
        ]
        small_grads = []
        rank_in_grads = []
        rank_out_grads = []
        magnitude_grads = []
        for member in range(2):
            pieces = dora_back(
                smalls_feed[member],
                grad_list[member],
                weights_part[member],
                rank_in_feedforward[member],
                rank_out_feedforward[member],
                magnitude_feedforward[member],
                raw_list[member],
                merged_list[member],
                norm_list[member],
            )
            grad_inputs = grad_inputs + pieces[0]
            small_grads.append(pieces[1])
            rank_in_grads.append(pieces[2])
            rank_out_grads.append(pieces[3])
            magnitude_grads.append(pieces[4])
        return (
            grad_inputs,
            jnp.stack(small_grads),
            jnp.stack(rank_in_grads),
            jnp.stack(rank_out_grads),
            jnp.stack(magnitude_grads),
        )

    feed_start = (
        jnp.zeros((tokens, D), float_type),
        jnp.zeros((2, tokens, RANK), float_type),
        jnp.zeros((2, D, RANK), float_type),
        jnp.zeros((2, RANK, FF), float_type),
        jnp.zeros((2, FF), float_type),
    )
    feed_carry = feed_fold(feed_start, lax.all_gather(base_feedforward, "dp", axis=2, tiled=True))
    grad_normed_feed = feed_carry[0]
    feed_rank_in_grads = []
    for member in range(2):
        grad_one, grad_normed_feed = finish_adapter(
            normed_feed,
            feed_carry[1][member],
            rank_in_feedforward[member],
            grad_normed_feed,
            feed_carry[2][member],
        )
        feed_rank_in_grads.append(grad_one)
    feed_pull = jax.vjp(lambda values_in: rms_scaled(values_in, gain_feedforward), residual)[1]
    grad_residual = grad_result + feed_pull(grad_normed_feed)[0]
    attention_back, output_back = fetch_attention(base_attention, base_output)
    out_base, out_small, out_rank_norm, grad_rank_out_output, grad_magnitude_output = back_blocks(
        mixed_low,
        small_output,
        grad_residual,
        output_back,
        rank_in_output,
        rank_out_output,
        magnitude_output,
        output_kept,
    )
    grad_rank_in_output, grad_mixed = finish_adapter(
        mixed_low, out_small, rank_in_output, out_base, out_rank_norm
    )
    grad_mixed_low = grad_mixed.astype(low_type).reshape(query_shape)
    row_delta = jnp.einsum("tajd,tajd->ajt", grad_mixed_low.astype(float_type), mixed_heads)
    grad_queries, grad_keys_all, grad_values_all = attention_backward(
        queries, keys_all, values_all, query_pos, seq_length, log_total, grad_mixed_low, row_delta
    )
    grad_keys, grad_values = (
        lax.psum_scatter(
            grad_keys_all.reshape(-1, key_width).astype(jnp.bfloat16),
            "blk",
            scatter_dimension=0,
            tiled=True,
        ).astype(jnp.float32),
        lax.psum_scatter(
            grad_values_all.reshape(-1, key_width).astype(jnp.bfloat16),
            "blk",
            scatter_dimension=0,
            tiled=True,
        ).astype(jnp.float32),
    )
    query_pull = jax.vjp(
        lambda values_in: rotate(values_in, cosine_query, sine_query),
        query_raw.reshape(query_shape),
    )[1]
    grad_query_raw = query_pull(grad_queries)[0].reshape(tokens, -1)
    key_pull = jax.vjp(
        lambda values_in: rotate(values_in, cosine_key, sine_key), key_raw.reshape(key_shape)
    )[1]
    grad_key_raw = key_pull(grad_keys.reshape(key_shape))[0].reshape(tokens, -1)
    query_back = back_blocks(
        normed,
        smalls_attention[0],
        grad_query_raw,
        attention_back[:groups],
        rank_in_attention[0],
        rank_out_attention[:groups],
        magnitude_attention[:groups],
        query_kept,
    )
    key_back = back_blocks(
        normed,
        smalls_attention[1],
        grad_key_raw,
        attention_back[groups : groups + 1],
        rank_in_attention[1],
        rank_out_attention[groups : groups + 1],
        magnitude_attention[groups : groups + 1],
        key_kept,
    )
    value_back = back_blocks(
        normed,
        smalls_attention[2],
        grad_values,
        attention_back[groups + 1 :],
        rank_in_attention[2],
        rank_out_attention[groups + 1 :],
        magnitude_attention[groups + 1 :],
        value_kept,
    )
    grad_normed = query_back[0] + key_back[0] + value_back[0]
    attention_rank_in_grads = []
    for member, back_parts in enumerate((query_back, key_back, value_back)):
        grad_one, grad_normed = finish_adapter(
            normed, back_parts[1], rank_in_attention[member], grad_normed, back_parts[2]
        )
        attention_rank_in_grads.append(grad_one)
    attention_pull = jax.vjp(lambda values_in: rms_scaled(values_in, gain_attention), rows_in)[1]
    input_grad = (grad_residual + attention_pull(grad_normed)[0]).astype(low_type)[None]
    summed = lax.psum(
        (
            jnp.stack(attention_rank_in_grads),
            jnp.concatenate([query_back[3], key_back[3], value_back[3]], axis=0),
            jnp.concatenate([query_back[4], key_back[4], value_back[4]], axis=0),
            grad_rank_in_output,
            grad_rank_out_output,
            grad_magnitude_output,
            jnp.stack(feed_rank_in_grads),
            feed_carry[3],
            feed_carry[4],
            grad_rank_in_down,
            down_carry[3],
            down_carry[4],
        ),
        ("dp", "blk"),
    )
    return (block_out, input_grad) + tuple(summed)


def solution(mesh):
    placed = (
        P("dp", "blk", None),
        P("dp", "blk", None),
        P("dp"),
        P("dp", "blk"),
        P(),
        P(),
        P(None, None, "dp"),
        P(None, None, "dp"),
        P(None, None, "dp"),
        P(None, "dp"),
        P(),
        P(),
        P(),
        P(),
        P(),
        P(),
        P(),
        P(),
        P(),
        P(),
        P(),
        P(),
    )
    return jax.shard_map(
        shards,
        mesh=mesh,
        in_specs=placed,
        out_specs=(
            P("dp", "blk", None),
            P("dp", "blk", None),
            P(),
            P(),
            P(),
            P(),
            P(),
            P(),
            P(),
            P(),
            P(),
            P(),
            P(),
            P(),
        ),
        check_vma=False,
    )
```

profile of v0, /device:TPU:1, one launch (start us, length us, event | category | flops | bytes accessed | tf_op | source)
XLA Modules:
  0.0 1595.3 jit_solution(1355920798640270442)
XLA Ops:
  17.3 67.3 %all-gather.7.cloned.1.call-done = bf16[6,2048,512]{1,2,0:T(8,128)(2,1)} async-done(((bf16[6,2048,64]{1,2,0:T(8,128)(2,1)}), bf16[6,2048,512]{1,2,0:T(8,128)(2,1)}) %all-gather.7.cloned.1.call-update) | async-done | bytes 12582928 | tf_op jit(solution)/shard_map/all_gather | solution.py:151
  84.6 8.9 fusion.605
  93.6 4.1 copy.142
  115.9 4.7 multiply_reduce_fusion.12
  151.7 11.7 copy.105
  170.1 27.7 %fusion.606 = (bf16[1,2048,512]{1,0,2:T(2,128)(2,1)}, bf16[1,2048,512]{1,0,2:T(2,128)(2,1)}, bf16[1,2048,512]{1,0,2:T(2,128)(2,1)}, bf16[1,2048,512]{1,0,2:T(2,128)(2,1)}) fusion(bf16[4,2048,512]{1,0,2:T(4,128)(2,1)} %all-gather.13.cloned.1.call-done), kind=kLoop, calls=%fused_computation.749 | loop fusion | bytes 16777216 | tf_op jit(solution)/shard_map/slice | solution.py:108
  197.8 10.5 copy.146
  208.3 10.8 copy.147
  219.1 9.0 copy.149
  228.1 10.9 copy.148
  239.0 4.8 multiply_reduce_fusion.8
  273.6 21.7 %while.48 = (s32[]{:T(128)}, f32[4,4,256]{2,0,1:T(4,128)S(1)}, f32[4,4,256]{2,0,1:T(4,128)S(1)}, s32[]{:T(128)}, bf16[1024,4,128]{2,0,1:T(8,128)(2,1)S(1)}, /*in...) while((s32[]{:T(128)}, f32[4,4,256]{2,0,1:T(4,128)S(1)}, ...), condition=%wide.region_9.0_spmd.clone, body=%wide.region_6.9_spmd.clone.sunk | while | flops 551835392 | bytes 18963648 | solution.py:199
  274.7 4.7 fusion.734
  279.4 5.1 fusion.735
  285.5 4.7 fusion.734
  290.2 5.1 fusion.735
  296.0 14.7 while.49
  298.4 4.5 bitcast_add_fusion.5
  305.3 5.4 bitcast_add_fusion.5
  326.7 25.3 %multiply_reduce_fusion = (f32[2048]{0:T(1024)S(1)}, f32[5632,2048]{1,0:T(8,128)}) fusion(bf16[5632,16]{0,1:T(8,128)(2,1)S(1)} %copy-done, bf16[16,2048]{1,0:T(8,128)(2,1)S(1)} %copy-done.94, bf16[5632,2048]{1,0:T(8,128)(2,1)} %all-gather.17.cloned.1.call-done), kind=kOutput, calls=%fused_computation.82 | convolution fusion | flops 426768384 | bytes 69459968 | tf_op jit(solution)/shard_map/dot_general | solution.py:44
  353.4 13.2 fusion.345
  366.7 6.0 convolution_add_fusion
  372.7 167.1 %all-gather.15.cloned.1.call-done = bf16[2,2048,5632]{1,0,2:T(2,128)(2,1)} async-done(((bf16[2,2048,704]{1,0,2:T(2,128)(2,1)}), bf16[2,2048,5632]{1,0,2:T(2,128)(2,1)}) %all-gather.15.cloned.1.call-update) | async-done | bytes 46137360 | tf_op jit(solution)/shard_map/all_gather | solution.py:378
  539.8 85.9 %fusion.604 = (bf16[1,2048,5632]{1,0,2:T(2,128)(2,1)}, bf16[1,2048,5632]{1,0,2:T(2,128)(2,1)}) fusion(bf16[2,2048,5632]{1,0,2:T(2,128)(2,1)} %all-gather.15.cloned.1.call-done), kind=kLoop, calls=%fused_computation.747 | loop fusion | bytes 92274688 | tf_op jit(solution)/shard_map/slice | solution.py:389
  625.7 90.3 %copy.151 = bf16[1,2048,5632]{2,1,0:T(8,128)(2,1)} copy(bf16[1,2048,5632]{1,0,2:T(2,128)(2,1)} %get-tuple-element.777) | data formatting | bytes 46137344
  716.0 13.2 fusion.74
  729.2 24.2 %multiply_reduce_fusion.1 = (f32[5632]{0:T(1024)S(1)}, f32[2048,5632]{1,0:T(8,128)}) fusion(bf16[2,16,5632]{2,1,0:T(8,128)(2,1)S(1)} %copy-done.59, bf16[2,2048,16]{1,2,0:T(8,128)(2,1)S(1)} %copy-done.62, bf16[1,2048,5632]{2,1,0:T(8,128)(2,1)} %copy.151), kind=kOutput, calls=%fused_computation.84 | convolution fusion | flops 426764800 | bytes 69474304 | tf_op jit(solution)/shard_map/dot_general | solution.py:44
  753.4 90.3 %copy.150 = bf16[1,2048,5632]{2,1,0:T(8,128)(2,1)} copy(bf16[1,2048,5632]{1,0,2:T(2,128)(2,1)} %get-tuple-element.776) | data formatting | bytes 46137344
  843.8 23.8 %multiply_reduce_fusion.2 = (f32[5632]{0:T(1024)S(1)}, f32[2048,5632]{1,0:T(8,128)}) fusion(bf16[2,16,5632]{2,1,0:T(8,128)(2,1)S(1)} %copy-done.59, bf16[2,2048,16]{1,2,0:T(8,128)(2,1)S(1)} %copy-done.62, bf16[1,2048,5632]{2,1,0:T(8,128)(2,1)} %copy.150), kind=kOutput, calls=%fused_computation.86 | convolution fusion | flops 426764800 | bytes 69474304 | tf_op jit(solution)/shard_map/dot_general | solution.py:44
  867.5 10.7 fusion.78
  878.9 5.5 fusion.84
  884.6 12.1 multiply_reduce_fusion.4
  896.7 14.5 fusion.72
  911.2 6.2 fusion.331
  920.9 14.2 fusion.134
  939.0 10.8 fusion.609
  974.1 53.8 %while.50 = (s32[]{:T(128)}, f32[256,4,4,128]{0,3,1,2:T(8,128)S(1)}, f32[1024,4,128]{0,2,1:T(8,128)}, f32[1024,4,128]{2,0,1:T(8,128)}, bf16[1024,4,128]{2,0,1:T(...) while((s32[]{:T(128)}, ...), condition=%wide.region_23.24_spmd.clone, body=%wide.region_22.23_spmd.clone.sunk | while | flops 2707949312 | bytes 128900504 | solution.py:286
  994.3 6.7 fusion.753
  1006.6 4.0 fusion.751
  1021.2 6.7 fusion.753
  1048.6 29.4 %fusion.177 = f32[2048,16]{0,1:T(8,128)} fusion(f32[2048,5632]{1,0:T(8,128)} %get-tuple-element.897, f32[5632]{0:T(1024)S(1)} %get-tuple-element.674, bf16[2,16,5632]{2,1,0:T(8,128)(2,1)S(1)} %copy-done.60), kind=kOutput, calls=%fused_computation.230 | convolution fusion | flops 2226159616 | bytes 46473216 | tf_op jit(solution)/shard_map/dot_general | solution.py:85
  1078.0 20.9 %fusion.88 = f32[16,5632]{1,0:T(8,128)} fusion(f32[2048,5632]{1,0:T(8,128)} %get-tuple-element.897, f32[5632]{0:T(1024)S(1)} %get-tuple-element.674, bf16[2,2048,16]{1,2,0:T(8,128)(2,1)S(1)} %copy-done.63), kind=kOutput, calls=%fused_computation.112 | convolution fusion | flops 2214682624 | bytes 46587904 | tf_op jit(solution)/shard_map/dot_general | solution.py:83
  1098.9 29.6 %fusion.174 = f32[2048,16]{0,1:T(8,128)} fusion(f32[2048,5632]{1,0:T(8,128)} %get-tuple-element.895, f32[5632]{0:T(1024)S(1)} %get-tuple-element.673, bf16[2,16,5632]{2,1,0:T(8,128)(2,1)S(1)} %copy-done.60), kind=kOutput, calls=%fused_computation.229 | convolution fusion | flops 2226159616 | bytes 46473216 | tf_op jit(solution)/shard_map/dot_general | solution.py:85
  1128.5 21.1 %fusion.87 = f32[16,5632]{1,0:T(8,128)} fusion(f32[2048,5632]{1,0:T(8,128)} %get-tuple-element.895, f32[5632]{0:T(1024)S(1)} %get-tuple-element.673, bf16[2,2048,16]{1,2,0:T(8,128)(2,1)S(1)} %copy-done.63), kind=kOutput, calls=%fused_computation.111 | convolution fusion | flops 2214682624 | bytes 46587904 | tf_op jit(solution)/shard_map/dot_general | solution.py:83
  1187.1 20.6 %fusion.180 = f32[16,2048]{1,0:T(8,128)S(1)} fusion(f32[5632,2048]{1,0:T(8,128)} %get-tuple-element.899, bf16[5632,16]{0,1:T(8,128)(2,1)S(1)} %copy-done, f32[2048]{0:T(1024)S(1)} %get-tuple-element.809), kind=kOutput, calls=%fused_computation.232 | convolution fusion | flops 2214625280 | bytes 46456832 | tf_op jit(solution)/shard_map/dot_general | solution.py:83
  1212.8 26.5 %fusion.91 = f32[5632,16]{0,1:T(8,128)S(1)} fusion(bf16[16,2048]{1,0:T(8,128)(2,1)S(1)} %copy-done.96, f32[5632,2048]{1,0:T(8,128)} %get-tuple-element.899, f32[2048]{0:T(1024)S(1)} %get-tuple-element.809), kind=kOutput, calls=%fused_computation.115 | convolution fusion | flops 2226216960 | bytes 46571520 | tf_op jit(solution)/shard_map/dot_general | solution.py:85
  1311.8 116.0 %all-reduce.9.cloned.1.call-done = (f32[6,512]{1,0:T(8,128)}, f32[4,512]{1,0:T(4,128)}, f32[2,5632]{1,0:T(2,128)}, f32[2048]{0:T(1024)}) async-done(((f32[6,512]{1,0:T(8,128)}, f32[4,512]{1,0:T(4,128)}, f32[2,5632]{1,0:T(2,128)}, f32[2048]{0:T(1024)}), (f32[6,512]{1,0:T(8,128)}, f32[4,512]{1,0:T(4,128)}, f32[2,5632]{1,0:T(2,128)}, f32[2048]{0:T(1024)})) %all-reduce.9.cloned.1.call-update) | async-done | bytes 73744 | tf_op jit(solution)/shard_map/psum | solution.py:581
  1427.8 145.0 %all-reduce.11.cloned.1.call-done = (f32[3,2048,16]{1,2,0:T(8,128)}, f32[6,16,512]{2,1,0:T(8,128)}, f32[2048,16]{0,1:T(8,128)}, f32[4,16,512]{2,1,0:T(8,128)}, f...) async-done(((f32[3,2048,16]{1,2,0:T(8,128)}, f32[6,16,512]{2,1,0:T(8,128)}, f32[2048,16]{0,1:T(8,128)}, ...) | async-done | bytes 2326544 | tf_op jit(solution)/shard_map/psum | solution.py:581
  (838 shorter events, 337.2 us)
Async XLA Ops:
  7.2 319.5 %copy-start = (bf16[5632,16]{0,1:T(8,128)(2,1)S(1)}, bf16[5632,16]{0,1:T(8,128)(2,1)}, u32[]{:S(2)}) copy-start(bf16[5632,16]{0,1:T(8,128)(2,1)} %param.47) | copy-start | bytes 540676
  7.2 77.4 %all-gather.7.cloned.1.call-start = ((), (), s32[]{:S(2)}) async-start(), calls=%async_computation.2 | async-start | bytes 14155776 | tf_op jit(solution)/shard_map/all_gather | solution.py:151
  8.0 162.1 %all-gather.13.cloned.1.call-start = ((), (), s32[]{:S(2)}) async-start(), calls=%async_computation.5 | async-start | bytes 9437184 | tf_op jit(solution)/shard_map/all_gather | solution.py:152
  11.0 259.0 %all-gather.9.cloned.1.call-start = ((), (), s32[]{:S(2)}) async-start(), calls=%async_computation.3 | async-start | bytes 1310720 | tf_op jit(solution)/shard_map/all_gather | solution.py:362
  121.2 17.8 %copy-start.209 = (f32[512]{0:T(512)}, f32[512]{0:T(512)S(1)}, u32[]{:S(2)}) copy-start(f32[512]{0:T(512)S(1)} %get-tuple-element.843) | copy-start | bytes 6148
  124.8 14.2 copy-start.211
  142.9 129.3 %all-gather.11.cloned.1.call-start = ((), (), s32[]{:S(2)}) async-start(), calls=%async_computation.4 | async-start | bytes 1310720 | tf_op jit(solution)/shard_map/all_gather | solution.py:361
  151.1 175.6 %all-gather.17.cloned.1.call-start = ((), (), s32[]{:S(2)}) async-start(), calls=%async_computation.7 | async-start | bytes 25952256 | tf_op jit(solution)/shard_map/all_gather | solution.py:395
  151.7 388.1 %all-gather.15.cloned.1.call-start = ((), (), s32[]{:S(2)}) async-start(), calls=%async_computation.6 | async-start | bytes 51904512 | tf_op jit(solution)/shard_map/all_gather | solution.py:378
  163.5 1102.9 %reduce-scatter.3.cloned.1.call-start = ((), (), s32[]{:S(2)}) async-start(), calls=%async_computation.8 | async-start | bytes 1310720 | tf_op jit(solution)/shard_map/reduce_scatter | solution.py:520
  165.2 32.6 %copy-start.78 = (f32[256,16]{0,1:T(8,128)}, f32[256,16]{0,1:T(8,128)S(1)}, u32[]{:S(2)}) copy-start(f32[256,16]{0,1:T(8,128)S(1)} %fusion.465) | copy-start | bytes 49156
  228.1 19.8 %copy-start.33 = (bf16[1,2048,512]{2,1,0:T(8,128)(2,1)}, bf16[1,2048,512]{2,1,0:T(8,128)(2,1)S(1)}, u32[]{:S(2)}) copy-start(bf16[1,2048,512]{2,1,0:T(8,128)(2,1)S(1)} %copy.149) | copy-start | bytes 6291460
  228.1 10.9 copy-start.56
  228.1 10.9 copy-start.84
  239.0 17.5 %slice-start = ((s8[12582912]{0:T(1024)(128)(4,1)}), s8[4194304]{0:T(1024)(128)(4,1)S(1)}, s32[]{:S(2)}) async-start(s8[12582912]{0:T(1024)(128)(4,1)} %bitcast.903), calls=%async_computation.12 | async-start | bytes 8388608
  244.4 11.5 copy-start.221
  244.4 12.1 slice-start.1
  326.7 25.3 %copy-start.194 = (f32[2048]{0:T(1024)S(1)}, f32[2048]{0:T(1024)}, u32[]{:S(2)}) copy-start(f32[2048]{0:T(1024)} %param.49) | copy-start | bytes 24580
  326.7 25.3 %copy-start.88 = (bf16[1,256,2048]{2,1,0:T(8,128)(2,1)S(1)}, bf16[1,256,2048]{2,1,0:T(8,128)(2,1)}, u32[]{:S(2)}) copy-start(bf16[1,256,2048]{2,1,0:T(8,128)(2,1)} %param.29) | copy-start | bytes 3145732
  326.7 25.3 %copy-start.259 = (f32[256]{0:T(256)S(1)}, f32[256]{0:T(256)}, u32[]{:S(2)}) copy-start(f32[256]{0:T(256)} %compare_convert_fusion) | copy-start | bytes 3076
  352.0 14.6 copy-start.149
  352.1 14.6 copy-start.190
  353.4 13.3 copy-start.178
  716.0 13.2 copy-start.59
  867.5 11.4 copy-start.120
  884.6 12.1 copy-start.109
  884.6 12.1 copy-start.112
  896.7 42.2 %copy-start.45 = (bf16[256,5632]{1,0:T(8,128)(2,1)}, bf16[256,5632]{1,0:T(8,128)(2,1)S(1)}, u32[]{:S(2)}) copy-start(bf16[256,5632]{1,0:T(8,128)(2,1)S(1)} %get-tuple-element.786) | copy-start | bytes 8650756
  920.9 14.2 copy-start.143
  938.9 10.9 copy-start.153
  938.9 10.9 copy-start.89
  938.9 10.9 copy-start.95
  1048.6 29.4 %copy-start.63 = (bf16[2,2048,16]{1,2,0:T(8,128)(2,1)S(1)}, bf16[2,2048,16]{1,2,0:T(8,128)(2,1)}, u32[]{:S(2)}) copy-start(bf16[2,2048,16]{1,2,0:T(8,128)(2,1)} %param.44) | copy-start | bytes 393220
  1128.5 21.1 %copy-start.16 = (f32[1024,4,128]{0,2,1:T(8,128)S(1)}, f32[1024,4,128]{0,2,1:T(8,128)}, u32[]{:S(2)}) copy-start(f32[1024,4,128]{0,2,1:T(8,128)} %get-tuple-element.483) | copy-start | bytes 6291460
  1150.7 123.7 %reduce-scatter.5.cloned.1.call-start = ((), (), s32[]{:S(2)}) async-start(), calls=%async_computation.9 | async-start | bytes 1310720 | tf_op jit(solution)/shard_map/reduce_scatter | solution.py:526
  1167.8 11.7 slice-start.5
  1187.1 20.6 %copy-start.90 = (bf16[1,256,2048]{2,1,0:T(8,128)(2,1)S(1)}, bf16[1,256,2048]{2,1,0:T(8,128)(2,1)}, u32[]{:S(2)}) copy-start(bf16[1,256,2048]{2,1,0:T(8,128)(2,1)} %param.29) | copy-start | bytes 3145732
  1187.1 20.6 %copy-start.154 = (f32[256,16]{0,1:T(8,128)S(1)}, f32[256,16]{0,1:T(8,128)}, u32[]{:S(2)}) copy-start(f32[256,16]{0,1:T(8,128)} %copy-done.153) | copy-start | bytes 49156
  1187.1 20.6 %copy-start.192 = (f32[2048]{0:T(1024)S(1)}, f32[2048]{0:T(1024)}, u32[]{:S(2)}) copy-start(f32[2048]{0:T(1024)} %copy-done.190) | copy-start | bytes 24580
  1187.1 20.6 %copy-start.261 = (f32[256]{0:T(256)S(1)}, f32[256]{0:T(256)}, u32[]{:S(2)}) copy-start(f32[256]{0:T(256)} %compare_convert_fusion) | copy-start | bytes 3076
  1187.1 22.7 %copy-start.92 = (f32[2048,16]{0,1:T(8,128)S(1)}, f32[2048,16]{0,1:T(8,128)}, u32[]{:S(2)}) copy-start(f32[2048,16]{0,1:T(8,128)} %fusion.174) | copy-start | bytes 393220
  1187.1 22.7 %copy-start.144 = (bf16[256,16]{0,1:T(8,128)(2,1)S(1)}, bf16[256,16]{0,1:T(8,128)(2,1)}, u32[]{:S(2)}) copy-start(bf16[256,16]{0,1:T(8,128)(2,1)} %fusion.334) | copy-start | bytes 24580
  1239.4 188.3 %all-reduce.9.cloned.1.call-start = ((), (), s32[]{:S(2)}) async-start(), calls=%async_computation.10 | async-start | bytes 155648 | tf_op jit(solution)/shard_map/psum | solution.py:581
  1306.1 266.7 %all-reduce.11.cloned.1.call-start = ((), (), s32[]{:S(2)}) async-start(), calls=%async_computation.11 | async-start | bytes 4653056 | tf_op jit(solution)/shard_map/psum | solution.py:581
  1427.8 157.9 %copy-start.164 = (f32[2,5632]{1,0:T(2,128)S(1)}, f32[2,5632]{1,0:T(2,128)}, u32[]{:S(2)}) copy-start(f32[2,5632]{1,0:T(2,128)} %get-tuple-element.1202) | copy-start | bytes 135172
  1427.8 159.9 %copy-start.254 = (f32[2048]{0:T(1024)S(1)}, f32[2048]{0:T(1024)}, u32[]{:S(2)}) copy-start(f32[2048]{0:T(1024)} %get-tuple-element.1205) | copy-start | bytes 24580
  1572.8 13.5 copy-start.107
  1572.8 14.2 copy-start.138
  (238 other events, 965.4 us)
Sparse Core Ops, SparseCore 0:
  10.0 74.6 all-gather.6
  87.1 54.3 all-gather.12
  143.7 27.3 all-gather.8
  173.1 27.4 all-gather.10
  202.2 121.0 all-gather.16
  325.1 214.6 all-gather.14
  1150.8 26.5 reduce-scatter.2
  1239.6 26.5 reduce-scatter.4
  1306.2 121.4 all-reduce.8
  1435.2 137.5 all-reduce.10
where the time goes:
time: 1610 us; the launch traced here: 1600 us
  matrix products  567 us (35%)
  waiting for transfers between devices  497 us (31%)
  local copies, waits for them, and re-layouts  453 us (28%)
  other arithmetic  58.7 us (4%)
  between operations  17.8 us (1%)
    unnamed x558, local copies, waits for them, and re-layouts  291 us
    psum x2, waiting for transfers between devices, shards(): lax.psum((jnp.stack(attention_rank_in_grads), jnp.concatenate([query_back...  261 us
    all_gather x1, waiting for transfers between devices, shards(): weights_part = lax.all_gather(base_feedforward, 'dp', axis=2, tiled=True)  167 us
    dot_general x13, matrix products, dora_back(): lax.dot_general(merged * norm_coeff[None, :], rank_out_wide, contract_las...  109 us
    dot_general x13, matrix products, merge_norm(): jnp.dot(rank_in, rank_out, preferred_element_type=float_type)  107 us
    slice x1, local copies, waits for them, and re-layouts, shards(): weights_part[feed_member]  85.9 us
    dot_general x13, matrix products, dora_back(): lax.dot_general(rank_in_wide, merged, contract_first, precision=highest)  79.7 us
    all_gather x1, waiting for transfers between devices, fetch_attention(): lax.all_gather(base_attention, 'dp', axis=2, tiled=True)  67.3 us
  transfers between devices with their start and end apart: 10, of which 4 were waited for; matrix products, arithmetic and copies ran while one was open for 26% of the time, Pallas kernels for 0%

commit v1 on v0

v1 whole, which is shorter than its diff:
```python
import functools

import jax
import jax.numpy as jnp
from jax import lax
from jax.experimental import pallas as pl
from jax.experimental.pallas import tpu as pltpu
from jax.sharding import PartitionSpec as P

D = 2048
KV_HEADS = 4
HEAD = 128
FF = 5632
RANK = 16
GROUP = 4
KVW = 512

factor = 32.0 / RANK
rms_eps = 1e-05
rope_base = 10000.0
masked_score = -1e30
log2_e = 1.4426950408889634
score_scale = HEAD ** (-0.5)
f32 = jnp.float32
bf16 = jnp.bfloat16


def dot_nt(left, right):
    return lax.dot_general(left, right, (((1,), (1,)), ((), ())), preferred_element_type=f32)


def dot_nn(left, right):
    return lax.dot_general(left, right, (((1,), (0,)), ((), ())), preferred_element_type=f32)


def dot_tn(left, right):
    return lax.dot_general(left, right, (((0,), (0,)), ((), ())), preferred_element_type=f32)


def fold_kernel(weight_ref, rank_in_ref, rank_out_ref, mag_ref, out_ref, norm_ref, proj_ref, merged_ref, *, chunk):
    inputs, columns = weight_ref.shape[1], weight_ref.shape[2]
    row = lax.broadcasted_iota(jnp.int32, (columns, columns), 0)
    col = lax.broadcasted_iota(jnp.int32, (columns, columns), 1)
    eye = jnp.where(row == col, 1.0, 0.0).astype(bf16)

    def merge(index, total):
        part = pl.ds(pl.multiple_of(index * chunk, chunk), chunk)
        merged = dot_nt(eye, weight_ref[0, part, :]) + dot_nt(rank_out_ref[0], rank_in_ref[0, part, :])
        merged_ref[:, part] = merged
        return total + jnp.sum(merged * merged, axis=1, keepdims=True)

    total = lax.fori_loop(0, inputs // chunk, merge, jnp.zeros((columns, 1), f32))
    norm = jnp.sqrt(total)
    norm_ref[0] = norm
    scale = mag_ref[0] / norm

    def finish(index, proj):
        part = pl.ds(pl.multiple_of(index * chunk, chunk), chunk)
        folded = (merged_ref[:, part] * scale).astype(bf16)
        out_ref[0, :, part] = folded
        return proj + dot_nn(folded, rank_in_ref[0, part, :])

    proj_ref[0] = lax.fori_loop(0, inputs // chunk, finish, jnp.zeros((columns, RANK), f32))


def fold(weights, rank_in, rank_out, magnitude, rank_of, name):
    members, inputs, columns = weights.shape
    doubled = (factor * rank_out.astype(f32)).astype(bf16).transpose(0, 2, 1)
    return pl.pallas_call(
        functools.partial(fold_kernel, chunk=256),
        out_shape=(
            jax.ShapeDtypeStruct((members, columns, inputs), bf16),
            jax.ShapeDtypeStruct((members, columns, 1), f32),
            jax.ShapeDtypeStruct((members, columns, RANK), f32),
        ),
        grid=(members,),
        in_specs=[
            pl.BlockSpec((1, inputs, columns), lambda b: (b, 0, 0)),
            pl.BlockSpec((1, inputs, RANK), lambda b: (rank_of(b), 0, 0)),
            pl.BlockSpec((1, columns, RANK), lambda b: (b, 0, 0)),
            pl.BlockSpec((1, columns, 1), lambda b: (b, 0, 0)),
        ],
        out_specs=(
            pl.BlockSpec((1, columns, inputs), lambda b: (b, 0, 0)),
            pl.BlockSpec((1, columns, 1), lambda b: (b, 0, 0)),
            pl.BlockSpec((1, columns, RANK), lambda b: (b, 0, 0)),
        ),
        scratch_shapes=[pltpu.VMEM((columns, inputs), f32)],
        compiler_params=pltpu.CompilerParams(vmem_limit_bytes=48 << 20),
        name=name,
    )(weights, rank_in, doubled, magnitude[:, :, None])


def rope_kernel(x_ref, weight_ref, cos_ref, sin_ref, out_ref, *, plain_from):
    raw = dot_nt(x_ref[...], weight_ref[0])
    roped = pl.program_id(0) < plain_from
    for head in range(KVW // HEAD):
        part = raw[:, head * HEAD : (head + 1) * HEAD]
        turned = part * cos_ref[...] + pltpu.roll(part, HEAD // 2, 1) * sin_ref[...]
        out_ref[:, head * HEAD : (head + 1) * HEAD] = jnp.where(roped, turned, part).astype(bf16)


def project_rope(inputs, weights, cosine, sine, plain_from, name):
    tokens = inputs.shape[0]
    blocks = weights.shape[0]
    return pl.pallas_call(
        functools.partial(rope_kernel, plain_from=plain_from),
        out_shape=jax.ShapeDtypeStruct((tokens, blocks * KVW), bf16),
        grid=(blocks,),
        in_specs=[
            pl.BlockSpec((tokens, D), lambda b: (0, 0)),
            pl.BlockSpec((1, KVW, D), lambda b: (b, 0, 0)),
            pl.BlockSpec((tokens, HEAD), lambda b: (0, 0)),
            pl.BlockSpec((tokens, HEAD), lambda b: (0, 0)),
        ],
        out_specs=pl.BlockSpec((tokens, KVW), lambda b: (0, b)),
        compiler_params=pltpu.CompilerParams(vmem_limit_bytes=32 << 20),
        name=name,
    )(inputs, weights, cosine, sine)


def lane_block(start, head):
    return pl.ds(pl.multiple_of(start + head * HEAD, HEAD), HEAD)


def masked_scores(keys, queries, key_first, length, causal):
    tokens, lanes = keys.shape[0], queries.shape[0]
    scores = dot_nt(keys, queries)
    key_pos = key_first + lax.broadcasted_iota(jnp.int32, (tokens, 1), 0)
    scores = scores + jnp.where(key_pos < length, 0.0, masked_score)
    if causal:
        key_index = lax.broadcasted_iota(jnp.int32, (tokens, lanes), 0)
        token_index = lax.broadcasted_iota(jnp.int32, (tokens, lanes), 1) & (tokens - 1)
        scores = jnp.where(key_index <= token_index, scores, masked_score)
    return scores


def attend_kernel(scalar_ref, query_ref, *refs, steps):
    kv_refs = refs[:steps]
    mixed_ref, lse_ref, stacked_ref, max_ref, sum_ref, accum_ref = refs[steps:]
    head = pl.program_id(0)
    tokens = query_ref.shape[0]
    block_index, length = scalar_ref[0], scalar_ref[1]
    scale = score_scale * log2_e
    for group in range(GROUP):
        stacked_ref[group * tokens : (group + 1) * tokens, :] = query_ref[:, lane_block(group * KVW, head)]

    for distance in range(steps):

        def step(distance=distance):
            keys = kv_refs[distance][:, lane_block(0, head)]
            values = kv_refs[distance][:, lane_block(KVW, head)]
            key_first = (block_index - distance) * tokens
            scores = masked_scores(keys, stacked_ref[...], key_first, length, distance == 0)
            block_max = jnp.max(scores, axis=0, keepdims=True)
            new_max = block_max if distance == 0 else jnp.maximum(max_ref[...], block_max)
            terms = jnp.exp2((scores - new_max) * scale)
            added = jnp.sum(terms, axis=0, keepdims=True)
            product = dot_tn(values, terms.astype(bf16))
            if distance == 0:
                sum_ref[...] = added
                accum_ref[...] = product
            else:
                fade = jnp.exp2((max_ref[...] - new_max) * scale)
                sum_ref[...] = sum_ref[...] * fade + added
                accum_ref[...] = accum_ref[...] * fade + product
            max_ref[...] = new_max

        if distance == 0:
            step()
        else:
            pl.when(block_index >= distance)(step)
    mixed = accum_ref[...] / sum_ref[...]
    for group in range(GROUP):
        part = mixed[:, group * tokens : (group + 1) * tokens]
        mixed_ref[:, lane_block(group * KVW, head)] = part.T.astype(bf16)
    lse_ref[0] = max_ref[...] * scale + jnp.log(sum_ref[...]) * log2_e


def attend(scalars, queries, kv_blocks):
    tokens = queries.shape[0]
    steps = len(kv_blocks)
    lanes = GROUP * tokens
    whole = lambda *shape: pl.BlockSpec(shape, lambda j, s: (0,) * len(shape))
    return pl.pallas_call(
        functools.partial(attend_kernel, steps=steps),
        out_shape=(
            jax.ShapeDtypeStruct((tokens, D), bf16),
            jax.ShapeDtypeStruct((KV_HEADS, 1, lanes), f32),
        ),
        grid_spec=pltpu.PrefetchScalarGridSpec(
            num_scalar_prefetch=1,
            grid=(KV_HEADS,),
            in_specs=[whole(tokens, D)] + [whole(tokens, 2 * KVW)] * steps,
            out_specs=(whole(tokens, D), pl.BlockSpec((1, 1, lanes), lambda j, s: (j, 0, 0))),
            scratch_shapes=[
                pltpu.VMEM((lanes, HEAD), bf16),
                pltpu.VMEM((1, lanes), f32),
                pltpu.VMEM((1, lanes), f32),
                pltpu.VMEM((HEAD, lanes), f32),
            ],
        ),
        compiler_params=pltpu.CompilerParams(vmem_limit_bytes=48 << 20),
        name="attend",
    )(scalars, queries, *kv_blocks)


def attend_back_kernel(scalar_ref, query_ref, grad_ref, lse_ref, delta_ref, kv_ref, *refs, distance, chained):
    if chained:
        sent_ref, before_ref, grad_query_ref, grad_kv_ref, stacked_ref, stacked_grad_ref = refs
    else:
        grad_query_ref, grad_kv_ref, stacked_ref, stacked_grad_ref = refs
    head = pl.program_id(0)
    tokens = query_ref.shape[0]
    block_index, length = scalar_ref[0], scalar_ref[1]
    active = (block_index >= distance) & (block_index * tokens < length)
    key_lanes, value_lanes = lane_block(0, head), lane_block(KVW, head)

    @pl.when(active)
    def _():
        for group in range(GROUP):
            rows = slice(group * tokens, (group + 1) * tokens)
            stacked_ref[rows, :] = query_ref[:, lane_block(group * KVW, head)]
            stacked_grad_ref[rows, :] = grad_ref[:, lane_block(group * KVW, head)]
        keys = kv_ref[:, key_lanes]
        values = kv_ref[:, value_lanes]
        key_first = (block_index - distance) * tokens
        scores = masked_scores(keys, stacked_ref[...], key_first, length, distance == 0)
        probs = jnp.exp2(scores * (score_scale * log2_e) - lse_ref[0])
        grad_probs = dot_nt(values, stacked_grad_ref[...])
        grad_scores = (probs * (grad_probs - delta_ref[0])).astype(bf16)
        grad_values = dot_nn(probs.astype(bf16), stacked_grad_ref[...])
        grad_keys = dot_nn(grad_scores, stacked_ref[...]) * score_scale
        grad_queries = dot_tn(grad_scores, keys) * score_scale
        for group in range(GROUP):
            lanes = lane_block(group * KVW, head)
            part = grad_queries[group * tokens : (group + 1) * tokens, :]
            if chained:
                part = part + before_ref[:, lanes]
            grad_query_ref[:, lanes] = part
        if chained:
            grad_keys = grad_keys + sent_ref[:, key_lanes].astype(f32)
            grad_values = grad_values + sent_ref[:, value_lanes].astype(f32)
        grad_kv_ref[:, key_lanes] = grad_keys.astype(grad_kv_ref.dtype)
        grad_kv_ref[:, value_lanes] = grad_values.astype(grad_kv_ref.dtype)

    @pl.when(jnp.logical_not(active))
    def _():
        for group in range(GROUP):
            lanes = lane_block(group * KVW, head)
            if chained:
                grad_query_ref[:, lanes] = before_ref[:, lanes]
            else:
                grad_query_ref[:, lanes] = jnp.zeros((tokens, HEAD), f32)
        for lanes in (key_lanes, value_lanes):
            if chained:
                grad_kv_ref[:, lanes] = sent_ref[:, lanes].astype(grad_kv_ref.dtype)
            else:
                grad_kv_ref[:, lanes] = jnp.zeros((tokens, HEAD), grad_kv_ref.dtype)


def attend_back(scalars, queries, grad_mixed, lse, delta, kv_block, sent, before, distance):
    tokens = queries.shape[0]
    lanes = GROUP * tokens
    whole = lambda *shape: pl.BlockSpec(shape, lambda j, s: (0,) * len(shape))
    row = pl.BlockSpec((1, 1, lanes), lambda j, s: (j, 0, 0))
    chained = before is not None
    operands = [scalars, queries, grad_mixed, lse, delta, kv_block]
    specs = [whole(tokens, D), whole(tokens, D), row, row, whole(tokens, 2 * KVW)]
    if chained:
        operands += [sent, before]
        specs += [whole(tokens, 2 * KVW), whole(tokens, D)]
    return pl.pallas_call(
        functools.partial(attend_back_kernel, distance=distance, chained=chained),
        out_shape=(
            jax.ShapeDtypeStruct((tokens, D), f32),
            jax.ShapeDtypeStruct((tokens, 2 * KVW), f32 if distance == 0 else bf16),
        ),
        grid_spec=pltpu.PrefetchScalarGridSpec(
            num_scalar_prefetch=1,
            grid=(KV_HEADS,),
            in_specs=specs,
            out_specs=(whole(tokens, D), whole(tokens, 2 * KVW)),
            scratch_shapes=[pltpu.VMEM((lanes, HEAD), bf16), pltpu.VMEM((lanes, HEAD), bf16)],
        ),
        input_output_aliases={7: 0} if chained else {},
        compiler_params=pltpu.CompilerParams(vmem_limit_bytes=48 << 20),
        name=f"attend_back_{distance}",
    )(*operands)


def rms_parts(values, gain):
    inverse = lax.rsqrt(jnp.mean(values * values, axis=-1, keepdims=True) + rms_eps)
    return (values * inverse * gain).astype(bf16), inverse


def rms_back(values, inverse, gain, grad):
    scaled = grad * gain
    return inverse * (scaled - values * (inverse * inverse * jnp.mean(scaled * values, axis=-1, keepdims=True)))


class Links:
    def __init__(self, devices):
        self.devices = devices
        self.chips = devices // 2
        self.index = lax.axis_index("dp")
        self.core = self.index % 2
        self.square = self.chips == 4

    def swap(self, value, bits):
        return lax.ppermute(value, "dp", [(i, i ^ bits) for i in range(self.devices)])

    def split_swap(self, value, even_bits, odd_bits):
        return lax.ppermute(
            value, "dp", [(i, i ^ (odd_bits if i % 2 else even_bits)) for i in range(self.devices)]
        )

    def chip_gather(self, value):
        if not self.square:
            return [value] + [self.swap(value, 2 * r) for r in range(1, self.chips)]
        side = self.swap(value, 2)
        other = self.swap(value, 4)
        across = self.split_swap(jnp.where(self.core == 0, other, side), 2, 4)
        return [value, side, other, across]

    def chip_reduce(self, shares):
        add = lambda *parts: sum(part.astype(f32) for part in parts)
        if not self.square:
            return add(shares[0], *[self.swap(shares[r], 2 * r) for r in range(1, self.chips)])
        across = self.split_swap(shares[3], 2, 4)
        first = self.split_swap(jnp.where(self.core == 0, shares[1], shares[2]), 2, 4)
        late = jnp.where(self.core == 0, shares[2], shares[1])
        second = self.split_swap(add(late, across).astype(bf16), 4, 2)
        return add(shares[0], first, second)

    def gather(self, value):
        entries = [None] * self.devices
        for r, piece in enumerate(self.chip_gather(value)):
            entries[2 * r] = piece
            entries[2 * r + 1] = self.swap(piece, 1)
        return entries

    def gather_rows(self, value):
        groups, rows, width = value.shape
        whole = jnp.zeros((groups, self.devices, rows, width), value.dtype)
        for i, piece in enumerate(self.gather(value)):
            whole = lax.dynamic_update_slice(whole, piece[:, None], (0, self.index ^ i, 0, 0))
        return whole.reshape(groups, self.devices * rows, width)


def after(value, *others):
    return lax.optimization_barrier((value,) + others)[0]


def shards(
    block_input,
    out_cotangent,
    row_lengths,
    rope_positions,
    gain_attention,
    gain_feedforward,
    base_attention,
    base_output,
    base_feedforward,
    base_down,
    rank_in_attention,
    rank_out_attention,
    magnitude_attention,
    rank_in_output,
    rank_out_output,
    magnitude_output,
    rank_in_feedforward,
    rank_out_feedforward,
    magnitude_feedforward,
    rank_in_down,
    rank_out_down,
    magnitude_down,
    *,
    devices,
    blocks,
):
    links = Links(devices)
    index, core, chips = links.index, links.core, links.chips
    chip = index // 2
    block_index = lax.axis_index("blk")
    rows_in = block_input[0].astype(f32)
    tokens = rows_in.shape[0]
    length = row_lengths[0]
    token_pos = block_index * tokens + jnp.arange(tokens, dtype=jnp.int32)
    valid = (token_pos < length)[:, None]
    scalars = jnp.stack([block_index.astype(jnp.int32), length])

    frequency = rope_base ** (-(jnp.arange(HEAD // 2, dtype=f32) * 2.0) / HEAD)
    angles = rope_positions[0].astype(f32)[:, None] * frequency[None, :]
    cos_half, sin_half = jnp.cos(angles), jnp.sin(angles)
    cosine = jnp.concatenate([cos_half, cos_half], axis=-1)
    sine = jnp.concatenate([-sin_half, sin_half], axis=-1)

    def columns_of(value, width):
        return lax.dynamic_slice_in_dim(value, index * width, width, value.ndim - 1)

    attn_cols = base_attention.shape[2]
    out_cols = base_output.shape[2]
    feed_cols = base_feedforward.shape[2]
    down_cols = base_down.shape[1]
    attn_rank = columns_of(rank_out_attention, attn_cols)
    attn_mag = columns_of(magnitude_attention, attn_cols)
    kv_fold, kv_norm, kv_proj = fold(
        base_attention[GROUP:], rank_in_attention[1:], attn_rank[GROUP:], attn_mag[GROUP:], lambda b: b, "fold_kv"
    )
    q_fold, q_norm, q_proj = fold(
        base_attention[:GROUP], rank_in_attention[:1], attn_rank[:GROUP], attn_mag[:GROUP], lambda b: 0, "fold_q"
    )
    o_fold, o_norm, o_proj = fold(
        base_output,
        rank_in_output[None],
        columns_of(rank_out_output, out_cols),
        columns_of(magnitude_output, out_cols),
        lambda b: 0,
        "fold_o",
    )
    f_fold, f_norm, f_proj = fold(
        base_feedforward,
        rank_in_feedforward,
        columns_of(rank_out_feedforward, feed_cols),
        columns_of(magnitude_feedforward, feed_cols),
        lambda b: b,
        "fold_f",
    )
    d_fold, d_norm, d_proj = fold(
        base_down[None],
        rank_in_down[None],
        columns_of(rank_out_down, down_cols)[None],
        columns_of(magnitude_down, down_cols)[None],
        lambda b: 0,
        "fold_d",
    )

    kv_weights = links.gather_rows(kv_fold)
    q_weights = links.gather_rows(after(q_fold, kv_weights))
    o_weights = links.gather_rows(after(o_fold, q_weights)).reshape(D, D)

    feed_weights = jnp.zeros((2, 2, feed_cols, D), bf16)
    feed_weights = lax.dynamic_update_slice(feed_weights, f_fold[:, None], (0, core, 0, 0))
    feed_weights = lax.dynamic_update_slice(feed_weights, links.swap(f_fold, 1)[:, None], (0, 1 - core, 0, 0))
    feed_weights = feed_weights.reshape(2, 2 * feed_cols, D)
    chip_cols = 2 * feed_cols
    gate_weights, up_weights = feed_weights[0], feed_weights[1]

    d_source = after(d_fold[0], o_weights)
    down_weights = jnp.zeros((devices, down_cols, chip_cols), bf16)
    for r in range(chips):
        piece = lax.dynamic_slice_in_dim(d_source, (chip ^ r) * chip_cols, chip_cols, 1)
        if r:
            piece = links.swap(piece, 2 * r)
        down_weights = lax.dynamic_update_slice(down_weights, piece[None], (index ^ (2 * r), 0, 0))
        down_weights = lax.dynamic_update_slice(
            down_weights, links.swap(piece, 1)[None], (index ^ (2 * r + 1), 0, 0)
        )
    down_weights = down_weights.reshape(D, chip_cols)

    grad_out = jnp.where(valid, out_cotangent[0], jnp.zeros((), bf16))
    grad_blocks = links.chip_gather(after(grad_out, o_weights))

    normed, inverse_in = rms_parts(rows_in, gain_attention)
    kv_own = project_rope(normed, kv_weights, cosine, sine, 1, "project_kv")
    kv_blocks = [kv_own]
    for _ in range(1, blocks):
        kv_blocks.append(lax.ppermute(kv_blocks[-1], "blk", [(i, i + 1) for i in range(blocks - 1)]))
    queries = project_rope(normed, q_weights, cosine, sine, GROUP, "project_q")
    mixed, lse = attend(scalars, queries, kv_blocks)
    out_value = dot_nt(mixed, o_weights)
    residual = rows_in + out_value
    normed_feed, inverse_feed = rms_parts(residual, gain_feedforward)

    feed_blocks = links.chip_gather(normed_feed)
    shares_out, shares_grad = [], []
    hiddens, grad_gates, grad_ups = [], [], []
    gate_mag_sum = jnp.zeros((chip_cols,), f32)
    up_mag_sum = jnp.zeros((chip_cols,), f32)
    down_mag_sum = jnp.zeros((D,), f32)
    for r in range(chips):
        gate = dot_nt(feed_blocks[r], gate_weights)
        up = dot_nt(feed_blocks[r], up_weights)
        sigma = jax.nn.sigmoid(gate)
        hidden = (gate * sigma * up).astype(bf16)
        grad_hidden = dot_nn(grad_blocks[r], down_weights)
        grad_gate = grad_hidden * up * sigma * (1.0 + gate * (1.0 - sigma))
        grad_up = grad_hidden * gate * sigma
        gate_mag_sum = gate_mag_sum + jnp.sum(grad_gate * gate, axis=0)
        up_mag_sum = up_mag_sum + jnp.sum(grad_up * up, axis=0)
        grad_gate, grad_up = grad_gate.astype(bf16), grad_up.astype(bf16)
        shares_grad.append((dot_nn(grad_gate, gate_weights) + dot_nn(grad_up, up_weights)).astype(bf16))
        down_value = dot_nt(hidden, down_weights)
        down_mag_sum = down_mag_sum + jnp.sum(grad_blocks[r].astype(f32) * down_value, axis=0)
        shares_out.append(down_value.astype(bf16))
        hiddens.append(hidden)
        grad_gates.append(grad_gate)
        grad_ups.append(grad_up)
    grad_normed_feed = links.chip_reduce(shares_grad)
    grad_residual = grad_out.astype(f32) + rms_back(residual, inverse_feed, gain_feedforward, grad_normed_feed)
    block_out = (residual + links.chip_reduce(shares_out)).astype(bf16)[None]

    grad_residual_low = grad_residual.astype(bf16)
    grad_mixed = dot_nn(grad_residual_low, o_weights).astype(bf16)
    delta = jnp.sum(
        (grad_mixed.astype(f32) * mixed.astype(f32)).reshape(tokens, GROUP, KV_HEADS, HEAD), axis=-1
    )
    delta = delta.transpose(2, 1, 0).reshape(KV_HEADS, 1, GROUP * tokens)
    grad_queries, grad_kv = None, None
    for distance in reversed(range(blocks)):
        if grad_kv is not None:
            grad_kv = lax.ppermute(grad_kv, "blk", [(i + 1, i) for i in range(blocks - 1)])
        grad_queries, grad_kv = attend_back(
            scalars, queries, grad_mixed, lse, delta, kv_blocks[distance], grad_kv, grad_queries, distance
        )

    def rope_back(grads):
        heads = grads.reshape(tokens, -1, HEAD)
        return (heads * cosine[:, None] - jnp.roll(heads, HEAD // 2, axis=-1) * sine[:, None]).reshape(tokens, -1)

    grad_q_raw = rope_back(grad_queries)
    grad_k_raw = rope_back(grad_kv[:, :KVW])
    grad_v_raw = grad_kv[:, KVW:]
    q_flat = q_weights.reshape(GROUP * KVW, D)
    grad_q_low = grad_q_raw.astype(bf16)
    grad_kv_low = jnp.concatenate([grad_k_raw, grad_v_raw], axis=1).astype(bf16)
    grad_normed = dot_nn(grad_q_low, q_flat) + dot_nn(grad_kv_low, kv_weights.reshape(2 * KVW, D))
    input_grad = (grad_residual + rms_back(rows_in, inverse_in, gain_attention, grad_normed)).astype(bf16)[None]

    def all_columns(value):
        gathered = lax.all_gather(value, "dp", axis=0)
        return jnp.moveaxis(gathered, 0, -2).reshape(value.shape[:-1] + (-1,))

    def rows_first(norm, proj):
        return jnp.concatenate([norm, proj], axis=2).transpose(0, 2, 1)

    attn_aux = all_columns(
        jnp.concatenate([rows_first(q_norm, q_proj), rows_first(kv_norm, kv_proj), rows_first(o_norm, o_proj)])
    )
    feed_aux = rows_first(f_norm, f_proj)
    feed_other = links.swap(feed_aux, 1)
    feed_aux = jnp.where(
        core == 0,
        jnp.concatenate([feed_aux, feed_other], axis=2),
        jnp.concatenate([feed_other, feed_aux], axis=2),
    )
    down_norm = lax.all_gather(d_norm.reshape(-1), "dp", axis=0, tiled=True)

    def adapter(inputs, grads, weights, rank_in, rank_out, magnitude, norm, proj, mag_sum):
        small = dot_nn(inputs, rank_in).astype(bf16)
        scale = magnitude / norm
        grad_mag = mag_sum / magnitude
        turn = -(grad_mag / norm)
        wide = rank_out.astype(f32)
        grad_small = (factor * dot_nt(grads, (wide * scale).astype(bf16))).astype(bf16)
        grad_rank_out = factor * (dot_tn(small, grads) * scale + proj * turn)
        grad_rank_in = dot_tn(inputs, grad_small) + factor * lax.dot_general(
            weights, (wide * turn).astype(bf16), (((0,), (1,)), ((), ())), preferred_element_type=f32
        )
        return grad_rank_in, grad_rank_out, grad_mag

    def flat_blocks(value):
        return value.transpose(1, 0, 2).reshape(value.shape[1], -1)

    def block_form(value):
        return value.reshape(value.shape[0], -1, KVW).transpose(1, 0, 2)

    o_aux = flat_blocks(attn_aux[GROUP + 2 :])
    out_in, out_out, out_mag = adapter(
        mixed,
        grad_residual_low,
        o_weights,
        rank_in_output,
        flat_blocks(rank_out_output),
        magnitude_output.reshape(-1),
        o_aux[0],
        o_aux[1:],
        jnp.sum(grad_residual * out_value, axis=0),
    )

    feed_all = jnp.concatenate(feed_blocks)
    feed_ins, feed_outs, feed_mags = [], [], []
    for member, (grads, mag_sum) in enumerate(
        ((jnp.concatenate(grad_gates), gate_mag_sum), (jnp.concatenate(grad_ups), up_mag_sum))
    ):
        grad_in, grad_rank, grad_mag = adapter(
            feed_all,
            grads,
            feed_weights[member],
            rank_in_feedforward[member],
            lax.dynamic_slice_in_dim(rank_out_feedforward[member], chip * chip_cols, chip_cols, 1),
            lax.dynamic_slice_in_dim(magnitude_feedforward[member], chip * chip_cols, chip_cols, 0),
            feed_aux[member, 0],
            feed_aux[member, 1:],
            mag_sum,
        )
        feed_ins.append(grad_in)
        feed_outs.append(
            lax.dynamic_update_slice(jnp.zeros((RANK, FF), f32), grad_rank, (0, chip * chip_cols))
        )
        feed_mags.append(lax.dynamic_update_slice(jnp.zeros((FF,), f32), grad_mag, (chip * chip_cols,)))

    down_grad_mag = lax.psum(down_mag_sum / magnitude_down, ("dp", "blk"))
    hidden_all = jnp.concatenate(hiddens)
    grad_all = jnp.concatenate(grad_blocks)
    down_scale = magnitude_down / down_norm
    down_wide = rank_out_down.astype(f32)
    down_small = dot_nn(
        hidden_all, lax.dynamic_slice_in_dim(rank_in_down, chip * chip_cols, chip_cols, 0)
    ).astype(bf16)
    down_grad_small = (factor * dot_nt(grad_all, (down_wide * down_scale).astype(bf16))).astype(bf16)
    down_out = factor * dot_tn(down_small, grad_all) * down_scale
    down_in = lax.dynamic_update_slice(
        jnp.zeros((FF, RANK), f32), dot_tn(hidden_all, down_grad_small), (chip * chip_cols, 0)
    )
    own_turn = columns_of(-(down_grad_mag / down_norm), down_cols) * (1.0 / blocks)
    own_wide = columns_of(down_wide, down_cols)
    down_in = down_in + factor * lax.dot_general(
        d_fold[0], (own_wide * own_turn).astype(bf16), (((0,), (1,)), ((), ())), preferred_element_type=f32
    )
    own_out = factor * d_proj[0].T * own_turn
    down_out = down_out + lax.dynamic_update_slice(jnp.zeros((RANK, D), f32), own_out, (0, index * down_cols))

    def turned_back(low):
        heads = low.astype(f32).reshape(tokens, -1, HEAD)
        return (heads * cosine[:, None] - jnp.roll(heads, HEAD // 2, axis=-1) * sine[:, None]).reshape(tokens, -1)

    kv_wide = kv_weights.reshape(2, KVW, D)
    values_in = (
        (grad_q_raw, q_flat, 0, slice(0, GROUP), turned_back(queries)),
        (grad_k_raw, kv_wide[0], 1, slice(GROUP, GROUP + 1), turned_back(kv_own[:, :KVW])),
        (grad_v_raw, kv_wide[1], 2, slice(GROUP + 1, GROUP + 2), kv_own[:, KVW:].astype(f32)),
    )
    attn_ins, attn_outs, attn_mags = [], [], []
    for grads, weights, member, span, raw in values_in:
        aux = flat_blocks(attn_aux[span])
        grad_in, grad_rank, grad_mag = adapter(
            normed,
            grads.astype(bf16),
            weights,
            rank_in_attention[member],
            flat_blocks(rank_out_attention[span]),
            magnitude_attention[span].reshape(-1),
            aux[0],
            aux[1:],
            jnp.sum(grads * raw, axis=0),
        )
        attn_ins.append(grad_in)
        attn_outs.append(block_form(grad_rank))
        attn_mags.append(grad_mag.reshape(-1, KVW))

    early = lax.psum(
        (
            out_in,
            block_form(out_out),
            out_mag.reshape(-1, KVW),
            jnp.stack(feed_ins),
            jnp.stack(feed_outs),
            jnp.stack(feed_mags),
            down_in,
            down_out,
        ),
        ("dp", "blk"),
    )
    late = lax.psum(
        (jnp.stack(attn_ins), jnp.concatenate(attn_outs), jnp.concatenate(attn_mags)), ("dp", "blk")
    )
    return (block_out, input_grad) + tuple(late) + tuple(early) + (down_grad_mag,)


def solution(mesh):
    split_tokens = P("dp", "blk", None)
    placed = (
        split_tokens,
        split_tokens,
        P("dp"),
        P("dp", "blk"),
        P(),
        P(),
        P(None, None, "dp"),
        P(None, None, "dp"),
        P(None, None, "dp"),
        P(None, "dp"),
    ) + (P(),) * 12
    return jax.shard_map(
        functools.partial(shards, devices=mesh.shape["dp"], blocks=mesh.shape["blk"]),
        mesh=mesh,
        in_specs=placed,
        out_specs=(split_tokens, split_tokens) + (P(),) * 12,
        check_vma=False,
    )
```

time: 1610 us -> 977 us (0.61)
  matrix products: 567 us -> 180 us
  local copies, waits for them, and re-layouts: 453 us -> 162 us
  waiting for transfers between devices: 497 us -> 373 us
  Pallas kernels: 0 us -> 97.4 us
  starting transfers between devices: 1.68 us -> 61.5 us
  blocking collectives: 0 us -> 22.6 us
    dot_general x139 -> x49, matrix products: 567 us -> 180 us  [the longest x14 57.3 us: dot_tn(): lax.dot_general(left, right, (((0,), (0,)), ((), ())), preferred_element_...]
    unnamed x558 -> x383, local copies, waits for them, and re-layouts: 291 us -> 54.1 us
    all_gather x6 -> x0, waiting for transfers between devices: 234 us -> none  [the longest x1 167 us: shards(): weights_part = lax.all_gather(base_feedforward, 'dp', axis=2, tiled=True)]
    ppermute x0 -> x48, waiting for transfers between devices: none -> 116 us  [the longest x31 56.1 us: swap(): lax.ppermute(value, 'dp', [(i, i ^ bits) for i in range(self.devices)])]
    pallas_call x0 -> x12, Pallas kernels: none -> 97.4 us  [the longest x5 70.5 us: fold(): pl.pallas_call(functools.partial(fold_kernel, chunk=256), out_shape=(jax....]
    slice x3 -> x29, local copies, waits for them, and re-layouts: 123 us -> 32.6 us  [the longest x1 11 us: shards(): gate_weights, up_weights = (feed_weights[0], feed_weights[1])]
    ppermute x0 -> x48, starting transfers between devices: none -> 61.5 us  [the longest x31 38.9 us: swap(): lax.ppermute(value, 'dp', [(i, i ^ bits) for i in range(self.devices)])]
    dynamic_update_slice x4 -> x34, local copies, waits for them, and re-layouts: 2.86 us -> 41.2 us  [the longest x24 28.1 us: gather_rows(): lax.dynamic_update_slice(whole, piece[:, None], (0, self.index ^ i, 0, 0))]
  transfers between devices with their start and end apart: 10 -> 50, of which waited for: 4 -> 18; matrix products, arithmetic and copies ran while one was open for 26% -> 29% of each run, Pallas kernels for 0% -> 8%
where the time goes in v1:
time: 977 us; the launch traced here: 966 us
  waiting for transfers between devices  373 us (38%)
  matrix products  180 us (18%)
  local copies, waits for them, and re-layouts  162 us (17%)
  Pallas kernels  97.4 us (10%)
  starting transfers between devices  61.5 us (6%)
  other arithmetic  52.2 us (5%)
  blocking collectives  22.6 us (2%)
  between operations  17.4 us (2%)
    psum x2, waiting for transfers between devices, shards(): lax.psum((jnp.stack(attn_ins), jnp.concatenate(attn_outs), jnp.concatenat...  258 us
    pallas_call x5, Pallas kernels, fold(): pl.pallas_call(functools.partial(fold_kernel, chunk=256), out_shape=(jax....  70.5 us
    dot_general x14, matrix products, dot_tn(): lax.dot_general(left, right, (((0,), (0,)), ((), ())), preferred_element_...  57.3 us
    ppermute x31, waiting for transfers between devices, swap(): lax.ppermute(value, 'dp', [(i, i ^ bits) for i in range(self.devices)])  56.1 us
    dot_general x15, matrix products, dot_nn(): lax.dot_general(left, right, (((1,), (0,)), ((), ())), preferred_element_...  54.3 us
    unnamed x383, local copies, waits for them, and re-layouts  54.1 us
    dot_general x13, matrix products, dot_nt(): lax.dot_general(left, right, (((1,), (1,)), ((), ())), preferred_element_...  46.7 us
    ppermute x31, starting transfers between devices, swap(): lax.ppermute(value, 'dp', [(i, i ^ bits) for i in range(self.devices)])  38.9 us
  transfers between devices with their start and end apart: 50, of which 18 were waited for; matrix products, arithmetic and copies ran while one was open for 29% of the time, Pallas kernels for 8%

profile of v1, /device:TPU:1, one launch (start us, length us, event | category | flops | bytes accessed | tf_op | source)
XLA Modules:
  0.0 965.8 jit_solution(3704689963843779560)
XLA Ops:
  10.4 7.9 fold_kv.1
  23.6 8.6 copy.241.weight_ref
  34.8 19.6 %fold_f.1 = (bf16[2,704,2048]{2,1,0:T(8,128)(2,1)}, f32[2,704,1]{2,1,0:T(8,128)S(1)}, f32[2,704,16]{2,1,0:T(8,128)S(1)}) custom-call(bf16[2,2048,704]{2,1,0:T(8,128)(2,1)} %copy.241.weight_ref, bf16[2,2048,16]{2,1,0:T(8,128)(2,1)S(1)} %copy.242.rank_in_ref, bf16[2,704,16]{2,1,0:T(8,128)(2,1)S(1)} %bitcast.559, f32[2,704,1]{2,1,0:T(8,128)S(1)} %copy.243.mag_ref), custom_call_target="tpu_custom_call" | custom-call | tf_op jit(solution)/shard_map/fold_f/pallas_call | solution.py:69
  68.2 14.4 %fold_o.1 = (bf16[4,64,2048]{2,1,0:T(8,128)(2,1)S(1)}, f32[4,64,1]{2,1,0:T(8,128)S(1)}, f32[4,64,16]{2,1,0:T(8,128)S(1)}) custom-call(bf16[4,2048,64]{2,1,0:T(8,128)(2,1)S(1)} %copy-done.17, bf16[1,2048,16]{2,1,0:T(8,128)(2,1)S(1)} %bitcast.558, bf16[4,64,16]{2,1,0:T(8,128)(2,1)S(1)} %fusion.87.rank_out_ref, f32[4,64,1]{2,1,0:T(8,128)S(1)} %copy.230.mag_ref), custom_call_target="tpu_custom_call" | custom-call | tf_op jit(solution)/shard_map/fold_o/pallas_call | solution.py:69
  88.8 14.5 %fold_q.1 = (bf16[4,64,2048]{2,1,0:T(8,128)(2,1)S(1)}, f32[4,64,1]{2,1,0:T(8,128)S(1)}, f32[4,64,16]{2,1,0:T(8,128)S(1)}) custom-call(bf16[4,2048,64]{2,1,0:T(8,128)(2,1)S(1)} %copy.275.weight_ref, bf16[1,2048,16]{2,1,0:T(8,128)(2,1)S(1)} %copy.276.rank_in_ref, bf16[4,64,16]{2,1,0:T(8,128)(2,1)S(1)} %fusion.86.rank_out_ref, f32[4,64,1]{2,1,0:T(8,128)S(1)} %copy.207.mag_ref), custom_call_target="tpu_custom_call" | custom-call | tf_op jit(solution)/shard_map/fold_q/pallas_call | solution.py:69
  104.5 10.2 %all-gather = f32[80,17,64]{2,1,0:T(8,128)S(1)} all-gather(f32[10,17,64]{2,1,0:T(8,128)S(1)} %pad_maximum_fusion.21), channel_id=2, replica_groups=mesh['dp'=8,'blk'=4] {'dp'}, dimensions={0}, use_global_device_ids=true | all-gather | bytes 391680 | tf_op jit(solution)/shard_map/all_gather | solution.py:532
  129.3 14.1 %fold_d.1 = (bf16[1,256,5632]{2,1,0:T(8,128)(2,1)S(1)}, f32[1,256,1]{2,1,0:T(8,128)S(1)}, f32[1,256,16]{2,1,0:T(8,128)S(1)}) custom-call(bf16[1,5632,256]{2,1,0:T(8,128)(2,1)} %bitcast.605, bf16[1,5632,16]{2,1,0:T(8,128)(2,1)S(1)} %bitcast.557, bf16[1,256,16]{2,1,0:T(8,128)(2,1)S(1)} %fusion.88.rank_out_ref, f32[1,256,1]{2,1,0:T(8,128)S(1)} %copy.246.mag_ref), custom_call_target="tpu_custom_call" | custom-call | tf_op jit(solution)/shard_map/fold_d/pallas_call | solution.py:69
  143.4 12.4 %all-gather.1 = f32[1,2048,1]{2,1,0:T(8,128)} all-gather(f32[1,256,1]{2,1,0:T(8,128)S(1)} %get-tuple-element.70), channel_id=3, replica_groups=mesh['dp'=8,'blk'=4] {'dp'}, dimensions={1}, use_global_device_ids=true | all-gather | bytes 9216 | tf_op jit(solution)/shard_map/all_gather | solution.py:548
  162.3 5.7 broadcast_in_dim.229
  168.1 6.2 bitcast_dynamic-update-slice_fusion.1
  204.9 4.7 fusion.232
  210.9 7.4 collective-permute-done.8
  230.5 8.2 collective-permute-done.15.refs_2_.kv_ref
  238.7 4.1 collective-permute-start.16
  253.3 4.4 attend.1
  263.5 6.1 bitcast_dynamic-update-slice_fusion
  269.5 5.8 collective-permute-done.18
  280.3 11.0 %fusion.231 = (bf16[1,2,704,2048]{3,2,0,1:T(8,128)(2,1)}, bf16[1,2,704,2048]{3,2,0,1:T(8,128)(2,1)}) fusion(bf16[2,2,704,2048]{3,2,0,1:T(8,128)(2,1)} %bitcast_dynamic-update-slice_fusion), kind=kLoop, calls=%fused_computation.425 | loop fusion | bytes 23068672 | tf_op jit(solution)/shard_map/slice | solution.py:448
  305.7 5.9 multiply_reduce_fusion.6
  324.2 20.2 %collective-permute-done.26 = bf16[256,1408]{1,0:T(8,128)(2,1)S(1)} collective-permute-done((bf16[256,1408]{1,0:T(8,128)(2,1)S(1)}, bf16[256,1408]{1,0:T(8,128)(2,1)S(1)}, u32[]{:S(2)}, u32[]{:S(2)}) %collective-permute-start.26) | collective-permute-done | bytes 720928 | tf_op jit(solution)/shard_map/ppermute | solution.py:311
  346.8 20.9 %collective-permute-done.28 = bf16[256,1408]{1,0:T(8,128)(2,1)S(1)} collective-permute-done((bf16[256,1408]{1,0:T(8,128)(2,1)S(1)}, bf16[256,1408]{1,0:T(8,128)(2,1)S(1)}, u32[]{:S(2)}, u32[]{:S(2)}) %collective-permute-start.28) | collective-permute-done | bytes 720928 | tf_op jit(solution)/shard_map/ppermute | solution.py:311
  367.7 16.5 %collective-permute-start.27 = (bf16[256,1408]{1,0:T(8,128)(2,1)S(1)}, bf16[256,1408]{1,0:T(8,128)(2,1)S(1)}, u32[]{:S(2)}, u32[]{:S(2)}) collective-permute-start(bf16[256,1408]{1,0:T(8,128)(2,1)S(1)} %collective-permute-done.26), channel_id=1, source_target_pairs={{0,4},{4,0},{8,12},{12,8},{16,20},{20,16},{24,28},{28,24},{1,5},{5... | collective-permute-start | bytes 2162696 | tf_op jit(solution)/shard_map/ppermute | solution.py:311
  397.4 4.9 multiply_reduce_fusion.13
  408.4 5.1 multiply_reduce_fusion.12
  423.1 4.6 fusion.11
  442.6 3.9 multiply_reduce_fusion.11
  458.5 7.0 fusion.22
  465.5 6.8 fusion.20
  473.2 7.3 fusion.31
  480.5 4.3 convolution_multiply_fusion.5
  484.8 7.9 fusion.32
  492.8 6.2 add_convert_fusion
  506.6 15.2 %collective-permute-done.43 = bf16[256,2048]{1,0:T(8,128)(2,1)S(1)} collective-permute-done((bf16[256,2048]{1,0:T(8,128)(2,1)S(1)}, bf16[256,2048]{1,0:T(8,128)(2,1)S(1)}, u32[]{:S(2)}, u32[]{:S(2)}) %collective-permute-start.43) | collective-permute-done | bytes 1048608 | tf_op jit(solution)/shard_map/ppermute | solution.py:314
  526.7 8.8 collective-permute-done.37
  539.2 4.0 convert_multiply_fusion.2
  562.6 4.7 convolution_multiply_fusion.10
  576.7 9.0 collective-permute-done.45.refs_0_
  592.3 6.1 convolution_multiply_fusion.1
  598.4 11.2 %collective-permute-done.46.refs_0_ = bf16[256,1024]{1,0:T(8,128)(2,1)} collective-permute-done((bf16[256,1024]{1,0:T(8,128)(2,1)}, bf16[256,1024]{1,0:T(8,128)(2,1)}, u32[]{:S(2)}, u32[]{:S(2)}) %collective-permute-start.46) | collective-permute-done | bytes 524320 | tf_op jit(solution)/shard_map/ppermute | solution.py:513
  611.9 7.6 attend_back_0.1
  634.6 4.6 maximum_multiply_fusion.1
  639.4 4.4 fusion.37
  650.4 5.1 fusion.70
  662.8 4.9 fusion.34
  670.7 125.1 %all-reduce.5.cloned.1.call-done = (f32[6,512]{1,0:T(8,128)}, f32[4,512]{1,0:T(4,128)}, f32[2,5632]{1,0:T(2,128)}, f32[2048]{0:T(1024)}) async-done(((f32[6,512]{1,0:T(8,128)}, f32[4,512]{1,0:T(4,128)}, f32[2,5632]{1,0:T(2,128)}, f32[2048]{0:T(1024)}), (f32[6,512]{1,0:T(8,128)}, f32[4,512]{1,0:T(4,128)}, f32[2,5632]{1,0:T(2,128)}, f32[2048]{0:T(1024)})) %all-reduce.5.cloned.1.call-update) | async-done | bytes 73744 | tf_op jit(solution)/shard_map/psum | solution.py:666
  797.8 4.6 fusion.14
  804.4 6.6 fusion.41
  812.5 132.7 %all-reduce.7.cloned.1.call-done = (f32[3,2048,16]{1,2,0:T(8,128)}, f32[6,16,512]{2,1,0:T(8,128)}, f32[2048,16]{0,1:T(8,128)}, f32[4,16,512]{2,1,0:T(8,128)}, f3...) async-done(((f32[3,2048,16]{1,2,0:T(8,128)}, f32[6,16,512]{2,1,0:T(8,128)}, f32[2048,16]{0,1:T(8,128)}, ...) | async-done | bytes 2326544 | tf_op jit(solution)/shard_map/psum | solution.py:666
  (687 shorter events, 306.9 us)
Async XLA Ops:
  7.2 788.6 %all-reduce.5.cloned.1.call-start = ((), (), s32[]{:S(2)}) async-start(), calls=%async_computation | async-start | bytes 155648 | tf_op jit(solution)/shard_map/psum | solution.py:666
  19.6 161.1 %collective-permute-start = (bf16[2,64,2048]{2,1,0:T(8,128)(2,1)}, bf16[2,64,2048]{2,1,0:T(8,128)(2,1)}, u32[]{:S(2)}, u32[]{:S(2)}) collective-permute-start(bf16[2,64,2048]{2,1,0:T(8,128)(2,1)} %get-tuple-element.44), channel_id=1, source_target_pairs={{0,4},{4,0},{8,12},{12,8},{16,20},{20,16},{24,28},{28,24},{1,5},{5... | collective-permute-start | bytes 1572872 | tf_op jit(solution)/shard_map/ppermute | solution.py:311
  19.7 158.5 %collective-permute-start.1 = (bf16[2,64,2048]{2,1,0:T(8,128)(2,1)}, bf16[2,64,2048]{2,1,0:T(8,128)(2,1)}, u32[]{:S(2)}, u32[]{:S(2)}) collective-permute-start(bf16[2,64,2048]{2,1,0:T(8,128)(2,1)} %get-tuple-element.44), channel_id=1, source_target_pairs={{0,8},{4,12},{8,0},{12,4},{16,24},{20,28},{24,16},{28,20},{1,9},{5... | collective-permute-start | bytes 1572872 | tf_op jit(solution)/shard_map/ppermute | solution.py:311
  22.4 155.8 %collective-permute-start.3 = (bf16[2,64,2048]{2,1,0:T(8,128)(2,1)}, bf16[2,64,2048]{2,1,0:T(8,128)(2,1)}, u32[]{:S(2)}, u32[]{:S(2)}) collective-permute-start(bf16[2,64,2048]{2,1,0:T(8,128)(2,1)} %get-tuple-element.44), channel_id=1, source_target_pairs={{0,16},{4,20},{8,24},{12,28},{16,0},{20,4},{24,8},{28,12},{1,17},{... | collective-permute-start | bytes 1572872 | tf_op jit(solution)/shard_map/ppermute | solution.py:311
  55.3 208.1 %collective-permute-start.24 = (bf16[2,704,2048]{2,1,0:T(8,128)(2,1)}, bf16[2,704,2048]{2,1,0:T(8,128)(2,1)}, u32[]{:S(2)}, u32[]{:S(2)}) collective-permute-start(bf16[2,704,2048]{2,1,0:T(8,128)(2,1)} %get-tuple-element.49), channel_id=1, source_target_pairs={{0,4},{4,0},{8,12},{12,8},{16,20},{20,16},{24,28},{28,24},{1,5},{5... | collective-permute-start | bytes 17301512 | tf_op jit(solution)/shard_map/ppermute | solution.py:311
  58.2 117.9 %collective-permute-start.47 = (f32[2,17,704]{2,0,1:T(2,128)}, f32[2,17,704]{2,0,1:T(2,128)}, u32[]{:S(2)}, u32[]{:S(2)}) collective-permute-start(f32[2,17,704]{2,0,1:T(2,128)} %maximum_bitcast_fusion), channel_id=1, source_target_pairs={{0,4},{4,0},{8,12},{12,8},{16,20},{20,16},{24,28},{28,24},{1,5},{5... | collective-permute-start | bytes 287240 | tf_op jit(solution)/shard_map/ppermute | solution.py:311
  179.3 8.4 collective-permute-start.5
  180.3 8.4 collective-permute-start.2
  180.6 10.8 %collective-permute-start.4 = (bf16[2,64,2048]{2,1,0:T(8,128)(2,1)}, bf16[2,64,2048]{2,1,0:T(8,128)(2,1)S(1)}, u32[]{:S(2)}, u32[]{:S(2)}) collective-permute-start(bf16[2,64,2048]{2,1,0:T(8,128)(2,1)} %collective-permute-done.3), channel_id=1, source_target_pairs={{0,4},{4,0},{8,12},{12,8},{16,20},{20,16},{24,28},{28,24},{1,5},{5... | collective-permute-start | bytes 1572872 | tf_op jit(solution)/shard_map/ppermute | solution.py:311
  194.0 33.4 %collective-permute-start.7 = (bf16[4,64,2048]{2,1,0:T(8,128)(2,1)S(1)}, bf16[4,64,2048]{2,1,0:T(8,128)(2,1)}, u32[]{:S(2)}, u32[]{:S(2)}) collective-permute-start(bf16[4,64,2048]{2,1,0:T(8,128)(2,1)S(1)} %copy-done.36), channel_id=1, source_target_pairs={{0,4},{4,0},{8,12},{12,8},{16,20},{20,16},{24,28},{28,24},{1,5},{5... | collective-permute-start | bytes 3145736 | tf_op jit(solution)/shard_map/ppermute | solution.py:311
  194.0 24.3 %collective-permute-start.8 = (bf16[4,64,2048]{2,1,0:T(8,128)(2,1)S(1)}, bf16[4,64,2048]{2,1,0:T(8,128)(2,1)}, u32[]{:S(2)}, u32[]{:S(2)}) collective-permute-start(bf16[4,64,2048]{2,1,0:T(8,128)(2,1)S(1)} %copy-done.36), channel_id=1, source_target_pairs={{0,8},{4,12},{8,0},{12,4},{16,24},{20,28},{24,16},{28,20},{1,9},{5... | collective-permute-start | bytes 3145736 | tf_op jit(solution)/shard_map/ppermute | solution.py:311
  194.9 24.0 %collective-permute-start.10 = (bf16[4,64,2048]{2,1,0:T(8,128)(2,1)S(1)}, bf16[4,64,2048]{2,1,0:T(8,128)(2,1)}, u32[]{:S(2)}, u32[]{:S(2)}) collective-permute-start(bf16[4,64,2048]{2,1,0:T(8,128)(2,1)S(1)} %copy-done.36), channel_id=1, source_target_pairs={{0,16},{4,20},{8,24},{12,28},{16,0},{20,4},{24,8},{28,12},{1,17},{... | collective-permute-start | bytes 3145736 | tf_op jit(solution)/shard_map/ppermute | solution.py:311
  198.8 25.3 %collective-permute-start.14 = (bf16[256,1024]{1,0:T(8,128)(2,1)S(1)}, bf16[256,1024]{1,0:T(8,128)(2,1)S(1)}, u32[]{:S(2)}, u32[]{:S(2)}) collective-permute-start(bf16[256,1024]{1,0:T(8,128)(2,1)S(1)} %project_kv.1.refs_0_.kv_ref), channel_id=1, source_target_pairs={{0,1},{1,2},{2,3},{4,5},{5,6},{6,7},{8,9},{9,10},{10,11},{12,13},{... | collective-permute-start | bytes 1572872 | tf_op jit(solution)/shard_map/ppermute | solution.py:469
  220.2 22.6 %collective-permute-start.12 = (bf16[4,64,2048]{2,1,0:T(8,128)(2,1)S(1)}, bf16[4,64,2048]{2,1,0:T(8,128)(2,1)S(1)}, u32[]{:S(2)}, u32[]{:S(2)}) collective-permute-start(bf16[4,64,2048]{2,1,0:T(8,128)(2,1)S(1)} %broadcast_select_fusion.5), channel_id=1, source_target_pairs={{0,8},{4,20},{8,0},{12,28},{16,24},{20,4},{24,16},{28,12},{1,9},{5... | collective-permute-start | bytes 3145736 | tf_op jit(solution)/shard_map/ppermute | solution.py:314
  220.8 23.2 %collective-permute-start.9 = (bf16[4,64,2048]{2,1,0:T(8,128)(2,1)}, bf16[4,64,2048]{2,1,0:T(8,128)(2,1)S(1)}, u32[]{:S(2)}, u32[]{:S(2)}) collective-permute-start(bf16[4,64,2048]{2,1,0:T(8,128)(2,1)} %collective-permute-done.8), channel_id=1, source_target_pairs={{0,4},{4,0},{8,12},{12,8},{16,20},{20,16},{24,28},{28,24},{1,5},{5... | collective-permute-start | bytes 3145736 | tf_op jit(solution)/shard_map/ppermute | solution.py:311
  224.2 14.5 %collective-permute-start.15 = (bf16[256,1024]{1,0:T(8,128)(2,1)S(1)}, bf16[256,1024]{1,0:T(8,128)(2,1)S(1)}, u32[]{:S(2)}, u32[]{:S(2)}) collective-permute-start(bf16[256,1024]{1,0:T(8,128)(2,1)S(1)} %collective-permute-done.14.refs_1_.kv_ref), channel_id=1, source_target_pairs={{0,1},{1,2},{2,3},{4,5},{5,6},{6,7},{8,9},{9,10},{10,11},{12,13},{... | collective-permute-start | bytes 1572872 | tf_op jit(solution)/shard_map/ppermute | solution.py:469
  227.4 18.1 %collective-permute-start.11 = (bf16[4,64,2048]{2,1,0:T(8,128)(2,1)}, bf16[4,64,2048]{2,1,0:T(8,128)(2,1)S(1)}, u32[]{:S(2)}, u32[]{:S(2)}) collective-permute-start(bf16[4,64,2048]{2,1,0:T(8,128)(2,1)} %collective-permute-done.10), channel_id=1, source_target_pairs={{0,4},{4,0},{8,12},{12,8},{16,20},{20,16},{24,28},{28,24},{1,5},{5... | collective-permute-start | bytes 3145736 | tf_op jit(solution)/shard_map/ppermute | solution.py:311
  238.7 14.5 %collective-permute-start.16 = (bf16[256,1024]{1,0:T(8,128)(2,1)S(1)}, bf16[256,1024]{1,0:T(8,128)(2,1)S(1)}, u32[]{:S(2)}, u32[]{:S(2)}) collective-permute-start(bf16[256,1024]{1,0:T(8,128)(2,1)S(1)} %collective-permute-done.15.refs_2_.kv_ref), channel_id=1, source_target_pairs={{0,1},{1,2},{2,3},{4,5},{5,6},{6,7},{8,9},{9,10},{10,11},{12,13},{... | collective-permute-start | bytes 1572872 | tf_op jit(solution)/shard_map/ppermute | solution.py:469
  250.1 41.2 %collective-permute-start.17 = (bf16[4,64,2048]{2,1,0:T(8,128)(2,1)S(1)}, bf16[4,64,2048]{2,1,0:T(8,128)(2,1)}, u32[]{:S(2)}, u32[]{:S(2)}) collective-permute-start(bf16[4,64,2048]{2,1,0:T(8,128)(2,1)S(1)} %copy-done.34), channel_id=1, source_target_pairs={{0,4},{4,0},{8,12},{12,8},{16,20},{20,16},{24,28},{28,24},{1,5},{5... | collective-permute-start | bytes 3145736 | tf_op jit(solution)/shard_map/ppermute | solution.py:311
  250.6 24.7 %collective-permute-start.18 = (bf16[4,64,2048]{2,1,0:T(8,128)(2,1)S(1)}, bf16[4,64,2048]{2,1,0:T(8,128)(2,1)}, u32[]{:S(2)}, u32[]{:S(2)}) collective-permute-start(bf16[4,64,2048]{2,1,0:T(8,128)(2,1)S(1)} %copy-done.34), channel_id=1, source_target_pairs={{0,8},{4,12},{8,0},{12,4},{16,24},{20,28},{24,16},{28,20},{1,9},{5... | collective-permute-start | bytes 3145736 | tf_op jit(solution)/shard_map/ppermute | solution.py:311
  251.5 24.4 %collective-permute-start.20 = (bf16[4,64,2048]{2,1,0:T(8,128)(2,1)S(1)}, bf16[4,64,2048]{2,1,0:T(8,128)(2,1)}, u32[]{:S(2)}, u32[]{:S(2)}) collective-permute-start(bf16[4,64,2048]{2,1,0:T(8,128)(2,1)S(1)} %copy-done.34), channel_id=1, source_target_pairs={{0,16},{4,20},{8,24},{12,28},{16,0},{20,4},{24,8},{28,12},{1,17},{... | collective-permute-start | bytes 3145736 | tf_op jit(solution)/shard_map/ppermute | solution.py:311
  278.2 17.8 %collective-permute-start.22 = (bf16[4,64,2048]{2,1,0:T(8,128)(2,1)}, bf16[4,64,2048]{2,1,0:T(8,128)(2,1)}, u32[]{:S(2)}, u32[]{:S(2)}) collective-permute-start(bf16[4,64,2048]{2,1,0:T(8,128)(2,1)} %broadcast_select_fusion.4), channel_id=1, source_target_pairs={{0,8},{4,20},{8,0},{12,28},{16,24},{20,4},{24,16},{28,12},{1,9},{5... | collective-permute-start | bytes 3145736 | tf_op jit(solution)/shard_map/ppermute | solution.py:314
  278.7 17.8 %collective-permute-start.19 = (bf16[4,64,2048]{2,1,0:T(8,128)(2,1)}, bf16[4,64,2048]{2,1,0:T(8,128)(2,1)S(1)}, u32[]{:S(2)}, u32[]{:S(2)}) collective-permute-start(bf16[4,64,2048]{2,1,0:T(8,128)(2,1)} %collective-permute-done.18), channel_id=1, source_target_pairs={{0,4},{4,0},{8,12},{12,8},{16,20},{20,16},{24,28},{28,24},{1,5},{5... | collective-permute-start | bytes 3145736 | tf_op jit(solution)/shard_map/ppermute | solution.py:311
  291.3 8.5 collective-permute-start.21
  296.0 7.2 collective-permute-start.23
  304.2 41.1 %collective-permute-start.38 = (bf16[256,2048]{1,0:T(8,128)(2,1)S(1)}, bf16[256,2048]{1,0:T(8,128)(2,1)S(1)}, u32[]{:S(2)}, u32[]{:S(2)}) collective-permute-start(bf16[256,2048]{1,0:T(8,128)(2,1)S(1)} %copy-done.55), channel_id=1, source_target_pairs={{0,8},{4,12},{8,0},{12,4},{16,24},{20,28},{24,16},{28,20},{1,9},{5... | collective-permute-start | bytes 3145736 | tf_op jit(solution)/shard_map/ppermute | solution.py:311
  305.2 79.2 %collective-permute-start.39 = (bf16[256,2048]{1,0:T(8,128)(2,1)S(1)}, bf16[256,2048]{1,0:T(8,128)(2,1)S(1)}, u32[]{:S(2)}, u32[]{:S(2)}) collective-permute-start(bf16[256,2048]{1,0:T(8,128)(2,1)S(1)} %copy-done.55), channel_id=1, source_target_pairs={{0,16},{4,20},{8,24},{12,28},{16,0},{20,4},{24,8},{28,12},{1,17},{... | collective-permute-start | bytes 3145736 | tf_op jit(solution)/shard_map/ppermute | solution.py:311
  314.3 8.8 collective-permute-start.25
  315.1 29.4 %collective-permute-start.26 = (bf16[256,1408]{1,0:T(8,128)(2,1)S(1)}, bf16[256,1408]{1,0:T(8,128)(2,1)S(1)}, u32[]{:S(2)}, u32[]{:S(2)}) collective-permute-start(bf16[256,1408]{1,0:T(8,128)(2,1)S(1)} %get-tuple-element.185), channel_id=1, source_target_pairs={{0,8},{4,12},{8,0},{12,4},{16,24},{20,28},{24,16},{28,20},{1,9},{5... | collective-permute-start | bytes 2162696 | tf_op jit(solution)/shard_map/ppermute | solution.py:311
  316.5 68.8 %collective-permute-start.33 = (bf16[256,2048]{1,0:T(8,128)(2,1)S(1)}, bf16[256,2048]{1,0:T(8,128)(2,1)S(1)}, u32[]{:S(2)}, u32[]{:S(2)}) collective-permute-start(bf16[256,2048]{1,0:T(8,128)(2,1)S(1)} %multiply_convert_fusion), channel_id=1, source_target_pairs={{0,16},{4,20},{8,24},{12,28},{16,0},{20,4},{24,8},{28,12},{1,17},{... | collective-permute-start | bytes 3145736 | tf_op jit(solution)/shard_map/ppermute | solution.py:311
  323.1 62.8 %collective-permute-start.32 = (bf16[256,2048]{1,0:T(8,128)(2,1)S(1)}, bf16[256,2048]{1,0:T(8,128)(2,1)S(1)}, u32[]{:S(2)}, u32[]{:S(2)}) collective-permute-start(bf16[256,2048]{1,0:T(8,128)(2,1)S(1)} %multiply_convert_fusion), channel_id=1, source_target_pairs={{0,8},{4,12},{8,0},{12,4},{16,24},{20,28},{24,16},{28,20},{1,9},{5... | collective-permute-start | bytes 3145736 | tf_op jit(solution)/shard_map/ppermute | solution.py:311
  344.4 23.2 %collective-permute-start.28 = (bf16[256,1408]{1,0:T(8,128)(2,1)S(1)}, bf16[256,1408]{1,0:T(8,128)(2,1)S(1)}, u32[]{:S(2)}, u32[]{:S(2)}) collective-permute-start(bf16[256,1408]{1,0:T(8,128)(2,1)S(1)} %get-tuple-element.184), channel_id=1, source_target_pairs={{0,16},{4,20},{8,24},{12,28},{16,0},{20,4},{24,8},{28,12},{1,17},{... | collective-permute-start | bytes 2162696 | tf_op jit(solution)/shard_map/ppermute | solution.py:311
  345.3 38.8 %collective-permute-start.30 = (bf16[256,1408]{1,0:T(8,128)(2,1)S(1)}, bf16[256,1408]{1,0:T(8,128)(2,1)S(1)}, u32[]{:S(2)}, u32[]{:S(2)}) collective-permute-start(bf16[256,1408]{1,0:T(8,128)(2,1)S(1)} %get-tuple-element.183), channel_id=1, source_target_pairs={{0,24},{4,28},{8,16},{12,20},{16,8},{20,12},{24,0},{28,4},{1,25},{... | collective-permute-start | bytes 2162696 | tf_op jit(solution)/shard_map/ppermute | solution.py:311
  367.7 26.2 %collective-permute-start.27 = (bf16[256,1408]{1,0:T(8,128)(2,1)S(1)}, bf16[256,1408]{1,0:T(8,128)(2,1)S(1)}, u32[]{:S(2)}, u32[]{:S(2)}) collective-permute-start(bf16[256,1408]{1,0:T(8,128)(2,1)S(1)} %collective-permute-done.26), channel_id=1, source_target_pairs={{0,4},{4,0},{8,12},{12,8},{16,20},{20,16},{24,28},{28,24},{1,5},{5... | collective-permute-start | bytes 2162696 | tf_op jit(solution)/shard_map/ppermute | solution.py:311
  384.1 10.0 %collective-permute-start.29 = (bf16[256,1408]{1,0:T(8,128)(2,1)S(1)}, bf16[256,1408]{1,0:T(8,128)(2,1)S(1)}, u32[]{:S(2)}, u32[]{:S(2)}) collective-permute-start(bf16[256,1408]{1,0:T(8,128)(2,1)S(1)} %collective-permute-done.28), channel_id=1, source_target_pairs={{0,4},{4,0},{8,12},{12,8},{16,20},{20,16},{24,28},{28,24},{1,5},{5... | collective-permute-start | bytes 2162696 | tf_op jit(solution)/shard_map/ppermute | solution.py:311
  384.3 10.0 %collective-permute-start.31 = (bf16[256,1408]{1,0:T(8,128)(2,1)S(1)}, bf16[256,1408]{1,0:T(8,128)(2,1)S(1)}, u32[]{:S(2)}, u32[]{:S(2)}) collective-permute-start(bf16[256,1408]{1,0:T(8,128)(2,1)S(1)} %collective-permute-done.30), channel_id=1, source_target_pairs={{0,4},{4,0},{8,12},{12,8},{16,20},{20,16},{24,28},{28,24},{1,5},{5... | collective-permute-start | bytes 2162696 | tf_op jit(solution)/shard_map/ppermute | solution.py:311
  385.3 52.0 %collective-permute-start.41 = (bf16[256,2048]{1,0:T(8,128)(2,1)S(1)}, bf16[256,2048]{1,0:T(8,128)(2,1)S(1)}, u32[]{:S(2)}, u32[]{:S(2)}) collective-permute-start(bf16[256,2048]{1,0:T(8,128)(2,1)S(1)} %get-tuple-element.198), channel_id=1, source_target_pairs={{0,8},{4,20},{8,0},{12,28},{16,24},{20,4},{24,16},{28,12},{1,9},{5... | collective-permute-start | bytes 3145736 | tf_op jit(solution)/shard_map/ppermute | solution.py:314
  387.4 52.2 %collective-permute-start.35 = (bf16[256,2048]{1,0:T(8,128)(2,1)S(1)}, bf16[256,2048]{1,0:T(8,128)(2,1)}, u32[]{:S(2)}, u32[]{:S(2)}) collective-permute-start(bf16[256,2048]{1,0:T(8,128)(2,1)S(1)} %broadcast_select_fusion.2), channel_id=1, source_target_pairs={{0,8},{4,20},{8,0},{12,28},{16,24},{20,4},{24,16},{28,12},{1,9},{5... | collective-permute-start | bytes 3145736 | tf_op jit(solution)/shard_map/ppermute | solution.py:314
  422.1 104.5 %collective-permute-start.34 = (bf16[256,2048]{1,0:T(8,128)(2,1)}, bf16[256,2048]{1,0:T(8,128)(2,1)}, u32[]{:S(2)}, u32[]{:S(2)}) collective-permute-start(bf16[256,2048]{1,0:T(8,128)(2,1)} %get-tuple-element.249), channel_id=1, source_target_pairs={{0,8},{4,20},{8,0},{12,28},{16,24},{20,4},{24,16},{28,12},{1,9},{5... | collective-permute-start | bytes 3145736 | tf_op jit(solution)/shard_map/ppermute | solution.py:314
  451.1 41.6 %collective-permute-start.42 = (bf16[256,2048]{1,0:T(8,128)(2,1)}, bf16[256,2048]{1,0:T(8,128)(2,1)}, u32[]{:S(2)}, u32[]{:S(2)}) collective-permute-start(bf16[256,2048]{1,0:T(8,128)(2,1)} %fusion.13), channel_id=1, source_target_pairs={{0,8},{4,20},{8,0},{12,28},{16,24},{20,4},{24,16},{28,12},{1,9},{5... | collective-permute-start | bytes 3145736 | tf_op jit(solution)/shard_map/ppermute | solution.py:314
  455.1 47.3 %collective-permute-start.36 = (bf16[256,2048]{1,0:T(8,128)(2,1)}, bf16[256,2048]{1,0:T(8,128)(2,1)}, u32[]{:S(2)}, u32[]{:S(2)}) collective-permute-start(bf16[256,2048]{1,0:T(8,128)(2,1)} %get-tuple-element.191), channel_id=1, source_target_pairs={{0,8},{4,20},{8,0},{12,28},{16,24},{20,4},{24,16},{28,12},{1,9},{5... | collective-permute-start | bytes 3145736 | tf_op jit(solution)/shard_map/ppermute | solution.py:314
  499.0 22.8 %collective-permute-start.43 = (bf16[256,2048]{1,0:T(8,128)(2,1)S(1)}, bf16[256,2048]{1,0:T(8,128)(2,1)S(1)}, u32[]{:S(2)}, u32[]{:S(2)}) collective-permute-start(bf16[256,2048]{1,0:T(8,128)(2,1)S(1)} %get-tuple-element.244), channel_id=1, source_target_pairs={{0,16},{4,12},{8,24},{12,4},{16,0},{20,28},{24,8},{28,20},{1,17},{... | collective-permute-start | bytes 3145736 | tf_op jit(solution)/shard_map/ppermute | solution.py:314
  499.7 24.6 %collective-permute-start.40 = (bf16[256,2048]{1,0:T(8,128)(2,1)S(1)}, bf16[256,2048]{1,0:T(8,128)(2,1)S(1)}, u32[]{:S(2)}, u32[]{:S(2)}) collective-permute-start(bf16[256,2048]{1,0:T(8,128)(2,1)S(1)} %broadcast_select_fusion.1), channel_id=1, source_target_pairs={{0,8},{4,20},{8,0},{12,28},{16,24},{20,4},{24,16},{28,12},{1,9},{5... | collective-permute-start | bytes 3145736 | tf_op jit(solution)/shard_map/ppermute | solution.py:314
  505.3 30.2 %collective-permute-start.37 = (bf16[256,2048]{1,0:T(8,128)(2,1)S(1)}, bf16[256,2048]{1,0:T(8,128)(2,1)S(1)}, u32[]{:S(2)}, u32[]{:S(2)}) collective-permute-start(bf16[256,2048]{1,0:T(8,128)(2,1)S(1)} %get-tuple-element.188), channel_id=1, source_target_pairs={{0,16},{4,12},{8,24},{12,4},{16,0},{20,28},{24,8},{28,20},{1,17},{... | collective-permute-start | bytes 3145736 | tf_op jit(solution)/shard_map/ppermute | solution.py:314
  553.7 14.6 %collective-permute-start.44 = (bf16[256,1024]{1,0:T(8,128)(2,1)}, bf16[256,1024]{1,0:T(8,128)(2,1)}, u32[]{:S(2)}, u32[]{:S(2)}) collective-permute-start(bf16[256,1024]{1,0:T(8,128)(2,1)} %get-tuple-element.54), channel_id=1, source_target_pairs={{1,0},{2,1},{3,2},{5,4},{6,5},{7,6},{9,8},{10,9},{11,10},{13,12},{... | collective-permute-start | bytes 1572872 | tf_op jit(solution)/shard_map/ppermute | solution.py:513
  571.3 14.4 %collective-permute-start.45 = (bf16[256,1024]{1,0:T(8,128)(2,1)}, bf16[256,1024]{1,0:T(8,128)(2,1)}, u32[]{:S(2)}, u32[]{:S(2)}) collective-permute-start(bf16[256,1024]{1,0:T(8,128)(2,1)} %get-tuple-element.56), channel_id=1, source_target_pairs={{1,0},{2,1},{3,2},{5,4},{6,5},{7,6},{9,8},{10,9},{11,10},{13,12},{... | collective-permute-start | bytes 1572872 | tf_op jit(solution)/shard_map/ppermute | solution.py:513
  591.0 18.6 %collective-permute-start.46 = (bf16[256,1024]{1,0:T(8,128)(2,1)}, bf16[256,1024]{1,0:T(8,128)(2,1)}, u32[]{:S(2)}, u32[]{:S(2)}) collective-permute-start(bf16[256,1024]{1,0:T(8,128)(2,1)} %get-tuple-element.58), channel_id=1, source_target_pairs={{1,0},{2,1},{3,2},{5,4},{6,5},{7,6},{9,8},{10,9},{11,10},{13,12},{... | collective-permute-start | bytes 1572872 | tf_op jit(solution)/shard_map/ppermute | solution.py:513
  669.2 276.0 %all-reduce.7.cloned.1.call-start = ((), (), s32[]{:S(2)}) async-start(), calls=%async_computation.1 | async-start | bytes 6488064 | tf_op jit(solution)/shard_map/psum | solution.py:666
  (177 other events, 2550.8 us)
Sparse Core Ops, SparseCore 0:
  669.3 126.4 all-reduce.4
  804.4 140.7 all-reduce.6

commit v2 on v1

v2 whole, which is shorter than its diff:
```python
import functools

import jax
import jax.numpy as jnp
from jax import lax
from jax.experimental import pallas as pl
from jax.experimental.pallas import tpu as pltpu
from jax.sharding import PartitionSpec as P

D = 2048
KV_HEADS = 4
HEAD = 128
FF = 5632
RANK = 16
GROUP = 4
KVW = 512

EXT = 128
WIDE = D + EXT
SLOTS = 3
INV_AT = 48
PROJ_AT = 64
AUX = 32

factor = 32.0 / RANK
rms_eps = 1e-05
rope_base = 10000.0
masked_score = -1e30
log2_e = 1.4426950408889634
score_scale = HEAD ** (-0.5)
f32 = jnp.float32
bf16 = jnp.bfloat16


def dot_nt(left, right):
    return lax.dot_general(left, right, (((1,), (1,)), ((), ())), preferred_element_type=f32)


def dot_nn(left, right):
    return lax.dot_general(left, right, (((1,), (0,)), ((), ())), preferred_element_type=f32)


def dot_tn(left, right):
    return lax.dot_general(left, right, (((0,), (0,)), ((), ())), preferred_element_type=f32)


def limits(mebibytes):
    return pltpu.CompilerParams(vmem_limit_bytes=mebibytes << 20)


kernel_call = functools.partial(
    pl.pallas_call, cost_estimate=pl.CostEstimate(flops=0, transcendentals=0, bytes_accessed=0)
)


anywhere = pl.BlockSpec(memory_space=pltpu.HBM)
in_vmem = pl.BlockSpec(memory_space=pltpu.VMEM)
in_smem = pl.BlockSpec(memory_space=pltpu.SMEM)


def shape_of(shape, dtype=f32):
    return jax.ShapeDtypeStruct(shape, dtype)


def split_low(value):
    high = value.astype(bf16)
    return high, (value - high.astype(f32)).astype(bf16)


def iota(shape, dim):
    return lax.broadcasted_iota(jnp.int32, shape, dim)


def lanes_at(start):
    return pl.ds(pl.multiple_of(start, HEAD), HEAD)


def fold_kernel(weight_ref, rank_in_ref, rank_out_ref, mag_ref, out_ref, column_ref, *, first_slot, moving):
    slot = first_slot + (pl.program_id(0) if moving else 0)
    rows = weight_ref.shape[1]

    def placed_at(start):
        spot = iota((RANK, EXT), 1) == iota((RANK, EXT), 0) + start
        return jnp.where(spot, 1.0, 0.0).astype(bf16)

    @pl.when(pl.program_id(1) == 0)
    def _():
        column_ref[0] = dot_tn(rank_out_ref[0], placed_at(0))
        column_ref[1] = dot_tn(rank_out_ref[0], placed_at(RANK * slot))
        mags = jnp.broadcast_to(mag_ref[0], (8, mag_ref.shape[2]))
        one = jnp.where(iota((8, EXT), 0) == 0, 1.0, 0.0)
        column_ref[2] = lax.dot_general(
            mags, one, (((0,), (0,)), ((), ())), precision=lax.Precision.HIGHEST, preferred_element_type=f32
        )

    own = pl.ds(pl.multiple_of(pl.program_id(1) * rows, 16), rows)
    doubled = (factor * column_ref[0, own, :RANK]).astype(bf16)
    merged = weight_ref[0].astype(f32) + dot_nn(doubled, rank_in_ref[0])
    inverse = 1.0 / jnp.sqrt(jnp.sum(merged * merged, axis=1, keepdims=True))
    scale = column_ref[2, own, :1] * inverse
    folded = (merged * scale).astype(bf16)
    out_ref[0, :, :D] = folded
    ext = column_ref[1, own, :] * (factor * scale)
    for index, part in enumerate(split_low(dot_nt(folded, rank_in_ref[0]))):
        ext = ext + dot_nn(part, placed_at(PROJ_AT + RANK * index))
    lane = iota(ext.shape, 1)
    for index, part in enumerate(split_low(inverse)):
        ext = ext + jnp.where(lane == INV_AT + index, part.astype(f32), 0.0)
    out_ref[0, :, D:] = ext.astype(bf16)


def fold(weights, rank_in_t, rank_out, magnitude, rank_first, moving, name, first=0):
    members, columns = magnitude.shape
    pieces = 4 if columns % 64 == 0 and columns > 256 else 1
    rows = columns // pieces
    rank_block = (lambda b, c: (b + rank_first, 0, 0)) if moving else (lambda b, c: (rank_first, 0, 0))
    return kernel_call(
        functools.partial(fold_kernel, first_slot=rank_first, moving=moving),
        out_shape=shape_of((members, columns, WIDE), bf16),
        grid=(members, pieces),
        in_specs=[
            pl.BlockSpec((1, rows, D), lambda b, c: (b + first, c, 0)),
            pl.BlockSpec((1, RANK, D), rank_block),
            pl.BlockSpec((1, RANK, columns), lambda b, c: (b, 0, 0)),
            pl.BlockSpec((1, 1, columns), lambda b, c: (b, 0, 0)),
        ],
        out_specs=pl.BlockSpec((1, rows, WIDE), lambda b, c: (b, c, 0)),
        scratch_shapes=[pltpu.VMEM((3, columns, EXT), f32)],
        compiler_params=limits(32),
        name=name,
    )(weights, rank_in_t, rank_out, magnitude[:, None, :])


def fold_down_kernel(weight_ref, rank_in_ref, rank_out_ref, mag_ref, out_ref, proj_ref, merged_ref, *, chips):
    rows = weight_ref.shape[0] // chips
    total = 0.0
    doubled = (factor * rank_out_ref[...].astype(f32)).astype(bf16)
    for part in range(chips):
        span = slice(part * rows, (part + 1) * rows)
        merged = weight_ref[span, :].astype(f32) + dot_tn(rank_in_ref[:, span], doubled)
        merged_ref[span, :] = merged
        total = total + jnp.sum(merged * merged, axis=0, keepdims=True)
    inverse = 1.0 / jnp.sqrt(total)
    scale = mag_ref[...] * inverse
    high, low = split_low(inverse)
    row = iota((AUX - RANK, scale.shape[1]), 0)
    tail = jnp.where(row == 0, high.astype(f32), jnp.where(row == 1, low.astype(f32), 0.0))
    aux = jnp.concatenate([doubled.astype(f32) * scale, tail], axis=0).astype(bf16)
    proj = 0.0
    for part in range(chips):
        span = slice(part * rows, (part + 1) * rows)
        folded = (merged_ref[span, :] * scale).astype(bf16)
        out_ref[part, :rows, :] = folded
        out_ref[part, rows:, :] = aux
        proj = proj + dot_nn(rank_in_ref[:, span], folded)
    proj_ref[...] = proj


def fold_down(weights, rank_in_t, rank_out, magnitude, chips):
    inputs, columns = weights.shape
    return kernel_call(
        functools.partial(fold_down_kernel, chips=chips),
        out_shape=(shape_of((chips, inputs // chips + AUX, columns), bf16), shape_of((RANK, columns))),
        scratch_shapes=[pltpu.VMEM((inputs, columns), f32)],
        compiler_params=limits(32),
        name="fold_down",
    )(weights, rank_in_t, rank_out, magnitude[None])


def head_kernel(scalar_ref, first_ref, second_ref, input_ref, cos_ref, sin_ref, *refs, roped):
    before_refs, (weight_ref, out_ref, token_ref) = refs[:-3], refs[-3:]
    members, half = first_ref.shape[0], first_ref.shape[1]
    for member in range(members):
        for order, ref in ((scalar_ref[0], first_ref), (1 - scalar_ref[0], second_ref)):
            weight_ref[pl.ds(pl.multiple_of((2 * member + order) * half, half), half), :] = ref[member]
    wide = members * HEAD
    for index, ref in enumerate(before_refs):
        out_ref[:, pl.ds(pl.multiple_of(scalar_ref[2 + index] * wide, wide), wide)] = ref[...]
    raw = dot_nt(input_ref[...], weight_ref[:, :D])
    for member in range(members):
        part = raw[:, member * HEAD : (member + 1) * HEAD]
        if member < roped:
            part = part * cos_ref[...] + pltpu.roll(part, HEAD // 2, 1) * sin_ref[...]
        start = (scalar_ref[1] * wide if before_refs else 0) + member * HEAD
        out_ref[:, lanes_at(start)] = part.astype(bf16)
    token_ref[...] = jnp.zeros(token_ref.shape, f32)


def head_step(scalars, first, second, inputs, tables, roped, before, name):
    members, half, _ = first.shape
    tokens = inputs.shape[0]
    wide = members * HEAD
    return kernel_call(
        functools.partial(head_kernel, roped=roped),
        out_shape=(
            shape_of((wide, WIDE), bf16),
            shape_of((tokens, (1 + len(before)) * wide), bf16),
            shape_of((8, HEAD)),
        ),
        in_specs=[in_smem] + [in_vmem] * (5 + len(before)),
        out_specs=(in_vmem,) * 3,
        compiler_params=limits(24),
        name=name,
    )(scalars, first, second, inputs, *tables, *before)


def head_copies(weight_ref, head, out_ref, semaphores, first=0):
    devices, members, part = weight_ref.shape[:3]
    parts = devices // KV_HEADS
    copies = []
    for at in range(parts):
        for member in range(members):
            copies.append(
                pltpu.make_async_copy(
                    weight_ref.at[parts * head + at, member],
                    out_ref.at[pl.ds((parts * member + at) * part, part), :],
                    semaphores.at[first + len(copies)],
                )
            )
    return copies


def head_scratch(weights):
    each = weights.shape[0] // KV_HEADS * weights.shape[1]
    return [
        pltpu.VMEM((KV_HEADS, weights.shape[1] * HEAD, WIDE), bf16),
        pltpu.SemaphoreType.DMA((KV_HEADS * each,)),
    ]


def all_head_copies(weight_ref, out_ref, semaphores):
    each = weight_ref.shape[0] // KV_HEADS * weight_ref.shape[1]
    return [head_copies(weight_ref, head, out_ref.at[head], semaphores, head * each) for head in range(KV_HEADS)]


def next_head(copies, head):
    if head == 0:
        for copy in copies[0] + copies[1]:
            copy.start()
    elif head + 1 < len(copies):
        for copy in copies[head + 1]:
            copy.start()
    for copy in copies[head]:
        copy.wait()


def query_kernel(input_ref, cos_ref, sin_ref, weight_hbm, out_ref, weight_ref, semaphores):
    copies = all_head_copies(weight_hbm, weight_ref, semaphores)
    for head in range(KV_HEADS):
        next_head(copies, head)
        raw = dot_nt(input_ref[...], weight_ref[head, :, :D])
        for group in range(GROUP):
            part = raw[:, group * HEAD : (group + 1) * HEAD]
            part = part * cos_ref[...] + pltpu.roll(part, HEAD // 2, 1) * sin_ref[...]
            start = (head * GROUP + group) * HEAD
            out_ref[:, start : start + HEAD] = part.astype(bf16)


def query_project(inputs, tables, weights):
    return kernel_call(
        query_kernel,
        out_shape=shape_of((inputs.shape[0], D), bf16),
        in_specs=[in_vmem] * 3 + [anywhere],
        out_specs=in_vmem,
        scratch_shapes=head_scratch(weights),
        compiler_params=limits(24),
        name="query_project",
    )(inputs, *tables, weights)


def masked_scores(keys, queries, key_first, length, causal):
    tokens, lanes = keys.shape[0], queries.shape[0]
    scores = dot_nt(keys, queries)
    key_pos = key_first + iota((tokens, 1), 0)
    scores = scores + jnp.where(key_pos < length, 0.0, masked_score)
    if causal:
        allowed = iota((tokens, lanes), 0) <= (iota((tokens, lanes), 1) & (tokens - 1))
        scores = jnp.where(allowed, scores, masked_score)
    return scores


def attend_kernel(scalar_ref, query_ref, *refs, steps):
    kv_refs = refs[:steps]
    mixed_ref, lse_ref, stacked_ref, max_ref, sum_ref, accum_ref = refs[steps:]
    head = pl.program_id(0)
    tokens = query_ref.shape[0]
    block_index, length = scalar_ref[0], scalar_ref[1]
    scale = score_scale * log2_e
    for group in range(GROUP):
        stacked_ref[group * tokens : (group + 1) * tokens, :] = query_ref[:, group * HEAD : (group + 1) * HEAD]

    for distance in range(steps):

        def step(distance=distance):
            keys = kv_refs[distance][:, :HEAD]
            values = kv_refs[distance][:, HEAD:]
            key_first = (block_index - distance) * tokens
            scores = masked_scores(keys, stacked_ref[...], key_first, length, distance == 0)
            block_max = jnp.max(scores, axis=0, keepdims=True)
            new_max = block_max if distance == 0 else jnp.maximum(max_ref[...], block_max)
            terms = jnp.exp2((scores - new_max) * scale)
            added = jnp.sum(terms, axis=0, keepdims=True)
            product = dot_tn(values, terms.astype(bf16))
            if distance == 0:
                sum_ref[...] = added
                accum_ref[...] = product
            else:
                fade = jnp.exp2((max_ref[...] - new_max) * scale)
                sum_ref[...] = sum_ref[...] * fade + added
                accum_ref[...] = accum_ref[...] * fade + product
            max_ref[...] = new_max

        if distance == 0:
            step()
        else:
            pl.when(block_index >= distance)(step)
    mixed = accum_ref[...] / sum_ref[...]
    for group in range(GROUP):
        part = mixed[:, group * tokens : (group + 1) * tokens]
        mixed_ref[:, lanes_at(group * KVW + head * HEAD)] = part.T.astype(bf16)
    lse_ref[0] = max_ref[...] * scale + jnp.log(sum_ref[...]) * log2_e


def attend(scalars, queries, kv_blocks):
    tokens = queries.shape[0]
    steps = len(kv_blocks)
    lanes = GROUP * tokens
    return kernel_call(
        functools.partial(attend_kernel, steps=steps),
        out_shape=(shape_of((tokens, D), bf16), shape_of((KV_HEADS, 1, lanes))),
        grid_spec=pltpu.PrefetchScalarGridSpec(
            num_scalar_prefetch=1,
            grid=(KV_HEADS,),
            in_specs=[pl.BlockSpec((tokens, GROUP * HEAD), lambda j, s: (0, j))]
            + [pl.BlockSpec((tokens, 2 * HEAD), lambda j, s: (0, j))] * steps,
            out_specs=(
                pl.BlockSpec((tokens, D), lambda j, s: (0, 0)),
                pl.BlockSpec((1, 1, lanes), lambda j, s: (j, 0, 0)),
            ),
            scratch_shapes=[
                pltpu.VMEM((lanes, HEAD), bf16),
                pltpu.VMEM((1, lanes), f32),
                pltpu.VMEM((1, lanes), f32),
                pltpu.VMEM((HEAD, lanes), f32),
            ],
        ),
        compiler_params=limits(40),
        name="attend",
    )(scalars, queries, *kv_blocks)


def attend_back_kernel(scalar_ref, query_ref, grad_ref, lse_ref, delta_ref, kv_ref, *refs, distance, chained):
    if chained:
        before_ref, grad_query_ref, grad_kv_ref, stacked_ref, stacked_grad_ref = refs
    else:
        grad_query_ref, grad_kv_ref, stacked_ref, stacked_grad_ref = refs
    head = pl.program_id(0)
    tokens = query_ref.shape[0]
    block_index, length = scalar_ref[0], scalar_ref[1]
    active = (block_index >= distance) & (block_index * tokens < length)

    @pl.when(active)
    def _():
        for group in range(GROUP):
            rows = slice(group * tokens, (group + 1) * tokens)
            stacked_ref[rows, :] = query_ref[:, group * HEAD : (group + 1) * HEAD]
            stacked_grad_ref[rows, :] = grad_ref[:, lanes_at(group * KVW + head * HEAD)]
        keys = kv_ref[:, :HEAD]
        values = kv_ref[:, HEAD:]
        key_first = (block_index - distance) * tokens
        scores = masked_scores(keys, stacked_ref[...], key_first, length, distance == 0)
        probs = jnp.exp2(scores * (score_scale * log2_e) - lse_ref[0])
        grad_probs = dot_nt(values, stacked_grad_ref[...])
        grad_scores = (probs * (grad_probs - delta_ref[0])).astype(bf16)
        grad_values = dot_nn(probs.astype(bf16), stacked_grad_ref[...])
        grad_keys = dot_nn(grad_scores, stacked_ref[...]) * score_scale
        grad_queries = dot_tn(grad_scores, keys) * score_scale
        for group in range(GROUP):
            lanes = slice(group * HEAD, (group + 1) * HEAD)
            part = grad_queries[group * tokens : (group + 1) * tokens, :]
            if chained:
                part = part + before_ref[:, lanes]
            grad_query_ref[:, lanes] = part
        grad_kv_ref[:, :HEAD] = grad_keys.astype(grad_kv_ref.dtype)
        grad_kv_ref[:, HEAD:] = grad_values.astype(grad_kv_ref.dtype)

    @pl.when(jnp.logical_not(active))
    def _():
        grad_query_ref[...] = before_ref[...] if chained else jnp.zeros(grad_query_ref.shape, f32)
        grad_kv_ref[...] = jnp.zeros(grad_kv_ref.shape, grad_kv_ref.dtype)


def attend_back(scalars, queries, grad_mixed, lse, delta, kv_block, before, distance):
    tokens = queries.shape[0]
    lanes = GROUP * tokens
    row = pl.BlockSpec((1, 1, lanes), lambda j, s: (j, 0, 0))
    per_query = pl.BlockSpec((tokens, GROUP * HEAD), lambda j, s: (0, j))
    per_key = pl.BlockSpec((tokens, 2 * HEAD), lambda j, s: (0, j))
    chained = before is not None
    operands = [scalars, queries, grad_mixed, lse, delta, kv_block]
    specs = [per_query, pl.BlockSpec((tokens, D), lambda j, s: (0, 0)), row, row, per_key]
    if chained:
        operands += [before]
        specs += [per_query]
    return kernel_call(
        functools.partial(attend_back_kernel, distance=distance, chained=chained),
        out_shape=(shape_of((tokens, D)), shape_of((tokens, 2 * KVW), f32 if distance == 0 else bf16)),
        grid_spec=pltpu.PrefetchScalarGridSpec(
            num_scalar_prefetch=1,
            grid=(KV_HEADS,),
            in_specs=specs,
            out_specs=(per_query, per_key),
            scratch_shapes=[pltpu.VMEM((lanes, HEAD), bf16), pltpu.VMEM((lanes, HEAD), bf16)],
        ),
        input_output_aliases={6: 0} if chained else {},
        compiler_params=limits(40),
        name=f"attend_back_{distance}",
    )(*operands)


def rms_inverse(values):
    return lax.rsqrt(jnp.mean(values * values, axis=-1, keepdims=True) + rms_eps)


def rms_back(values, inverse, gain, grad):
    scaled = grad * gain
    return inverse * (scaled - values * (inverse * inverse * jnp.mean(scaled * values, axis=-1, keepdims=True)))


def output_kernel(mixed_ref, input_ref, gain_ref, weight_hbm, residual_ref, normed_ref, weight_ref, semaphores):
    copies = all_head_copies(weight_hbm, weight_ref, semaphores)
    for head in range(KV_HEADS):
        next_head(copies, head)
        value = dot_nt(mixed_ref[...], weight_ref[head, :, :D])
        for group in range(GROUP):
            start = group * KVW + head * HEAD
            lanes = slice(start, start + HEAD)
            residual_ref[:, lanes] = input_ref[:, lanes].astype(f32) + value[:, group * HEAD : (group + 1) * HEAD]
    values = residual_ref[...]
    normed_ref[...] = (values * rms_inverse(values) * gain_ref[...]).astype(bf16)


def output_project(mixed, weights, inputs, gain):
    tokens = mixed.shape[0]
    return kernel_call(
        output_kernel,
        out_shape=(shape_of((tokens, D)), shape_of((tokens, D), bf16)),
        in_specs=[in_vmem] * 3 + [anywhere],
        out_specs=(in_vmem,) * 2,
        scratch_shapes=head_scratch(weights),
        compiler_params=limits(28),
        name="output_project",
    )(mixed, inputs, gain[None], weights)


def feed_forward_kernel(normed_ref, own_ref, partner_ref, gate_ref, up_ref, weight_ref, semaphores, *, block):
    copies = []
    for half, ref in enumerate((own_ref, partner_ref)):
        for member in range(2):
            at = 2 * half + member
            copies.append(pltpu.make_async_copy(ref.at[member], weight_ref.at[at], semaphores.at[at]))
    copies[0].start()
    copies[1].start()
    for half in range(2):
        for member, out_ref in enumerate((gate_ref, up_ref)):
            at = 2 * half + member
            copies[at].wait()
            if at + 2 < 4:
                copies[at + 2].start()
            for start in range(0, normed_ref.shape[0], block):
                rows = slice(start, start + block)
                out_ref[half, rows, :] = dot_nt(normed_ref[rows, :], weight_ref[at, :, :D])


def feed_forward(normed, own, partner, block):
    tokens = normed.shape[0]
    columns = own.shape[1]
    return kernel_call(
        functools.partial(feed_forward_kernel, block=block),
        out_shape=(shape_of((2, tokens, columns)), shape_of((2, tokens, columns))),
        in_specs=[in_vmem, anywhere, anywhere],
        out_specs=(in_vmem,) * 2,
        scratch_shapes=[pltpu.VMEM((4, columns, WIDE), bf16), pltpu.SemaphoreType.DMA((4,))],
        compiler_params=limits(24),
        name="feed_forward",
    )(normed, own, partner)


def grad_copies(place_ref, grad_hbm, grad_ref, semaphores, chips, block, first):
    return [
        pltpu.make_async_copy(
            grad_hbm.at[0 if r is None else place_ref[1] ^ (2 * r)], grad_ref.at[pl.ds(turn * block, block), :], semaphores.at[first + turn]
        )
        for turn, r in enumerate(chips)
    ]


def feed_back_kernel(place_ref, grad_hbm, gate_ref, up_ref, own_ref, partner_ref, *refs, block, devices, chips):
    piece_refs, refs = refs[:devices], refs[devices:]
    share_refs, down_refs, refs = refs[: len(chips)], refs[len(chips) : 2 * len(chips)], refs[2 * len(chips) :]
    ext_ref, hidden_ref, grad_gate_ref, grad_up_ref, down_ext_ref, mag_ref, down_mag_ref = refs[:7]
    aux_ref, weight_ref, down_weight_ref, grad_ref, semaphores = refs[7:]
    core = place_ref[0]
    columns = own_ref.shape[1]
    width = piece_refs[0].shape[1]
    copies = grad_copies(place_ref, grad_hbm, grad_ref, semaphores, chips, block, devices + 2)
    for i, ref in enumerate(piece_refs):
        lanes = pl.ds(pl.multiple_of((place_ref[1] ^ i) * width, width), width)
        copies.append(pltpu.make_async_copy(ref, down_weight_ref.at[:, lanes], semaphores.at[i]))
    for copy in copies:
        copy.start()
    weight_copies = [
        pltpu.make_async_copy(ref, weight_ref.at[half], semaphores.at[devices + half])
        for half, ref in enumerate((own_ref, partner_ref))
    ]
    mag_ref[...] = jnp.zeros(mag_ref.shape, f32)
    down_mag_ref[...] = jnp.zeros(down_mag_ref.shape, f32)
    weight_copies[0].start()
    for copy in copies:
        copy.wait()
    weight_copies[1].start()
    aux_ref[...] = down_weight_ref[2 * columns :, :]

    def step(turn, carry):
        rows = pl.ds(pl.multiple_of(turn * block, block), block)
        grad = grad_ref[rows, :]
        down_ext_ref[rows, :] = dot_nt(grad, down_weight_ref[2 * columns :, :]).astype(bf16)
        share, down = None, None
        for half in range(2):
            order = core if half == 0 else 1 - core
            down_rows = pl.ds(pl.multiple_of(order * columns, 16), columns)
            gate, up = gate_ref[half, rows, :], up_ref[half, rows, :]
            grad_hidden = dot_nt(grad, down_weight_ref[down_rows, :])
            sigma = 1.0 / (1.0 + jnp.exp(-gate))
            silu = gate * sigma
            hidden = (silu * up).astype(bf16)
            grad_gate = grad_hidden * up * (sigma + silu * (1.0 - sigma))
            grad_up = grad_hidden * silu
            mag_ref[half : half + 1, :] += jnp.sum(grad_gate * gate, axis=0, keepdims=True)
            mag_ref[2 + half : 3 + half, :] += jnp.sum(grad_up * up, axis=0, keepdims=True)
            grad_gate, grad_up = grad_gate.astype(bf16), grad_up.astype(bf16)
            hidden_ref[half, rows, :] = hidden
            grad_gate_ref[half, rows, :] = grad_gate
            grad_up_ref[half, rows, :] = grad_up
            part = dot_nn(hidden, down_weight_ref[down_rows, :])
            down = part if down is None else down + part
            pl.when(turn == 0)(weight_copies[half].wait)
            part = dot_nn(grad_gate, weight_ref[half, 0]) + dot_nn(grad_up, weight_ref[half, 1])
            share = part if share is None else share + part
        ext_ref[rows, :] = share[:, D:].astype(bf16)
        for at in range(len(chips)):

            @pl.when((turn ^ core if len(chips) == 2 else turn) == at)
            def _(at=at):
                share_refs[at][...] = share[:, :D].astype(bf16)
                down_refs[at][...] = down.astype(bf16)

        down_mag_ref[0:1, :] += jnp.sum(grad.astype(f32) * down, axis=0, keepdims=True)
        return carry

    lax.fori_loop(0, len(chips), step, 0)


def feed_back(place, grads, chips, gate, up, own, partner, pieces, block):
    tokens = len(chips) * block
    columns = own.shape[1]
    devices = len(pieces)
    return kernel_call(
        functools.partial(feed_back_kernel, block=block, devices=devices, chips=chips),
        out_shape=(shape_of((block, D), bf16),) * (2 * len(chips))
        + (
            shape_of((tokens, EXT), bf16),
            shape_of((2, tokens, columns), bf16),
            shape_of((2, tokens, columns), bf16),
            shape_of((2, tokens, columns), bf16),
            shape_of((tokens, AUX), bf16),
            shape_of((4, columns)),
            shape_of((8, D)),
            shape_of((AUX, D), bf16),
        ),
        in_specs=[in_smem, anywhere, in_vmem, in_vmem] + [anywhere] * (2 + devices),
        out_specs=(in_vmem,) * (8 + 2 * len(chips)),
        scratch_shapes=[
            pltpu.VMEM((2, 2, columns, WIDE), bf16),
            pltpu.VMEM((2 * columns + AUX, D), bf16),
            pltpu.VMEM((tokens, D), bf16),
            pltpu.SemaphoreType.DMA((2 + devices + len(chips),)),
        ],
        compiler_params=limits(40),
        name="feed_back",
    )(place, grads, gate, up, own, partner, *pieces)


def feed_adapter_kernel(
    place_ref, normed_ref, grad_hbm, hidden_ref, grad_gate_ref, grad_up_ref, ext_ref, down_ext_ref, rank_in_ref,
    down_in_ref, in_ref, out_ref, down_rank_in_ref, down_out_ref, grad_ref, semaphores, *, chips, block,
):
    copies = grad_copies(place_ref, grad_hbm, grad_ref, semaphores, chips, block, 0)
    for copy in copies:
        copy.start()
    normed = normed_ref[...]
    small = dot_nt(rank_in_ref[...], normed).astype(bf16)
    in_ref[...] = dot_nn(ext_ref[...].T[: 2 * RANK], normed)
    down_small = 0.0
    grad_small = down_ext_ref[...].T[:RANK]
    for half in range(2):
        hidden = hidden_ref[half]
        out_ref[half, :RANK] = dot_nn(small[:RANK], grad_gate_ref[half])
        out_ref[half, RANK:] = dot_nn(small[RANK:], grad_up_ref[half])
        down_small = down_small + dot_nt(down_in_ref[half], hidden)
        down_rank_in_ref[half] = dot_nn(grad_small, hidden)
    for copy in copies:
        copy.wait()
    down_out_ref[...] = dot_nn(down_small.astype(bf16), grad_ref[...])


def feed_adapter(place, normed, grads, chips, hidden, grad_gate, grad_up, ext, down_ext, rank_in_t, down_in_t):
    columns = hidden.shape[2]
    return kernel_call(
        functools.partial(feed_adapter_kernel, chips=chips, block=normed.shape[0] // len(chips)),
        out_shape=(
            shape_of((2 * RANK, D)),
            shape_of((2, 2 * RANK, columns)),
            shape_of((2, RANK, columns)),
            shape_of((RANK, D)),
        ),
        in_specs=[in_smem, in_vmem, anywhere] + [in_vmem] * 7,
        out_specs=(in_vmem,) * 4,
        scratch_shapes=[pltpu.VMEM(normed.shape, bf16), pltpu.SemaphoreType.DMA((len(chips),))],
        compiler_params=limits(24),
        name="feed_adapter",
    )(place, normed, grads, hidden, grad_gate, grad_up, ext, down_ext, rank_in_t, down_in_t)


def adapter_columns(products, mag_raw, mag, weights, slot):
    ext = weights[:, D:].astype(f32).T
    inverse = ext[INV_AT : INV_AT + 1] + ext[INV_AT + 1 : INV_AT + 2]
    proj = ext[PROJ_AT : PROJ_AT + RANK] + ext[PROJ_AT + RANK : PROJ_AT + 2 * RANK]
    grad_mag = mag_raw / mag
    grad_out = factor * (products * (mag * inverse) - proj * (grad_mag * inverse))
    turned = ext[RANK * slot : RANK * (slot + 1)] * (-grad_mag / mag)
    return grad_mag, grad_out, dot_nn(turned.astype(bf16), weights[:, :D])


def finish_kernel(weight_ref, products_ref, mag_raw_ref, mag_ref, grad_mag_ref, grad_out_ref, grad_in_ref):
    for slot in range(2):
        grad_mag, grad_out, grad_in = adapter_columns(
            products_ref[slot * RANK : (slot + 1) * RANK],
            mag_raw_ref[slot : slot + 1],
            mag_ref[slot : slot + 1],
            weight_ref[slot],
            slot,
        )
        grad_mag_ref[slot : slot + 1] = grad_mag
        grad_out_ref[slot * RANK : (slot + 1) * RANK] = grad_out
        grad_in_ref[slot * RANK : (slot + 1) * RANK] = grad_in


def finish_columns(weights, products, mag_raw, mag):
    columns = weights.shape[1]
    return kernel_call(
        finish_kernel,
        out_shape=(shape_of((2, columns)), shape_of((2 * RANK, columns)), shape_of((2 * RANK, D))),
        compiler_params=limits(40),
        name="feed_finish",
    )(weights, products, mag_raw, mag)


def output_adapter_kernel(
    grad_ref, mag_raw_ref, mag_ref, mixed_ref, ext_ref, rank_in_ref, weight_hbm,
    grad_mag_ref, grad_out_ref, grad_in_ref, weight_ref, semaphores,
):
    copies = all_head_copies(weight_hbm, weight_ref, semaphores)
    small = dot_nt(rank_in_ref[...], mixed_ref[...]).astype(bf16)
    grad_in_total = dot_nn(ext_ref[...].T[:RANK], mixed_ref[...])
    wide = GROUP * HEAD
    for head in range(KV_HEADS):
        next_head(copies, head)
        lanes = slice(head * wide, (head + 1) * wide)
        place = slice(head * HEAD, (head + 1) * HEAD)
        mag = jnp.concatenate([mag_ref[group : group + 1, place] for group in range(GROUP)], axis=1)
        grad_mag, grad_out, grad_in = adapter_columns(
            dot_nn(small, grad_ref[:, lanes]), mag_raw_ref[:, lanes], mag, weight_ref[head], 0
        )
        for group in range(GROUP):
            own = slice(group * HEAD, (group + 1) * HEAD)
            at = slice(group * KVW + head * HEAD, group * KVW + (head + 1) * HEAD)
            grad_mag_ref[:, at] = grad_mag[:, own]
            grad_out_ref[:, at] = grad_out[:, own]
        grad_in_total = grad_in_total + grad_in
    grad_in_ref[...] = grad_in_total


def output_adapter(grads, mag_raw, mag, weights, mixed, ext, rank_in_t):
    return kernel_call(
        output_adapter_kernel,
        out_shape=(shape_of((1, D)), shape_of((RANK, D)), shape_of((RANK, D))),
        in_specs=[in_vmem] * 6 + [anywhere],
        out_specs=(in_vmem,) * 3,
        scratch_shapes=head_scratch(weights),
        compiler_params=limits(28),
        name="output_adapter",
    )(grads, mag_raw, mag, mixed, ext, rank_in_t, weights)


def residual_back_kernel(
    first_ref, second_ref, third_ref, residual_ref, gain_ref, cotangent_ref, input_ref, mixed_ref, weight_hbm,
    grad_ref, ordered_ref, mag_ref, ext_ref, grad_mixed_ref, delta_ref, weight_ref, semaphores, column_ref,
):
    tokens = residual_ref.shape[0]
    copies = all_head_copies(weight_hbm, weight_ref, semaphores)
    for head in range(KV_HEADS):
        for copy in copies[head]:
            copy.start()
    normed_grad = first_ref[...].astype(f32) + second_ref[...].astype(f32) + third_ref[...].astype(f32)
    values = residual_ref[...]
    grad_ref[...] = cotangent_ref[...].astype(f32) + rms_back(
        values, rms_inverse(values), gain_ref[...], normed_grad
    )
    wide = GROUP * HEAD
    total = None
    for head in range(KV_HEADS):
        for group in range(GROUP):
            start = group * KVW + head * HEAD
            lanes = slice(start, start + HEAD)
            own = slice(head * wide + group * HEAD, head * wide + (group + 1) * HEAD)
            grad = grad_ref[:, lanes]
            ordered_ref[:, own] = grad.astype(bf16)
            value = residual_ref[:, lanes] - input_ref[:, lanes].astype(f32)
            mag_ref[:, own] = jnp.sum(grad * value, axis=0, keepdims=True)
        for copy in copies[head]:
            copy.wait()
        part = dot_nn(ordered_ref[:, head * wide : (head + 1) * wide], weight_ref[head])
        total = part if total is None else total + part
    ext_ref[...] = total[:, D:].astype(bf16)
    grad_mixed_ref[...] = total[:, :D].astype(bf16)
    for head in range(KV_HEADS):
        for group in range(GROUP):
            start = group * KVW + head * HEAD
            lanes = slice(start, start + HEAD)
            both = grad_mixed_ref[:, lanes].astype(f32) * mixed_ref[:, lanes].astype(f32)
            column_ref[:, head * GROUP + group : head * GROUP + group + 1] = jnp.sum(both, axis=1, keepdims=True)
    rows = column_ref[...].T
    for head in range(KV_HEADS):
        for group in range(GROUP):
            at = head * GROUP + group
            delta_ref[head, :, group * tokens : (group + 1) * tokens] = rows[at : at + 1]


def residual_back(shares, residual, gain, cotangent, inputs, mixed, weights):
    tokens = residual.shape[0]
    lanes = GROUP * tokens
    return kernel_call(
        residual_back_kernel,
        out_shape=(
            shape_of((tokens, D)),
            shape_of((tokens, D), bf16),
            shape_of((1, D)),
            shape_of((tokens, EXT), bf16),
            shape_of((tokens, D), bf16),
            shape_of((KV_HEADS, 1, lanes)),
        ),
        in_specs=[in_vmem] * 8 + [anywhere],
        out_specs=(in_vmem,) * 6,
        scratch_shapes=head_scratch(weights) + [pltpu.VMEM((tokens, HEAD), f32)],
        compiler_params=limits(40),
        name="residual_back",
    )(*shares, residual, gain[None], cotangent, inputs, mixed, weights)


def turn_back(values, cosine, sine):
    return values * cosine - pltpu.roll(values, HEAD // 2, 1) * sine


def query_back_kernel(
    grad_ref, query_ref, cos_ref, sin_ref, normed_ref, rank_in_ref, mag_ref, weight_hbm,
    accum_ref, grad_in_ref, out_ref, grad_mag_ref, turned_ref, weight_ref, semaphores,
):
    copies = all_head_copies(weight_hbm, weight_ref, semaphores)
    wide = GROUP * HEAD
    small = dot_nt(rank_in_ref[...], normed_ref[...]).astype(bf16)
    total, grad_in_total = None, None
    for head in range(KV_HEADS):
        mags = []
        for group in range(GROUP):
            lanes = slice(head * wide + group * HEAD, head * wide + (group + 1) * HEAD)
            grad = turn_back(grad_ref[:, lanes], cos_ref[...], sin_ref[...])
            raw = turn_back(query_ref[:, lanes].astype(f32), cos_ref[...], sin_ref[...])
            mags.append(jnp.sum(grad * raw, axis=0, keepdims=True))
            turned_ref[:, lanes] = grad.astype(bf16)
        turned = turned_ref[:, head * wide : (head + 1) * wide]
        next_head(copies, head)
        part = dot_nn(turned, weight_ref[head])
        total = part if total is None else total + part
        place = slice(head * HEAD, (head + 1) * HEAD)
        mag = jnp.concatenate([mag_ref[group : group + 1, place] for group in range(GROUP)], axis=1)
        grad_mag, grad_out, grad_in = adapter_columns(
            dot_nn(small, turned), jnp.concatenate(mags, axis=1), mag, weight_ref[head], 0
        )
        grad_in_total = grad_in if grad_in_total is None else grad_in_total + grad_in
        for group in range(GROUP):
            own = slice(group * HEAD, (group + 1) * HEAD)
            at = slice(group * KVW + head * HEAD, group * KVW + (head + 1) * HEAD)
            grad_mag_ref[:, at] = grad_mag[:, own]
            out_ref[:, at] = grad_out[:, own]
    accum_ref[...] = total
    grad_in_ref[...] = grad_in_total + dot_nn(total[:, D:].astype(bf16).T[:RANK], normed_ref[...])


def query_back(grads, queries, weights, cosine, sine, normed, rank_in_t, mag):
    tokens = normed.shape[0]
    return kernel_call(
        query_back_kernel,
        out_shape=(
            shape_of((tokens, WIDE)),
            shape_of((RANK, D)),
            shape_of((RANK, D)),
            shape_of((1, D)),
        ),
        in_specs=[in_vmem] * 7 + [anywhere],
        out_specs=(in_vmem,) * 4,
        scratch_shapes=[pltpu.VMEM((tokens, D), bf16)] + head_scratch(weights),
        compiler_params=limits(40),
        name="query_back",
    )(grads, queries, cosine, sine, normed, rank_in_t, mag, weights)


def key_back_kernel(
    heads_ref, sent_ref, grad_ref, kv_ref, cos_ref, sin_ref, normed_ref, input_ref, gain_ref, residual_ref,
    before_ref, rank_in_ref, mag_ref, *refs,
):
    weight_refs = refs[:KV_HEADS]
    input_grad_ref, grad_in_ref, out_ref, grad_mag_ref, turned_ref = refs[KV_HEADS:]
    small = dot_nt(rank_in_ref[...], normed_ref[...]).astype(bf16)
    total = before_ref[...]
    near = 2 * HEAD
    grad_ins = [None, None]
    for slot in range(KV_HEADS):
        place = heads_ref[slot] * HEAD
        mags = []
        for part in range(2):
            lanes = lanes_at(2 * place + part * HEAD)
            grad = grad_ref[:, lanes] + sent_ref[:, lanes].astype(f32)
            raw = kv_ref[:, lanes].astype(f32)
            if part == 0:
                grad = turn_back(grad, cos_ref[...], sin_ref[...])
                raw = turn_back(raw, cos_ref[...], sin_ref[...])
            mags.append(jnp.sum(grad * raw, axis=0, keepdims=True))
            turned_ref[:, slot * near + part * HEAD : slot * near + (part + 1) * HEAD] = grad.astype(bf16)
        total = total + dot_nn(turned_ref[:, slot * near : (slot + 1) * near], weight_refs[slot][...])
        for part in range(2):
            lanes = slice(slot * near + part * HEAD, slot * near + (part + 1) * HEAD)
            grad_mag, grad_out, grad_in = adapter_columns(
                dot_nn(small[part * RANK : (part + 1) * RANK], turned_ref[:, lanes]),
                mags[part],
                mag_ref[part : part + 1, lanes_at(place)],
                weight_refs[slot][part * HEAD : (part + 1) * HEAD, :],
                1 + part,
            )
            grad_mag_ref[:, lanes_at(part * KVW + place)] = grad_mag
            out_ref[:, lanes_at(part * KVW + place)] = grad_out
            grad_ins[part] = grad_in if grad_ins[part] is None else grad_ins[part] + grad_in
    ext = total[:, D:].astype(bf16).T
    for part in range(2):
        rows = slice(part * RANK, (part + 1) * RANK)
        grad_in_ref[rows] = grad_ins[part] + dot_nn(ext[(1 + part) * RANK : (2 + part) * RANK], normed_ref[...])
    values = input_ref[...].astype(f32)
    back = rms_back(values, rms_inverse(values), gain_ref[...], total[:, :D])
    input_grad_ref[...] = (residual_ref[...] + back).astype(bf16)


def key_back(heads, sent, grads, kv, weights, cosine, sine, normed, inputs, gain, grad_residual, before, rank_in_t, mag):
    tokens = normed.shape[0]
    return kernel_call(
        key_back_kernel,
        out_shape=(
            shape_of((tokens, D), bf16),
            shape_of((2 * RANK, D)),
            shape_of((RANK, 2 * KVW)),
            shape_of((1, 2 * KVW)),
        ),
        in_specs=[in_smem] + [in_vmem] * (12 + KV_HEADS),
        out_specs=(in_vmem,) * 4,
        scratch_shapes=[pltpu.VMEM((tokens, 2 * KVW), bf16)],
        compiler_params=limits(40),
        name="key_back",
    )(
        heads, sent, grads, kv, cosine, sine, normed, inputs, gain[None], grad_residual,
        before, rank_in_t, mag, *weights,
    )


def cut_kernel(place_ref, value_ref, *out_refs):
    rows = out_refs[0].shape[0]
    for r, ref in enumerate(out_refs):
        ref[...] = value_ref[pl.ds(pl.multiple_of((place_ref[2] ^ r) * rows, rows), rows), :]


def cut_rows(place, value, chips):
    shape = shape_of((value.shape[0] // chips, value.shape[1]), value.dtype)
    return kernel_call(
        cut_kernel,
        out_shape=(shape,) * chips,
        in_specs=[in_smem, in_vmem],
        out_specs=(in_vmem,) * chips,
        name="cut_rows",
    )(place, value)


def join_kernel(place_ref, *refs):
    piece_refs, out_ref = refs[:-1], refs[-1]
    rows = piece_refs[0].shape[0]
    for r, ref in enumerate(piece_refs):
        out_ref[pl.ds(pl.multiple_of((place_ref[2] ^ r) * rows, rows), rows), :] = ref[...]


def join_rows(place, pieces):
    rows, lanes = pieces[0].shape
    return kernel_call(
        join_kernel,
        out_shape=shape_of((rows * len(pieces), lanes), pieces[0].dtype),
        in_specs=[in_smem] + [in_vmem] * len(pieces),
        out_specs=in_vmem,
        name="join_rows",
    )(place, *pieces)


class Order:
    def __init__(self):
        self.last = None

    def __call__(self, *values):
        if self.last is not None:
            values = lax.optimization_barrier(tuple(values) + (self.last,))[:-1]
        return values[0] if len(values) == 1 else values

    def mark(self, value):
        self.last = value
        return value

    def pin(self, *values):
        values = self(*values)
        self.last = values[0] if isinstance(values, (tuple, list)) else values
        return values


def after(value, *others):
    return lax.optimization_barrier((value,) + others)[0]


class Links:
    def __init__(self, devices, blocks):
        self.devices = devices
        self.blocks = blocks
        self.chips = devices // 2
        self.index = lax.axis_index("dp")
        self.core = self.index % 2
        self.chip = self.index // 2
        self.block = lax.axis_index("blk")
        self.square = self.chips == 4
        self.place = jnp.stack([self.core, self.index, self.chip]).astype(jnp.int32)

    def swap(self, value, bits):
        return lax.ppermute(value, "dp", [(i, i ^ bits) for i in range(self.devices)])

    def split_swap(self, value, even_bits, odd_bits):
        return lax.ppermute(
            value, "dp", [(i, i ^ (odd_bits if i % 2 else even_bits)) for i in range(self.devices)]
        )

    def row_swap(self, value, bits):
        return lax.ppermute(value, "blk", [(i, i ^ bits) for i in range(self.blocks)])

    def row_shift(self, value, distance):
        pairs = [(i, i + distance) for i in range(self.blocks) if 0 <= i + distance < self.blocks]
        return lax.ppermute(value, "blk", pairs)

    def sides(self, value):
        return self.swap(value, 2), self.swap(value, 4)

    def across(self, side, other):
        return self.split_swap(jnp.where(self.core == 0, other, side), 2, 4)

    def total(self, value, order):
        part = value.shape[1] // 2
        value = value.astype(bf16)
        cut = lambda core: lax.dynamic_slice_in_dim(value, core * part, part, 1)
        sent = self.swap(cut(1 - self.core), 1)
        kept = cut(self.core)
        yield
        sent = order(sent)
        value = (kept.astype(f32) + sent.astype(f32)).astype(bf16)
        cuts = cut_rows(self.place, value, self.chips)
        order.mark(cuts[0])
        sent = [self.swap(cuts[r], 2 * r) for r in range(1, self.chips)]
        yield
        sent = order(*sent)
        value = order.mark(sum([cuts[0].astype(f32)] + [part.astype(f32) for part in sent]).astype(bf16))
        bits = 1
        while bits < self.blocks:
            sent = self.row_swap(value, bits)
            yield
            sent = order(sent)
            value = order.mark((value.astype(f32) + sent.astype(f32)).astype(bf16))
            bits *= 2
        sent = [self.swap(value, 2 * r) for r in range(1, self.chips)]
        yield
        sent = order(*sent)
        value = order.mark(join_rows(self.place, [value, *sent]))
        sent = self.swap(value, 1)
        yield
        sent = order(sent)
        pair = lambda first, second: jnp.concatenate([first, second], axis=1)
        yield jnp.where(self.core == 0, pair(value, sent), pair(sent, value)).astype(f32)

    def small_total(self, value, order):
        for swap, count in ((self.swap, self.devices), (self.row_swap, self.blocks)):
            bits = 1
            while bits < count:
                sent = swap(value, bits)
                yield
                sent = order(sent)
                value = order.mark(value + sent)
                bits *= 2
        yield value


def shards(
    block_input,
    out_cotangent,
    row_lengths,
    rope_positions,
    gain_attention,
    gain_feedforward,
    base_attention,
    base_output,
    base_feedforward,
    base_down,
    rank_in_attention,
    rank_out_attention,
    magnitude_attention,
    rank_in_output,
    rank_out_output,
    magnitude_output,
    rank_in_feedforward,
    rank_out_feedforward,
    magnitude_feedforward,
    rank_in_down,
    rank_out_down,
    magnitude_down,
    *,
    devices,
    blocks,
):
    links = Links(devices, blocks)
    order = Order()
    mark = order.mark
    index, core, chip, chips = links.index, links.core, links.chip, links.chips
    place = links.place
    partner = lambda value: links.swap(value, 1)
    rows_in = block_input[0]
    tokens = rows_in.shape[0]
    length = row_lengths[0]
    token_pos = links.block * tokens + jnp.arange(tokens, dtype=jnp.int32)
    fast = links.square and base_attention.shape[2] * devices == KVW and blocks == 4
    heads = jnp.arange(KV_HEADS, dtype=jnp.int32)
    heads = chip ^ heads if fast else heads
    scalars = jnp.stack([links.block.astype(jnp.int32), length])

    def columns_of(value, width):
        return lax.dynamic_slice_in_dim(value, index * width, width, value.ndim - 1)

    attn_cols, out_cols = base_attention.shape[2], base_output.shape[2]
    feed_cols, down_cols = base_feedforward.shape[2], base_down.shape[1]
    chip_cols = 2 * feed_cols
    attn_rank = columns_of(rank_out_attention, attn_cols)
    attn_mag = columns_of(magnitude_attention, attn_cols)
    attn_base = base_attention.transpose(0, 2, 1)
    attn_in_t = rank_in_attention.transpose(0, 2, 1)
    out_in_t = rank_in_output.T
    feed_in_t = rank_in_feedforward.transpose(0, 2, 1)
    down_in_t = rank_in_down.T

    def fold_out():
        return fold(
            order(base_output).transpose(0, 2, 1),
            out_in_t[None],
            columns_of(rank_out_output, out_cols),
            columns_of(magnitude_output, out_cols),
            0,
            False,
            "fold_o",
        )

    def fold_feed():
        return fold(
            order(base_feedforward).transpose(0, 2, 1),
            feed_in_t,
            columns_of(rank_out_feedforward, feed_cols),
            columns_of(magnitude_feedforward, feed_cols),
            0,
            True,
            "fold_feed",
        )

    def folded_down():
        return fold_down(
            order(base_down),
            down_in_t,
            columns_of(rank_out_down, down_cols),
            columns_of(magnitude_down, down_cols),
            chips,
        )

    def norm_in():
        values = order(rows_in).astype(f32)
        return (values * rms_inverse(values) * gain_attention).astype(bf16)

    frequency = rope_base ** (-(jnp.arange(HEAD // 2, dtype=f32) * 2.0) / HEAD)
    angles = rope_positions[0].astype(f32)[:, None] * frequency[None, :]
    cos_half, sin_half = jnp.cos(angles), jnp.sin(angles)
    cosine = jnp.concatenate([cos_half, cos_half], axis=-1)
    sine = jnp.concatenate([-sin_half, sin_half], axis=-1)
    tables = (cosine, sine)

    wheres = [jnp.stack([core, chip ^ r, chip, chip ^ 1, chip ^ 2]).astype(jnp.int32) for r in range(KV_HEADS)]

    settle = order.pin

    def project(where, first, second, roped, name, before=()):
        first, second = order(first, second)
        weights, out, token = head_step(where, first, second, normed, tables, roped, before, name)
        mark(token)
        return weights, out

    def send_kv(kv_blocks):
        kv_blocks.append(links.row_shift(kv_blocks[-1], 1))

    kv_fold = mark(
        fold(attn_base, attn_in_t, attn_rank[GROUP:], attn_mag[GROUP:], 1, True, "fold_kv", first=GROUP)
    )
    down_cut = lambda r: lax.dynamic_index_in_dim(down_fold, chip ^ r, 0, keepdims=False)
    spread = lambda value: lax.all_gather(value, "dp", axis=0)
    grad_out = jnp.where((token_pos < length)[:, None], out_cotangent[0], jnp.zeros((), bf16))
    grad_own = grad_out[None]
    chip_in_t = lax.dynamic_slice_in_dim(down_in_t, chip * chip_cols, chip_cols, 1)
    halves_in_t = jnp.stack(
        [lax.dynamic_slice_in_dim(chip_in_t, at * feed_cols, feed_cols, 1) for at in (core, 1 - core)]
    )
    feed_mag = lax.dynamic_slice_in_dim(magnitude_feedforward, chip * chip_cols, chip_cols, 1)
    if fast:
        kv_side, kv_other = links.sides(kv_fold)
        kv_partner = partner(kv_fold)
        q_fold = mark(fold(order(attn_base), attn_in_t, attn_rank[:GROUP], attn_mag[:GROUP], 0, False, "fold_q"))
        q_weights = spread(q_fold)
        kv_side, kv_other, kv_partner = settle(kv_side, kv_other, kv_partner)
        kv_across = links.across(kv_side, kv_other)
        kv_side_p, kv_other_p = partner(kv_side), partner(kv_other)
        o_fold = mark(fold_out())
        o_weights = spread(after(o_fold, q_fold))
        normed = mark(norm_in())
        kv_made = [
            project(wheres[0], kv_fold, kv_partner, 1, "head_kv"),
            project(wheres[1], kv_side, kv_side_p, 1, "head_kv"),
            project(wheres[2], kv_other, kv_other_p, 1, "head_kv"),
        ]
        kv_across = settle(kv_across)
        kv_across_p = partner(kv_across)
        kv_made.append(project(wheres[3], kv_across, kv_across_p, 1, "head_kv", [out for _, out in kv_made]))
        kv_own = kv_made[-1][1]
        kv_blocks = [kv_own]
        send_kv(kv_blocks)
        grad_own, halves_in_t, feed_mag = settle(grad_own, halves_in_t, feed_mag)
        feed_own = mark(fold_feed())
        kv_blocks[1] = settle(kv_blocks[1])
        send_kv(kv_blocks)
        down_fold, down_proj = folded_down()
        mark(down_proj)
        down_0, down_c1, down_c2, down_c3 = settle(*[down_cut(r) for r in range(4)])
        grad_all = spread(order(grad_out))
        kv_blocks[2] = settle(kv_blocks[2])
        send_kv(kv_blocks)
        queries = mark(query_project(order(normed), tables, q_weights))
        kv_blocks[3] = settle(kv_blocks[3])
        down_1, down_2, down_3 = links.swap(down_c1, 2), links.swap(down_c2, 4), links.swap(down_c3, 6)
        mixed, lse = attend(scalars, order(queries), kv_blocks)
        mark(lse)
        down_1, down_2, down_3 = settle(down_1, down_2, down_3)
        down_pieces = [down_0, None, down_1, None, down_2, None, down_3, None]
        for at in range(0, 8, 2):
            down_pieces[at + 1] = partner(order(down_pieces[at]))
        feed_partner = partner(order(feed_own))

        def feed_late():
            down_pieces[1::2] = settle(*down_pieces[1::2])
    else:
        q_fold = fold(attn_base, attn_in_t, attn_rank[:GROUP], attn_mag[:GROUP], 0, False, "fold_q")
        q_weights, o_weights, normed = spread(q_fold), spread(fold_out()), norm_in()
        down_fold, down_proj = folded_down()
        feed_own = fold_feed()
        feed_partner = partner(feed_own)
        whole = lax.all_gather(kv_fold, "dp", axis=1, tiled=True).reshape(2, KV_HEADS, 2, HEAD // 2, WIDE)
        kv_made = []
        for j in range(KV_HEADS):
            before = [out for _, out in kv_made] if j == KV_HEADS - 1 else ()
            where = jnp.array([0, j, 0, 1, 2], jnp.int32)
            kv_made.append(project(where, whole[:, j, 0], whole[:, j, 1], 1, "head_kv", before))
        kv_own = kv_made[-1][1]
        kv_blocks = [kv_own]
        for _ in range(1, blocks):
            send_kv(kv_blocks)
        queries = query_project(normed, tables, q_weights)
        grad_all = spread(grad_out)
        mixed, lse = attend(scalars, queries, kv_blocks)
        down_pieces = []
        for r in range(chips):
            piece = links.swap(down_cut(r), 2 * r) if r else down_cut(r)
            down_pieces += [piece, partner(piece)]
    residual, normed_feed = output_project(order(mixed), o_weights, rows_in, gain_feedforward)
    mark(normed_feed)

    forward = lambda normed_group: settle(*feed_forward(order(normed_group), feed_own, feed_partner, tokens))
    aux = []

    def backward(members, kept):
        grads = grad_own if members == (None,) else grad_all
        made = feed_back(place, grads, members, *order(*kept), feed_own, feed_partner, down_pieces, tokens)
        mark(made[0])
        count = len(members)
        return made[:count], made[count : 2 * count], made[2 * count :]

    def adapters(members, normed_group, made):
        ext, hidden, grad_gate, grad_up, down_ext, mag_sum, down_mag, down_aux = made[2]
        parts = feed_adapter(
            place, order(normed_group), grad_own if members == (None,) else grad_all, members, hidden, grad_gate, grad_up, ext, down_ext,
            feed_in_t.reshape(2 * RANK, D), halves_in_t,
        )
        mark(parts[0])
        aux.append(down_aux)
        return tuple(parts) + (mag_sum, down_mag)

    if fast:
        side, other = links.sides(normed_feed)
        kept = forward(normed_feed)
        feed_late()
        own_made = backward((None,), kept)
        side, other = settle(side, other)
        crossed = links.across(side, other)
        near = settle(jnp.concatenate([side, other]))
        near_kept = forward(near)
        own_sums = adapters((None,), normed_feed, own_made)
        crossed = settle(crossed)
        far_kept = forward(crossed)
        far_made = backward((3,), far_kept)
        from_far = links.split_swap(far_made[0][0], 2, 4)
        near_made = backward((1, 2), near_kept)
        early_first = links.split_swap(near_made[0][0], 2, 4)
        from_far = settle(from_far)
        late_share = settle((near_made[0][1].astype(f32) + from_far.astype(f32)).astype(bf16))
        early_second = links.split_swap(late_share, 4, 2)
        down_mag_steps = links.small_total(own_made[2][6][:1] + near_made[2][6][:1] + far_made[2][6][:1], order)
        next(down_mag_steps)
        near_sums = adapters((1, 2), near, near_made)
        next(down_mag_steps)
        far_sums = adapters((3,), crossed, far_made)
        next(down_mag_steps)
        early_first = settle(early_first)
        all_sums = [own_sums, near_sums, far_sums]
        reduced = (own_made[0][0], early_first, early_second)
        shares_out = [own_made[1][0], *near_made[1], far_made[1][0]]
    else:
        all_sums, shares_grad, shares_out = [], [], []
        for r in range(chips):
            normed_group = links.swap(normed_feed, 2 * r) if r else normed_feed
            made = backward((r,), forward(normed_group))
            all_sums.append(adapters((r,), normed_group, made))
            shares_grad.append(made[0][0])
            shares_out.append(made[1][0])
        rest = sum(links.swap(shares_grad[r], 2 * r).astype(f32) for r in range(1, chips)).astype(bf16)
        reduced = (shares_grad[0], rest, jnp.zeros(rest.shape, bf16))
        down_mag_steps = links.small_total(sum(part[5][:1] for part in all_sums), order)
        next(down_mag_steps)
    feed_in, feed_products, down_in, down_products, feed_mag_raw, _ = (sum(parts) for parts in zip(*all_sums))

    finished = []
    for half, (weights, at) in enumerate(((feed_own, core), (feed_partner, 1 - core))):
        finished.append(
            finish_columns(
                weights,
                order(feed_products[half]),
                feed_mag_raw[half::2],
                lax.dynamic_slice_in_dim(feed_mag, at * feed_cols, feed_cols, 1),
            )
        )
        mark(finished[-1][0])
        next(down_mag_steps)
    reduced = settle(*reduced)
    grad_residual, grad_ordered, out_mag_raw, out_ext, grad_mixed, delta = residual_back(
        reduced, residual, gain_feedforward, grad_out, rows_in, mixed, o_weights
    )
    mark(delta)

    def pack_early(down_mag_total):
        grad_mag, grad_out_part, grad_in_part = zip(*finished)
        columns = [
            jnp.concatenate([part.astype(bf16) for part in parts])
            for parts in zip(grad_out_part, down_in, grad_mag)
        ]
        columns = jnp.where(core == 0, jnp.concatenate(columns, axis=1), jnp.concatenate(columns[::-1], axis=1))
        full = lax.dynamic_update_slice(jnp.zeros((64, 3 * D), bf16), columns, (0, chip * chip_cols))
        down_aux = aux[0]
        down_inverse = (down_aux[RANK].astype(f32) + down_aux[RANK + 1].astype(f32))[None]
        down_grad_mag = down_mag_total / magnitude_down[None]
        down_out = factor * down_products * (magnitude_down[None] * down_inverse)
        own_turn = columns_of(-down_grad_mag * down_inverse, down_cols) * (factor / blocks)
        down_out = lax.dynamic_update_slice(
            down_out, columns_of(down_out, down_cols) + down_proj * own_turn, (0, index * down_cols)
        )
        own_wide = (columns_of(rank_out_down.astype(f32), down_cols) * own_turn).astype(bf16)
        down_norm_in = lax.dot_general(
            own_wide, down_fold[:, :chip_cols], (((1,), (2,)), ((), ())), preferred_element_type=f32
        ).reshape(RANK, FF)
        down_full = (full[2 * RANK : 3 * RANK, :FF].astype(f32) + down_norm_in).astype(bf16)
        full = lax.dynamic_update_slice(full, down_full, (2 * RANK, 0))
        top = jnp.concatenate([(feed_in + sum(grad_in_part)).astype(bf16), down_out.astype(bf16)])
        return down_grad_mag, jnp.concatenate(
            [jnp.pad(top, ((0, 16), (0, 0)))] + [full[:, i * D : (i + 1) * D] for i in range(3)]
        )

    grad_queries, grad_kvs = None, []

    def keys_back(distance):
        grad_queries_next, grad_kv = attend_back(
            scalars, order(queries), grad_mixed, lse, delta, kv_blocks[distance], grad_queries, distance
        )
        mark(grad_kv)
        return grad_queries_next, grad_kv

    def pass_down(passed, grad_kv):
        passed = order(passed)
        passed = settle((passed.astype(f32) + grad_kv.astype(f32)).astype(bf16))
        return links.row_shift(passed, -1)

    grad_queries, grad_kv = keys_back(blocks - 1)
    passed = links.row_shift(grad_kv, -1)
    held = None
    for distance in reversed(range(1, blocks - 1)):
        grad_queries, grad_kv = keys_back(distance)
        if held is not None:
            passed = pass_down(passed, held)
        held = grad_kv
    grad_queries, grad_kv = keys_back(0)
    for down_mag_total in down_mag_steps:
        pass
    if fast:
        out_far = links.split_swap(order(shares_out[3]), 2, 4)
        out_first = links.split_swap(order(shares_out[1]), 2, 4)
    out_grad_mag, out_out, out_in = output_adapter(
        order(grad_ordered), out_mag_raw, magnitude_output, o_weights, mixed, out_ext, out_in_t
    )
    mark(out_in)
    passed = pass_down(passed, held)
    q_acc, q_in, q_out, q_grad_mag = query_back(
        order(grad_queries), queries, q_weights, cosine, sine, normed, attn_in_t[0], magnitude_attention[:GROUP]
    )
    mark(q_in)
    if fast:
        out_far, out_first = settle(out_far, out_first)
        out_late = settle((shares_out[2].astype(f32) + out_far.astype(f32)).astype(bf16))
        out_second = links.split_swap(out_late, 4, 2)
        out_parts = [shares_out[0], out_first, out_second]
    else:
        out_parts = [shares_out[0]] + [links.swap(shares_out[r], 2 * r) for r in range(1, chips)]
    down_grad_mag, early = pack_early(down_mag_total)
    early_steps = links.total(settle(early), order)
    next(early_steps)
    out_parts = settle(*out_parts)
    next(early_steps)
    next(early_steps)
    input_grad, kv_in, kv_out, kv_grad_mag = key_back(
        heads, order(passed), grad_kv, kv_own, [weights for weights, _ in kv_made], cosine, sine, normed, rows_in,
        gain_attention, grad_residual, q_acc, attn_in_t[1:].reshape(2 * RANK, D), magnitude_attention[GROUP:],
    )
    mark(kv_in)
    rows = lambda *parts: jnp.concatenate([part.astype(bf16) for part in parts])
    late = jnp.concatenate(
        [
            rows(q_in, kv_in, q_out),
            rows(out_in, out_out, out_grad_mag, jnp.zeros((31, D), bf16)),
            rows(
                kv_out[:, :KVW],
                kv_out[:, KVW:],
                q_grad_mag.reshape(-1, KVW),
                kv_grad_mag.reshape(-1, KVW),
                jnp.zeros((26, KVW), bf16),
            ),
        ],
        axis=1,
    )
    late_steps = links.total(settle(late), order)
    late = early = None
    while late is None:
        late = next(late_steps)
        if early is None:
            early = next(early_steps)
    while early is None:
        early = next(early_steps)

    block_out = (residual + sum(part.astype(f32) for part in out_parts)).astype(bf16)[None]
    feed_full = jnp.concatenate([early[64 * (1 + i) : 64 * (2 + i)] for i in range(3)], axis=1)[:, :FF]
    late_in, late_out = late[: 3 * RANK, :D], late[3 * RANK :, :D]
    mid, side = late[:, D : 2 * D], late[:, 2 * D :]
    return (
        block_out,
        input_grad[None],
        late_in.reshape(3, RANK, D).transpose(0, 2, 1),
        jnp.concatenate(
            [
                late_out.reshape(RANK, GROUP, KVW).transpose(1, 0, 2),
                jnp.stack([side[:RANK], side[RANK : 2 * RANK]]),
            ]
        ),
        side[2 * RANK : 2 * RANK + 6],
        mid[:RANK].T,
        mid[RANK : 2 * RANK].reshape(RANK, GROUP, KVW).transpose(1, 0, 2),
        mid[2 * RANK].reshape(GROUP, KVW),
        early[: 2 * RANK].reshape(2, RANK, D).transpose(0, 2, 1),
        feed_full[: 2 * RANK].reshape(2, RANK, FF),
        feed_full[3 * RANK : 3 * RANK + 2],
        feed_full[2 * RANK : 3 * RANK].T,
        early[2 * RANK : 3 * RANK],
        down_grad_mag[0],
    )


def solution(mesh):
    split_tokens = P("dp", "blk", None)
    placed = (
        split_tokens,
        split_tokens,
        P("dp"),
        P("dp", "blk"),
        P(),
        P(),
        P(None, None, "dp"),
        P(None, None, "dp"),
        P(None, None, "dp"),
        P(None, "dp"),
    ) + (P(),) * 12
    return jax.shard_map(
        functools.partial(shards, devices=mesh.shape["dp"], blocks=mesh.shape["blk"]),
        mesh=mesh,
        in_specs=placed,
        out_specs=(split_tokens, split_tokens) + (P(),) * 12,
        check_vma=False,
    )
```

time: 977 us -> 564 us (0.58)
  waiting for transfers between devices: 373 us -> 82.2 us
  matrix products: 180 us -> 0.85 us
  Pallas kernels: 97.4 us -> 189 us
  local copies, waits for them, and re-layouts: 162 us -> 120 us
  starting transfers between devices: 61.5 us -> 101 us
  blocking collectives: 22.6 us -> 0 us
    psum x2 -> x0, waiting for transfers between devices: 258 us -> none  [shards(): lax.psum((jnp.stack(attn_ins), jnp.concatenate(attn_outs), jnp.concatenat...]
    dot_general x49 -> x1, matrix products: 180 us -> 0.85 us  [pack_early(): lax.dot_general(own_wide, down_fold[:, :chip_cols], (((1,), (2,)), ((), (...]
    pallas_call x12 -> x35, Pallas kernels: 97.4 us -> 189 us  [the longest x3 53.1 us: feed_back(): kernel_call(functools.partial(feed_back_kernel, block=block, devices=devi...]
    dynamic_update_slice x34 -> x1, local copies, waits for them, and re-layouts: 41.2 us -> 3.27 us  [pack_early(): lax.dynamic_update_slice(jnp.zeros((64, 3 * D), bf16), columns, (0, chip...]
    unnamed x383 -> x402, local copies, waits for them, and re-layouts: 54.1 us -> 87.2 us
    slice x27 -> x17, local copies, waits for them, and re-layouts: 31.8 us -> 8.51 us  [the longest x2 2.62 us: shards(): feed_mag_raw[half::2]]
    all_gather x2 -> x0, blocking collectives: 22.6 us -> none  [the longest x1 12.4 us: shards(): down_norm = lax.all_gather(d_norm.reshape(-1), 'dp', axis=0, tiled=True)]
    ppermute x6 -> x12, starting transfers between devices: 14.8 us -> 36.8 us  [the longest x6 20.4 us: row_swap(): lax.ppermute(value, 'blk', [(i, i ^ bits) for i in range(self.blocks)])]
  transfers between devices with their start and end apart: 50 -> 58, of which waited for: 18 -> 20; matrix products, arithmetic and copies ran while one was open for 29% -> 12% of each run, Pallas kernels for 8% -> 28%
where the time goes in v2:
time: 564 us; the launch traced here: 555 us
  Pallas kernels  189 us (34%)
  local copies, waits for them, and re-layouts  120 us (21%)
  starting transfers between devices  101 us (18%)
  waiting for transfers between devices  82.2 us (15%)
  other arithmetic  45.3 us (8%)
  between operations  16.9 us (3%)
    unnamed x402, local copies, waits for them, and re-layouts  87.2 us
    ppermute x35, starting transfers between devices, swap(): lax.ppermute(value, 'dp', [(i, i ^ bits) for i in range(self.devices)])  55.3 us
    pallas_call x3, Pallas kernels, feed_back(): kernel_call(functools.partial(feed_back_kernel, block=block, devices=devi...  53.1 us
    ppermute x35, waiting for transfers between devices, swap(): lax.ppermute(value, 'dp', [(i, i ^ bits) for i in range(self.devices)])  47.5 us
    pallas_call x3, Pallas kernels, feed_forward(): kernel_call(functools.partial(feed_forward_kernel, block=block), out_shap...  25.5 us
    ppermute x8, waiting for transfers between devices, split_swap(): lax.ppermute(value, 'dp', [(i, i ^ (odd_bits if i % 2 else even_bits)) fo...  25.1 us
    pallas_call x4, Pallas kernels, fold(): kernel_call(functools.partial(fold_kernel, first_slot=rank_first, moving=...  23.4 us
    ppermute x6, starting transfers between devices, row_swap(): lax.ppermute(value, 'blk', [(i, i ^ bits) for i in range(self.blocks)])  20.4 us
  transfers between devices with their start and end apart: 58, of which 20 were waited for; matrix products, arithmetic and copies ran while one was open for 12% of the time, Pallas kernels for 28%

profile of v2, /device:TPU:1, one launch (start us, length us, event | category | flops | bytes accessed | tf_op | source)
XLA Modules:
  0.0 555.4 jit_solution(16564804011067169430)
XLA Ops:
  13.9 4.5 fold_q.1
  24.7 9.7 %collective-permute-done.first_ref = bf16[2,64,2176]{2,1,0:T(8,128)(2,1)} collective-permute-done((bf16[2,64,2176]{2,1,0:T(8,128)(2,1)S(1)}, bf16[2,64,2176]{2,1,0:T(8,128)(2,1)}, u32[]{:S(2)}, u32[]{:S(2)}) %collective-permute-start) | collective-permute-done | bytes 557088 | tf_op jit(solution)/shard_map/ppermute | solution.py:964
  36.9 4.5 fold_o.1
  55.9 15.0 %collective-permute-done.3.first_ref = bf16[2,64,2176]{2,1,0:T(8,128)(2,1)S(1)} collective-permute-done((bf16[2,64,2176]{2,1,0:T(8,128)(2,1)S(1)}, bf16[2,64,2176]{2,1,0:T(8,128)(2,1)S(1)}, u32[]{:S(2)}, u32[]{:S(2)}) %collective-permute-start.3) | collective-permute-done | bytes 557088 | tf_op jit(solution)/shard_map/ppermute | solution.py:967
  70.9 4.6 collective-permute-start.4
  87.3 3.1 collective-permute-start.7
  95.3 12.5 %fold_feed.1.own_ref.weight_ref = bf16[2,704,2176]{2,1,0:T(8,128)(2,1)} custom-call(bf16[2,704,2048]{2,1,0:T(8,128)(2,1)S(1)} %bitcast.122, bf16[2,16,2048]{2,1,0:T(8,128)(2,1)S(1)} %bitcast.123, bf16[2,16,704]{2,1,0:T(8,128)(2,1)S(1)} %copy-done.113, f32[2,1,704]{2,1,0:T(1,128)S(1)} %broadcast_in_dim.73.mag_ref), custom_call_target="tpu_custom_call" | custom-call | tf_op jit(solution)/shard_map/fold_feed/pallas_call | solution.py:117
  117.3 4.1 collective-permute-start.8
  121.4 3.4 collective-permute-start.11
  126.0 5.5 collective-permute-done.8.refs_2_.kv_ref
  131.5 5.2 collective-permute-start.9
  137.4 3.6 copy-done.5
  140.9 5.1 query_project.1.query_ref
  146.1 5.2 attend.1
  152.2 3.4 collective-permute-done.10.refs_2_
  157.7 17.8 %collective-permute-done.12.refs_6_ = bf16[1440,256]{1,0:T(8,128)(2,1)} collective-permute-done((bf16[1440,256]{1,0:T(8,128)(2,1)}, bf16[1440,256]{1,0:T(8,128)(2,1)}, u32[]{:S(2)}, u32[]{:S(2)}) %collective-permute-start.12) | collective-permute-done | bytes 737312 | tf_op jit(solution)/shard_map/ppermute | solution.py:964
  176.3 4.2 copy-done.4
  182.6 4.9 output_project.1
  190.2 7.1 %feed_forward.3 = (f32[2,256,704]{2,1,0:T(8,128)S(1)}, f32[2,256,704]{2,1,0:T(8,128)S(1)}) custom-call(bf16[256,2048]{1,0:T(8,128)(2,1)S(1)} %get-tuple-element.301.normed_ref, bf16[2,704,2176]{2,1,0:T(8,128)(2,1)} %fold_feed.1.own_ref.weight_ref, bf16[2,704,2176]{2,1,0:T(8,128)(2,1)} %collective-permute-done.13.partner_ref.weight_ref), custom_call_target="tpu_custom_call" | custom-call | tf_op jit(solution)/shard_map/feed_forward/pallas_call | solution.py:478
  198.6 15.0 %feed_back.3 = (bf16[256,2048]{1,0:T(8,128)(2,1)S(1)}, bf16[256,2048]{1,0:T(8,128)(2,1)S(1)}, bf16[256,128]{1,0:T(8,128)(2,1)S(1)}, bf16[2,256,704]{2,1,0:T(8,12...) custom-call(s32[3]{0:T(128)S(1)} %pad_add_fusion.1.place_ref, ...), custom_call_target="tpu_custom_call" | custom-call | tf_op jit(solution)/shard_map/feed_back/pallas_call | solution.py:568
  221.3 5.2 collective-permute-done.18
  235.0 10.1 %feed_forward.4 = (f32[2,512,704]{2,1,0:T(8,128)S(1)}, f32[2,512,704]{2,1,0:T(8,128)S(1)}) custom-call(bf16[512,2048]{1,0:T(8,128)(2,1)S(1)} %pad_maximum_fusion.normed_ref, bf16[2,704,2176]{2,1,0:T(8,128)(2,1)} %fold_feed.1.own_ref.weight_ref, bf16[2,704,2176]{2,1,0:T(8,128)(2,1)} %collective-permute-done.13.partner_ref.weight_ref), custom_call_target="tpu_custom_call" | custom-call | tf_op jit(solution)/shard_map/feed_forward/pallas_call | solution.py:478
  252.2 8.2 %feed_forward.5 = (f32[2,256,704]{2,1,0:T(8,128)S(1)}, f32[2,256,704]{2,1,0:T(8,128)S(1)}) custom-call(bf16[256,2048]{1,0:T(8,128)(2,1)} %collective-permute-done.20.normed_ref, bf16[2,704,2176]{2,1,0:T(8,128)(2,1)} %fold_feed.1.own_ref.weight_ref, bf16[2,704,2176]{2,1,0:T(8,128)(2,1)} %collective-permute-done.13.partner_ref.weight_ref), custom_call_target="tpu_custom_call" | custom-call | tf_op jit(solution)/shard_map/feed_forward/pallas_call | solution.py:478
  269.6 13.1 %feed_back.4 = (bf16[256,2048]{1,0:T(8,128)(2,1)}, bf16[256,2048]{1,0:T(8,128)(2,1)S(1)}, bf16[256,128]{1,0:T(8,128)(2,1)S(1)}, bf16[2,256,704]{2,1,0:T(8,128)(2...) custom-call(s32[3]{0:T(128)S(1)} %copy-done.142, ...), custom_call_target="tpu_custom_call" | custom-call | tf_op jit(solution)/shard_map/feed_back/pallas_call | solution.py:568
  289.6 25.1 %feed_back.5 = (bf16[256,2048]{1,0:T(8,128)(2,1)S(1)}, bf16[256,2048]{1,0:T(8,128)(2,1)S(1)}, bf16[256,2048]{1,0:T(8,128)(2,1)S(1)}, bf16[256,2048]{1,0:T(8,128)...) custom-call(s32[3]{0:T(128)S(1)} %copy-done.142, ...), custom_call_target="tpu_custom_call" | custom-call | tf_op jit(solution)/shard_map/feed_back/pallas_call | solution.py:568
  327.3 3.1 collective-permute-start.21
  333.4 3.4 copy-done.2
  341.1 3.2 feed_adapter.4
  346.0 3.5 feed_adapter.5
  350.9 3.7 feed_finish.2
  356.0 3.8 feed_finish.3
  360.2 6.7 %residual_back.1 = (f32[256,2048]{1,0:T(8,128)S(1)}, bf16[256,2048]{1,0:T(8,128)(2,1)S(1)}, f32[1,2048]{1,0:T(1,128)S(1)}, bf16[256,128]{1,0:T(8,128)(2,1)S(1)},...) custom-call(bf16[256,2048]{1,0:T(8,128)(2,1)S(1)} %copy-done.89, ...), custom_call_target="tpu_custom_call" | custom-call | tf_op jit(solution)/shard_map/residual_back/pallas_call | solution.py:753
  368.9 4.1 attend_back_3.1
  377.3 3.3 dynamic_update_slice.10
  387.0 3.1 attend_back_2.1
  394.9 5.1 attend_back_0.1
  404.0 4.7 output_adapter.1
  411.0 7.3 %query_back.1 = (f32[256,2176]{1,0:T(8,128)S(1)}, f32[16,2048]{1,0:T(8,128)S(1)}, f32[16,2048]{1,0:T(8,128)S(1)}, f32[1,2048]{1,0:T(1,128)S(1)}) custom-call(f32[256,2048]{1,0:T(8,128)S(1)} %copy-done.9, bf16[256,2048]{1,0:T(8,128)(2,1)S(1)} %query_project.1.query_ref, f32[256,128]{1,0:T(8,128)S(1)} %get-tuple-element.484.cos_ref, ...), custom_call_target="tpu_custom_call" | custom-call | tf_op jit(solution)/shard_map/query_back/pallas_call | solution.py:812
  418.3 7.2 %collective-permute-done.31 = bf16[256,2048]{1,0:T(8,128)(2,1)} collective-permute-done((bf16[256,2048]{1,0:T(8,128)(2,1)S(1)}, bf16[256,2048]{1,0:T(8,128)(2,1)}, u32[]{:S(2)}, u32[]{:S(2)}) %collective-permute-start.31) | collective-permute-done | bytes 1048608 | tf_op jit(solution)/shard_map/ppermute | solution.py:967
  430.7 8.5 %collective-permute-start.35 = (bf16[256,1024]{1,0:T(8,128)(2,1)}, bf16[256,1024]{1,0:T(8,128)(2,1)}, u32[]{:S(2)}, u32[]{:S(2)}) collective-permute-start(bf16[256,1024]{1,0:T(8,128)(2,1)} %constant_dynamic-slice_fusion.1), channel_id=1, source_target_pairs={{0,4},{4,0},{8,12},{12,8},{16,20},{20,16},{24,28},{28,24},{1,5},{5... | collective-permute-start | bytes 1572872 | tf_op jit(solution)/shard_map/ppermute | solution.py:964
  440.7 2.9 collective-permute-done.33
  457.9 6.8 %collective-permute-start.40 = (bf16[64,1024]{1,0:T(8,128)(2,1)S(1)}, bf16[64,1024]{1,0:T(8,128)(2,1)}, u32[]{:S(2)}, u32[]{:S(2)}) collective-permute-start(bf16[64,1024]{1,0:T(8,128)(2,1)S(1)} %add_convert_fusion.10), channel_id=1, source_target_pairs={{0,1},{1,0},{2,3},{3,2},{4,5},{5,4},{6,7},{7,6},{8,9},{9,8},{10,11... | collective-permute-start | bytes 393224 | tf_op jit(solution)/shard_map/ppermute | solution.py:972
  474.1 5.4 key_back.1
  482.3 9.6 %collective-permute-start.39 = (bf16[64,2304]{1,0:T(8,128)(2,1)}, bf16[64,2304]{1,0:T(8,128)(2,1)}, u32[]{:S(2)}, u32[]{:S(2)}) collective-permute-start(bf16[64,2304]{1,0:T(8,128)(2,1)} %constant_dynamic-slice_fusion), channel_id=1, source_target_pairs={{0,4},{4,0},{8,12},{12,8},{16,20},{20,16},{24,28},{28,24},{1,5},{5... | collective-permute-start | bytes 884744 | tf_op jit(solution)/shard_map/ppermute | solution.py:964
  492.8 8.9 %collective-permute-start.44 = (bf16[64,1024]{1,0:T(8,128)(2,1)S(1)}, bf16[64,1024]{1,0:T(8,128)(2,1)S(1)}, u32[]{:S(2)}, u32[]{:S(2)}) collective-permute-start(bf16[64,1024]{1,0:T(8,128)(2,1)S(1)} %add_convert_fusion.9), channel_id=1, source_target_pairs={{0,2},{1,3},{2,0},{3,1},{4,6},{5,7},{6,4},{7,5},{8,10},{9,11},{10,... | collective-permute-start | bytes 393224 | tf_op jit(solution)/shard_map/ppermute | solution.py:972
  518.8 3.8 collective-permute-done.49
  530.6 5.0 collective-permute-start.53
  535.6 3.1 fusion.8
  (632 shorter events, 222.4 us)
Async XLA Ops:
  7.2 130.2 %all-gather.7.cloned.1.call-start = ((), (), s32[]{:S(2)}) async-start(), calls=%async_computation | async-start | bytes 10027008 | tf_op jit(solution)/shard_map/all_gather | solution.py:1143
  18.5 157.8 %all-gather.9.cloned.1.call-start = ((), (), s32[]{:S(2)}) async-start(), calls=%async_computation.1 | async-start | bytes 10027008 | tf_op jit(solution)/shard_map/all_gather | solution.py:1143
  18.5 15.9 %collective-permute-start = (bf16[2,64,2176]{2,1,0:T(8,128)(2,1)S(1)}, bf16[2,64,2176]{2,1,0:T(8,128)(2,1)}, u32[]{:S(2)}, u32[]{:S(2)}) collective-permute-start(bf16[2,64,2176]{2,1,0:T(8,128)(2,1)S(1)} %fold_kv.1.first_ref), channel_id=1, source_target_pairs={{0,8},{4,12},{8,0},{12,4},{16,24},{20,28},{24,16},{28,20},{1,9},{5... | collective-permute-start | bytes 1671176 | tf_op jit(solution)/shard_map/ppermute | solution.py:964
  20.6 15.1 %collective-permute-start.1 = (bf16[2,64,2176]{2,1,0:T(8,128)(2,1)S(1)}, bf16[2,64,2176]{2,1,0:T(8,128)(2,1)S(1)}, u32[]{:S(2)}, u32[]{:S(2)}) collective-permute-start(bf16[2,64,2176]{2,1,0:T(8,128)(2,1)S(1)} %fold_kv.1.first_ref), channel_id=1, source_target_pairs={{0,16},{4,20},{8,24},{12,28},{16,0},{20,4},{24,8},{28,12},{1,17},{... | collective-permute-start | bytes 1671176 | tf_op jit(solution)/shard_map/ppermute | solution.py:964
  21.9 13.8 %collective-permute-start.2 = (bf16[2,64,2176]{2,1,0:T(8,128)(2,1)S(1)}, bf16[2,64,2176]{2,1,0:T(8,128)(2,1)S(1)}, u32[]{:S(2)}, u32[]{:S(2)}) collective-permute-start(bf16[2,64,2176]{2,1,0:T(8,128)(2,1)S(1)} %fold_kv.1.first_ref), channel_id=1, source_target_pairs={{0,4},{4,0},{8,12},{12,8},{16,20},{20,16},{24,28},{28,24},{1,5},{5... | collective-permute-start | bytes 1671176 | tf_op jit(solution)/shard_map/ppermute | solution.py:964
  41.4 221.4 %all-gather.11.cloned.1.call-start = ((), (), s32[]{:S(2)}) async-start(), calls=%async_computation.2 | async-start | bytes 9437184 | tf_op jit(solution)/shard_map/all_gather | solution.py:1143
  50.3 20.6 %collective-permute-start.3 = (bf16[2,64,2176]{2,1,0:T(8,128)(2,1)S(1)}, bf16[2,64,2176]{2,1,0:T(8,128)(2,1)S(1)}, u32[]{:S(2)}, u32[]{:S(2)}) collective-permute-start(bf16[2,64,2176]{2,1,0:T(8,128)(2,1)S(1)} %broadcast_select_fusion.2), channel_id=1, source_target_pairs={{0,8},{4,20},{8,0},{12,28},{16,24},{20,4},{24,16},{28,12},{1,9},{5... | collective-permute-start | bytes 1671176 | tf_op jit(solution)/shard_map/ppermute | solution.py:967
  53.8 24.8 %collective-permute-start.5 = (bf16[2,64,2176]{2,1,0:T(8,128)(2,1)}, bf16[2,64,2176]{2,1,0:T(8,128)(2,1)S(1)}, u32[]{:S(2)}, u32[]{:S(2)}) collective-permute-start(bf16[2,64,2176]{2,1,0:T(8,128)(2,1)} %collective-permute-done.first_ref), channel_id=1, source_target_pairs={{0,4},{4,0},{8,12},{12,8},{16,20},{20,16},{24,28},{28,24},{1,5},{5... | collective-permute-start | bytes 1671176 | tf_op jit(solution)/shard_map/ppermute | solution.py:964
  55.5 23.1 %collective-permute-start.6 = (bf16[2,64,2176]{2,1,0:T(8,128)(2,1)S(1)}, bf16[2,64,2176]{2,1,0:T(8,128)(2,1)S(1)}, u32[]{:S(2)}, u32[]{:S(2)}) collective-permute-start(bf16[2,64,2176]{2,1,0:T(8,128)(2,1)S(1)} %collective-permute-done.1.first_ref), channel_id=1, source_target_pairs={{0,4},{4,0},{8,12},{12,8},{16,20},{20,16},{24,28},{28,24},{1,5},{5... | collective-permute-start | bytes 1671176 | tf_op jit(solution)/shard_map/ppermute | solution.py:964
  70.9 13.6 %collective-permute-start.4 = (bf16[2,64,2176]{2,1,0:T(8,128)(2,1)S(1)}, bf16[2,64,2176]{2,1,0:T(8,128)(2,1)S(1)}, u32[]{:S(2)}, u32[]{:S(2)}) collective-permute-start(bf16[2,64,2176]{2,1,0:T(8,128)(2,1)S(1)} %collective-permute-done.3.first_ref), channel_id=1, source_target_pairs={{0,4},{4,0},{8,12},{12,8},{16,20},{20,16},{24,28},{28,24},{1,5},{5... | collective-permute-start | bytes 1671176 | tf_op jit(solution)/shard_map/ppermute | solution.py:964
  87.3 21.7 %collective-permute-start.7 = (bf16[256,1024]{1,0:T(8,128)(2,1)S(1)}, bf16[256,1024]{1,0:T(8,128)(2,1)S(1)}, u32[]{:S(2)}, u32[]{:S(2)}) collective-permute-start(bf16[256,1024]{1,0:T(8,128)(2,1)S(1)} %get-tuple-element.251.refs_0_.kv_ref), channel_id=1, source_target_pairs={{0,1},{1,2},{2,3},{4,5},{5,6},{6,7},{8,9},{9,10},{10,11},{12,13},{... | collective-permute-start | bytes 1572872 | tf_op jit(solution)/shard_map/ppermute | solution.py:976
  117.3 14.2 %collective-permute-start.8 = (bf16[256,1024]{1,0:T(8,128)(2,1)S(1)}, bf16[256,1024]{1,0:T(8,128)(2,1)}, u32[]{:S(2)}, u32[]{:S(2)}) collective-permute-start(bf16[256,1024]{1,0:T(8,128)(2,1)S(1)} %collective-permute-done.7.refs_1_.kv_ref), channel_id=1, source_target_pairs={{0,1},{1,2},{2,3},{4,5},{5,6},{6,7},{8,9},{9,10},{10,11},{12,13},{... | collective-permute-start | bytes 1572872 | tf_op jit(solution)/shard_map/ppermute | solution.py:976
  121.4 34.2 %collective-permute-start.10 = (bf16[1440,256]{1,0:T(8,128)(2,1)}, bf16[1440,256]{1,0:T(8,128)(2,1)}, u32[]{:S(2)}, u32[]{:S(2)}) collective-permute-start(bf16[1440,256]{1,0:T(8,128)(2,1)} %get-tuple-element.264), channel_id=1, source_target_pairs={{0,8},{4,12},{8,0},{12,4},{16,24},{20,28},{24,16},{28,20},{1,9},{5... | collective-permute-start | bytes 2211848 | tf_op jit(solution)/shard_map/ppermute | solution.py:964
  121.4 36.3 %collective-permute-start.11 = (bf16[1440,256]{1,0:T(8,128)(2,1)}, bf16[1440,256]{1,0:T(8,128)(2,1)}, u32[]{:S(2)}, u32[]{:S(2)}) collective-permute-start(bf16[1440,256]{1,0:T(8,128)(2,1)} %get-tuple-element.265), channel_id=1, source_target_pairs={{0,16},{4,20},{8,24},{12,28},{16,0},{20,4},{24,8},{28,12},{1,17},{... | collective-permute-start | bytes 2211848 | tf_op jit(solution)/shard_map/ppermute | solution.py:964
  124.8 50.7 %collective-permute-start.12 = (bf16[1440,256]{1,0:T(8,128)(2,1)}, bf16[1440,256]{1,0:T(8,128)(2,1)}, u32[]{:S(2)}, u32[]{:S(2)}) collective-permute-start(bf16[1440,256]{1,0:T(8,128)(2,1)} %get-tuple-element.266), channel_id=1, source_target_pairs={{0,24},{4,28},{8,16},{12,20},{16,8},{20,12},{24,0},{28,4},{1,25},{... | collective-permute-start | bytes 2211848 | tf_op jit(solution)/shard_map/ppermute | solution.py:964
  131.5 14.5 %collective-permute-start.9 = (bf16[256,1024]{1,0:T(8,128)(2,1)}, bf16[256,1024]{1,0:T(8,128)(2,1)}, u32[]{:S(2)}, u32[]{:S(2)}) collective-permute-start(bf16[256,1024]{1,0:T(8,128)(2,1)} %collective-permute-done.8.refs_2_.kv_ref), channel_id=1, source_target_pairs={{0,1},{1,2},{2,3},{4,5},{5,6},{6,7},{8,9},{9,10},{10,11},{12,13},{... | collective-permute-start | bytes 1572872 | tf_op jit(solution)/shard_map/ppermute | solution.py:976
  175.5 14.1 %collective-permute-start.13 = (bf16[2,704,2176]{2,1,0:T(8,128)(2,1)}, bf16[2,704,2176]{2,1,0:T(8,128)(2,1)}, u32[]{:S(2)}, u32[]{:S(2)}) collective-permute-start(bf16[2,704,2176]{2,1,0:T(8,128)(2,1)} %fold_feed.1.own_ref.weight_ref), channel_id=1, source_target_pairs={{0,4},{4,0},{8,12},{12,8},{16,20},{20,16},{24,28},{28,24},{1,5},{5... | collective-permute-start | bytes 18382856 | tf_op jit(solution)/shard_map/ppermute | solution.py:964
  176.2 13.4 %collective-permute-start.14 = (bf16[1440,256]{1,0:T(8,128)(2,1)}, bf16[1440,256]{1,0:T(8,128)(2,1)}, u32[]{:S(2)}, u32[]{:S(2)}) collective-permute-start(bf16[1440,256]{1,0:T(8,128)(2,1)} %get-tuple-element.279.refs_0_), channel_id=1, source_target_pairs={{0,4},{4,0},{8,12},{12,8},{16,20},{20,16},{24,28},{28,24},{1,5},{5... | collective-permute-start | bytes 2211848 | tf_op jit(solution)/shard_map/ppermute | solution.py:964
  188.8 37.7 %collective-permute-start.18 = (bf16[256,2048]{1,0:T(8,128)(2,1)S(1)}, bf16[256,2048]{1,0:T(8,128)(2,1)S(1)}, u32[]{:S(2)}, u32[]{:S(2)}) collective-permute-start(bf16[256,2048]{1,0:T(8,128)(2,1)S(1)} %get-tuple-element.301.normed_ref), channel_id=1, source_target_pairs={{0,8},{4,12},{8,0},{12,4},{16,24},{20,28},{24,16},{28,20},{1,9},{5... | collective-permute-start | bytes 3145736 | tf_op jit(solution)/shard_map/ppermute | solution.py:964
  188.8 38.7 %collective-permute-start.19 = (bf16[256,2048]{1,0:T(8,128)(2,1)S(1)}, bf16[256,2048]{1,0:T(8,128)(2,1)}, u32[]{:S(2)}, u32[]{:S(2)}) collective-permute-start(bf16[256,2048]{1,0:T(8,128)(2,1)S(1)} %get-tuple-element.301.normed_ref), channel_id=1, source_target_pairs={{0,16},{4,20},{8,24},{12,28},{16,0},{20,4},{24,8},{28,12},{1,17},{... | collective-permute-start | bytes 3145736 | tf_op jit(solution)/shard_map/ppermute | solution.py:964
  188.8 9.7 %collective-permute-start.15 = (bf16[1440,256]{1,0:T(8,128)(2,1)}, bf16[1440,256]{1,0:T(8,128)(2,1)S(1)}, u32[]{:S(2)}, u32[]{:S(2)}) collective-permute-start(bf16[1440,256]{1,0:T(8,128)(2,1)} %collective-permute-done.10.refs_2_), channel_id=1, source_target_pairs={{0,4},{4,0},{8,12},{12,8},{16,20},{20,16},{24,28},{28,24},{1,5},{5... | collective-permute-start | bytes 2211848 | tf_op jit(solution)/shard_map/ppermute | solution.py:964
  189.6 8.9 %collective-permute-start.16 = (bf16[1440,256]{1,0:T(8,128)(2,1)}, bf16[1440,256]{1,0:T(8,128)(2,1)S(1)}, u32[]{:S(2)}, u32[]{:S(2)}) collective-permute-start(bf16[1440,256]{1,0:T(8,128)(2,1)} %collective-permute-done.11.refs_4_), channel_id=1, source_target_pairs={{0,4},{4,0},{8,12},{12,8},{16,20},{20,16},{24,28},{28,24},{1,5},{5... | collective-permute-start | bytes 2211848 | tf_op jit(solution)/shard_map/ppermute | solution.py:964
  189.6 8.9 %collective-permute-start.17 = (bf16[1440,256]{1,0:T(8,128)(2,1)}, bf16[1440,256]{1,0:T(8,128)(2,1)S(1)}, u32[]{:S(2)}, u32[]{:S(2)}) collective-permute-start(bf16[1440,256]{1,0:T(8,128)(2,1)} %collective-permute-done.12.refs_6_), channel_id=1, source_target_pairs={{0,4},{4,0},{8,12},{12,8},{16,20},{20,16},{24,28},{28,24},{1,5},{5... | collective-permute-start | bytes 2211848 | tf_op jit(solution)/shard_map/ppermute | solution.py:964
  228.6 23.6 %collective-permute-start.20 = (bf16[256,2048]{1,0:T(8,128)(2,1)}, bf16[256,2048]{1,0:T(8,128)(2,1)}, u32[]{:S(2)}, u32[]{:S(2)}) collective-permute-start(bf16[256,2048]{1,0:T(8,128)(2,1)} %broadcast_select_fusion.1), channel_id=1, source_target_pairs={{0,8},{4,20},{8,0},{12,28},{16,24},{20,4},{24,16},{28,12},{1,9},{5... | collective-permute-start | bytes 3145736 | tf_op jit(solution)/shard_map/ppermute | solution.py:967
  287.1 44.4 %collective-permute-start.22 = (bf16[256,2048]{1,0:T(8,128)(2,1)}, bf16[256,2048]{1,0:T(8,128)(2,1)}, u32[]{:S(2)}, u32[]{:S(2)}) collective-permute-start(bf16[256,2048]{1,0:T(8,128)(2,1)} %get-tuple-element.320), channel_id=1, source_target_pairs={{0,8},{4,20},{8,0},{12,28},{16,24},{20,4},{24,16},{28,12},{1,9},{5... | collective-permute-start | bytes 3145736 | tf_op jit(solution)/shard_map/ppermute | solution.py:967
  327.3 17.0 %collective-permute-start.21 = (f32[1,2048]{1,0:T(1,128)S(1)}, f32[1,2048]{1,0:T(1,128)S(1)}, u32[]{:S(2)}, u32[]{:S(2)}) collective-permute-start(f32[1,2048]{1,0:T(1,128)S(1)} %slice_add_fusion), channel_id=1, source_target_pairs={{0,4},{4,0},{8,12},{12,8},{16,20},{20,16},{24,28},{28,24},{1,5},{5... | collective-permute-start | bytes 24584 | tf_op jit(solution)/shard_map/ppermute | solution.py:964
  330.4 20.4 %collective-permute-start.25 = (bf16[256,2048]{1,0:T(8,128)(2,1)}, bf16[256,2048]{1,0:T(8,128)(2,1)S(1)}, u32[]{:S(2)}, u32[]{:S(2)}) collective-permute-start(bf16[256,2048]{1,0:T(8,128)(2,1)} %copy-done.170), channel_id=1, source_target_pairs={{0,8},{4,20},{8,0},{12,28},{16,24},{20,4},{24,16},{28,12},{1,9},{5... | collective-permute-start | bytes 3145736 | tf_op jit(solution)/shard_map/ppermute | solution.py:967
  344.3 5.9 %collective-permute-start.23 = (f32[1,2048]{1,0:T(1,128)S(1)}, f32[1,2048]{1,0:T(1,128)S(1)}, u32[]{:S(2)}, u32[]{:S(2)}) collective-permute-start(f32[1,2048]{1,0:T(1,128)S(1)} %add.241), channel_id=1, source_target_pairs={{0,8},{4,12},{8,0},{12,4},{16,24},{20,28},{24,16},{28,20},{1,9},{5... | collective-permute-start | bytes 24584 | tf_op jit(solution)/shard_map/ppermute | solution.py:964
  344.8 15.0 %collective-permute-start.28 = (bf16[256,2048]{1,0:T(8,128)(2,1)S(1)}, bf16[256,2048]{1,0:T(8,128)(2,1)S(1)}, u32[]{:S(2)}, u32[]{:S(2)}) collective-permute-start(bf16[256,2048]{1,0:T(8,128)(2,1)S(1)} %add_convert_fusion.2), channel_id=1, source_target_pairs={{0,16},{4,12},{8,24},{12,4},{16,0},{20,28},{24,8},{28,20},{1,17},{... | collective-permute-start | bytes 3145736 | tf_op jit(solution)/shard_map/ppermute | solution.py:967
  374.2 17.2 %collective-permute-start.29 = (bf16[256,1024]{1,0:T(8,128)(2,1)}, bf16[256,1024]{1,0:T(8,128)(2,1)}, u32[]{:S(2)}, u32[]{:S(2)}) collective-permute-start(bf16[256,1024]{1,0:T(8,128)(2,1)} %get-tuple-element.365), channel_id=1, source_target_pairs={{1,0},{2,1},{3,2},{5,4},{6,5},{7,6},{9,8},{10,9},{11,10},{13,12},{... | collective-permute-start | bytes 1572872 | tf_op jit(solution)/shard_map/ppermute | solution.py:976
  382.6 17.5 %collective-permute-start.27 = (f32[1,2048]{1,0:T(1,128)S(1)}, f32[1,2048]{1,0:T(1,128)S(1)}, u32[]{:S(2)}, u32[]{:S(2)}) collective-permute-start(f32[1,2048]{1,0:T(1,128)S(1)} %add.248), channel_id=1, source_target_pairs={{0,2},{1,3},{2,0},{3,1},{4,6},{5,7},{6,4},{7,5},{8,10},{9,11},{10,... | collective-permute-start | bytes 24584 | tf_op jit(solution)/shard_map/ppermute | solution.py:972
  393.6 15.2 %collective-permute-start.32 = (bf16[256,1024]{1,0:T(8,128)(2,1)}, bf16[256,1024]{1,0:T(8,128)(2,1)}, u32[]{:S(2)}, u32[]{:S(2)}) collective-permute-start(bf16[256,1024]{1,0:T(8,128)(2,1)} %add_convert_fusion.5), channel_id=1, source_target_pairs={{1,0},{2,1},{3,2},{5,4},{6,5},{7,6},{9,8},{10,9},{11,10},{13,12},{... | collective-permute-start | bytes 1572872 | tf_op jit(solution)/shard_map/ppermute | solution.py:976
  400.1 18.2 %collective-permute-start.30 = (bf16[256,2048]{1,0:T(8,128)(2,1)S(1)}, bf16[256,2048]{1,0:T(8,128)(2,1)}, u32[]{:S(2)}, u32[]{:S(2)}) collective-permute-start(bf16[256,2048]{1,0:T(8,128)(2,1)S(1)} %copy-done.167), channel_id=1, source_target_pairs={{0,8},{4,20},{8,0},{12,28},{16,24},{20,4},{24,16},{28,12},{1,9},{5... | collective-permute-start | bytes 3145736 | tf_op jit(solution)/shard_map/ppermute | solution.py:967
  401.2 24.3 %collective-permute-start.31 = (bf16[256,2048]{1,0:T(8,128)(2,1)S(1)}, bf16[256,2048]{1,0:T(8,128)(2,1)}, u32[]{:S(2)}, u32[]{:S(2)}) collective-permute-start(bf16[256,2048]{1,0:T(8,128)(2,1)S(1)} %copy-done.169), channel_id=1, source_target_pairs={{0,8},{4,20},{8,0},{12,28},{16,24},{20,4},{24,16},{28,12},{1,9},{5... | collective-permute-start | bytes 3145736 | tf_op jit(solution)/shard_map/ppermute | solution.py:967
  428.1 15.6 %collective-permute-start.33 = (bf16[256,2048]{1,0:T(8,128)(2,1)}, bf16[256,2048]{1,0:T(8,128)(2,1)}, u32[]{:S(2)}, u32[]{:S(2)}) collective-permute-start(bf16[256,2048]{1,0:T(8,128)(2,1)} %add_convert_fusion.1), channel_id=1, source_target_pairs={{0,16},{4,12},{8,24},{12,4},{16,0},{20,28},{24,8},{28,20},{1,17},{... | collective-permute-start | bytes 3145736 | tf_op jit(solution)/shard_map/ppermute | solution.py:967
  430.7 13.0 %collective-permute-start.35 = (bf16[256,1024]{1,0:T(8,128)(2,1)}, bf16[256,1024]{1,0:T(8,128)(2,1)}, u32[]{:S(2)}, u32[]{:S(2)}) collective-permute-start(bf16[256,1024]{1,0:T(8,128)(2,1)} %constant_dynamic-slice_fusion.1), channel_id=1, source_target_pairs={{0,4},{4,0},{8,12},{12,8},{16,20},{20,16},{24,28},{28,24},{1,5},{5... | collective-permute-start | bytes 1572872 | tf_op jit(solution)/shard_map/ppermute | solution.py:964
  439.2 25.4 %collective-permute-start.34 = (bf16[256,1024]{1,0:T(8,128)(2,1)}, bf16[256,1024]{1,0:T(8,128)(2,1)}, u32[]{:S(2)}, u32[]{:S(2)}) collective-permute-start(bf16[256,1024]{1,0:T(8,128)(2,1)} %add_convert_fusion.4), channel_id=1, source_target_pairs={{1,0},{2,1},{3,2},{5,4},{6,5},{7,6},{9,8},{10,9},{11,10},{13,12},{... | collective-permute-start | bytes 1572872 | tf_op jit(solution)/shard_map/ppermute | solution.py:976
  447.7 9.0 %collective-permute-start.36 = (bf16[64,1024]{1,0:T(8,128)(2,1)}, bf16[64,1024]{1,0:T(8,128)(2,1)}, u32[]{:S(2)}, u32[]{:S(2)}) collective-permute-start(bf16[64,1024]{1,0:T(8,128)(2,1)} %get-tuple-element.412), channel_id=1, source_target_pairs={{0,8},{4,12},{8,0},{12,4},{16,24},{20,28},{24,16},{28,20},{1,9},{5... | collective-permute-start | bytes 393224 | tf_op jit(solution)/shard_map/ppermute | solution.py:964
  449.0 7.7 %collective-permute-start.37 = (bf16[64,1024]{1,0:T(8,128)(2,1)}, bf16[64,1024]{1,0:T(8,128)(2,1)}, u32[]{:S(2)}, u32[]{:S(2)}) collective-permute-start(bf16[64,1024]{1,0:T(8,128)(2,1)} %get-tuple-element.413), channel_id=1, source_target_pairs={{0,16},{4,20},{8,24},{12,28},{16,0},{20,4},{24,8},{28,12},{1,17},{... | collective-permute-start | bytes 393224 | tf_op jit(solution)/shard_map/ppermute | solution.py:964
  449.1 7.6 %collective-permute-start.38 = (bf16[64,1024]{1,0:T(8,128)(2,1)}, bf16[64,1024]{1,0:T(8,128)(2,1)}, u32[]{:S(2)}, u32[]{:S(2)}) collective-permute-start(bf16[64,1024]{1,0:T(8,128)(2,1)} %get-tuple-element.414), channel_id=1, source_target_pairs={{0,24},{4,28},{8,16},{12,20},{16,8},{20,12},{24,0},{28,4},{1,25},{... | collective-permute-start | bytes 393224 | tf_op jit(solution)/shard_map/ppermute | solution.py:964
  457.9 34.0 %collective-permute-start.40 = (bf16[64,1024]{1,0:T(8,128)(2,1)S(1)}, bf16[64,1024]{1,0:T(8,128)(2,1)}, u32[]{:S(2)}, u32[]{:S(2)}) collective-permute-start(bf16[64,1024]{1,0:T(8,128)(2,1)S(1)} %add_convert_fusion.10), channel_id=1, source_target_pairs={{0,1},{1,0},{2,3},{3,2},{4,5},{5,4},{6,7},{7,6},{8,9},{9,8},{10,11... | collective-permute-start | bytes 393224 | tf_op jit(solution)/shard_map/ppermute | solution.py:972
  482.3 19.4 %collective-permute-start.39 = (bf16[64,2304]{1,0:T(8,128)(2,1)}, bf16[64,2304]{1,0:T(8,128)(2,1)}, u32[]{:S(2)}, u32[]{:S(2)}) collective-permute-start(bf16[64,2304]{1,0:T(8,128)(2,1)} %constant_dynamic-slice_fusion), channel_id=1, source_target_pairs={{0,4},{4,0},{8,12},{12,8},{16,20},{20,16},{24,28},{28,24},{1,5},{5... | collective-permute-start | bytes 884744 | tf_op jit(solution)/shard_map/ppermute | solution.py:964
  492.8 15.2 %collective-permute-start.44 = (bf16[64,1024]{1,0:T(8,128)(2,1)S(1)}, bf16[64,1024]{1,0:T(8,128)(2,1)S(1)}, u32[]{:S(2)}, u32[]{:S(2)}) collective-permute-start(bf16[64,1024]{1,0:T(8,128)(2,1)S(1)} %add_convert_fusion.9), channel_id=1, source_target_pairs={{0,2},{1,3},{2,0},{3,1},{4,6},{5,7},{6,4},{7,5},{8,10},{9,11},{10,... | collective-permute-start | bytes 393224 | tf_op jit(solution)/shard_map/ppermute | solution.py:972
  505.3 5.5 collective-permute-start.42
  505.3 5.5 collective-permute-start.43
  508.7 7.5 %collective-permute-start.48 = (bf16[64,1024]{1,0:T(8,128)(2,1)S(1)}, bf16[64,1024]{1,0:T(8,128)(2,1)}, u32[]{:S(2)}, u32[]{:S(2)}) collective-permute-start(bf16[64,1024]{1,0:T(8,128)(2,1)S(1)} %add_convert_fusion.8.refs_0_), channel_id=1, source_target_pairs={{0,24},{4,28},{8,16},{12,20},{16,8},{20,12},{24,0},{28,4},{1,25},{... | collective-permute-start | bytes 393224 | tf_op jit(solution)/shard_map/ppermute | solution.py:964
  511.7 6.4 %collective-permute-start.45 = (bf16[16,2304]{1,0:T(8,128)(2,1)S(1)}, bf16[16,2304]{1,0:T(8,128)(2,1)S(1)}, u32[]{:S(2)}, u32[]{:S(2)}) collective-permute-start(bf16[16,2304]{1,0:T(8,128)(2,1)S(1)} %add_convert_fusion.14), channel_id=1, source_target_pairs={{0,1},{1,0},{2,3},{3,2},{4,5},{5,4},{6,7},{7,6},{8,9},{9,8},{10,11... | collective-permute-start | bytes 221192 | tf_op jit(solution)/shard_map/ppermute | solution.py:972
  530.6 8.2 %collective-permute-start.53 = (bf16[64,2304]{1,0:T(8,128)(2,1)}, bf16[64,2304]{1,0:T(8,128)(2,1)S(1)}, u32[]{:S(2)}, u32[]{:S(2)}) collective-permute-start(bf16[64,2304]{1,0:T(8,128)(2,1)} %join_rows.3), channel_id=1, source_target_pairs={{0,4},{4,0},{8,12},{12,8},{16,20},{20,16},{24,28},{28,24},{1,5},{5... | collective-permute-start | bytes 884744 | tf_op jit(solution)/shard_map/ppermute | solution.py:964
  (211 other events, 1368.2 us)
Sparse Core Ops, SparseCore 0:
  18.6 68.1 all-gather.6
  88.7 75.0 all-gather.8
  166.3 78.0 all-gather.10

commit v3 on v2

--- a/solution.py
+++ b/solution.py
@@ -48,9 +48,16 @@
     return pltpu.CompilerParams(vmem_limit_bytes=mebibytes << 20)
 
 
-kernel_call = functools.partial(
-    pl.pallas_call, cost_estimate=pl.CostEstimate(flops=0, transcendentals=0, bytes_accessed=0)
-)
+def kernel_call(*args, in_specs=None, **options):
+    if in_specs is not None:
+        options["in_specs"] = in_specs
+    call = pl.pallas_call(
+        *args, cost_estimate=pl.CostEstimate(flops=0, transcendentals=0, bytes_accessed=0), **options
+    )
+    if in_specs is None:
+        return call
+    keep = lambda value, spec: pltpu.with_memory_space_constraint(value, pltpu.HBM) if spec is anywhere else value
+    return lambda *operands: call(*[keep(value, spec) for value, spec in zip(operands, in_specs)])
 
 
 anywhere = pl.BlockSpec(memory_space=pltpu.HBM)
@@ -453,23 +460,42 @@
     )(mixed, inputs, gain[None], weights)
 
 
-def feed_forward_kernel(normed_ref, own_ref, partner_ref, gate_ref, up_ref, weight_ref, semaphores, *, block):
-    copies = []
-    for half, ref in enumerate((own_ref, partner_ref)):
-        for member in range(2):
-            at = 2 * half + member
-            copies.append(pltpu.make_async_copy(ref.at[member], weight_ref.at[at], semaphores.at[at]))
-    copies[0].start()
-    copies[1].start()
-    for half in range(2):
-        for member, out_ref in enumerate((gate_ref, up_ref)):
-            at = 2 * half + member
-            copies[at].wait()
-            if at + 2 < 4:
-                copies[at + 2].start()
-            for start in range(0, normed_ref.shape[0], block):
-                rows = slice(start, start + block)
-                out_ref[half, rows, :] = dot_nt(normed_ref[rows, :], weight_ref[at, :, :D])
+class Copies:
+    def __init__(self, semaphores):
+        self.semaphores = semaphores
+        self.made = []
+
+    def __call__(self, source, target):
+        copy = pltpu.make_async_copy(source, target, self.semaphores.at[len(self.made)])
+        self.made.append(copy)
+        return copy
+
+    def started(self, source, target):
+        copy = self(source, target)
+        copy.start()
+        return copy
+
+
+def feed_forward_kernel(normed_ref, own_ref, partner_ref, gate_hbm, up_hbm, weight_ref, value_ref, semaphores, *, block):
+    copies = Copies(semaphores)
+    pairs = [(half, member) for half in range(2) for member in range(2)]
+    fetches = [
+        copies((own_ref, partner_ref)[half].at[member], weight_ref.at[2 * half + member]) for half, member in pairs
+    ]
+    fetches[0].start()
+    fetches[1].start()
+    stores = []
+    for half, member in pairs:
+        at = 2 * half + member
+        fetches[at].wait()
+        if at + 2 < 4:
+            fetches[at + 2].start()
+        for start in range(0, normed_ref.shape[0], block):
+            rows = slice(start, start + block)
+            value_ref[at, rows, :] = dot_nt(normed_ref[rows, :], weight_ref[at, :, :D])
+        stores.append(copies.started(value_ref.at[at], (gate_hbm, up_hbm)[member].at[half]))
+    for store in stores:
+        store.wait()
 
 
 def feed_forward(normed, own, partner, block):
@@ -479,157 +505,196 @@
         functools.partial(feed_forward_kernel, block=block),
         out_shape=(shape_of((2, tokens, columns)), shape_of((2, tokens, columns))),
         in_specs=[in_vmem, anywhere, anywhere],
-        out_specs=(in_vmem,) * 2,
-        scratch_shapes=[pltpu.VMEM((4, columns, WIDE), bf16), pltpu.SemaphoreType.DMA((4,))],
-        compiler_params=limits(24),
+        out_specs=(anywhere,) * 2,
+        scratch_shapes=[
+            pltpu.VMEM((4, columns, WIDE), bf16),
+            pltpu.VMEM((4, tokens, columns), f32),
+            pltpu.SemaphoreType.DMA((8,)),
+        ],
+        compiler_params=limits(28),
         name="feed_forward",
     )(normed, own, partner)
 
 
-def grad_copies(place_ref, grad_hbm, grad_ref, semaphores, chips, block, first):
+def grad_copies(copies, place_ref, grad_hbm, grad_ref, chips, block):
     return [
-        pltpu.make_async_copy(
-            grad_hbm.at[0 if r is None else place_ref[1] ^ (2 * r)], grad_ref.at[pl.ds(turn * block, block), :], semaphores.at[first + turn]
+        copies(
+            grad_hbm.at[0 if r is None else place_ref[1] ^ (2 * r)], grad_ref.at[pl.ds(turn * block, block), :]
         )
         for turn, r in enumerate(chips)
     ]
 
 
-def feed_back_kernel(place_ref, grad_hbm, gate_ref, up_ref, own_ref, partner_ref, *refs, block, devices, chips):
+MAGS = 8
+
+
+def feed_back_kernel(place_ref, grad_hbm, own_ref, partner_ref, *refs, block, devices, chips, fused):
+    kept, refs = refs[: 2 - fused], refs[2 - fused :]
     piece_refs, refs = refs[:devices], refs[devices:]
-    share_refs, down_refs, refs = refs[: len(chips)], refs[len(chips) : 2 * len(chips)], refs[2 * len(chips) :]
-    ext_ref, hidden_ref, grad_gate_ref, grad_up_ref, down_ext_ref, mag_ref, down_mag_ref = refs[:7]
-    aux_ref, weight_ref, down_weight_ref, grad_ref, semaphores = refs[7:]
+    count = len(chips)
+    share_hbm, down_hbm, refs = refs[:count], refs[count : 2 * count], refs[2 * count :]
+    hidden_hbm, grad_gate_hbm, grad_up_hbm, ext_ref, mag_ref, aux_ref, refs = *refs[:6], refs[6:]
+    weight_ref, down_weight_ref, grad_ref, share_ref, made_ref, value_ref, semaphores = refs
     core = place_ref[0]
     columns = own_ref.shape[1]
     width = piece_refs[0].shape[1]
-    copies = grad_copies(place_ref, grad_hbm, grad_ref, semaphores, chips, block, devices + 2)
+    copies = Copies(semaphores)
+    fetches = grad_copies(copies, place_ref, grad_hbm, grad_ref, chips, block)
     for i, ref in enumerate(piece_refs):
         lanes = pl.ds(pl.multiple_of((place_ref[1] ^ i) * width, width), width)
-        copies.append(pltpu.make_async_copy(ref, down_weight_ref.at[:, lanes], semaphores.at[i]))
-    for copy in copies:
-        copy.start()
-    weight_copies = [
-        pltpu.make_async_copy(ref, weight_ref.at[half], semaphores.at[devices + half])
-        for half, ref in enumerate((own_ref, partner_ref))
-    ]
+        fetches.append(copies(ref, down_weight_ref.at[:, lanes]))
+    if not fused:
+        fetches.append(copies(kept[0], value_ref.at[0]))
+        fetches.append(copies(kept[1], value_ref.at[1]))
+    weight_fetches = [copies(ref, weight_ref.at[half]) for half, ref in enumerate((own_ref, partner_ref))]
+    if fused:
+        weight_fetches[0].start()
+    for fetch in fetches:
+        fetch.start()
     mag_ref[...] = jnp.zeros(mag_ref.shape, f32)
-    down_mag_ref[...] = jnp.zeros(down_mag_ref.shape, f32)
-    weight_copies[0].start()
-    for copy in copies:
-        copy.wait()
-    weight_copies[1].start()
+    if fused:
+        weight_fetches[0].wait()
+        value_ref[0, 0] = dot_nt(kept[0][...], weight_ref[0, 0, :, :D])
+        value_ref[1, 0] = dot_nt(kept[0][...], weight_ref[0, 1, :, :D])
+    else:
+        weight_fetches[0].start()
+    for fetch in fetches:
+        fetch.wait()
+    weight_fetches[1].start()
     aux_ref[...] = down_weight_ref[2 * columns :, :]
-
-    def step(turn, carry):
-        rows = pl.ds(pl.multiple_of(turn * block, block), block)
+    stores = []
+    for turn in range(count):
+        rows = slice(turn * block, (turn + 1) * block)
         grad = grad_ref[rows, :]
-        down_ext_ref[rows, :] = dot_nt(grad, down_weight_ref[2 * columns :, :]).astype(bf16)
         share, down = None, None
         for half in range(2):
             order = core if half == 0 else 1 - core
             down_rows = pl.ds(pl.multiple_of(order * columns, 16), columns)
-            gate, up = gate_ref[half, rows, :], up_ref[half, rows, :]
+            if fused and half:
+                weight_fetches[1].wait()
+                value_ref[0, 1] = dot_nt(kept[0][...], weight_ref[1, 0, :, :D])
+                value_ref[1, 1] = dot_nt(kept[0][...], weight_ref[1, 1, :, :D])
+            gate, up = value_ref[0, half, rows, :], value_ref[1, half, rows, :]
             grad_hidden = dot_nt(grad, down_weight_ref[down_rows, :])
             sigma = 1.0 / (1.0 + jnp.exp(-gate))
             silu = gate * sigma
             hidden = (silu * up).astype(bf16)
             grad_gate = grad_hidden * up * (sigma + silu * (1.0 - sigma))
             grad_up = grad_hidden * silu
-            mag_ref[half : half + 1, :] += jnp.sum(grad_gate * gate, axis=0, keepdims=True)
-            mag_ref[2 + half : 3 + half, :] += jnp.sum(grad_up * up, axis=0, keepdims=True)
+            mag_ref[half : half + 1, :columns] += jnp.sum(grad_gate * gate, axis=0, keepdims=True)
+            mag_ref[2 + half : 3 + half, :columns] += jnp.sum(grad_up * up, axis=0, keepdims=True)
             grad_gate, grad_up = grad_gate.astype(bf16), grad_up.astype(bf16)
-            hidden_ref[half, rows, :] = hidden
-            grad_gate_ref[half, rows, :] = grad_gate
-            grad_up_ref[half, rows, :] = grad_up
+            for at, (value, ref) in enumerate(((hidden, hidden_hbm), (grad_gate, grad_gate_hbm), (grad_up, grad_up_hbm))):
+                made_ref[at, half, rows, :] = value
+                stores.append(copies.started(made_ref.at[at, half, rows, :], ref.at[half, rows, :]))
             part = dot_nn(hidden, down_weight_ref[down_rows, :])
             down = part if down is None else down + part
-            pl.when(turn == 0)(weight_copies[half].wait)
+            if turn == 0 and not fused:
+                weight_fetches[half].wait()
             part = dot_nn(grad_gate, weight_ref[half, 0]) + dot_nn(grad_up, weight_ref[half, 1])
             share = part if share is None else share + part
-        ext_ref[rows, :] = share[:, D:].astype(bf16)
-        for at in range(len(chips)):
-
-            @pl.when((turn ^ core if len(chips) == 2 else turn) == at)
-            def _(at=at):
-                share_refs[at][...] = share[:, :D].astype(bf16)
-                down_refs[at][...] = down.astype(bf16)
-
-        down_mag_ref[0:1, :] += jnp.sum(grad.astype(f32) * down, axis=0, keepdims=True)
-        return carry
-
-    lax.fori_loop(0, len(chips), step, 0)
-
-
-def feed_back(place, grads, chips, gate, up, own, partner, pieces, block):
-    tokens = len(chips) * block
+        share_ref[0, rows, :] = share[:, :D].astype(bf16)
+        share_ref[1, rows, :] = down.astype(bf16)
+        ext_ref[rows, :EXT] = share[:, D:].astype(bf16)
+        small = dot_nt(grad, down_weight_ref[2 * columns :, :])
+        ext_ref[rows, EXT : EXT + AUX] = small.astype(bf16)
+        mag_ref[4:5, :] += jnp.sum(grad.astype(f32) * down, axis=0, keepdims=True)
+    for at in range(count):
+        turn = at ^ core if count == 2 else at
+        rows = pl.ds(pl.multiple_of(turn * block, block), block)
+        stores.append(copies.started(share_ref.at[0, rows, :], share_hbm[at]))
+        stores.append(copies.started(share_ref.at[1, rows, :], down_hbm[at]))
+    for store in stores:
+        store.wait()
+
+
+def feed_back(place, grads, chips, kept, own, partner, pieces, block):
+    fused = int(len(kept) == 1)
+    count = len(chips)
+    tokens = count * block
     columns = own.shape[1]
     devices = len(pieces)
     return kernel_call(
-        functools.partial(feed_back_kernel, block=block, devices=devices, chips=chips),
-        out_shape=(shape_of((block, D), bf16),) * (2 * len(chips))
+        functools.partial(feed_back_kernel, block=block, devices=devices, chips=chips, fused=fused),
+        out_shape=(shape_of((block, D), bf16),) * (2 * count)
         + (
-            shape_of((tokens, EXT), bf16),
             shape_of((2, tokens, columns), bf16),
             shape_of((2, tokens, columns), bf16),
             shape_of((2, tokens, columns), bf16),
-            shape_of((tokens, AUX), bf16),
-            shape_of((4, columns)),
-            shape_of((8, D)),
+            shape_of((tokens, 2 * EXT), bf16),
+            shape_of((MAGS, D)),
             shape_of((AUX, D), bf16),
         ),
-        in_specs=[in_smem, anywhere, in_vmem, in_vmem] + [anywhere] * (2 + devices),
-        out_specs=(in_vmem,) * (8 + 2 * len(chips)),
+        in_specs=[in_smem] + [anywhere] * 3 + ([in_vmem] if fused else [anywhere] * 2) + [anywhere] * devices,
+        out_specs=(anywhere,) * (3 + 2 * count) + (in_vmem,) * 3,
         scratch_shapes=[
             pltpu.VMEM((2, 2, columns, WIDE), bf16),
             pltpu.VMEM((2 * columns + AUX, D), bf16),
             pltpu.VMEM((tokens, D), bf16),
-            pltpu.SemaphoreType.DMA((2 + devices + len(chips),)),
+            pltpu.VMEM((2, tokens, D), bf16),
+            pltpu.VMEM((3, 2, tokens, columns), bf16),
+            pltpu.VMEM((2, 2, tokens, columns), f32),
+            pltpu.SemaphoreType.DMA((4 + devices + 9 * count,)),
         ],
-        compiler_params=limits(40),
+        compiler_params=limits(54),
         name="feed_back",
-    )(place, grads, gate, up, own, partner, *pieces)
+    )(place, grads, own, partner, *kept, *pieces)
 
 
 def feed_adapter_kernel(
-    place_ref, normed_ref, grad_hbm, hidden_ref, grad_gate_ref, grad_up_ref, ext_ref, down_ext_ref, rank_in_ref,
-    down_in_ref, in_ref, out_ref, down_rank_in_ref, down_out_ref, grad_ref, semaphores, *, chips, block,
+    place_ref, normed_ref, grad_hbm, hidden_hbm, grad_gate_hbm, grad_up_hbm, ext_ref, rank_in_ref, down_in_ref, *refs,
+    chips, block, before,
 ):
-    copies = grad_copies(place_ref, grad_hbm, grad_ref, semaphores, chips, block, 0)
-    for copy in copies:
-        copy.start()
+    before_refs, refs = refs[: 4 * before], refs[4 * before :]
+    in_ref, out_ref, down_rank_in_ref, down_out_ref, grad_ref, made_ref, semaphores = refs
+    copies = Copies(semaphores)
+    fetches = [
+        copies.started(ref, made_ref.at[at]) for at, ref in enumerate((hidden_hbm, grad_gate_hbm, grad_up_hbm))
+    ]
+    for fetch in grad_copies(copies, place_ref, grad_hbm, grad_ref, chips, block):
+        fetch.start()
+        fetches.append(fetch)
+
+    def put(ref, index, value, at):
+        ref[index] = value + before_refs[at][index] if before else value
+
     normed = normed_ref[...]
     small = dot_nt(rank_in_ref[...], normed).astype(bf16)
-    in_ref[...] = dot_nn(ext_ref[...].T[: 2 * RANK], normed)
+    ext = ext_ref[...].T
+    put(in_ref, ..., dot_nn(ext[: 2 * RANK], normed), 0)
+    for fetch in fetches:
+        fetch.wait()
     down_small = 0.0
-    grad_small = down_ext_ref[...].T[:RANK]
     for half in range(2):
-        hidden = hidden_ref[half]
-        out_ref[half, :RANK] = dot_nn(small[:RANK], grad_gate_ref[half])
-        out_ref[half, RANK:] = dot_nn(small[RANK:], grad_up_ref[half])
-        down_small = down_small + dot_nt(down_in_ref[half], hidden)
-        down_rank_in_ref[half] = dot_nn(grad_small, hidden)
-    for copy in copies:
-        copy.wait()
-    down_out_ref[...] = dot_nn(down_small.astype(bf16), grad_ref[...])
-
-
-def feed_adapter(place, normed, grads, chips, hidden, grad_gate, grad_up, ext, down_ext, rank_in_t, down_in_t):
+        put(out_ref, (half, slice(0, RANK)), dot_nn(small[:RANK], made_ref[1, half]), 1)
+        put(out_ref, (half, slice(RANK, 2 * RANK)), dot_nn(small[RANK:], made_ref[2, half]), 1)
+        down_small = down_small + dot_nt(down_in_ref[half], made_ref[0, half])
+        put(down_rank_in_ref, half, dot_nn(ext[EXT : EXT + RANK], made_ref[0, half]), 2)
+    put(down_out_ref, ..., dot_nn(down_small.astype(bf16), grad_ref[...]), 3)
+
+
+def feed_adapter(place, normed, grads, chips, hidden, grad_gate, grad_up, ext, rank_in_t, down_in_t, before):
     columns = hidden.shape[2]
     return kernel_call(
-        functools.partial(feed_adapter_kernel, chips=chips, block=normed.shape[0] // len(chips)),
+        functools.partial(
+            feed_adapter_kernel, chips=chips, block=normed.shape[0] // len(chips), before=int(before is not None)
+        ),
         out_shape=(
             shape_of((2 * RANK, D)),
             shape_of((2, 2 * RANK, columns)),
             shape_of((2, RANK, columns)),
             shape_of((RANK, D)),
         ),
-        in_specs=[in_smem, in_vmem, anywhere] + [in_vmem] * 7,
+        in_specs=[in_smem, in_vmem] + [anywhere] * 4 + [in_vmem] * (3 + 4 * (before is not None)),
         out_specs=(in_vmem,) * 4,
-        scratch_shapes=[pltpu.VMEM(normed.shape, bf16), pltpu.SemaphoreType.DMA((len(chips),))],
-        compiler_params=limits(24),
+        scratch_shapes=[
+            pltpu.VMEM(normed.shape, bf16),
+            pltpu.VMEM((3,) + hidden.shape, bf16),
+            pltpu.SemaphoreType.DMA((3 + len(chips),)),
+        ],
+        compiler_params=limits(28),
         name="feed_adapter",
-    )(place, normed, grads, hidden, grad_gate, grad_up, ext, down_ext, rank_in_t, down_in_t)
+    )(place, normed, grads, hidden, grad_gate, grad_up, ext, rank_in_t, down_in_t, *(before or ()))
 
 
 def adapter_columns(products, mag_raw, mag, weights, slot):
@@ -664,6 +729,88 @@
         compiler_params=limits(40),
         name="feed_finish",
     )(weights, products, mag_raw, mag)
+
+
+def feed_pack_kernel(
+    place_ref, own_hbm, partner_hbm, fold_hbm, products_ref, mag_raw_ref, mag_ref, in_ref, down_in_ref,
+    down_products_ref, down_total_ref, down_mag_ref, down_aux_ref, down_proj_ref, down_rank_ref,
+    out_ref, down_grad_ref, weight_ref, fold_ref, full_ref, semaphores, *, share,
+):
+    copies = Copies(semaphores)
+    fold_fetch = copies(fold_hbm, fold_ref)
+    fetches = [
+        copies.started((own_hbm, partner_hbm)[half].at[slot], weight_ref.at[half, slot])
+        for half in range(2)
+        for slot in range(2)
+    ]
+    columns = own_hbm.shape[1]
+    chips, rows = fold_ref.shape[0], 2 * columns
+    core, index, chip = place_ref[0], place_ref[1], place_ref[2]
+    width = fold_ref.shape[2]
+    full_ref[...] = jnp.zeros(full_ref.shape, f32)
+    down_grad_ref[...] = down_total_ref[...] / down_mag_ref[...]
+    inverse = down_aux_ref[RANK : RANK + 1].astype(f32) + down_aux_ref[RANK + 1 : RANK + 2].astype(f32)
+    down_out = factor * down_products_ref[...] * (down_mag_ref[...] * inverse)
+    turn = down_grad_ref[...] * inverse * (-factor * share)
+    full_ref[:1, :D] = turn
+    full_ref[RANK : 2 * RANK, :D] = down_out
+    own = pl.ds(pl.multiple_of(index * width, width), width)
+    own_turn = full_ref[:1, own]
+    full_ref[RANK : 2 * RANK, own] += down_proj_ref[...] * own_turn
+    out_ref[2 * RANK : 3 * RANK] = full_ref[RANK : 2 * RANK, :D].astype(bf16)
+    out_ref[3 * RANK : 4 * RANK] = jnp.zeros((RANK, D), bf16)
+    own_wide = (down_rank_ref[:, own].astype(f32) * own_turn).astype(bf16)
+    full_ref[: 2 * RANK, :D] = jnp.zeros((2 * RANK, D), f32)
+    fetches[0].wait()
+    fold_fetch.start()
+    parts = []
+    ins = [in_ref[slot * RANK : (slot + 1) * RANK] for slot in range(2)]
+    for half in range(2):
+        outs, mags = [], []
+        for slot in range(2):
+            at = 2 * half + slot
+            if at:
+                fetches[at].wait()
+            grad_mag, grad_out, grad_in = adapter_columns(
+                products_ref[half, slot * RANK : (slot + 1) * RANK],
+                mag_raw_ref[half + 2 * slot : half + 2 * slot + 1, :columns],
+                mag_ref[half, slot : slot + 1],
+                weight_ref[half, slot],
+                slot,
+            )
+            outs.append(grad_out)
+            mags.append(grad_mag)
+            ins[slot] = ins[slot] + grad_in
+        row = iota((RANK, columns), 0)
+        tail = jnp.where(row == 0, mags[0], jnp.where(row == 1, mags[1], 0.0))
+        parts.append(jnp.concatenate([*outs, down_in_ref[half], tail], axis=0))
+    first, second = jnp.where(core == 0, parts[0], parts[1]), jnp.where(core == 0, parts[1], parts[0])
+    full_ref[:, pl.ds(pl.multiple_of(chip * rows, HEAD), rows)] = jnp.concatenate([first, second], axis=1)
+    for slot in range(2):
+        out_ref[slot * RANK : (slot + 1) * RANK] = ins[slot].astype(bf16)
+    fold_fetch.wait()
+    for part in range(chips):
+        lanes = slice(part * rows, (part + 1) * rows)
+        full_ref[2 * RANK : 3 * RANK, lanes] += dot_nt(own_wide, fold_ref[part, :rows])
+    for part in range(3):
+        out_ref[64 * (1 + part) : 64 * (2 + part)] = full_ref[:, part * D : (part + 1) * D].astype(bf16)
+
+
+def feed_pack(place, own, partner, fold_down, *rest, share):
+    return kernel_call(
+        functools.partial(feed_pack_kernel, share=share),
+        out_shape=(shape_of((256, D), bf16), shape_of((1, D))),
+        in_specs=[in_smem] + [anywhere] * 3 + [in_vmem] * 11,
+        out_specs=(in_vmem,) * 2,
+        scratch_shapes=[
+            pltpu.VMEM((2,) + own.shape, bf16),
+            pltpu.VMEM(fold_down.shape, bf16),
+            pltpu.VMEM((64, 3 * D), f32),
+            pltpu.SemaphoreType.DMA((5,)),
+        ],
+        compiler_params=limits(40),
+        name="feed_pack",
+    )(place, own, partner, fold_down, *rest)
 
 
 def output_adapter_kernel(
@@ -826,13 +973,18 @@
 
 
 def key_back_kernel(
-    heads_ref, sent_ref, grad_ref, kv_ref, cos_ref, sin_ref, normed_ref, input_ref, gain_ref, residual_ref,
-    before_ref, rank_in_ref, mag_ref, *refs,
+    heads_ref, sent_ref, grad_ref, kv_ref, cos_ref, sin_ref, normed_ref, input_ref, gain_ref, residual_hbm,
+    before_hbm, rank_in_ref, mag_ref, *refs,
 ):
-    weight_refs = refs[:KV_HEADS]
-    input_grad_ref, grad_in_ref, out_ref, grad_mag_ref, turned_ref = refs[KV_HEADS:]
+    weight_hbm = refs[:KV_HEADS]
+    input_grad_ref, grad_in_ref, out_ref, grad_mag_ref, turned_ref = refs[KV_HEADS : KV_HEADS + 5]
+    weight_refs, before_ref, residual_ref, semaphores = refs[KV_HEADS + 5 :]
+    copies = Copies(semaphores)
+    fetches = [copies.started(ref, weight_refs.at[slot]) for slot, ref in enumerate(weight_hbm)]
+    before_fetch = copies.started(before_hbm, before_ref)
+    residual_fetch = copies.started(residual_hbm, residual_ref)
     small = dot_nt(rank_in_ref[...], normed_ref[...]).astype(bf16)
-    total = before_ref[...]
+    total = None
     near = 2 * HEAD
     grad_ins = [None, None]
     for slot in range(KV_HEADS):
@@ -847,19 +999,24 @@
                 raw = turn_back(raw, cos_ref[...], sin_ref[...])
             mags.append(jnp.sum(grad * raw, axis=0, keepdims=True))
             turned_ref[:, slot * near + part * HEAD : slot * near + (part + 1) * HEAD] = grad.astype(bf16)
-        total = total + dot_nn(turned_ref[:, slot * near : (slot + 1) * near], weight_refs[slot][...])
+        fetches[slot].wait()
+        part = dot_nn(turned_ref[:, slot * near : (slot + 1) * near], weight_refs[slot])
+        total = part if total is None else total + part
         for part in range(2):
             lanes = slice(slot * near + part * HEAD, slot * near + (part + 1) * HEAD)
             grad_mag, grad_out, grad_in = adapter_columns(
                 dot_nn(small[part * RANK : (part + 1) * RANK], turned_ref[:, lanes]),
                 mags[part],
                 mag_ref[part : part + 1, lanes_at(place)],
-                weight_refs[slot][part * HEAD : (part + 1) * HEAD, :],
+                weight_refs[slot, part * HEAD : (part + 1) * HEAD, :],
                 1 + part,
             )
             grad_mag_ref[:, lanes_at(part * KVW + place)] = grad_mag
             out_ref[:, lanes_at(part * KVW + place)] = grad_out
             grad_ins[part] = grad_in if grad_ins[part] is None else grad_ins[part] + grad_in
+    before_fetch.wait()
+    total = total + before_ref[...]
+    residual_fetch.wait()
     ext = total[:, D:].astype(bf16).T
     for part in range(2):
         rows = slice(part * RANK, (part + 1) * RANK)
@@ -879,9 +1036,15 @@
             shape_of((RANK, 2 * KVW)),
             shape_of((1, 2 * KVW)),
         ),
-        in_specs=[in_smem] + [in_vmem] * (12 + KV_HEADS),
+        in_specs=[in_smem] + [in_vmem] * 8 + [anywhere] * 2 + [in_vmem] * 2 + [anywhere] * KV_HEADS,
         out_specs=(in_vmem,) * 4,
-        scratch_shapes=[pltpu.VMEM((tokens, 2 * KVW), bf16)],
+        scratch_shapes=[
+            pltpu.VMEM((tokens, 2 * KVW), bf16),
+            pltpu.VMEM((KV_HEADS, 2 * HEAD, WIDE), bf16),
+            pltpu.VMEM((tokens, WIDE), f32),
+            pltpu.VMEM((tokens, D), f32),
+            pltpu.SemaphoreType.DMA((KV_HEADS + 2,)),
+        ],
         compiler_params=limits(40),
         name="key_back",
     )(
@@ -923,6 +1086,63 @@
         out_specs=in_vmem,
         name="join_rows",
     )(place, *pieces)
+
+
+def sides_of(place_ref, mine_ref, other_ref):
+    mine, other = mine_ref[...].astype(f32), other_ref[...].astype(f32)
+    first = place_ref[0] == 0
+    return jnp.where(first, mine, other), jnp.where(first, other, mine)
+
+
+def unpack_late_kernel(place_ref, mine_ref, other_ref, *out_refs):
+    attn_in_ref, attn_out_ref, attn_mag_ref, out_in_ref, out_out_ref, out_mag_ref = out_refs
+    left, right = sides_of(place_ref, mine_ref, other_ref)
+    split = left.shape[1] - D
+    for member in range(3):
+        attn_in_ref[member] = left[member * RANK : (member + 1) * RANK, :D]
+    for group in range(GROUP):
+        attn_out_ref[group] = left[3 * RANK :, group * KVW : (group + 1) * KVW]
+    side = right[:, D - split :]
+    attn_out_ref[GROUP] = side[:RANK]
+    attn_out_ref[GROUP + 1] = side[RANK : 2 * RANK]
+    attn_mag_ref[...] = side[2 * RANK : 2 * RANK + GROUP + 2]
+    mid = jnp.concatenate([left[:, D:], right[:, : D - split]], axis=1)
+    out_in_ref[...] = mid[:RANK]
+    for group in range(GROUP):
+        lanes = slice(group * KVW, (group + 1) * KVW)
+        out_out_ref[group] = mid[RANK : 2 * RANK, lanes]
+        out_mag_ref[group : group + 1, :] = mid[2 * RANK : 2 * RANK + 1, lanes]
+
+
+def unpack_early_kernel(place_ref, mine_ref, other_ref, in_ref, out_ref, mag_ref, down_in_ref, down_out_ref):
+    half = D // 2
+    for at, values in enumerate(sides_of(place_ref, mine_ref, other_ref)):
+        lanes = slice(at * half, (at + 1) * half)
+        for member in range(2):
+            in_ref[member, :, lanes] = values[member * RANK : (member + 1) * RANK]
+        down_out_ref[:, lanes] = values[2 * RANK : 3 * RANK]
+        for part in range(3):
+            start = part * D + at * half
+            width = min(half, FF - start)
+            if width <= 0:
+                continue
+            block = values[64 * (1 + part) : 64 * (2 + part), :width]
+            to = slice(start, start + width)
+            for member in range(2):
+                out_ref[member, :, to] = block[member * RANK : (member + 1) * RANK]
+            down_in_ref[:, to] = block[2 * RANK : 3 * RANK]
+            mag_ref[:, to] = block[3 * RANK : 3 * RANK + 2]
+
+
+def unpack(kernel, place, halves, shapes, name):
+    return kernel_call(
+        kernel,
+        out_shape=tuple(shape_of(shape) for shape in shapes),
+        in_specs=[in_smem, in_vmem, in_vmem],
+        out_specs=(in_vmem,) * len(shapes),
+        compiler_params=limits(24),
+        name=name,
+    )(place, *halves)
 
 
 class Order:
@@ -1010,8 +1230,7 @@
         sent = self.swap(value, 1)
         yield
         sent = order(sent)
-        pair = lambda first, second: jnp.concatenate([first, second], axis=1)
-        yield jnp.where(self.core == 0, pair(value, sent), pair(sent, value)).astype(f32)
+        yield value, sent
 
     def small_total(self, value, order):
         for swap, count in ((self.swap, self.devices), (self.row_swap, self.blocks)):
@@ -1185,14 +1404,15 @@
         down_1, down_2, down_3 = links.swap(down_c1, 2), links.swap(down_c2, 4), links.swap(down_c3, 6)
         mixed, lse = attend(scalars, order(queries), kv_blocks)
         mark(lse)
-        down_1, down_2, down_3 = settle(down_1, down_2, down_3)
-        down_pieces = [down_0, None, down_1, None, down_2, None, down_3, None]
-        for at in range(0, 8, 2):
-            down_pieces[at + 1] = partner(order(down_pieces[at]))
         feed_partner = partner(order(feed_own))
 
         def feed_late():
-            down_pieces[1::2] = settle(*down_pieces[1::2])
+            near = settle(down_1, down_2, down_3)
+            pieces = []
+            for piece in (down_0, *near):
+                pieces += [piece, partner(piece)]
+            return settle(*pieces)
+
     else:
         q_fold = fold(attn_base, attn_in_t, attn_rank[:GROUP], attn_mag[:GROUP], 0, False, "fold_q")
         q_weights, o_weights, normed = spread(q_fold), spread(fold_out()), norm_in()
@@ -1224,75 +1444,66 @@
 
     def backward(members, kept):
         grads = grad_own if members == (None,) else grad_all
-        made = feed_back(place, grads, members, *order(*kept), feed_own, feed_partner, down_pieces, tokens)
+        kept = list(order(*kept)) if isinstance(kept, (tuple, list)) else [order(kept)]
+        made = feed_back(place, grads, members, kept, feed_own, feed_partner, down_pieces, tokens)
         mark(made[0])
         count = len(members)
         return made[:count], made[count : 2 * count], made[2 * count :]
 
-    def adapters(members, normed_group, made):
-        ext, hidden, grad_gate, grad_up, down_ext, mag_sum, down_mag, down_aux = made[2]
+    mag_sums = []
+
+    def adapters(members, normed_group, made, before):
+        hidden, grad_gate, grad_up, ext, mags, down_aux = made[2]
         parts = feed_adapter(
-            place, order(normed_group), grad_own if members == (None,) else grad_all, members, hidden, grad_gate, grad_up, ext, down_ext,
-            feed_in_t.reshape(2 * RANK, D), halves_in_t,
+            place, order(normed_group), grad_own if members == (None,) else grad_all, members, hidden, grad_gate,
+            grad_up, ext, feed_in_t.reshape(2 * RANK, D), halves_in_t, before,
         )
         mark(parts[0])
         aux.append(down_aux)
-        return tuple(parts) + (mag_sum, down_mag)
+        mag_sums.append(mags)
+        return tuple(parts)
 
     if fast:
         side, other = links.sides(normed_feed)
-        kept = forward(normed_feed)
-        feed_late()
-        own_made = backward((None,), kept)
+        down_pieces = feed_late()
+        own_made = backward((None,), normed_feed)
         side, other = settle(side, other)
         crossed = links.across(side, other)
         near = settle(jnp.concatenate([side, other]))
         near_kept = forward(near)
-        own_sums = adapters((None,), normed_feed, own_made)
+        sums = adapters((None,), normed_feed, own_made, None)
         crossed = settle(crossed)
-        far_kept = forward(crossed)
-        far_made = backward((3,), far_kept)
+        far_made = backward((3,), crossed)
         from_far = links.split_swap(far_made[0][0], 2, 4)
         near_made = backward((1, 2), near_kept)
         early_first = links.split_swap(near_made[0][0], 2, 4)
         from_far = settle(from_far)
         late_share = settle((near_made[0][1].astype(f32) + from_far.astype(f32)).astype(bf16))
         early_second = links.split_swap(late_share, 4, 2)
-        down_mag_steps = links.small_total(own_made[2][6][:1] + near_made[2][6][:1] + far_made[2][6][:1], order)
+        down_mag_steps = links.small_total(own_made[2][4][4:5] + near_made[2][4][4:5] + far_made[2][4][4:5], order)
         next(down_mag_steps)
-        near_sums = adapters((1, 2), near, near_made)
+        sums = adapters((1, 2), near, near_made, sums)
         next(down_mag_steps)
-        far_sums = adapters((3,), crossed, far_made)
+        sums = adapters((3,), crossed, far_made, sums)
         next(down_mag_steps)
         early_first = settle(early_first)
-        all_sums = [own_sums, near_sums, far_sums]
         reduced = (own_made[0][0], early_first, early_second)
         shares_out = [own_made[1][0], *near_made[1], far_made[1][0]]
     else:
-        all_sums, shares_grad, shares_out = [], [], []
+        sums, shares_grad, shares_out = None, [], []
         for r in range(chips):
             normed_group = links.swap(normed_feed, 2 * r) if r else normed_feed
-            made = backward((r,), forward(normed_group))
-            all_sums.append(adapters((r,), normed_group, made))
+            made = backward((r,), normed_group)
+            sums = adapters((r,), normed_group, made, sums)
             shares_grad.append(made[0][0])
             shares_out.append(made[1][0])
         rest = sum(links.swap(shares_grad[r], 2 * r).astype(f32) for r in range(1, chips)).astype(bf16)
         reduced = (shares_grad[0], rest, jnp.zeros(rest.shape, bf16))
-        down_mag_steps = links.small_total(sum(part[5][:1] for part in all_sums), order)
+        down_mag_steps = links.small_total(sum(mags[4:5] for mags in mag_sums), order)
         next(down_mag_steps)
-    feed_in, feed_products, down_in, down_products, feed_mag_raw, _ = (sum(parts) for parts in zip(*all_sums))
-
-    finished = []
-    for half, (weights, at) in enumerate(((feed_own, core), (feed_partner, 1 - core))):
-        finished.append(
-            finish_columns(
-                weights,
-                order(feed_products[half]),
-                feed_mag_raw[half::2],
-                lax.dynamic_slice_in_dim(feed_mag, at * feed_cols, feed_cols, 1),
-            )
-        )
-        mark(finished[-1][0])
+    feed_in, feed_products, down_in, down_products = sums
+    mag_raw = sum(mag_sums)
+    for _ in range(2):
         next(down_mag_steps)
     reduced = settle(*reduced)
     grad_residual, grad_ordered, out_mag_raw, out_ext, grad_mixed, delta = residual_back(
@@ -1301,6 +1512,20 @@
     mark(delta)
 
     def pack_early(down_mag_total):
+        feed_mags = jnp.stack(
+            [lax.dynamic_slice_in_dim(feed_mag, at * feed_cols, feed_cols, 1) for at in (core, 1 - core)]
+        )
+        if fast:
+            early, down_grad_mag = feed_pack(
+                place, feed_own, feed_partner, down_fold, *order(feed_products, mag_raw), feed_mags, feed_in, down_in,
+                down_products, down_mag_total, magnitude_down[None], aux[0], down_proj, rank_out_down,
+                share=1.0 / blocks,
+            )
+            return down_grad_mag, early
+        finished = [
+            finish_columns(weights, feed_products[half], mag_raw[half:4:2, :feed_cols], feed_mags[half])
+            for half, weights in enumerate((feed_own, feed_partner))
+        ]
         grad_mag, grad_out_part, grad_in_part = zip(*finished)
         columns = [
             jnp.concatenate([part.astype(bf16) for part in parts])
@@ -1349,21 +1574,15 @@
         if held is not None:
             passed = pass_down(passed, held)
         held = grad_kv
-    grad_queries, grad_kv = keys_back(0)
-    for down_mag_total in down_mag_steps:
-        pass
     if fast:
         out_far = links.split_swap(order(shares_out[3]), 2, 4)
         out_first = links.split_swap(order(shares_out[1]), 2, 4)
+    grad_queries, grad_kv = keys_back(0)
     out_grad_mag, out_out, out_in = output_adapter(
         order(grad_ordered), out_mag_raw, magnitude_output, o_weights, mixed, out_ext, out_in_t
     )
     mark(out_in)
     passed = pass_down(passed, held)
-    q_acc, q_in, q_out, q_grad_mag = query_back(
-        order(grad_queries), queries, q_weights, cosine, sine, normed, attn_in_t[0], magnitude_attention[:GROUP]
-    )
-    mark(q_in)
     if fast:
         out_far, out_first = settle(out_far, out_first)
         out_late = settle((shares_out[2].astype(f32) + out_far.astype(f32)).astype(bf16))
@@ -1371,14 +1590,19 @@
         out_parts = [shares_out[0], out_first, out_second]
     else:
         out_parts = [shares_out[0]] + [links.swap(shares_out[r], 2 * r) for r in range(1, chips)]
+    q_acc, q_in, q_out, q_grad_mag = query_back(
+        order(grad_queries), queries, q_weights, cosine, sine, normed, attn_in_t[0], magnitude_attention[:GROUP]
+    )
+    mark(q_in)
+    for down_mag_total in down_mag_steps:
+        pass
     down_grad_mag, early = pack_early(down_mag_total)
     early_steps = links.total(settle(early), order)
     next(early_steps)
-    out_parts = settle(*out_parts)
-    next(early_steps)
+    passed, *out_parts = settle(passed, *out_parts)
     next(early_steps)
     input_grad, kv_in, kv_out, kv_grad_mag = key_back(
-        heads, order(passed), grad_kv, kv_own, [weights for weights, _ in kv_made], cosine, sine, normed, rows_in,
+        heads, passed, grad_kv, kv_own, [weights for weights, _ in kv_made], cosine, sine, normed, rows_in,
         gain_attention, grad_residual, q_acc, attn_in_t[1:].reshape(2 * RANK, D), magnitude_attention[GROUP:],
     )
     mark(kv_in)
@@ -1399,36 +1623,37 @@
     )
     late_steps = links.total(settle(late), order)
     late = early = None
+    next(late_steps)
+    block_out = settle((residual + sum(part.astype(f32) for part in out_parts)).astype(bf16))[None]
+    while early is None:
+        early = next(early_steps)
+        if late is None:
+            late = next(late_steps)
+    early_shapes = ((2, RANK, D), (2, RANK, FF), (2, FF), (RANK, FF), (RANK, D))
+    feed_in, feed_out, feed_mag, down_in, down_out = unpack(
+        unpack_early_kernel, place, order(*early), early_shapes, "unpack_early"
+    )
+    mark(feed_mag)
     while late is None:
         late = next(late_steps)
-        if early is None:
-            early = next(early_steps)
-    while early is None:
-        early = next(early_steps)
-
-    block_out = (residual + sum(part.astype(f32) for part in out_parts)).astype(bf16)[None]
-    feed_full = jnp.concatenate([early[64 * (1 + i) : 64 * (2 + i)] for i in range(3)], axis=1)[:, :FF]
-    late_in, late_out = late[: 3 * RANK, :D], late[3 * RANK :, :D]
-    mid, side = late[:, D : 2 * D], late[:, 2 * D :]
+    late_shapes = ((3, RANK, D), (GROUP + 2, RANK, KVW), (GROUP + 2, KVW), (RANK, D), (GROUP, RANK, KVW), (GROUP, KVW))
+    attn_in, attn_out, attn_mag, out_in, out_out, out_mag = unpack(
+        unpack_late_kernel, place, order(*late), late_shapes, "unpack_late"
+    )
     return (
         block_out,
         input_grad[None],
-        late_in.reshape(3, RANK, D).transpose(0, 2, 1),
-        jnp.concatenate(
-            [
-                late_out.reshape(RANK, GROUP, KVW).transpose(1, 0, 2),
-                jnp.stack([side[:RANK], side[RANK : 2 * RANK]]),
-            ]
-        ),
-        side[2 * RANK : 2 * RANK + 6],
-        mid[:RANK].T,
-        mid[RANK : 2 * RANK].reshape(RANK, GROUP, KVW).transpose(1, 0, 2),
-        mid[2 * RANK].reshape(GROUP, KVW),
-        early[: 2 * RANK].reshape(2, RANK, D).transpose(0, 2, 1),
-        feed_full[: 2 * RANK].reshape(2, RANK, FF),
-        feed_full[3 * RANK : 3 * RANK + 2],
-        feed_full[2 * RANK : 3 * RANK].T,
-        early[2 * RANK : 3 * RANK],
+        attn_in.transpose(0, 2, 1),
+        attn_out,
+        attn_mag,
+        out_in.T,
+        out_out,
+        out_mag,
+        feed_in.transpose(0, 2, 1),
+        feed_out,
+        feed_mag,
+        down_in.T,
+        down_out,
         down_grad_mag[0],
     )
 

time: 564 us -> 520 us (0.922)
  local copies, waits for them, and re-layouts: 120 us -> 59.9 us
  waiting for transfers between devices: 82.2 us -> 120 us
  starting transfers between devices: 101 us -> 82.4 us
  other arithmetic: 45.3 us -> 30.8 us
  Pallas kernels: 189 us -> 201 us
    unnamed x402 -> x274, local copies, waits for them, and re-layouts: 87.2 us -> 40.8 us
    ppermute x35, waiting for transfers between devices: 47.5 us -> 85.4 us  [swap(): lax.ppermute(value, 'dp', [(i, i ^ bits) for i in range(self.devices)])]
    pallas_call x29 -> x28, Pallas kernels: 167 us -> 181 us  [kernel_call(): call(*[keep(value, spec) for value, spec in zip(operands, in_specs)])]
    ppermute x6, waiting for transfers between devices: 5.54 us -> 18.9 us  [row_shift(): return lax.ppermute(value, 'blk', pairs)]
    ppermute x8, waiting for transfers between devices: 25.1 us -> 13.3 us  [split_swap(): lax.ppermute(value, 'dp', [(i, i ^ (odd_bits if i % 2 else even_bits)) fo...]
    ppermute x35, starting transfers between devices: 55.3 us -> 45.3 us  [swap(): lax.ppermute(value, 'dp', [(i, i ^ bits) for i in range(self.devices)])]
    ppermute x6, starting transfers between devices: 20.4 us -> 13.1 us  [row_swap(): lax.ppermute(value, 'blk', [(i, i ^ bits) for i in range(self.blocks)])]
    slice x11 -> x0, local copies, waits for them, and re-layouts: 7.17 us -> none  [the longest x2 2.62 us: shards(): feed_mag_raw[half::2]]
  transfers between devices with their start and end apart: 58 -> 58, of which waited for: 20 -> 25; matrix products, arithmetic and copies ran while one was open for 12% -> 9% of each run, Pallas kernels for 28% -> 32%
where the time goes in v3:
time: 520 us; the launch traced here: 511 us
  Pallas kernels  201 us (39%)
  waiting for transfers between devices  120 us (23%)
  starting transfers between devices  82.4 us (16%)
  local copies, waits for them, and re-layouts  59.9 us (12%)
  other arithmetic  30.8 us (6%)
  between operations  16.2 us (3%)
    pallas_call x28, Pallas kernels, kernel_call(): call(*[keep(value, spec) for value, spec in zip(operands, in_specs)])  181 us
    ppermute x35, waiting for transfers between devices, swap(): lax.ppermute(value, 'dp', [(i, i ^ bits) for i in range(self.devices)])  85.4 us
    ppermute x35, starting transfers between devices, swap(): lax.ppermute(value, 'dp', [(i, i ^ bits) for i in range(self.devices)])  45.3 us
    unnamed x274, local copies, waits for them, and re-layouts  40.8 us
    ppermute x6, waiting for transfers between devices, row_shift(): return lax.ppermute(value, 'blk', pairs)  18.9 us
    ppermute x6, starting transfers between devices, row_shift(): return lax.ppermute(value, 'blk', pairs)  16.3 us
    ppermute x8, waiting for transfers between devices, split_swap(): lax.ppermute(value, 'dp', [(i, i ^ (odd_bits if i % 2 else even_bits)) fo...  13.3 us
    ppermute x6, starting transfers between devices, row_swap(): lax.ppermute(value, 'blk', [(i, i ^ bits) for i in range(self.blocks)])  13.1 us
  transfers between devices with their start and end apart: 58, of which 25 were waited for; matrix products, arithmetic and copies ran while one was open for 9% of the time, Pallas kernels for 32%

profile of v3, /device:TPU:1, one launch (start us, length us, event | category | flops | bytes accessed | tf_op | source)
XLA Modules:
  0.0 510.6 jit_solution(1217254888115623798)
XLA Ops:
  13.9 4.5 fold_q.1
  24.6 9.7 %collective-permute-done.first_ref = bf16[2,64,2176]{2,1,0:T(8,128)(2,1)} collective-permute-done((bf16[2,64,2176]{2,1,0:T(8,128)(2,1)S(1)}, bf16[2,64,2176]{2,1,0:T(8,128)(2,1)}, u32[]{:S(2)}, u32[]{:S(2)}) %collective-permute-start) | collective-permute-done | bytes 557088 | tf_op jit(solution)/shard_map/ppermute | solution.py:1184
  37.0 4.5 fold_o.1
  48.7 2.4 collective-permute-start.3
  54.3 12.4 %collective-permute-done.3.first_ref = bf16[2,64,2176]{2,1,0:T(8,128)(2,1)S(1)} collective-permute-done((bf16[2,64,2176]{2,1,0:T(8,128)(2,1)S(1)}, bf16[2,64,2176]{2,1,0:T(8,128)(2,1)S(1)}, u32[]{:S(2)}, u32[]{:S(2)}) %collective-permute-start.3) | collective-permute-done | bytes 557088 | tf_op jit(solution)/shard_map/ppermute | solution.py:1187
  66.7 7.1 %collective-permute-start.4 = (bf16[2,64,2176]{2,1,0:T(8,128)(2,1)S(1)}, bf16[2,64,2176]{2,1,0:T(8,128)(2,1)S(1)}, u32[]{:S(2)}, u32[]{:S(2)}) collective-permute-start(bf16[2,64,2176]{2,1,0:T(8,128)(2,1)S(1)} %collective-permute-done.3.first_ref), channel_id=1, source_target_pairs={{0,4},{4,0},{8,12},{12,8},{16,20},{20,16},{24,28},{28,24},{1,5},{5... | collective-permute-start | bytes 1671176 | tf_op jit(solution)/shard_map/ppermute | solution.py:1184
  76.7 2.2 head_kv.5
  85.4 3.1 collective-permute-start.7
  91.8 2.6 copy-done.21
  95.3 12.5 %fold_feed.1.own_ref.own_hbm = bf16[2,704,2176]{2,1,0:T(8,128)(2,1)} custom-call(bf16[2,704,2048]{2,1,0:T(8,128)(2,1)S(1)} %bitcast.73, bf16[2,16,2048]{2,1,0:T(8,128)(2,1)S(1)} %bitcast.74, bf16[2,16,704]{2,1,0:T(8,128)(2,1)S(1)} %copy-done.75, f32[2,1,704]{2,1,0:T(1,128)S(1)} %broadcast_in_dim.68.mag_ref), custom_call_target="tpu_custom_call" | custom-call | tf_op jit(solution)/shard_map/fold_feed/pallas_call | solution.py:60
  111.8 2.8 fold_down.1
  117.2 4.0 collective-permute-start.8
  121.2 10.3 %collective-permute-done.8.refs_2_.kv_ref = bf16[256,1024]{1,0:T(8,128)(2,1)} collective-permute-done((bf16[256,1024]{1,0:T(8,128)(2,1)S(1)}, bf16[256,1024]{1,0:T(8,128)(2,1)}, u32[]{:S(2)}, u32[]{:S(2)}) %collective-permute-start.8) | collective-permute-done | bytes 524320 | tf_op jit(solution)/shard_map/ppermute | solution.py:1196
  131.5 5.2 %collective-permute-start.9 = (bf16[256,1024]{1,0:T(8,128)(2,1)}, bf16[256,1024]{1,0:T(8,128)(2,1)}, u32[]{:S(2)}, u32[]{:S(2)}) collective-permute-start(bf16[256,1024]{1,0:T(8,128)(2,1)} %collective-permute-done.8.refs_2_.kv_ref), channel_id=1, source_target_pairs={{0,1},{1,2},{2,3},{4,5},{5,6},{6,7},{8,9},{9,10},{10,11},{12,13},{... | collective-permute-start | bytes 1572872 | tf_op jit(solution)/shard_map/ppermute | solution.py:1196
  137.3 6.0 %query_project.1.query_ref = bf16[256,2048]{1,0:T(8,128)(2,1)S(1)} custom-call(bf16[256,2048]{1,0:T(8,128)(2,1)S(1)} %fusion.2.input_ref.normed_ref, f32[256,128]{1,0:T(8,128)S(1)} %get-tuple-element.454.cos_ref, f32[256,128]{1,0:T(8,128)S(1)} %get-tuple-element.455.sin_ref, bf16[8,4,64,2176]{3,2,1,0:T(8,128)(2,1)} %bitcast.102), custom_call_target="tpu_custom_call" | custom-call | tf_op jit(solution)/shard_map/query_project/pallas_call | solution.py:60
  143.4 2.8 collective-permute-done.9.refs_3_.kv_ref
  146.1 5.2 %attend.1 = (bf16[256,2048]{1,0:T(8,128)(2,1)S(1)}, f32[4,1,1024]{2,1,0:T(1,128)S(1)}) custom-call(s32[2]{0:T(128)S(1)} %copy-done.103, bf16[256,2048]{1,0:T(8,128)(2,1)S(1)} %query_project.1.query_ref, bf16[256,1024]{1,0:T(8,128)(2,1)S(1)} %copy-done.23, bf16[256,1024]{1,0:T(8,128)(2,1)S(1)} %copy-done.36, ...), custom_call_target="tpu_custom_call" | custom-call | tf_op jit(solution)/shard_map/attend/pallas_call | solution.py:335
  154.5 2.7 collective-permute-start.13
  160.8 5.8 %output_project.1 = (f32[256,2048]{1,0:T(8,128)S(1)}, bf16[256,2048]{1,0:T(8,128)(2,1)S(1)}) custom-call(bf16[256,2048]{1,0:T(8,128)(2,1)S(1)} %copy-done.14, bf16[256,2048]{1,0:T(8,128)(2,1)S(1)} %bitcast.68, f32[1,2048]{1,0:T(1,128)S(1)} %bitcast.87, bf16[8,4,64,2176]{3,2,1,0:T(8,128)(2,1)} %bitcast.99), custom_call_target="tpu_custom_call" | custom-call | tf_op jit(solution)/shard_map/output_project/pallas_call | solution.py:60
  168.0 15.9 %collective-permute-done.12.refs_3_.refs_4_ = bf16[1440,256]{1,0:T(8,128)(2,1)} collective-permute-done((bf16[1440,256]{1,0:T(8,128)(2,1)}, bf16[1440,256]{1,0:T(8,128)(2,1)}, u32[]{:S(2)}, u32[]{:S(2)}) %collective-permute-start.12) | collective-permute-done | bytes 737312 | tf_op jit(solution)/shard_map/ppermute | solution.py:1184
  185.6 30.9 %collective-permute-done.14.refs_7_.refs_8_ = bf16[1440,256]{1,0:T(8,128)(2,1)} collective-permute-done((bf16[1440,256]{1,0:T(8,128)(2,1)}, bf16[1440,256]{1,0:T(8,128)(2,1)}, u32[]{:S(2)}, u32[]{:S(2)}) %collective-permute-start.14) | collective-permute-done | bytes 737312 | tf_op jit(solution)/shard_map/ppermute | solution.py:1184
  223.0 19.4 %feed_back.3 = (bf16[256,2048]{1,0:T(8,128)(2,1)}, bf16[256,2048]{1,0:T(8,128)(2,1)}, bf16[2,256,704]{2,1,0:T(8,128)(2,1)}, bf16[2,256,704]{2,1,0:T(8,128)(2,1)}...) custom-call(s32[3]{0:T(128)} %pad_add_fusion.1.place_ref, ...), custom_call_target="tpu_custom_call" | custom-call | tf_op jit(solution)/shard_map/feed_back/pallas_call | solution.py:60
  242.4 2.4 collective-permute-done.18
  247.4 10.6 %feed_forward.1 = (f32[2,512,704]{2,1,0:T(8,128)S(1)}, f32[2,512,704]{2,1,0:T(8,128)S(1)}) custom-call(bf16[512,2048]{1,0:T(8,128)(2,1)S(1)} %pad_maximum_fusion.normed_ref, bf16[2,704,2176]{2,1,0:T(8,128)(2,1)} %fold_feed.1.own_ref.own_hbm, bf16[2,704,2176]{2,1,0:T(8,128)(2,1)} %collective-permute-done.10.partner_ref.partner_hbm), custom_call_target="tpu_custom_call" | custom-call | tf_op jit(solution)/shard_map/feed_forward/pallas_call | solution.py:60
  259.8 4.3 feed_adapter.3
  266.8 19.1 %feed_back.4 = (bf16[256,2048]{1,0:T(8,128)(2,1)}, bf16[256,2048]{1,0:T(8,128)(2,1)}, bf16[2,256,704]{2,1,0:T(8,128)(2,1)}, bf16[2,256,704]{2,1,0:T(8,128)(2,1)}...) custom-call(s32[3]{0:T(128)} %pad_add_fusion.1.place_ref, ...), custom_call_target="tpu_custom_call" | custom-call | tf_op jit(solution)/shard_map/feed_back/pallas_call | solution.py:60
  286.9 28.1 %feed_back.5 = (bf16[256,2048]{1,0:T(8,128)(2,1)}, bf16[256,2048]{1,0:T(8,128)(2,1)}, bf16[256,2048]{1,0:T(8,128)(2,1)}, bf16[256,2048]{1,0:T(8,128)(2,1)}, bf16...) custom-call(s32[3]{0:T(128)} %pad_add_fusion.1.place_ref, ...), custom_call_target="tpu_custom_call" | custom-call | tf_op jit(solution)/shard_map/feed_back/pallas_call | solution.py:60
  321.0 5.1 feed_adapter.4
  326.8 5.1 feed_adapter.5
  334.6 7.6 %collective-permute-done.24 = f32[1,2048]{1,0:T(1,128)S(1)} collective-permute-done((f32[1,2048]{1,0:T(1,128)S(1)}, f32[1,2048]{1,0:T(1,128)S(1)}, u32[]{:S(2)}, u32[]{:S(2)}) %collective-permute-start.24) | collective-permute-done | bytes 8224 | tf_op jit(solution)/shard_map/ppermute | solution.py:1184
  342.6 2.2 collective-permute-done.26
  348.0 6.9 %residual_back.1 = (f32[256,2048]{1,0:T(8,128)S(1)}, bf16[256,2048]{1,0:T(8,128)(2,1)S(1)}, f32[1,2048]{1,0:T(1,128)S(1)}, bf16[256,128]{1,0:T(8,128)(2,1)S(1)},...) custom-call(bf16[256,2048]{1,0:T(8,128)(2,1)S(1)} %copy-done.55, ...), custom_call_target="tpu_custom_call" | custom-call | tf_op jit(solution)/shard_map/residual_back/pallas_call | solution.py:60
  355.0 3.0 attend_back_3.1
  359.3 2.8 attend_back_2.1
  364.9 5.9 %collective-permute-done.28 = bf16[256,1024]{1,0:T(8,128)(2,1)S(1)} collective-permute-done((bf16[256,1024]{1,0:T(8,128)(2,1)S(1)}, bf16[256,1024]{1,0:T(8,128)(2,1)S(1)}, u32[]{:S(2)}, u32[]{:S(2)}) %collective-permute-start.28) | collective-permute-done | bytes 524320 | tf_op jit(solution)/shard_map/ppermute | solution.py:1196
  382.4 4.9 attend_back_0.1
  387.4 6.7 %output_adapter.1 = (f32[1,2048]{1,0:T(1,128)S(1)}, f32[16,2048]{1,0:T(8,128)S(1)}, f32[16,2048]{1,0:T(8,128)S(1)}) custom-call(bf16[256,2048]{1,0:T(8,128)(2,1)S(1)} %copy-done.54, f32[1,2048]{1,0:T(1,128)S(1)} %copy-done.109, f32[4,512]{1,0:T(4,128)S(1)} %copy-done.106, bf16[256,2048]{1,0:T(8,128)(2,1)S(1)} %copy-done.16, bf16[256,128]{1,0:T(8,128)(2,1)S(1)} %copy-done.94, ...), custom_call_target="tpu_custom_call" | custom-call | tf_op jit(solution)/shard_map/output_adapter/pallas_call | solution.py:60
  394.2 2.1 add_convert_fusion.4
  397.3 2.6 add_convert_fusion.1
  401.4 5.6 %collective-permute-start.34 = (f32[1,2048]{1,0:T(1,128)S(1)}, f32[1,2048]{1,0:T(1,128)S(1)}, u32[]{:S(2)}, u32[]{:S(2)}) collective-permute-start(f32[1,2048]{1,0:T(1,128)S(1)} %copy-done.132), channel_id=1, source_target_pairs={{0,2},{1,3},{2,0},{3,1},{4,6},{5,7},{6,4},{7,5},{8,10},{9,11},{10,... | collective-permute-start | bytes 24584 | tf_op jit(solution)/shard_map/ppermute | solution.py:1192
  410.0 7.5 %query_back.1 = (f32[256,2176]{1,0:T(8,128)S(1)}, f32[16,2048]{1,0:T(8,128)S(1)}, f32[16,2048]{1,0:T(8,128)S(1)}, f32[1,2048]{1,0:T(1,128)S(1)}) custom-call(f32[256,2048]{1,0:T(8,128)S(1)} %copy-done.5, bf16[256,2048]{1,0:T(8,128)(2,1)S(1)} %query_project.1.query_ref, f32[256,128]{1,0:T(8,128)S(1)} %get-tuple-element.454.cos_ref, ...), custom_call_target="tpu_custom_call" | custom-call | tf_op jit(solution)/shard_map/query_back/pallas_call | solution.py:60
  418.3 7.1 %feed_pack.1 = (bf16[256,2048]{1,0:T(8,128)(2,1)S(1)}, f32[1,2048]{1,0:T(1,128)}) custom-call(s32[3]{0:T(128)S(1)} %copy-done.86, bf16[2,704,2176]{2,1,0:T(8,128)(2,1)} %fold_feed.1.own_ref.own_hbm, bf16[2,704,2176]{2,1,0:T(8,128)(2,1)} %collective-permute-done.10.partner_ref.partner_hbm, bf16[4,1440,256]{2,1,0:T(8,128)(2,1)} %copy-done.11, ...), custom_call_target="tpu_custom_call" | custom-call | tf_op jit(solution)/shard_map/feed_pack/pallas_call | solution.py:60
  429.9 2.7 collective-permute-start.36
  433.9 8.2 %key_back.1 = (bf16[256,2048]{1,0:T(8,128)(2,1)}, f32[32,2048]{1,0:T(8,128)S(1)}, f32[16,1024]{1,0:T(8,128)S(1)}, f32[1,1024]{1,0:T(1,128)S(1)}) custom-call(s32[4]{0:T(128)S(1)} %copy-done.111, bf16[256,1024]{1,0:T(8,128)(2,1)} %collective-permute-done.30.sent_ref, f32[256,1024]{1,0:T(8,128)S(1)} %copy-done.52, bf16[256,1024]{1,0:T(8,128)(2,1)S(1)} %copy-done.25, ...), custom_call_target="tpu_custom_call" | custom-call | tf_op jit(solution)/shard_map/key_back/pallas_call | solution.py:60
  453.7 3.5 add_convert_fusion
  458.5 2.4 collective-permute-start.43
  467.5 2.3 collective-permute-start.45
  483.8 4.7 collective-permute-start.54
  (459 shorter events, 159.1 us)
Async XLA Ops:
  7.2 130.1 %all-gather.7.cloned.1.call-start = ((), (), s32[]{:S(2)}) async-start(), calls=%async_computation | async-start | bytes 10027008 | tf_op jit(solution)/shard_map/all_gather | solution.py:1362
  18.5 140.5 %all-gather.9.cloned.1.call-start = ((), (), s32[]{:S(2)}) async-start(), calls=%async_computation.1 | async-start | bytes 10027008 | tf_op jit(solution)/shard_map/all_gather | solution.py:1362
  18.5 15.9 %collective-permute-start = (bf16[2,64,2176]{2,1,0:T(8,128)(2,1)S(1)}, bf16[2,64,2176]{2,1,0:T(8,128)(2,1)}, u32[]{:S(2)}, u32[]{:S(2)}) collective-permute-start(bf16[2,64,2176]{2,1,0:T(8,128)(2,1)S(1)} %fold_kv.1.first_ref), channel_id=1, source_target_pairs={{0,8},{4,12},{8,0},{12,4},{16,24},{20,28},{24,16},{28,20},{1,9},{5... | collective-permute-start | bytes 1671176 | tf_op jit(solution)/shard_map/ppermute | solution.py:1184
  20.6 15.1 %collective-permute-start.1 = (bf16[2,64,2176]{2,1,0:T(8,128)(2,1)S(1)}, bf16[2,64,2176]{2,1,0:T(8,128)(2,1)S(1)}, u32[]{:S(2)}, u32[]{:S(2)}) collective-permute-start(bf16[2,64,2176]{2,1,0:T(8,128)(2,1)S(1)} %fold_kv.1.first_ref), channel_id=1, source_target_pairs={{0,16},{4,20},{8,24},{12,28},{16,0},{20,4},{24,8},{28,12},{1,17},{... | collective-permute-start | bytes 1671176 | tf_op jit(solution)/shard_map/ppermute | solution.py:1184
  21.9 13.8 %collective-permute-start.2 = (bf16[2,64,2176]{2,1,0:T(8,128)(2,1)S(1)}, bf16[2,64,2176]{2,1,0:T(8,128)(2,1)S(1)}, u32[]{:S(2)}, u32[]{:S(2)}) collective-permute-start(bf16[2,64,2176]{2,1,0:T(8,128)(2,1)S(1)} %fold_kv.1.first_ref), channel_id=1, source_target_pairs={{0,4},{4,0},{8,12},{12,8},{16,20},{20,16},{24,28},{28,24},{1,5},{5... | collective-permute-start | bytes 1671176 | tf_op jit(solution)/shard_map/ppermute | solution.py:1184
  41.4 225.3 %all-gather.11.cloned.1.call-start = ((), (), s32[]{:S(2)}) async-start(), calls=%async_computation.2 | async-start | bytes 9437184 | tf_op jit(solution)/shard_map/all_gather | solution.py:1362
  48.7 17.9 %collective-permute-start.3 = (bf16[2,64,2176]{2,1,0:T(8,128)(2,1)S(1)}, bf16[2,64,2176]{2,1,0:T(8,128)(2,1)S(1)}, u32[]{:S(2)}, u32[]{:S(2)}) collective-permute-start(bf16[2,64,2176]{2,1,0:T(8,128)(2,1)S(1)} %broadcast_select_fusion.2), channel_id=1, source_target_pairs={{0,8},{4,20},{8,0},{12,28},{16,24},{20,4},{24,16},{28,12},{1,9},{5... | collective-permute-start | bytes 1671176 | tf_op jit(solution)/shard_map/ppermute | solution.py:1187
  52.3 24.5 %collective-permute-start.5 = (bf16[2,64,2176]{2,1,0:T(8,128)(2,1)}, bf16[2,64,2176]{2,1,0:T(8,128)(2,1)S(1)}, u32[]{:S(2)}, u32[]{:S(2)}) collective-permute-start(bf16[2,64,2176]{2,1,0:T(8,128)(2,1)} %collective-permute-done.first_ref), channel_id=1, source_target_pairs={{0,4},{4,0},{8,12},{12,8},{16,20},{20,16},{24,28},{28,24},{1,5},{5... | collective-permute-start | bytes 1671176 | tf_op jit(solution)/shard_map/ppermute | solution.py:1184
  53.9 22.8 %collective-permute-start.6 = (bf16[2,64,2176]{2,1,0:T(8,128)(2,1)S(1)}, bf16[2,64,2176]{2,1,0:T(8,128)(2,1)S(1)}, u32[]{:S(2)}, u32[]{:S(2)}) collective-permute-start(bf16[2,64,2176]{2,1,0:T(8,128)(2,1)S(1)} %collective-permute-done.1.first_ref), channel_id=1, source_target_pairs={{0,4},{4,0},{8,12},{12,8},{16,20},{20,16},{24,28},{28,24},{1,5},{5... | collective-permute-start | bytes 1671176 | tf_op jit(solution)/shard_map/ppermute | solution.py:1184
  66.7 16.0 %collective-permute-start.4 = (bf16[2,64,2176]{2,1,0:T(8,128)(2,1)S(1)}, bf16[2,64,2176]{2,1,0:T(8,128)(2,1)S(1)}, u32[]{:S(2)}, u32[]{:S(2)}) collective-permute-start(bf16[2,64,2176]{2,1,0:T(8,128)(2,1)S(1)} %collective-permute-done.3.first_ref), channel_id=1, source_target_pairs={{0,4},{4,0},{8,12},{12,8},{16,20},{20,16},{24,28},{28,24},{1,5},{5... | collective-permute-start | bytes 1671176 | tf_op jit(solution)/shard_map/ppermute | solution.py:1184
  85.4 23.5 %collective-permute-start.7 = (bf16[256,1024]{1,0:T(8,128)(2,1)S(1)}, bf16[256,1024]{1,0:T(8,128)(2,1)S(1)}, u32[]{:S(2)}, u32[]{:S(2)}) collective-permute-start(bf16[256,1024]{1,0:T(8,128)(2,1)S(1)} %get-tuple-element.245.refs_0_.kv_ref), channel_id=1, source_target_pairs={{0,1},{1,2},{2,3},{4,5},{5,6},{6,7},{8,9},{9,10},{10,11},{12,13},{... | collective-permute-start | bytes 1572872 | tf_op jit(solution)/shard_map/ppermute | solution.py:1196
  117.2 14.2 %collective-permute-start.8 = (bf16[256,1024]{1,0:T(8,128)(2,1)S(1)}, bf16[256,1024]{1,0:T(8,128)(2,1)}, u32[]{:S(2)}, u32[]{:S(2)}) collective-permute-start(bf16[256,1024]{1,0:T(8,128)(2,1)S(1)} %collective-permute-done.7.refs_1_.kv_ref), channel_id=1, source_target_pairs={{0,1},{1,2},{2,3},{4,5},{5,6},{6,7},{8,9},{9,10},{10,11},{12,13},{... | collective-permute-start | bytes 1572872 | tf_op jit(solution)/shard_map/ppermute | solution.py:1196
  131.5 14.7 %collective-permute-start.9 = (bf16[256,1024]{1,0:T(8,128)(2,1)}, bf16[256,1024]{1,0:T(8,128)(2,1)}, u32[]{:S(2)}, u32[]{:S(2)}) collective-permute-start(bf16[256,1024]{1,0:T(8,128)(2,1)} %collective-permute-done.8.refs_2_.kv_ref), channel_id=1, source_target_pairs={{0,1},{1,2},{2,3},{4,5},{5,6},{6,7},{8,9},{9,10},{10,11},{12,13},{... | collective-permute-start | bytes 1572872 | tf_op jit(solution)/shard_map/ppermute | solution.py:1196
  152.3 69.8 %collective-permute-start.10 = (bf16[2,704,2176]{2,1,0:T(8,128)(2,1)}, bf16[2,704,2176]{2,1,0:T(8,128)(2,1)}, u32[]{:S(2)}, u32[]{:S(2)}) collective-permute-start(bf16[2,704,2176]{2,1,0:T(8,128)(2,1)} %fold_feed.1.own_ref.own_hbm), channel_id=1, source_target_pairs={{0,4},{4,0},{8,12},{12,8},{16,20},{20,16},{24,28},{28,24},{1,5},{5... | collective-permute-start | bytes 18382856 | tf_op jit(solution)/shard_map/ppermute | solution.py:1184
  154.3 29.7 %collective-permute-start.12 = (bf16[1440,256]{1,0:T(8,128)(2,1)}, bf16[1440,256]{1,0:T(8,128)(2,1)}, u32[]{:S(2)}, u32[]{:S(2)}) collective-permute-start(bf16[1440,256]{1,0:T(8,128)(2,1)} %get-tuple-element.263), channel_id=1, source_target_pairs={{0,8},{4,12},{8,0},{12,4},{16,24},{20,28},{24,16},{28,20},{1,9},{5... | collective-permute-start | bytes 2211848 | tf_op jit(solution)/shard_map/ppermute | solution.py:1184
  154.5 31.1 %collective-permute-start.13 = (bf16[1440,256]{1,0:T(8,128)(2,1)}, bf16[1440,256]{1,0:T(8,128)(2,1)}, u32[]{:S(2)}, u32[]{:S(2)}) collective-permute-start(bf16[1440,256]{1,0:T(8,128)(2,1)} %get-tuple-element.264), channel_id=1, source_target_pairs={{0,16},{4,20},{8,24},{12,28},{16,0},{20,4},{24,8},{28,12},{1,17},{... | collective-permute-start | bytes 2211848 | tf_op jit(solution)/shard_map/ppermute | solution.py:1184
  157.2 59.4 %collective-permute-start.14 = (bf16[1440,256]{1,0:T(8,128)(2,1)}, bf16[1440,256]{1,0:T(8,128)(2,1)}, u32[]{:S(2)}, u32[]{:S(2)}) collective-permute-start(bf16[1440,256]{1,0:T(8,128)(2,1)} %get-tuple-element.265), channel_id=1, source_target_pairs={{0,24},{4,28},{8,16},{12,20},{16,8},{20,12},{24,0},{28,4},{1,25},{... | collective-permute-start | bytes 2211848 | tf_op jit(solution)/shard_map/ppermute | solution.py:1184
  158.3 59.2 %collective-permute-start.11 = (bf16[1440,256]{1,0:T(8,128)(2,1)}, bf16[1440,256]{1,0:T(8,128)(2,1)}, u32[]{:S(2)}, u32[]{:S(2)}) collective-permute-start(bf16[1440,256]{1,0:T(8,128)(2,1)} %get-tuple-element.269.refs_1_.refs_2_), channel_id=1, source_target_pairs={{0,4},{4,0},{8,12},{12,8},{16,20},{20,16},{24,28},{28,24},{1,5},{5... | collective-permute-start | bytes 2211848 | tf_op jit(solution)/shard_map/ppermute | solution.py:1184
  217.4 27.5 %collective-permute-start.18 = (bf16[256,2048]{1,0:T(8,128)(2,1)S(1)}, bf16[256,2048]{1,0:T(8,128)(2,1)S(1)}, u32[]{:S(2)}, u32[]{:S(2)}) collective-permute-start(bf16[256,2048]{1,0:T(8,128)(2,1)S(1)} %get-tuple-element.288.refs_0_.normed_ref), channel_id=1, source_target_pairs={{0,8},{4,12},{8,0},{12,4},{16,24},{20,28},{24,16},{28,20},{1,9},{5... | collective-permute-start | bytes 3145736 | tf_op jit(solution)/shard_map/ppermute | solution.py:1184
  217.6 28.9 %collective-permute-start.19 = (bf16[256,2048]{1,0:T(8,128)(2,1)S(1)}, bf16[256,2048]{1,0:T(8,128)(2,1)S(1)}, u32[]{:S(2)}, u32[]{:S(2)}) collective-permute-start(bf16[256,2048]{1,0:T(8,128)(2,1)S(1)} %get-tuple-element.288.refs_0_.normed_ref), channel_id=1, source_target_pairs={{0,16},{4,20},{8,24},{12,28},{16,0},{20,4},{24,8},{28,12},{1,17},{... | collective-permute-start | bytes 3145736 | tf_op jit(solution)/shard_map/ppermute | solution.py:1184
  246.6 20.1 %collective-permute-start.20 = (bf16[256,2048]{1,0:T(8,128)(2,1)S(1)}, bf16[256,2048]{1,0:T(8,128)(2,1)}, u32[]{:S(2)}, u32[]{:S(2)}) collective-permute-start(bf16[256,2048]{1,0:T(8,128)(2,1)S(1)} %broadcast_select_fusion.1), channel_id=1, source_target_pairs={{0,8},{4,20},{8,0},{12,28},{16,24},{20,4},{24,16},{28,12},{1,9},{5... | collective-permute-start | bytes 3145736 | tf_op jit(solution)/shard_map/ppermute | solution.py:1187
  285.8 29.8 %collective-permute-start.23 = (bf16[256,2048]{1,0:T(8,128)(2,1)}, bf16[256,2048]{1,0:T(8,128)(2,1)S(1)}, u32[]{:S(2)}, u32[]{:S(2)}) collective-permute-start(bf16[256,2048]{1,0:T(8,128)(2,1)} %get-tuple-element.297), channel_id=1, source_target_pairs={{0,8},{4,20},{8,0},{12,28},{16,24},{20,4},{24,16},{28,12},{1,9},{5... | collective-permute-start | bytes 3145736 | tf_op jit(solution)/shard_map/ppermute | solution.py:1187
  315.1 27.5 %collective-permute-start.21 = (bf16[256,2048]{1,0:T(8,128)(2,1)}, bf16[256,2048]{1,0:T(8,128)(2,1)S(1)}, u32[]{:S(2)}, u32[]{:S(2)}) collective-permute-start(bf16[256,2048]{1,0:T(8,128)(2,1)} %get-tuple-element.300), channel_id=1, source_target_pairs={{0,8},{4,20},{8,0},{12,28},{16,24},{20,4},{24,16},{28,12},{1,9},{5... | collective-permute-start | bytes 3145736 | tf_op jit(solution)/shard_map/ppermute | solution.py:1187
  317.6 30.3 %collective-permute-start.25 = (bf16[256,2048]{1,0:T(8,128)(2,1)S(1)}, bf16[256,2048]{1,0:T(8,128)(2,1)S(1)}, u32[]{:S(2)}, u32[]{:S(2)}) collective-permute-start(bf16[256,2048]{1,0:T(8,128)(2,1)S(1)} %add_convert_fusion.2), channel_id=1, source_target_pairs={{0,16},{4,12},{8,24},{12,4},{16,0},{20,28},{24,8},{28,20},{1,17},{... | collective-permute-start | bytes 3145736 | tf_op jit(solution)/shard_map/ppermute | solution.py:1187
  319.4 6.7 %collective-permute-start.22 = (f32[1,2048]{1,0:T(1,128)S(1)}, f32[1,2048]{1,0:T(1,128)S(1)}, u32[]{:S(2)}, u32[]{:S(2)}) collective-permute-start(f32[1,2048]{1,0:T(1,128)S(1)} %slice_add_fusion), channel_id=1, source_target_pairs={{0,4},{4,0},{8,12},{12,8},{16,20},{20,16},{24,28},{28,24},{1,5},{5... | collective-permute-start | bytes 24584 | tf_op jit(solution)/shard_map/ppermute | solution.py:1184
  326.1 16.1 %collective-permute-start.24 = (f32[1,2048]{1,0:T(1,128)S(1)}, f32[1,2048]{1,0:T(1,128)S(1)}, u32[]{:S(2)}, u32[]{:S(2)}) collective-permute-start(f32[1,2048]{1,0:T(1,128)S(1)} %add.189), channel_id=1, source_target_pairs={{0,8},{4,12},{8,0},{12,4},{16,24},{20,28},{24,16},{28,20},{1,9},{5... | collective-permute-start | bytes 24584 | tf_op jit(solution)/shard_map/ppermute | solution.py:1184
  358.0 12.8 %collective-permute-start.28 = (bf16[256,1024]{1,0:T(8,128)(2,1)S(1)}, bf16[256,1024]{1,0:T(8,128)(2,1)S(1)}, u32[]{:S(2)}, u32[]{:S(2)}) collective-permute-start(bf16[256,1024]{1,0:T(8,128)(2,1)S(1)} %get-tuple-element.336), channel_id=1, source_target_pairs={{1,0},{2,1},{3,2},{5,4},{6,5},{7,6},{9,8},{10,9},{11,10},{13,12},{... | collective-permute-start | bytes 1572872 | tf_op jit(solution)/shard_map/ppermute | solution.py:1196
  371.8 24.6 %collective-permute-start.31 = (bf16[256,2048]{1,0:T(8,128)(2,1)}, bf16[256,2048]{1,0:T(8,128)(2,1)}, u32[]{:S(2)}, u32[]{:S(2)}) collective-permute-start(bf16[256,2048]{1,0:T(8,128)(2,1)} %get-tuple-element.357), channel_id=1, source_target_pairs={{0,8},{4,20},{8,0},{12,28},{16,24},{20,4},{24,16},{28,12},{1,9},{5... | collective-permute-start | bytes 3145736 | tf_op jit(solution)/shard_map/ppermute | solution.py:1187
  372.5 24.7 %collective-permute-start.32 = (bf16[256,2048]{1,0:T(8,128)(2,1)}, bf16[256,2048]{1,0:T(8,128)(2,1)}, u32[]{:S(2)}, u32[]{:S(2)}) collective-permute-start(bf16[256,2048]{1,0:T(8,128)(2,1)} %get-tuple-element.359), channel_id=1, source_target_pairs={{0,8},{4,20},{8,0},{12,28},{16,24},{20,4},{24,16},{28,12},{1,9},{5... | collective-permute-start | bytes 3145736 | tf_op jit(solution)/shard_map/ppermute | solution.py:1187
  373.2 20.9 %collective-permute-start.29 = (bf16[256,1024]{1,0:T(8,128)(2,1)}, bf16[256,1024]{1,0:T(8,128)(2,1)}, u32[]{:S(2)}, u32[]{:S(2)}) collective-permute-start(bf16[256,1024]{1,0:T(8,128)(2,1)} %add_convert_fusion.5), channel_id=1, source_target_pairs={{1,0},{2,1},{3,2},{5,4},{6,5},{7,6},{9,8},{10,9},{11,10},{13,12},{... | collective-permute-start | bytes 1572872 | tf_op jit(solution)/shard_map/ppermute | solution.py:1196
  399.9 32.8 %collective-permute-start.33 = (bf16[256,2048]{1,0:T(8,128)(2,1)}, bf16[256,2048]{1,0:T(8,128)(2,1)}, u32[]{:S(2)}, u32[]{:S(2)}) collective-permute-start(bf16[256,2048]{1,0:T(8,128)(2,1)} %add_convert_fusion.1), channel_id=1, source_target_pairs={{0,16},{4,12},{8,24},{12,4},{16,0},{20,28},{24,8},{28,20},{1,17},{... | collective-permute-start | bytes 3145736 | tf_op jit(solution)/shard_map/ppermute | solution.py:1187
  401.4 16.7 %collective-permute-start.34 = (f32[1,2048]{1,0:T(1,128)S(1)}, f32[1,2048]{1,0:T(1,128)S(1)}, u32[]{:S(2)}, u32[]{:S(2)}) collective-permute-start(f32[1,2048]{1,0:T(1,128)S(1)} %copy-done.132), channel_id=1, source_target_pairs={{0,2},{1,3},{2,0},{3,1},{4,6},{5,7},{6,4},{7,5},{8,10},{9,11},{10,... | collective-permute-start | bytes 24584 | tf_op jit(solution)/shard_map/ppermute | solution.py:1192
  407.1 25.6 %collective-permute-start.30 = (bf16[256,1024]{1,0:T(8,128)(2,1)}, bf16[256,1024]{1,0:T(8,128)(2,1)}, u32[]{:S(2)}, u32[]{:S(2)}) collective-permute-start(bf16[256,1024]{1,0:T(8,128)(2,1)} %add_convert_fusion.4), channel_id=1, source_target_pairs={{1,0},{2,1},{3,2},{5,4},{6,5},{7,6},{9,8},{10,9},{11,10},{13,12},{... | collective-permute-start | bytes 1572872 | tf_op jit(solution)/shard_map/ppermute | solution.py:1196
  429.9 17.2 %collective-permute-start.36 = (bf16[256,1024]{1,0:T(8,128)(2,1)}, bf16[256,1024]{1,0:T(8,128)(2,1)}, u32[]{:S(2)}, u32[]{:S(2)}) collective-permute-start(bf16[256,1024]{1,0:T(8,128)(2,1)} %constant_dynamic-slice_fusion.1), channel_id=1, source_target_pairs={{0,4},{4,0},{8,12},{12,8},{16,20},{20,16},{24,28},{28,24},{1,5},{5... | collective-permute-start | bytes 1572872 | tf_op jit(solution)/shard_map/ppermute | solution.py:1184
  447.1 13.8 %collective-permute-start.35 = (bf16[64,2304]{1,0:T(8,128)(2,1)}, bf16[64,2304]{1,0:T(8,128)(2,1)}, u32[]{:S(2)}, u32[]{:S(2)}) collective-permute-start(bf16[64,2304]{1,0:T(8,128)(2,1)} %constant_dynamic-slice_fusion.2), channel_id=1, source_target_pairs={{0,4},{4,0},{8,12},{12,8},{16,20},{20,16},{24,28},{28,24},{1,5},{5... | collective-permute-start | bytes 884744 | tf_op jit(solution)/shard_map/ppermute | solution.py:1184
  451.0 6.1 %collective-permute-start.37 = (bf16[64,1024]{1,0:T(8,128)(2,1)}, bf16[64,1024]{1,0:T(8,128)(2,1)S(1)}, u32[]{:S(2)}, u32[]{:S(2)}) collective-permute-start(bf16[64,1024]{1,0:T(8,128)(2,1)} %get-tuple-element.399), channel_id=1, source_target_pairs={{0,8},{4,12},{8,0},{12,4},{16,24},{20,28},{24,16},{28,20},{1,9},{5... | collective-permute-start | bytes 393224 | tf_op jit(solution)/shard_map/ppermute | solution.py:1184
  451.8 5.3 %collective-permute-start.38 = (bf16[64,1024]{1,0:T(8,128)(2,1)}, bf16[64,1024]{1,0:T(8,128)(2,1)S(1)}, u32[]{:S(2)}, u32[]{:S(2)}) collective-permute-start(bf16[64,1024]{1,0:T(8,128)(2,1)} %get-tuple-element.400), channel_id=1, source_target_pairs={{0,16},{4,20},{8,24},{12,28},{16,0},{20,4},{24,8},{28,12},{1,17},{... | collective-permute-start | bytes 393224 | tf_op jit(solution)/shard_map/ppermute | solution.py:1184
  453.0 5.5 %collective-permute-start.39 = (bf16[64,1024]{1,0:T(8,128)(2,1)}, bf16[64,1024]{1,0:T(8,128)(2,1)S(1)}, u32[]{:S(2)}, u32[]{:S(2)}) collective-permute-start(bf16[64,1024]{1,0:T(8,128)(2,1)} %get-tuple-element.401), channel_id=1, source_target_pairs={{0,24},{4,28},{8,16},{12,20},{16,8},{20,12},{24,0},{28,4},{1,25},{... | collective-permute-start | bytes 393224 | tf_op jit(solution)/shard_map/ppermute | solution.py:1184
  458.5 8.9 %collective-permute-start.43 = (bf16[64,1024]{1,0:T(8,128)(2,1)S(1)}, bf16[64,1024]{1,0:T(8,128)(2,1)S(1)}, u32[]{:S(2)}, u32[]{:S(2)}) collective-permute-start(bf16[64,1024]{1,0:T(8,128)(2,1)S(1)} %add_convert_fusion.9), channel_id=1, source_target_pairs={{0,1},{1,0},{2,3},{3,2},{4,5},{5,4},{6,7},{7,6},{8,9},{9,8},{10,11... | collective-permute-start | bytes 393224 | tf_op jit(solution)/shard_map/ppermute | solution.py:1192
  464.4 5.4 %collective-permute-start.40 = (bf16[16,2304]{1,0:T(8,128)(2,1)}, bf16[16,2304]{1,0:T(8,128)(2,1)S(1)}, u32[]{:S(2)}, u32[]{:S(2)}) collective-permute-start(bf16[16,2304]{1,0:T(8,128)(2,1)} %get-tuple-element.407), channel_id=1, source_target_pairs={{0,8},{4,12},{8,0},{12,4},{16,24},{20,28},{24,16},{28,20},{1,9},{5... | collective-permute-start | bytes 221192 | tf_op jit(solution)/shard_map/ppermute | solution.py:1184
  466.9 4.6 collective-permute-start.42
  467.5 6.5 %collective-permute-start.45 = (bf16[64,1024]{1,0:T(8,128)(2,1)S(1)}, bf16[64,1024]{1,0:T(8,128)(2,1)S(1)}, u32[]{:S(2)}, u32[]{:S(2)}) collective-permute-start(bf16[64,1024]{1,0:T(8,128)(2,1)S(1)} %add_convert_fusion.8), channel_id=1, source_target_pairs={{0,2},{1,3},{2,0},{3,1},{4,6},{5,7},{6,4},{7,5},{8,10},{9,11},{10,... | collective-permute-start | bytes 393224 | tf_op jit(solution)/shard_map/ppermute | solution.py:1192
  472.5 5.0 collective-permute-start.44
  474.0 4.7 collective-permute-start.47
  476.4 4.9 collective-permute-start.49
  477.5 11.0 %collective-permute-start.46 = (bf16[16,2304]{1,0:T(8,128)(2,1)S(1)}, bf16[16,2304]{1,0:T(8,128)(2,1)S(1)}, u32[]{:S(2)}, u32[]{:S(2)}) collective-permute-start(bf16[16,2304]{1,0:T(8,128)(2,1)S(1)} %add_convert_fusion.11), channel_id=1, source_target_pairs={{0,2},{1,3},{2,0},{3,1},{4,6},{5,7},{6,4},{7,5},{8,10},{9,11},{10,... | collective-permute-start | bytes 221192 | tf_op jit(solution)/shard_map/ppermute | solution.py:1192
  483.8 14.8 %collective-permute-start.54 = (bf16[256,1024]{1,0:T(8,128)(2,1)}, bf16[256,1024]{1,0:T(8,128)(2,1)S(1)}, u32[]{:S(2)}, u32[]{:S(2)}) collective-permute-start(bf16[256,1024]{1,0:T(8,128)(2,1)} %join_rows.2.mine_ref), channel_id=1, source_target_pairs={{0,4},{4,0},{8,12},{12,8},{16,20},{20,16},{24,28},{28,24},{1,5},{5... | collective-permute-start | bytes 1572872 | tf_op jit(solution)/shard_map/ppermute | solution.py:1184
  496.9 4.5 collective-permute-start.53
  (147 other events, 1131.6 us)
Sparse Core Ops, SparseCore 0:
  18.6 68.2 all-gather.6
  88.7 56.6 all-gather.8
  147.8 82.3 all-gather.10

commit v4 on v3

--- a/solution.py
+++ b/solution.py
@@ -516,10 +516,20 @@
     )(normed, own, partner)
 
 
+NEAR = ("first", "last")
+
+
+def near_turn(place_ref, r):
+    return place_ref[0] ^ NEAR.index(r)
+
+
 def grad_copies(copies, place_ref, grad_hbm, grad_ref, chips, block):
     return [
         copies(
-            grad_hbm.at[0 if r is None else place_ref[1] ^ (2 * r)], grad_ref.at[pl.ds(turn * block, block), :]
+            grad_hbm.at[
+                0 if r is None else place_ref[2] ^ (1 + near_turn(place_ref, r) if r in NEAR else r)
+            ],
+            grad_ref.at[pl.ds(turn * block, block), :]
         )
         for turn, r in enumerate(chips)
     ]
@@ -544,8 +554,9 @@
         lanes = pl.ds(pl.multiple_of((place_ref[1] ^ i) * width, width), width)
         fetches.append(copies(ref, down_weight_ref.at[:, lanes]))
     if not fused:
-        fetches.append(copies(kept[0], value_ref.at[0]))
-        fetches.append(copies(kept[1], value_ref.at[1]))
+        start = pl.multiple_of(near_turn(place_ref, chips[0]) * block, block)
+        for at in range(2):
+            fetches.append(copies(kept[at].at[:, pl.ds(start, block), :], value_ref.at[at]))
     weight_fetches = [copies(ref, weight_ref.at[half]) for half, ref in enumerate((own_ref, partner_ref))]
     if fused:
         weight_fetches[0].start()
@@ -642,12 +653,14 @@
 
 
 def feed_adapter_kernel(
-    place_ref, normed_ref, grad_hbm, hidden_hbm, grad_gate_hbm, grad_up_hbm, ext_ref, rank_in_ref, down_in_ref, *refs,
+    place_ref, normed_hbm, grad_hbm, hidden_hbm, grad_gate_hbm, grad_up_hbm, ext_ref, rank_in_ref, down_in_ref, *refs,
     chips, block, before,
 ):
     before_refs, refs = refs[: 4 * before], refs[4 * before :]
-    in_ref, out_ref, down_rank_in_ref, down_out_ref, grad_ref, made_ref, semaphores = refs
+    in_ref, out_ref, down_rank_in_ref, down_out_ref, grad_ref, normed_ref, made_ref, semaphores = refs
     copies = Copies(semaphores)
+    start = near_turn(place_ref, chips[0]) * block if chips[0] in NEAR else 0
+    normed_fetch = copies.started(normed_hbm.at[pl.ds(pl.multiple_of(start, block), block), :], normed_ref)
     fetches = [
         copies.started(ref, made_ref.at[at]) for at, ref in enumerate((hidden_hbm, grad_gate_hbm, grad_up_hbm))
     ]
@@ -658,6 +671,7 @@
     def put(ref, index, value, at):
         ref[index] = value + before_refs[at][index] if before else value
 
+    normed_fetch.wait()
     normed = normed_ref[...]
     small = dot_nt(rank_in_ref[...], normed).astype(bf16)
     ext = ext_ref[...].T
@@ -677,7 +691,7 @@
     columns = hidden.shape[2]
     return kernel_call(
         functools.partial(
-            feed_adapter_kernel, chips=chips, block=normed.shape[0] // len(chips), before=int(before is not None)
+            feed_adapter_kernel, chips=chips, block=hidden.shape[1], before=int(before is not None)
         ),
         out_shape=(
             shape_of((2 * RANK, D)),
@@ -685,12 +699,13 @@
             shape_of((2, RANK, columns)),
             shape_of((RANK, D)),
         ),
-        in_specs=[in_smem, in_vmem] + [anywhere] * 4 + [in_vmem] * (3 + 4 * (before is not None)),
+        in_specs=[in_smem] + [anywhere] * 5 + [in_vmem] * (3 + 4 * (before is not None)),
         out_specs=(in_vmem,) * 4,
         scratch_shapes=[
-            pltpu.VMEM(normed.shape, bf16),
+            pltpu.VMEM((hidden.shape[1], D), bf16),
+            pltpu.VMEM((hidden.shape[1], D), bf16),
             pltpu.VMEM((3,) + hidden.shape, bf16),
-            pltpu.SemaphoreType.DMA((3 + len(chips),)),
+            pltpu.SemaphoreType.DMA((5,)),
         ],
         compiler_params=limits(28),
         name="feed_adapter",
@@ -734,7 +749,7 @@
 def feed_pack_kernel(
     place_ref, own_hbm, partner_hbm, fold_hbm, products_ref, mag_raw_ref, mag_ref, in_ref, down_in_ref,
     down_products_ref, down_total_ref, down_mag_ref, down_aux_ref, down_proj_ref, down_rank_ref,
-    out_ref, down_grad_ref, weight_ref, fold_ref, full_ref, semaphores, *, share,
+    kept_ref, given_ref, down_grad_ref, out_ref, weight_ref, fold_ref, full_ref, semaphores, *, share,
 ):
     copies = Copies(semaphores)
     fold_fetch = copies(fold_hbm, fold_ref)
@@ -794,15 +809,17 @@
         full_ref[2 * RANK : 3 * RANK, lanes] += dot_nt(own_wide, fold_ref[part, :rows])
     for part in range(3):
         out_ref[64 * (1 + part) : 64 * (2 + part)] = full_ref[:, part * D : (part + 1) * D].astype(bf16)
+    give_halves(place_ref, out_ref, kept_ref, given_ref)
 
 
 def feed_pack(place, own, partner, fold_down, *rest, share):
     return kernel_call(
         functools.partial(feed_pack_kernel, share=share),
-        out_shape=(shape_of((256, D), bf16), shape_of((1, D))),
+        out_shape=(shape_of((256, D // 2), bf16), shape_of((256, D // 2), bf16), shape_of((1, D))),
         in_specs=[in_smem] + [anywhere] * 3 + [in_vmem] * 11,
-        out_specs=(in_vmem,) * 2,
+        out_specs=(in_vmem,) * 3,
         scratch_shapes=[
+            pltpu.VMEM((256, D), bf16),
             pltpu.VMEM((2,) + own.shape, bf16),
             pltpu.VMEM(fold_down.shape, bf16),
             pltpu.VMEM((64, 3 * D), f32),
@@ -972,13 +989,22 @@
     )(grads, queries, cosine, sine, normed, rank_in_t, mag, weights)
 
 
+def give_halves(place_ref, value_ref, kept_ref, given_ref):
+    half = value_ref.shape[1] // 2
+    left, right = value_ref[:, :half].astype(bf16), value_ref[:, half:].astype(bf16)
+    first = place_ref[0] == 0
+    kept_ref[...] = jnp.where(first, left, right)
+    given_ref[...] = jnp.where(first, right, left)
+
+
 def key_back_kernel(
     heads_ref, sent_ref, grad_ref, kv_ref, cos_ref, sin_ref, normed_ref, input_ref, gain_ref, residual_hbm,
-    before_hbm, rank_in_ref, mag_ref, *refs,
+    before_hbm, rank_in_ref, mag_ref, place_ref, q_in_ref, q_out_ref, q_mag_ref, out_in_ref, out_out_ref, out_mag_ref,
+    *refs,
 ):
     weight_hbm = refs[:KV_HEADS]
-    input_grad_ref, grad_in_ref, out_ref, grad_mag_ref, turned_ref = refs[KV_HEADS : KV_HEADS + 5]
-    weight_refs, before_ref, residual_ref, semaphores = refs[KV_HEADS + 5 :]
+    input_grad_ref, kept_ref, given_ref, late_ref, out_ref, grad_mag_ref, turned_ref = refs[KV_HEADS : KV_HEADS + 7]
+    weight_refs, before_ref, residual_ref, semaphores = refs[KV_HEADS + 7 :]
     copies = Copies(semaphores)
     fetches = [copies.started(ref, weight_refs.at[slot]) for slot, ref in enumerate(weight_hbm)]
     before_fetch = copies.started(before_hbm, before_ref)
@@ -1018,27 +1044,50 @@
     total = total + before_ref[...]
     residual_fetch.wait()
     ext = total[:, D:].astype(bf16).T
+    late_ref[:RANK, :D] = q_in_ref[...]
     for part in range(2):
-        rows = slice(part * RANK, (part + 1) * RANK)
-        grad_in_ref[rows] = grad_ins[part] + dot_nn(ext[(1 + part) * RANK : (2 + part) * RANK], normed_ref[...])
+        late_ref[(1 + part) * RANK : (2 + part) * RANK, :D] = grad_ins[part] + dot_nn(
+            ext[(1 + part) * RANK : (2 + part) * RANK], normed_ref[...]
+        )
+    late_ref[3 * RANK :, :D] = q_out_ref[...]
+    late_ref[:RANK, D : 2 * D] = out_in_ref[...]
+    late_ref[RANK : 2 * RANK, D : 2 * D] = out_out_ref[...]
+    late_ref[2 * RANK :, D : 2 * D] = jnp.where(iota((2 * RANK, D), 0) == 0, out_mag_ref[...], 0.0)
+    row = iota((2 * RANK, KVW), 0)
+    side = jnp.zeros((2 * RANK, KVW), f32)
+    for at in range(GROUP):
+        side = jnp.where(row == at, q_mag_ref[:, at * KVW : (at + 1) * KVW], side)
+    for part in range(2):
+        lanes = slice(part * KVW, (part + 1) * KVW)
+        late_ref[part * RANK : (part + 1) * RANK, 2 * D :] = out_ref[:, lanes]
+        side = jnp.where(row == GROUP + part, grad_mag_ref[:, lanes], side)
+    late_ref[2 * RANK :, 2 * D :] = side
+    give_halves(place_ref, late_ref, kept_ref, given_ref)
     values = input_ref[...].astype(f32)
     back = rms_back(values, rms_inverse(values), gain_ref[...], total[:, :D])
     input_grad_ref[...] = (residual_ref[...] + back).astype(bf16)
 
 
-def key_back(heads, sent, grads, kv, weights, cosine, sine, normed, inputs, gain, grad_residual, before, rank_in_t, mag):
+def key_back(
+    heads, sent, grads, kv, weights, cosine, sine, normed, inputs, gain, grad_residual, before, rank_in_t, mag, place,
+    *others
+):
     tokens = normed.shape[0]
+    wide = 2 * D + KVW
     return kernel_call(
         key_back_kernel,
         out_shape=(
             shape_of((tokens, D), bf16),
-            shape_of((2 * RANK, D)),
-            shape_of((RANK, 2 * KVW)),
-            shape_of((1, 2 * KVW)),
+            shape_of((4 * RANK, wide // 2), bf16),
+            shape_of((4 * RANK, wide // 2), bf16),
         ),
-        in_specs=[in_smem] + [in_vmem] * 8 + [anywhere] * 2 + [in_vmem] * 2 + [anywhere] * KV_HEADS,
-        out_specs=(in_vmem,) * 4,
+        in_specs=[in_smem] + [in_vmem] * 8 + [anywhere] * 2 + [in_vmem] * 2 + [in_smem] + [in_vmem] * 6
+        + [anywhere] * KV_HEADS,
+        out_specs=(in_vmem,) * 3,
         scratch_shapes=[
+            pltpu.VMEM((4 * RANK, wide), f32),
+            pltpu.VMEM((RANK, 2 * KVW), f32),
+            pltpu.VMEM((1, 2 * KVW), f32),
             pltpu.VMEM((tokens, 2 * KVW), bf16),
             pltpu.VMEM((KV_HEADS, 2 * HEAD, WIDE), bf16),
             pltpu.VMEM((tokens, WIDE), f32),
@@ -1049,25 +1098,28 @@
         name="key_back",
     )(
         heads, sent, grads, kv, cosine, sine, normed, inputs, gain[None], grad_residual,
-        before, rank_in_t, mag, *weights,
+        before, rank_in_t, mag, place, *others, *weights,
     )
 
 
-def cut_kernel(place_ref, value_ref, *out_refs):
+def cut_kernel(place_ref, mine_ref, other_ref, *refs):
+    out_refs, total_ref = refs[:-1], refs[-1]
     rows = out_refs[0].shape[0]
+    total_ref[...] = (mine_ref[...].astype(f32) + other_ref[...].astype(f32)).astype(bf16)
     for r, ref in enumerate(out_refs):
-        ref[...] = value_ref[pl.ds(pl.multiple_of((place_ref[2] ^ r) * rows, rows), rows), :]
-
-
-def cut_rows(place, value, chips):
-    shape = shape_of((value.shape[0] // chips, value.shape[1]), value.dtype)
+        ref[...] = total_ref[pl.ds(pl.multiple_of((place_ref[2] ^ r) * rows, rows), rows), :]
+
+
+def cut_rows(place, mine, other, chips):
+    shape = shape_of((mine.shape[0] // chips, mine.shape[1]), bf16)
     return kernel_call(
         cut_kernel,
         out_shape=(shape,) * chips,
-        in_specs=[in_smem, in_vmem],
+        in_specs=[in_smem, in_vmem, in_vmem],
         out_specs=(in_vmem,) * chips,
+        scratch_shapes=[pltpu.VMEM(mine.shape, bf16)],
         name="cut_rows",
-    )(place, value)
+    )(place, mine, other)
 
 
 def join_kernel(place_ref, *refs):
@@ -1201,16 +1253,11 @@
     def across(self, side, other):
         return self.split_swap(jnp.where(self.core == 0, other, side), 2, 4)
 
-    def total(self, value, order):
-        part = value.shape[1] // 2
-        value = value.astype(bf16)
-        cut = lambda core: lax.dynamic_slice_in_dim(value, core * part, part, 1)
-        sent = self.swap(cut(1 - self.core), 1)
-        kept = cut(self.core)
+    def total(self, kept, given, order):
+        sent = self.swap(given, 1)
         yield
         sent = order(sent)
-        value = (kept.astype(f32) + sent.astype(f32)).astype(bf16)
-        cuts = cut_rows(self.place, value, self.chips)
+        cuts = cut_rows(self.place, kept, sent, self.chips)
         order.mark(cuts[0])
         sent = [self.swap(cuts[r], 2 * r) for r in range(1, self.chips)]
         yield
@@ -1396,7 +1443,9 @@
         down_fold, down_proj = folded_down()
         mark(down_proj)
         down_0, down_c1, down_c2, down_c3 = settle(*[down_cut(r) for r in range(4)])
-        grad_all = spread(order(grad_out))
+        grad_all = lax.all_gather(
+            order(grad_out), "dp", axis=0, axis_index_groups=[[2 * c + k for c in range(chips)] for k in range(2)]
+        )
         kv_blocks[2] = settle(kv_blocks[2])
         send_kv(kv_blocks)
         queries = mark(query_project(order(normed), tables, q_weights))
@@ -1430,7 +1479,9 @@
         for _ in range(1, blocks):
             send_kv(kv_blocks)
         queries = query_project(normed, tables, q_weights)
-        grad_all = spread(grad_out)
+        grad_all = lax.all_gather(
+            grad_out, "dp", axis=0, axis_index_groups=[[2 * c + k for c in range(chips)] for k in range(2)]
+        )
         mixed, lse = attend(scalars, queries, kv_blocks)
         down_pieces = []
         for r in range(chips):
@@ -1475,20 +1526,20 @@
         crossed = settle(crossed)
         far_made = backward((3,), crossed)
         from_far = links.split_swap(far_made[0][0], 2, 4)
-        near_made = backward((1, 2), near_kept)
-        early_first = links.split_swap(near_made[0][0], 2, 4)
+        first_made = backward(("first",), near_kept)
+        early_first = links.split_swap(first_made[0][0], 2, 4)
+        last_made = backward(("last",), near_kept)
         from_far = settle(from_far)
-        late_share = settle((near_made[0][1].astype(f32) + from_far.astype(f32)).astype(bf16))
+        late_share = settle((last_made[0][0].astype(f32) + from_far.astype(f32)).astype(bf16))
         early_second = links.split_swap(late_share, 4, 2)
-        down_mag_steps = links.small_total(own_made[2][4][4:5] + near_made[2][4][4:5] + far_made[2][4][4:5], order)
+        down_mag_steps = links.small_total(sum(made[2][4][4:5] for made in (own_made, first_made, last_made, far_made)), order)
         next(down_mag_steps)
-        sums = adapters((1, 2), near, near_made, sums)
+        sums = adapters(("first",), near, first_made, sums)
         next(down_mag_steps)
-        sums = adapters((3,), crossed, far_made, sums)
-        next(down_mag_steps)
+        sums = adapters(("last",), near, last_made, sums)
         early_first = settle(early_first)
         reduced = (own_made[0][0], early_first, early_second)
-        shares_out = [own_made[1][0], *near_made[1], far_made[1][0]]
+        shares_out = [own_made[1][0], first_made[1][0], last_made[1][0], far_made[1][0]]
     else:
         sums, shares_grad, shares_out = None, [], []
         for r in range(chips):
@@ -1501,22 +1552,18 @@
         reduced = (shares_grad[0], rest, jnp.zeros(rest.shape, bf16))
         down_mag_steps = links.small_total(sum(mags[4:5] for mags in mag_sums), order)
         next(down_mag_steps)
-    feed_in, feed_products, down_in, down_products = sums
-    mag_raw = sum(mag_sums)
-    for _ in range(2):
-        next(down_mag_steps)
     reduced = settle(*reduced)
     grad_residual, grad_ordered, out_mag_raw, out_ext, grad_mixed, delta = residual_back(
         reduced, residual, gain_feedforward, grad_out, rows_in, mixed, o_weights
     )
     mark(delta)
-
+    next(down_mag_steps)
     def pack_early(down_mag_total):
         feed_mags = jnp.stack(
             [lax.dynamic_slice_in_dim(feed_mag, at * feed_cols, feed_cols, 1) for at in (core, 1 - core)]
         )
         if fast:
-            early, down_grad_mag = feed_pack(
+            *early, down_grad_mag = feed_pack(
                 place, feed_own, feed_partner, down_fold, *order(feed_products, mag_raw), feed_mags, feed_in, down_in,
                 down_products, down_mag_total, magnitude_down[None], aux[0], down_proj, rank_out_down,
                 share=1.0 / blocks,
@@ -1548,9 +1595,11 @@
         down_full = (full[2 * RANK : 3 * RANK, :FF].astype(f32) + down_norm_in).astype(bf16)
         full = lax.dynamic_update_slice(full, down_full, (2 * RANK, 0))
         top = jnp.concatenate([(feed_in + sum(grad_in_part)).astype(bf16), down_out.astype(bf16)])
-        return down_grad_mag, jnp.concatenate(
+        whole = jnp.concatenate(
             [jnp.pad(top, ((0, 16), (0, 0)))] + [full[:, i * D : (i + 1) * D] for i in range(3)]
         )
+        left, right = whole[:, : D // 2], whole[:, D // 2 :]
+        return down_grad_mag, (jnp.where(core == 0, left, right), jnp.where(core == 0, right, left))
 
     grad_queries, grad_kvs = None, []
 
@@ -1568,6 +1617,11 @@
 
     grad_queries, grad_kv = keys_back(blocks - 1)
     passed = links.row_shift(grad_kv, -1)
+    if fast:
+        sums = adapters((3,), crossed, far_made, sums)
+    feed_in, feed_products, down_in, down_products = sums
+    mag_raw = sum(mag_sums)
+    next(down_mag_steps)
     held = None
     for distance in reversed(range(1, blocks - 1)):
         grad_queries, grad_kv = keys_back(distance)
@@ -1577,13 +1631,21 @@
     if fast:
         out_far = links.split_swap(order(shares_out[3]), 2, 4)
         out_first = links.split_swap(order(shares_out[1]), 2, 4)
+    next(down_mag_steps)
     grad_queries, grad_kv = keys_back(0)
+    for down_mag_total in down_mag_steps:
+        pass
+    down_grad_mag, early = pack_early(down_mag_total)
+    mark(down_grad_mag)
+    early_steps = links.total(*early, order)
+    next(early_steps)
+    passed = pass_down(passed, held)
     out_grad_mag, out_out, out_in = output_adapter(
         order(grad_ordered), out_mag_raw, magnitude_output, o_weights, mixed, out_ext, out_in_t
     )
     mark(out_in)
-    passed = pass_down(passed, held)
     if fast:
+        next(early_steps)
         out_far, out_first = settle(out_far, out_first)
         out_late = settle((shares_out[2].astype(f32) + out_far.astype(f32)).astype(bf16))
         out_second = links.split_swap(out_late, 4, 2)
@@ -1594,34 +1656,18 @@
         order(grad_queries), queries, q_weights, cosine, sine, normed, attn_in_t[0], magnitude_attention[:GROUP]
     )
     mark(q_in)
-    for down_mag_total in down_mag_steps:
-        pass
-    down_grad_mag, early = pack_early(down_mag_total)
-    early_steps = links.total(settle(early), order)
-    next(early_steps)
-    passed, *out_parts = settle(passed, *out_parts)
-    next(early_steps)
-    input_grad, kv_in, kv_out, kv_grad_mag = key_back(
+    if fast:
+        next(early_steps)
+    passed = settle(passed)
+    input_grad, *late = key_back(
         heads, passed, grad_kv, kv_own, [weights for weights, _ in kv_made], cosine, sine, normed, rows_in,
         gain_attention, grad_residual, q_acc, attn_in_t[1:].reshape(2 * RANK, D), magnitude_attention[GROUP:],
+        place, q_in, q_out, q_grad_mag, out_in, out_out, out_grad_mag,
     )
-    mark(kv_in)
-    rows = lambda *parts: jnp.concatenate([part.astype(bf16) for part in parts])
-    late = jnp.concatenate(
-        [
-            rows(q_in, kv_in, q_out),
-            rows(out_in, out_out, out_grad_mag, jnp.zeros((31, D), bf16)),
-            rows(
-                kv_out[:, :KVW],
-                kv_out[:, KVW:],
-                q_grad_mag.reshape(-1, KVW),
-                kv_grad_mag.reshape(-1, KVW),
-                jnp.zeros((26, KVW), bf16),
-            ),
-        ],
-        axis=1,
-    )
-    late_steps = links.total(settle(late), order)
+    mark(late[0])
+    late_steps = links.total(*late, order)
+    next(late_steps)
+    out_parts = settle(*out_parts)
     late = early = None
     next(late_steps)
     block_out = settle((residual + sum(part.astype(f32) for part in out_parts)).astype(bf16))[None]

time: 520 us -> 488 us (0.938)
  waiting for transfers between devices: 120 us -> 101 us
  local copies, waits for them, and re-layouts: 59.9 us -> 42.1 us
  other arithmetic: 30.8 us -> 14.9 us
  starting transfers between devices: 82.4 us -> 95.6 us
  Pallas kernels: 201 us -> 211 us
    ppermute x35, waiting for transfers between devices: 85.4 us -> 69.9 us  [swap(): lax.ppermute(value, 'dp', [(i, i ^ bits) for i in range(self.devices)])]
    ppermute x6, waiting for transfers between devices: 18.9 us -> 4.57 us  [row_shift(): return lax.ppermute(value, 'blk', pairs)]
    convert_element_type x11 -> x1, other arithmetic: 10.3 us -> 1.74 us  [shards(): (last_made[0][0].astype(f32) + from_far.astype(f32)).astype(bf16)]
    unnamed x274 -> x234, local copies, waits for them, and re-layouts: 40.8 us -> 32.4 us
    pallas_call x28 -> x30, Pallas kernels: 181 us -> 189 us  [kernel_call(): call(*[keep(value, spec) for value, spec in zip(operands, in_specs)])]
    ppermute x6, starting transfers between devices: 13.1 us -> 20 us  [row_swap(): lax.ppermute(value, 'blk', [(i, i ^ bits) for i in range(self.blocks)])]
    ppermute x35, starting transfers between devices: 45.3 us -> 51.8 us  [swap(): lax.ppermute(value, 'dp', [(i, i ^ bits) for i in range(self.devices)])]
    all_gather x3 -> x2, waiting for transfers between devices: 0.01 us -> 5.5 us  [shards(): spread = lambda value: lax.all_gather(value, 'dp', axis=0)]
  transfers between devices with their start and end apart: 58 -> 58, of which waited for: 25 -> 27; matrix products, arithmetic and copies ran while one was open for 9% -> 4% of each run, Pallas kernels for 32% -> 38%
where the time goes in v4:
time: 488 us; the launch traced here: 480 us
  Pallas kernels  211 us (43%)
  waiting for transfers between devices  101 us (21%)
  starting transfers between devices  95.6 us (20%)
  local copies, waits for them, and re-layouts  42.1 us (9%)
  between operations  16.2 us (3%)
  other arithmetic  14.9 us (3%)
    pallas_call x30, Pallas kernels, kernel_call(): call(*[keep(value, spec) for value, spec in zip(operands, in_specs)])  189 us
    ppermute x35, waiting for transfers between devices, swap(): lax.ppermute(value, 'dp', [(i, i ^ bits) for i in range(self.devices)])  69.9 us
    ppermute x35, starting transfers between devices, swap(): lax.ppermute(value, 'dp', [(i, i ^ bits) for i in range(self.devices)])  51.8 us
    unnamed x234, local copies, waits for them, and re-layouts  32.4 us
    ppermute x6, starting transfers between devices, row_swap(): lax.ppermute(value, 'blk', [(i, i ^ bits) for i in range(self.blocks)])  20 us
    ppermute x8, waiting for transfers between devices, split_swap(): lax.ppermute(value, 'dp', [(i, i ^ (odd_bits if i % 2 else even_bits)) fo...  16.7 us
    ppermute x6, starting transfers between devices, row_shift(): return lax.ppermute(value, 'blk', pairs)  16.4 us
    pallas_call x4, Pallas kernels, attend_back(): kernel_call(functools.partial(attend_back_kernel, distance=distance, chai...  13.4 us
  transfers between devices with their start and end apart: 58, of which 27 were waited for; matrix products, arithmetic and copies ran while one was open for 4% of the time, Pallas kernels for 38%

profile of v4, /device:TPU:1, one launch (start us, length us, event | category | flops | bytes accessed | tf_op | source)
XLA Modules:
  0.0 480.1 jit_solution(2354631401820283736)
XLA Ops:
  13.9 4.5 fold_q.1
  24.7 9.7 %collective-permute-done.first_ref = bf16[2,64,2176]{2,1,0:T(8,128)(2,1)} collective-permute-done((bf16[2,64,2176]{2,1,0:T(8,128)(2,1)S(1)}, bf16[2,64,2176]{2,1,0:T(8,128)(2,1)}, u32[]{:S(2)}, u32[]{:S(2)}) %collective-permute-start) | collective-permute-done | bytes 557088 | tf_op jit(solution)/shard_map/ppermute | solution.py:1236
  37.8 4.5 fold_o.1
  50.9 6.1 %collective-permute-done.3.first_ref = bf16[2,64,2176]{2,1,0:T(8,128)(2,1)S(1)} collective-permute-done((bf16[2,64,2176]{2,1,0:T(8,128)(2,1)S(1)}, bf16[2,64,2176]{2,1,0:T(8,128)(2,1)S(1)}, u32[]{:S(2)}, u32[]{:S(2)}) %collective-permute-start.3) | collective-permute-done | bytes 557088 | tf_op jit(solution)/shard_map/ppermute | solution.py:1239
  57.0 7.6 %collective-permute-start.4 = (bf16[2,64,2176]{2,1,0:T(8,128)(2,1)S(1)}, bf16[2,64,2176]{2,1,0:T(8,128)(2,1)S(1)}, u32[]{:S(2)}, u32[]{:S(2)}) collective-permute-start(bf16[2,64,2176]{2,1,0:T(8,128)(2,1)S(1)} %collective-permute-done.3.first_ref), channel_id=1, source_target_pairs={{0,4},{4,0},{8,12},{12,8},{16,20},{20,16},{24,28},{28,24},{1,5},{5... | collective-permute-start | bytes 1671176 | tf_op jit(solution)/shard_map/ppermute | solution.py:1236
  76.2 3.7 collective-permute-start.7
  82.1 2.7 copy-done.21
  84.8 12.5 %fold_feed.1.own_ref.own_hbm = bf16[2,704,2176]{2,1,0:T(8,128)(2,1)} custom-call(bf16[2,704,2048]{2,1,0:T(8,128)(2,1)S(1)} %bitcast.73, bf16[2,16,2048]{2,1,0:T(8,128)(2,1)S(1)} %bitcast.74, bf16[2,16,704]{2,1,0:T(8,128)(2,1)S(1)} %constant_dynamic-slice_fusion.3.rank_out_ref, f32[2,1,704]{2,1,0:T(1,128)S(1)} %broadcast_in_dim.62.mag_ref), custom_call_target="tpu_custom_call" | custom-call | tf_op jit(solution)/shard_map/fold_feed/pallas_call | solution.py:60
  97.3 3.6 collective-permute-start.8
  104.1 2.8 fold_down.1
  111.4 5.1 %collective-permute-start.9 = (bf16[256,1024]{1,0:T(8,128)(2,1)}, bf16[256,1024]{1,0:T(8,128)(2,1)}, u32[]{:S(2)}, u32[]{:S(2)}) collective-permute-start(bf16[256,1024]{1,0:T(8,128)(2,1)} %collective-permute-done.8.refs_2_.kv_ref), channel_id=1, source_target_pairs={{0,1},{1,2},{2,3},{4,5},{5,6},{6,7},{8,9},{9,10},{10,11},{12,13},{... | collective-permute-start | bytes 1572872 | tf_op jit(solution)/shard_map/ppermute | solution.py:1248
  116.6 6.0 %query_project.1.query_ref = bf16[256,2048]{1,0:T(8,128)(2,1)S(1)} custom-call(bf16[256,2048]{1,0:T(8,128)(2,1)S(1)} %fusion.2.input_ref.normed_ref, f32[256,128]{1,0:T(8,128)S(1)} %copy-done.14, f32[256,128]{1,0:T(8,128)S(1)} %copy-done.16, bf16[8,4,64,2176]{3,2,1,0:T(8,128)(2,1)} %bitcast.105), custom_call_target="tpu_custom_call" | custom-call | tf_op jit(solution)/shard_map/query_project/pallas_call | solution.py:60
  122.6 3.3 collective-permute-done.9.refs_3_.kv_ref
  125.9 5.3 %attend.1 = (bf16[256,2048]{1,0:T(8,128)(2,1)S(1)}, f32[4,1,1024]{2,1,0:T(1,128)S(1)}) custom-call(s32[2]{0:T(128)S(1)} %pad_add_fusion.scalar_ref, bf16[256,2048]{1,0:T(8,128)(2,1)S(1)} %query_project.1.query_ref, bf16[256,1024]{1,0:T(8,128)(2,1)S(1)} %copy-done.23, bf16[256,1024]{1,0:T(8,128)(2,1)} %collective-permute-done.7.refs_1_.kv_ref, ...), custom_call_target="tpu_custom_call" | custom-call | tf_op jit(solution)/shard_map/attend/pallas_call | solution.py:335
  135.4 4.3 collective-permute-start.13
  141.3 5.5 %all-gather.9.cloned.1.call-done = bf16[32,64,2176]{2,1,0:T(8,128)(2,1)} async-done(((bf16[4,64,2176]{2,1,0:T(8,128)(2,1)}), bf16[32,64,2176]{2,1,0:T(8,128)(2,1)}) %all-gather.9.cloned.1.call-update) | async-done | bytes 8912912 | tf_op jit(solution)/shard_map/all_gather | solution.py:1409
  148.1 5.8 %output_project.1 = (f32[256,2048]{1,0:T(8,128)S(1)}, bf16[256,2048]{1,0:T(8,128)(2,1)S(1)}) custom-call(bf16[256,2048]{1,0:T(8,128)(2,1)S(1)} %copy-done.11, bf16[256,2048]{1,0:T(8,128)(2,1)S(1)} %bitcast.68, f32[1,2048]{1,0:T(1,128)S(1)} %bitcast.88, bf16[8,4,64,2176]{3,2,1,0:T(8,128)(2,1)} %bitcast.102), custom_call_target="tpu_custom_call" | custom-call | tf_op jit(solution)/shard_map/output_project/pallas_call | solution.py:60
  157.4 26.3 %collective-permute-done.14.refs_7_.refs_8_ = bf16[1440,256]{1,0:T(8,128)(2,1)} collective-permute-done((bf16[1440,256]{1,0:T(8,128)(2,1)}, bf16[1440,256]{1,0:T(8,128)(2,1)}, u32[]{:S(2)}, u32[]{:S(2)}) %collective-permute-start.14) | collective-permute-done | bytes 737312 | tf_op jit(solution)/shard_map/ppermute | solution.py:1236
  190.1 19.4 %feed_back.4 = (bf16[256,2048]{1,0:T(8,128)(2,1)}, bf16[256,2048]{1,0:T(8,128)(2,1)}, bf16[2,256,704]{2,1,0:T(8,128)(2,1)}, bf16[2,256,704]{2,1,0:T(8,128)(2,1)}...) custom-call(s32[3]{0:T(128)} %pad_add_fusion.1.place_ref, ...), custom_call_target="tpu_custom_call" | custom-call | tf_op jit(solution)/shard_map/feed_back/pallas_call | solution.py:60
  209.5 7.2 %collective-permute-done.18 = bf16[256,2048]{1,0:T(8,128)(2,1)S(1)} collective-permute-done((bf16[256,2048]{1,0:T(8,128)(2,1)S(1)}, bf16[256,2048]{1,0:T(8,128)(2,1)S(1)}, u32[]{:S(2)}, u32[]{:S(2)}) %collective-permute-start.18) | collective-permute-done | bytes 1048608 | tf_op jit(solution)/shard_map/ppermute | solution.py:1236
  217.4 10.7 %feed_forward.1 = (f32[2,512,704]{2,1,0:T(8,128)S(1)}, f32[2,512,704]{2,1,0:T(8,128)S(1)}) custom-call(bf16[512,2048]{1,0:T(8,128)(2,1)S(1)} %pad_maximum_fusion.normed_ref.normed_hbm, bf16[2,704,2176]{2,1,0:T(8,128)(2,1)} %fold_feed.1.own_ref.own_hbm, bf16[2,704,2176]{2,1,0:T(8,128)(2,1)} %collective-permute-done.10.partner_ref.partner_hbm), custom_call_target="tpu_custom_call" | custom-call | tf_op jit(solution)/shard_map/feed_forward/pallas_call | solution.py:60
  229.8 4.6 feed_adapter.4
  236.5 7.1 %collective-permute-done.20.refs_0_.normed_hbm = bf16[256,2048]{1,0:T(8,128)(2,1)S(1)} collective-permute-done((bf16[256,2048]{1,0:T(8,128)(2,1)S(1)}, bf16[256,2048]{1,0:T(8,128)(2,1)S(1)}, u32[]{:S(2)}, u32[]{:S(2)}) %collective-permute-start.20) | collective-permute-done | bytes 1048608 | tf_op jit(solution)/shard_map/ppermute | solution.py:1239
  244.6 19.0 %feed_back.5 = (bf16[256,2048]{1,0:T(8,128)(2,1)}, bf16[256,2048]{1,0:T(8,128)(2,1)}, bf16[2,256,704]{2,1,0:T(8,128)(2,1)}, bf16[2,256,704]{2,1,0:T(8,128)(2,1)}...) custom-call(s32[3]{0:T(128)} %pad_add_fusion.1.place_ref, ...), custom_call_target="tpu_custom_call" | custom-call | tf_op jit(solution)/shard_map/feed_back/pallas_call | solution.py:60
  264.1 17.1 %feed_back.6 = (bf16[256,2048]{1,0:T(8,128)(2,1)}, bf16[256,2048]{1,0:T(8,128)(2,1)}, bf16[2,256,704]{2,1,0:T(8,128)(2,1)}, bf16[2,256,704]{2,1,0:T(8,128)(2,1)}...) custom-call(s32[3]{0:T(128)} %pad_add_fusion.1.place_ref, ...), custom_call_target="tpu_custom_call" | custom-call | tf_op jit(solution)/shard_map/feed_back/pallas_call | solution.py:60
  282.3 17.3 %feed_back.7 = (bf16[256,2048]{1,0:T(8,128)(2,1)}, bf16[256,2048]{1,0:T(8,128)(2,1)}, bf16[2,256,704]{2,1,0:T(8,128)(2,1)}, bf16[2,256,704]{2,1,0:T(8,128)(2,1)}...) custom-call(s32[3]{0:T(128)} %pad_add_fusion.1.place_ref, ...), custom_call_target="tpu_custom_call" | custom-call | tf_op jit(solution)/shard_map/feed_back/pallas_call | solution.py:60
  303.4 4.1 feed_adapter.5
  307.7 4.4 feed_adapter.6
  312.1 3.5 collective-permute-done.25.third_ref
  315.7 6.9 %residual_back.1 = (f32[256,2048]{1,0:T(8,128)S(1)}, bf16[256,2048]{1,0:T(8,128)(2,1)S(1)}, f32[1,2048]{1,0:T(1,128)S(1)}, bf16[256,128]{1,0:T(8,128)(2,1)S(1)},...) custom-call(bf16[256,2048]{1,0:T(8,128)(2,1)S(1)} %copy-done.47, ...), custom_call_target="tpu_custom_call" | custom-call | tf_op jit(solution)/shard_map/residual_back/pallas_call | solution.py:60
  322.6 2.9 attend_back_3.1
  327.4 4.1 feed_adapter.7
  331.5 6.1 %collective-permute-start.30 = (f32[1,2048]{1,0:T(1,128)S(1)}, f32[1,2048]{1,0:T(1,128)S(1)}, u32[]{:S(2)}, u32[]{:S(2)}) collective-permute-start(f32[1,2048]{1,0:T(1,128)S(1)} %add.180), channel_id=1, source_target_pairs={{0,1},{1,0},{2,3},{3,2},{4,5},{5,4},{6,7},{7,6},{8,9},{9,8},{10,11... | collective-permute-start | bytes 24584 | tf_op jit(solution)/shard_map/ppermute | solution.py:1244
  337.6 2.8 attend_back_2.1
  340.4 2.8 attend_back_1.1
  346.4 11.9 %collective-permute-start.31 = (f32[1,2048]{1,0:T(1,128)S(1)}, f32[1,2048]{1,0:T(1,128)S(1)}, u32[]{:S(2)}, u32[]{:S(2)}) collective-permute-start(f32[1,2048]{1,0:T(1,128)S(1)} %add.185), channel_id=1, source_target_pairs={{0,2},{1,3},{2,0},{3,1},{4,6},{5,7},{6,4},{7,5},{8,10},{9,11},{10,... | collective-permute-start | bytes 24584 | tf_op jit(solution)/shard_map/ppermute | solution.py:1244
  358.3 4.9 %attend_back_0.1 = (f32[256,2048]{1,0:T(8,128)S(1)}, f32[256,1024]{1,0:T(8,128)S(1)}) custom-call(s32[2]{0:T(128)S(1)} %copy-done.84, bf16[256,2048]{1,0:T(8,128)(2,1)S(1)} %query_project.1.query_ref, bf16[256,2048]{1,0:T(8,128)(2,1)S(1)} %get-tuple-element.348.grad_ref, f32[4,1,1024]{2,1,0:T(1,128)S(1)} %copy-done.54, ...), custom_call_target="tpu_custom_call", output_to_operand_aliasing={{0}: (6, {})} | custom-call | tf_op jit(solution)/shard_map/attend_back_0/pallas_call | solution.py:412
  364.9 7.2 %feed_pack.1 = (bf16[256,1024]{1,0:T(8,128)(2,1)S(1)}, bf16[256,1024]{1,0:T(8,128)(2,1)S(1)}, f32[1,2048]{1,0:T(1,128)}) custom-call(s32[3]{0:T(128)S(1)} %copy-done.62, bf16[2,704,2176]{2,1,0:T(8,128)(2,1)} %fold_feed.1.own_ref.own_hbm, bf16[2,704,2176]{2,1,0:T(8,128)(2,1)} %collective-permute-done.10.partner_ref.partner_hbm, ...), custom_call_target="tpu_custom_call" | custom-call | tf_op jit(solution)/shard_map/feed_pack/pallas_call | solution.py:60
  372.1 8.2 %collective-permute-start.32 = (bf16[256,1024]{1,0:T(8,128)(2,1)S(1)}, bf16[256,1024]{1,0:T(8,128)(2,1)S(1)}, u32[]{:S(2)}, u32[]{:S(2)}) collective-permute-start(bf16[256,1024]{1,0:T(8,128)(2,1)S(1)} %get-tuple-element.384), channel_id=1, source_target_pairs={{0,4},{4,0},{8,12},{12,8},{16,20},{20,16},{24,28},{28,24},{1,5},{5... | collective-permute-start | bytes 1572872 | tf_op jit(solution)/shard_map/ppermute | solution.py:1236
  381.2 5.8 %output_adapter.1 = (f32[1,2048]{1,0:T(1,128)S(1)}, f32[16,2048]{1,0:T(8,128)S(1)}, f32[16,2048]{1,0:T(8,128)S(1)}) custom-call(bf16[256,2048]{1,0:T(8,128)(2,1)S(1)} %get-tuple-element.389.grad_ref, f32[1,2048]{1,0:T(1,128)S(1)} %get-tuple-element.390.mag_raw_ref, f32[4,512]{1,0:T(4,128)S(1)} %copy-done.85, bf16[256,2048]{1,0:T(8,128)(2,1)S(1)} %copy-done.12, ...), custom_call_target="tpu_custom_call" | custom-call | tf_op jit(solution)/shard_map/output_adapter/pallas_call | solution.py:60
  396.7 5.2 %collective-permute-start.37 = (bf16[64,1024]{1,0:T(8,128)(2,1)S(1)}, bf16[64,1024]{1,0:T(8,128)(2,1)S(1)}, u32[]{:S(2)}, u32[]{:S(2)}) collective-permute-start(bf16[64,1024]{1,0:T(8,128)(2,1)S(1)} %copy-done.116), channel_id=1, source_target_pairs={{0,16},{4,20},{8,24},{12,28},{16,0},{20,4},{24,8},{28,12},{1,17},{... | collective-permute-start | bytes 393224 | tf_op jit(solution)/shard_map/ppermute | solution.py:1236
  402.1 7.5 %query_back.1 = (f32[256,2176]{1,0:T(8,128)S(1)}, f32[16,2048]{1,0:T(8,128)S(1)}, f32[16,2048]{1,0:T(8,128)S(1)}, f32[1,2048]{1,0:T(1,128)S(1)}) custom-call(f32[256,2048]{1,0:T(8,128)S(1)} %copy-done.4, bf16[256,2048]{1,0:T(8,128)(2,1)S(1)} %query_project.1.query_ref, f32[256,128]{1,0:T(8,128)S(1)} %copy-done.14, f32[256,128]{1,0:T(8,128)S(1)} %copy-done.16, ...), custom_call_target="tpu_custom_call" | custom-call | tf_op jit(solution)/shard_map/query_back/pallas_call | solution.py:60
  411.8 6.0 %collective-permute-done.38 = bf16[64,1024]{1,0:T(8,128)(2,1)S(1)} collective-permute-done((bf16[64,1024]{1,0:T(8,128)(2,1)S(1)}, bf16[64,1024]{1,0:T(8,128)(2,1)S(1)}, u32[]{:S(2)}, u32[]{:S(2)}) %collective-permute-start.38) | collective-permute-done | bytes 131104 | tf_op jit(solution)/shard_map/ppermute | solution.py:1236
  419.8 7.7 %key_back.1 = (bf16[256,2048]{1,0:T(8,128)(2,1)}, bf16[64,2304]{1,0:T(8,128)(2,1)S(1)}, bf16[64,2304]{1,0:T(8,128)(2,1)S(1)}) custom-call(s32[4]{0:T(128)S(1)} %iota_xor_fusion.heads_ref, bf16[256,1024]{1,0:T(8,128)(2,1)S(1)} %collective-permute-done.35.sent_ref, f32[256,1024]{1,0:T(8,128)S(1)} %copy-done.45, bf16[256,1024]{1,0:T(8,128)(2,1)S(1)} %copy-done.25, ...), custom_call_target="tpu_custom_call" | custom-call | tf_op jit(solution)/shard_map/key_back/pallas_call | solution.py:60
  427.6 2.8 add_convert_fusion
  437.1 3.1 collective-permute-done.42
  441.2 3.2 collective-permute-done.45
  449.2 4.2 collective-permute-done.49.refs_3_
  (401 shorter events, 127.1 us)
Async XLA Ops:
  7.2 109.4 %all-gather.7.cloned.1.call-start = ((), (), s32[]{:S(2)}) async-start(), calls=%async_computation | async-start | bytes 10027008 | tf_op jit(solution)/shard_map/all_gather | solution.py:1409
  18.5 128.4 %all-gather.9.cloned.1.call-start = ((), (), s32[]{:S(2)}) async-start(), calls=%async_computation.1 | async-start | bytes 10027008 | tf_op jit(solution)/shard_map/all_gather | solution.py:1409
  18.5 15.9 %collective-permute-start = (bf16[2,64,2176]{2,1,0:T(8,128)(2,1)S(1)}, bf16[2,64,2176]{2,1,0:T(8,128)(2,1)}, u32[]{:S(2)}, u32[]{:S(2)}) collective-permute-start(bf16[2,64,2176]{2,1,0:T(8,128)(2,1)S(1)} %fold_kv.1.first_ref), channel_id=1, source_target_pairs={{0,8},{4,12},{8,0},{12,4},{16,24},{20,28},{24,16},{28,20},{1,9},{5... | collective-permute-start | bytes 1671176 | tf_op jit(solution)/shard_map/ppermute | solution.py:1236
  20.6 15.1 %collective-permute-start.1 = (bf16[2,64,2176]{2,1,0:T(8,128)(2,1)S(1)}, bf16[2,64,2176]{2,1,0:T(8,128)(2,1)S(1)}, u32[]{:S(2)}, u32[]{:S(2)}) collective-permute-start(bf16[2,64,2176]{2,1,0:T(8,128)(2,1)S(1)} %fold_kv.1.first_ref), channel_id=1, source_target_pairs={{0,16},{4,20},{8,24},{12,28},{16,0},{20,4},{24,8},{28,12},{1,17},{... | collective-permute-start | bytes 1671176 | tf_op jit(solution)/shard_map/ppermute | solution.py:1236
  21.9 13.8 %collective-permute-start.2 = (bf16[2,64,2176]{2,1,0:T(8,128)(2,1)S(1)}, bf16[2,64,2176]{2,1,0:T(8,128)(2,1)S(1)}, u32[]{:S(2)}, u32[]{:S(2)}) collective-permute-start(bf16[2,64,2176]{2,1,0:T(8,128)(2,1)S(1)} %fold_kv.1.first_ref), channel_id=1, source_target_pairs={{0,4},{4,0},{8,12},{12,8},{16,20},{20,16},{24,28},{28,24},{1,5},{5... | collective-permute-start | bytes 1671176 | tf_op jit(solution)/shard_map/ppermute | solution.py:1236
  42.3 202.3 %all-gather.11.cloned.1.call-start = ((), (), s32[]{:S(2)}) async-start(), calls=%async_computation.2 | async-start | bytes 5242880 | tf_op jit(solution)/shard_map/all_gather | solution.py:1446
  45.5 11.5 %collective-permute-start.3 = (bf16[2,64,2176]{2,1,0:T(8,128)(2,1)S(1)}, bf16[2,64,2176]{2,1,0:T(8,128)(2,1)S(1)}, u32[]{:S(2)}, u32[]{:S(2)}) collective-permute-start(bf16[2,64,2176]{2,1,0:T(8,128)(2,1)S(1)} %broadcast_select_fusion.2), channel_id=1, source_target_pairs={{0,8},{4,20},{8,0},{12,28},{16,24},{20,4},{24,16},{28,12},{1,9},{5... | collective-permute-start | bytes 1671176 | tf_op jit(solution)/shard_map/ppermute | solution.py:1239
  49.1 18.5 %collective-permute-start.5 = (bf16[2,64,2176]{2,1,0:T(8,128)(2,1)}, bf16[2,64,2176]{2,1,0:T(8,128)(2,1)S(1)}, u32[]{:S(2)}, u32[]{:S(2)}) collective-permute-start(bf16[2,64,2176]{2,1,0:T(8,128)(2,1)} %collective-permute-done.first_ref), channel_id=1, source_target_pairs={{0,4},{4,0},{8,12},{12,8},{16,20},{20,16},{24,28},{28,24},{1,5},{5... | collective-permute-start | bytes 1671176 | tf_op jit(solution)/shard_map/ppermute | solution.py:1236
  50.6 17.0 %collective-permute-start.6 = (bf16[2,64,2176]{2,1,0:T(8,128)(2,1)S(1)}, bf16[2,64,2176]{2,1,0:T(8,128)(2,1)S(1)}, u32[]{:S(2)}, u32[]{:S(2)}) collective-permute-start(bf16[2,64,2176]{2,1,0:T(8,128)(2,1)S(1)} %collective-permute-done.1.first_ref), channel_id=1, source_target_pairs={{0,4},{4,0},{8,12},{12,8},{16,20},{20,16},{24,28},{28,24},{1,5},{5... | collective-permute-start | bytes 1671176 | tf_op jit(solution)/shard_map/ppermute | solution.py:1236
  57.0 16.5 %collective-permute-start.4 = (bf16[2,64,2176]{2,1,0:T(8,128)(2,1)S(1)}, bf16[2,64,2176]{2,1,0:T(8,128)(2,1)S(1)}, u32[]{:S(2)}, u32[]{:S(2)}) collective-permute-start(bf16[2,64,2176]{2,1,0:T(8,128)(2,1)S(1)} %collective-permute-done.3.first_ref), channel_id=1, source_target_pairs={{0,4},{4,0},{8,12},{12,8},{16,20},{20,16},{24,28},{28,24},{1,5},{5... | collective-permute-start | bytes 1671176 | tf_op jit(solution)/shard_map/ppermute | solution.py:1236
  76.2 21.0 %collective-permute-start.7 = (bf16[256,1024]{1,0:T(8,128)(2,1)S(1)}, bf16[256,1024]{1,0:T(8,128)(2,1)}, u32[]{:S(2)}, u32[]{:S(2)}) collective-permute-start(bf16[256,1024]{1,0:T(8,128)(2,1)S(1)} %get-tuple-element.255.refs_0_.kv_ref), channel_id=1, source_target_pairs={{0,1},{1,2},{2,3},{4,5},{5,6},{6,7},{8,9},{9,10},{10,11},{12,13},{... | collective-permute-start | bytes 1572872 | tf_op jit(solution)/shard_map/ppermute | solution.py:1248
  97.3 14.1 %collective-permute-start.8 = (bf16[256,1024]{1,0:T(8,128)(2,1)}, bf16[256,1024]{1,0:T(8,128)(2,1)}, u32[]{:S(2)}, u32[]{:S(2)}) collective-permute-start(bf16[256,1024]{1,0:T(8,128)(2,1)} %collective-permute-done.7.refs_1_.kv_ref), channel_id=1, source_target_pairs={{0,1},{1,2},{2,3},{4,5},{5,6},{6,7},{8,9},{9,10},{10,11},{12,13},{... | collective-permute-start | bytes 1572872 | tf_op jit(solution)/shard_map/ppermute | solution.py:1248
  111.4 14.5 %collective-permute-start.9 = (bf16[256,1024]{1,0:T(8,128)(2,1)}, bf16[256,1024]{1,0:T(8,128)(2,1)}, u32[]{:S(2)}, u32[]{:S(2)}) collective-permute-start(bf16[256,1024]{1,0:T(8,128)(2,1)} %collective-permute-done.8.refs_2_.kv_ref), channel_id=1, source_target_pairs={{0,1},{1,2},{2,3},{4,5},{5,6},{6,7},{8,9},{9,10},{10,11},{12,13},{... | collective-permute-start | bytes 1572872 | tf_op jit(solution)/shard_map/ppermute | solution.py:1248
  132.1 57.1 %collective-permute-start.10 = (bf16[2,704,2176]{2,1,0:T(8,128)(2,1)}, bf16[2,704,2176]{2,1,0:T(8,128)(2,1)}, u32[]{:S(2)}, u32[]{:S(2)}) collective-permute-start(bf16[2,704,2176]{2,1,0:T(8,128)(2,1)} %fold_feed.1.own_ref.own_hbm), channel_id=1, source_target_pairs={{0,4},{4,0},{8,12},{12,8},{16,20},{20,16},{24,28},{28,24},{1,5},{5... | collective-permute-start | bytes 18382856 | tf_op jit(solution)/shard_map/ppermute | solution.py:1236
  135.3 22.1 %collective-permute-start.12 = (bf16[1440,256]{1,0:T(8,128)(2,1)}, bf16[1440,256]{1,0:T(8,128)(2,1)}, u32[]{:S(2)}, u32[]{:S(2)}) collective-permute-start(bf16[1440,256]{1,0:T(8,128)(2,1)} %get-tuple-element.273), channel_id=1, source_target_pairs={{0,8},{4,12},{8,0},{12,4},{16,24},{20,28},{24,16},{28,20},{1,9},{5... | collective-permute-start | bytes 2211848 | tf_op jit(solution)/shard_map/ppermute | solution.py:1236
  135.4 22.0 %collective-permute-start.13 = (bf16[1440,256]{1,0:T(8,128)(2,1)}, bf16[1440,256]{1,0:T(8,128)(2,1)}, u32[]{:S(2)}, u32[]{:S(2)}) collective-permute-start(bf16[1440,256]{1,0:T(8,128)(2,1)} %get-tuple-element.274), channel_id=1, source_target_pairs={{0,16},{4,20},{8,24},{12,28},{16,0},{20,4},{24,8},{28,12},{1,17},{... | collective-permute-start | bytes 2211848 | tf_op jit(solution)/shard_map/ppermute | solution.py:1236
  139.7 44.0 %collective-permute-start.14 = (bf16[1440,256]{1,0:T(8,128)(2,1)}, bf16[1440,256]{1,0:T(8,128)(2,1)}, u32[]{:S(2)}, u32[]{:S(2)}) collective-permute-start(bf16[1440,256]{1,0:T(8,128)(2,1)} %get-tuple-element.275), channel_id=1, source_target_pairs={{0,24},{4,28},{8,16},{12,20},{16,8},{20,12},{24,0},{28,4},{1,25},{... | collective-permute-start | bytes 2211848 | tf_op jit(solution)/shard_map/ppermute | solution.py:1236
  140.8 44.3 %collective-permute-start.11 = (bf16[1440,256]{1,0:T(8,128)(2,1)}, bf16[1440,256]{1,0:T(8,128)(2,1)}, u32[]{:S(2)}, u32[]{:S(2)}) collective-permute-start(bf16[1440,256]{1,0:T(8,128)(2,1)} %get-tuple-element.279.refs_1_.refs_2_), channel_id=1, source_target_pairs={{0,4},{4,0},{8,12},{12,8},{16,20},{20,16},{24,28},{28,24},{1,5},{5... | collective-permute-start | bytes 2211848 | tf_op jit(solution)/shard_map/ppermute | solution.py:1236
  184.7 32.0 %collective-permute-start.18 = (bf16[256,2048]{1,0:T(8,128)(2,1)S(1)}, bf16[256,2048]{1,0:T(8,128)(2,1)S(1)}, u32[]{:S(2)}, u32[]{:S(2)}) collective-permute-start(bf16[256,2048]{1,0:T(8,128)(2,1)S(1)} %get-tuple-element.298.refs_0_.normed_hbm), channel_id=1, source_target_pairs={{0,8},{4,12},{8,0},{12,4},{16,24},{20,28},{24,16},{28,20},{1,9},{5... | collective-permute-start | bytes 3145736 | tf_op jit(solution)/shard_map/ppermute | solution.py:1236
  184.9 31.9 %collective-permute-start.19 = (bf16[256,2048]{1,0:T(8,128)(2,1)S(1)}, bf16[256,2048]{1,0:T(8,128)(2,1)S(1)}, u32[]{:S(2)}, u32[]{:S(2)}) collective-permute-start(bf16[256,2048]{1,0:T(8,128)(2,1)S(1)} %get-tuple-element.298.refs_0_.normed_hbm), channel_id=1, source_target_pairs={{0,16},{4,20},{8,24},{12,28},{16,0},{20,4},{24,8},{28,12},{1,17},{... | collective-permute-start | bytes 3145736 | tf_op jit(solution)/shard_map/ppermute | solution.py:1236
  216.9 26.8 %collective-permute-start.20 = (bf16[256,2048]{1,0:T(8,128)(2,1)S(1)}, bf16[256,2048]{1,0:T(8,128)(2,1)S(1)}, u32[]{:S(2)}, u32[]{:S(2)}) collective-permute-start(bf16[256,2048]{1,0:T(8,128)(2,1)S(1)} %broadcast_select_fusion.1), channel_id=1, source_target_pairs={{0,8},{4,20},{8,0},{12,28},{16,24},{20,4},{24,16},{28,12},{1,9},{5... | collective-permute-start | bytes 3145736 | tf_op jit(solution)/shard_map/ppermute | solution.py:1239
  263.6 36.1 %collective-permute-start.22 = (bf16[256,2048]{1,0:T(8,128)(2,1)}, bf16[256,2048]{1,0:T(8,128)(2,1)S(1)}, u32[]{:S(2)}, u32[]{:S(2)}) collective-permute-start(bf16[256,2048]{1,0:T(8,128)(2,1)} %get-tuple-element.310), channel_id=1, source_target_pairs={{0,8},{4,20},{8,0},{12,28},{16,24},{20,4},{24,16},{28,12},{1,9},{5... | collective-permute-start | bytes 3145736 | tf_op jit(solution)/shard_map/ppermute | solution.py:1239
  281.2 30.9 %collective-permute-start.24 = (bf16[256,2048]{1,0:T(8,128)(2,1)}, bf16[256,2048]{1,0:T(8,128)(2,1)S(1)}, u32[]{:S(2)}, u32[]{:S(2)}) collective-permute-start(bf16[256,2048]{1,0:T(8,128)(2,1)} %get-tuple-element.314), channel_id=1, source_target_pairs={{0,8},{4,20},{8,0},{12,28},{16,24},{20,4},{24,16},{28,12},{1,9},{5... | collective-permute-start | bytes 3145736 | tf_op jit(solution)/shard_map/ppermute | solution.py:1239
  301.5 14.1 %collective-permute-start.25 = (bf16[256,2048]{1,0:T(8,128)(2,1)S(1)}, bf16[256,2048]{1,0:T(8,128)(2,1)S(1)}, u32[]{:S(2)}, u32[]{:S(2)}) collective-permute-start(bf16[256,2048]{1,0:T(8,128)(2,1)S(1)} %add_convert_fusion.2), channel_id=1, source_target_pairs={{0,16},{4,12},{8,24},{12,4},{16,0},{20,28},{24,8},{28,20},{1,17},{... | collective-permute-start | bytes 3145736 | tf_op jit(solution)/shard_map/ppermute | solution.py:1239
  302.8 4.7 collective-permute-start.21
  307.5 15.1 %collective-permute-start.23 = (f32[1,2048]{1,0:T(1,128)S(1)}, f32[1,2048]{1,0:T(1,128)S(1)}, u32[]{:S(2)}, u32[]{:S(2)}) collective-permute-start(f32[1,2048]{1,0:T(1,128)S(1)} %add.178), channel_id=1, source_target_pairs={{0,8},{4,12},{8,0},{12,4},{16,24},{20,28},{24,16},{28,20},{1,9},{5... | collective-permute-start | bytes 24584 | tf_op jit(solution)/shard_map/ppermute | solution.py:1236
  325.6 17.7 %collective-permute-start.26 = (bf16[256,1024]{1,0:T(8,128)(2,1)S(1)}, bf16[256,1024]{1,0:T(8,128)(2,1)S(1)}, u32[]{:S(2)}, u32[]{:S(2)}) collective-permute-start(bf16[256,1024]{1,0:T(8,128)(2,1)S(1)} %get-tuple-element.349), channel_id=1, source_target_pairs={{1,0},{2,1},{3,2},{5,4},{6,5},{7,6},{9,8},{10,9},{11,10},{13,12},{... | collective-permute-start | bytes 1572872 | tf_op jit(solution)/shard_map/ppermute | solution.py:1248
  326.9 4.6 collective-permute-start.27
  331.5 14.8 %collective-permute-start.30 = (f32[1,2048]{1,0:T(1,128)S(1)}, f32[1,2048]{1,0:T(1,128)S(1)}, u32[]{:S(2)}, u32[]{:S(2)}) collective-permute-start(f32[1,2048]{1,0:T(1,128)S(1)} %add.180), channel_id=1, source_target_pairs={{0,1},{1,0},{2,3},{3,2},{4,5},{5,4},{6,7},{7,6},{8,9},{9,8},{10,11... | collective-permute-start | bytes 24584 | tf_op jit(solution)/shard_map/ppermute | solution.py:1244
  343.5 48.0 %collective-permute-start.28 = (bf16[256,2048]{1,0:T(8,128)(2,1)}, bf16[256,2048]{1,0:T(8,128)(2,1)}, u32[]{:S(2)}, u32[]{:S(2)}) collective-permute-start(bf16[256,2048]{1,0:T(8,128)(2,1)} %get-tuple-element.368), channel_id=1, source_target_pairs={{0,8},{4,20},{8,0},{12,28},{16,24},{20,4},{24,16},{28,12},{1,9},{5... | collective-permute-start | bytes 3145736 | tf_op jit(solution)/shard_map/ppermute | solution.py:1239
  344.9 46.5 %collective-permute-start.29 = (bf16[256,2048]{1,0:T(8,128)(2,1)}, bf16[256,2048]{1,0:T(8,128)(2,1)}, u32[]{:S(2)}, u32[]{:S(2)}) collective-permute-start(bf16[256,2048]{1,0:T(8,128)(2,1)} %get-tuple-element.370), channel_id=1, source_target_pairs={{0,8},{4,20},{8,0},{12,28},{16,24},{20,4},{24,16},{28,12},{1,9},{5... | collective-permute-start | bytes 3145736 | tf_op jit(solution)/shard_map/ppermute | solution.py:1239
  345.0 35.2 %collective-permute-start.33 = (bf16[256,1024]{1,0:T(8,128)(2,1)S(1)}, bf16[256,1024]{1,0:T(8,128)(2,1)S(1)}, u32[]{:S(2)}, u32[]{:S(2)}) collective-permute-start(bf16[256,1024]{1,0:T(8,128)(2,1)S(1)} %add_convert_fusion.4), channel_id=1, source_target_pairs={{1,0},{2,1},{3,2},{5,4},{6,5},{7,6},{9,8},{10,9},{11,10},{13,12},{... | collective-permute-start | bytes 1572872 | tf_op jit(solution)/shard_map/ppermute | solution.py:1248
  346.4 18.4 %collective-permute-start.31 = (f32[1,2048]{1,0:T(1,128)S(1)}, f32[1,2048]{1,0:T(1,128)S(1)}, u32[]{:S(2)}, u32[]{:S(2)}) collective-permute-start(f32[1,2048]{1,0:T(1,128)S(1)} %add.185), channel_id=1, source_target_pairs={{0,2},{1,3},{2,0},{3,1},{4,6},{5,7},{6,4},{7,5},{8,10},{9,11},{10,... | collective-permute-start | bytes 24584 | tf_op jit(solution)/shard_map/ppermute | solution.py:1244
  372.1 16.3 %collective-permute-start.32 = (bf16[256,1024]{1,0:T(8,128)(2,1)S(1)}, bf16[256,1024]{1,0:T(8,128)(2,1)S(1)}, u32[]{:S(2)}, u32[]{:S(2)}) collective-permute-start(bf16[256,1024]{1,0:T(8,128)(2,1)S(1)} %get-tuple-element.384), channel_id=1, source_target_pairs={{0,4},{4,0},{8,12},{12,8},{16,20},{20,16},{24,28},{28,24},{1,5},{5... | collective-permute-start | bytes 1572872 | tf_op jit(solution)/shard_map/ppermute | solution.py:1236
  393.6 34.0 %collective-permute-start.34 = (bf16[256,2048]{1,0:T(8,128)(2,1)S(1)}, bf16[256,2048]{1,0:T(8,128)(2,1)S(1)}, u32[]{:S(2)}, u32[]{:S(2)}) collective-permute-start(bf16[256,2048]{1,0:T(8,128)(2,1)S(1)} %add_convert_fusion.1), channel_id=1, source_target_pairs={{0,16},{4,12},{8,24},{12,4},{16,0},{20,28},{24,8},{28,20},{1,17},{... | collective-permute-start | bytes 3145736 | tf_op jit(solution)/shard_map/ppermute | solution.py:1239
  393.7 26.1 %collective-permute-start.35 = (bf16[256,1024]{1,0:T(8,128)(2,1)S(1)}, bf16[256,1024]{1,0:T(8,128)(2,1)S(1)}, u32[]{:S(2)}, u32[]{:S(2)}) collective-permute-start(bf16[256,1024]{1,0:T(8,128)(2,1)S(1)} %copy-done.94), channel_id=1, source_target_pairs={{1,0},{2,1},{3,2},{5,4},{6,5},{7,6},{9,8},{10,9},{11,10},{13,12},{... | collective-permute-start | bytes 1572872 | tf_op jit(solution)/shard_map/ppermute | solution.py:1248
  395.2 16.6 %collective-permute-start.36 = (bf16[64,1024]{1,0:T(8,128)(2,1)}, bf16[64,1024]{1,0:T(8,128)(2,1)S(1)}, u32[]{:S(2)}, u32[]{:S(2)}) collective-permute-start(bf16[64,1024]{1,0:T(8,128)(2,1)} %get-tuple-element.399), channel_id=1, source_target_pairs={{0,8},{4,12},{8,0},{12,4},{16,24},{20,28},{24,16},{28,20},{1,9},{5... | collective-permute-start | bytes 393224 | tf_op jit(solution)/shard_map/ppermute | solution.py:1236
  396.7 15.1 %collective-permute-start.37 = (bf16[64,1024]{1,0:T(8,128)(2,1)S(1)}, bf16[64,1024]{1,0:T(8,128)(2,1)S(1)}, u32[]{:S(2)}, u32[]{:S(2)}) collective-permute-start(bf16[64,1024]{1,0:T(8,128)(2,1)S(1)} %copy-done.116), channel_id=1, source_target_pairs={{0,16},{4,20},{8,24},{12,28},{16,0},{20,4},{24,8},{28,12},{1,17},{... | collective-permute-start | bytes 393224 | tf_op jit(solution)/shard_map/ppermute | solution.py:1236
  401.9 15.9 %collective-permute-start.38 = (bf16[64,1024]{1,0:T(8,128)(2,1)S(1)}, bf16[64,1024]{1,0:T(8,128)(2,1)S(1)}, u32[]{:S(2)}, u32[]{:S(2)}) collective-permute-start(bf16[64,1024]{1,0:T(8,128)(2,1)S(1)} %copy-done.115), channel_id=1, source_target_pairs={{0,24},{4,28},{8,16},{12,20},{16,8},{20,12},{24,0},{28,4},{1,25},{... | collective-permute-start | bytes 393224 | tf_op jit(solution)/shard_map/ppermute | solution.py:1236
  417.9 18.1 %collective-permute-start.43 = (bf16[64,1024]{1,0:T(8,128)(2,1)S(1)}, bf16[64,1024]{1,0:T(8,128)(2,1)S(1)}, u32[]{:S(2)}, u32[]{:S(2)}) collective-permute-start(bf16[64,1024]{1,0:T(8,128)(2,1)S(1)} %add_convert_fusion.7), channel_id=1, source_target_pairs={{0,1},{1,0},{2,3},{3,2},{4,5},{5,4},{6,7},{7,6},{8,9},{9,8},{10,11... | collective-permute-start | bytes 393224 | tf_op jit(solution)/shard_map/ppermute | solution.py:1244
  434.8 5.3 %collective-permute-start.42 = (bf16[16,2304]{1,0:T(8,128)(2,1)}, bf16[16,2304]{1,0:T(8,128)(2,1)S(1)}, u32[]{:S(2)}, u32[]{:S(2)}) collective-permute-start(bf16[16,2304]{1,0:T(8,128)(2,1)} %get-tuple-element.430), channel_id=1, source_target_pairs={{0,24},{4,28},{8,16},{12,20},{16,8},{20,12},{24,0},{28,4},{1,25},{... | collective-permute-start | bytes 221192 | tf_op jit(solution)/shard_map/ppermute | solution.py:1236
  436.0 8.4 %collective-permute-start.45 = (bf16[64,1024]{1,0:T(8,128)(2,1)S(1)}, bf16[64,1024]{1,0:T(8,128)(2,1)S(1)}, u32[]{:S(2)}, u32[]{:S(2)}) collective-permute-start(bf16[64,1024]{1,0:T(8,128)(2,1)S(1)} %add_convert_fusion.6), channel_id=1, source_target_pairs={{0,2},{1,3},{2,0},{3,1},{4,6},{5,7},{6,4},{7,5},{8,10},{9,11},{10,... | collective-permute-start | bytes 393224 | tf_op jit(solution)/shard_map/ppermute | solution.py:1244
  441.2 6.3 %collective-permute-start.44 = (bf16[16,2304]{1,0:T(8,128)(2,1)S(1)}, bf16[16,2304]{1,0:T(8,128)(2,1)S(1)}, u32[]{:S(2)}, u32[]{:S(2)}) collective-permute-start(bf16[16,2304]{1,0:T(8,128)(2,1)S(1)} %add_convert_fusion.10), channel_id=1, source_target_pairs={{0,1},{1,0},{2,3},{3,2},{4,5},{5,4},{6,7},{7,6},{8,9},{9,8},{10,11... | collective-permute-start | bytes 221192 | tf_op jit(solution)/shard_map/ppermute | solution.py:1244
  445.1 4.1 collective-permute-start.48
  446.4 6.9 %collective-permute-start.49 = (bf16[64,1024]{1,0:T(8,128)(2,1)S(1)}, bf16[64,1024]{1,0:T(8,128)(2,1)S(1)}, u32[]{:S(2)}, u32[]{:S(2)}) collective-permute-start(bf16[64,1024]{1,0:T(8,128)(2,1)S(1)} %add_convert_fusion.5.refs_0_), channel_id=1, source_target_pairs={{0,24},{4,28},{8,16},{12,20},{16,8},{20,12},{24,0},{28,4},{1,25},{... | collective-permute-start | bytes 393224 | tf_op jit(solution)/shard_map/ppermute | solution.py:1236
  447.5 9.8 %collective-permute-start.46 = (bf16[16,2304]{1,0:T(8,128)(2,1)S(1)}, bf16[16,2304]{1,0:T(8,128)(2,1)S(1)}, u32[]{:S(2)}, u32[]{:S(2)}) collective-permute-start(bf16[16,2304]{1,0:T(8,128)(2,1)S(1)} %add_convert_fusion.9), channel_id=1, source_target_pairs={{0,2},{1,3},{2,0},{3,1},{4,6},{5,7},{6,4},{7,5},{8,10},{9,11},{10,... | collective-permute-start | bytes 221192 | tf_op jit(solution)/shard_map/ppermute | solution.py:1244
  456.0 12.1 %collective-permute-start.54 = (bf16[256,1024]{1,0:T(8,128)(2,1)}, bf16[256,1024]{1,0:T(8,128)(2,1)S(1)}, u32[]{:S(2)}, u32[]{:S(2)}) collective-permute-start(bf16[256,1024]{1,0:T(8,128)(2,1)} %join_rows.2.mine_ref), channel_id=1, source_target_pairs={{0,4},{4,0},{8,12},{12,8},{16,20},{20,16},{24,28},{28,24},{1,5},{5... | collective-permute-start | bytes 1572872 | tf_op jit(solution)/shard_map/ppermute | solution.py:1236
  466.4 4.5 collective-permute-start.53
  (127 other events, 1083.3 us)
Sparse Core Ops, SparseCore 0:
  18.6 65.2 all-gather.6
  85.8 60.9 all-gather.8
  149.3 89.9 all-gather.10

commit v5 on v4

--- a/solution.py
+++ b/solution.py
@@ -1617,10 +1617,6 @@
 
     grad_queries, grad_kv = keys_back(blocks - 1)
     passed = links.row_shift(grad_kv, -1)
-    if fast:
-        sums = adapters((3,), crossed, far_made, sums)
-    feed_in, feed_products, down_in, down_products = sums
-    mag_raw = sum(mag_sums)
     next(down_mag_steps)
     held = None
     for distance in reversed(range(1, blocks - 1)):
@@ -1633,6 +1629,10 @@
         out_first = links.split_swap(order(shares_out[1]), 2, 4)
     next(down_mag_steps)
     grad_queries, grad_kv = keys_back(0)
+    if fast:
+        sums = adapters((3,), crossed, far_made, sums)
+    feed_in, feed_products, down_in, down_products = sums
+    mag_raw = sum(mag_sums)
     for down_mag_total in down_mag_steps:
         pass
     down_grad_mag, early = pack_early(down_mag_total)

time: 488 us -> 490 us (level)
  transfers between devices with their start and end apart: 58 -> 58, of which waited for: 27 -> 26; matrix products, arithmetic and copies ran while one was open for 4% -> 4% of each run, Pallas kernels for 38% -> 38%
where the time goes in v5:
time: 490 us; the launch traced here: 481 us
  Pallas kernels  211 us (43%)
  waiting for transfers between devices  99.7 us (20%)
  starting transfers between devices  97.4 us (20%)
  local copies, waits for them, and re-layouts  41.8 us (9%)
  between operations  16.2 us (3%)
  other arithmetic  14.9 us (3%)
    pallas_call x30, Pallas kernels, kernel_call(): call(*[keep(value, spec) for value, spec in zip(operands, in_specs)])  190 us
    ppermute x35, waiting for transfers between devices, swap(): lax.ppermute(value, 'dp', [(i, i ^ bits) for i in range(self.devices)])  66.6 us
    ppermute x35, starting transfers between devices, swap(): lax.ppermute(value, 'dp', [(i, i ^ bits) for i in range(self.devices)])  49.2 us
    unnamed x234, local copies, waits for them, and re-layouts  32.1 us
    ppermute x6, starting transfers between devices, row_swap(): lax.ppermute(value, 'blk', [(i, i ^ bits) for i in range(self.blocks)])  22.8 us
    ppermute x8, waiting for transfers between devices, split_swap(): lax.ppermute(value, 'dp', [(i, i ^ (odd_bits if i % 2 else even_bits)) fo...  16.8 us
    ppermute x6, starting transfers between devices, row_shift(): return lax.ppermute(value, 'blk', pairs)  16.4 us
    pallas_call x4, Pallas kernels, attend_back(): kernel_call(functools.partial(attend_back_kernel, distance=distance, chai...  13.3 us
  transfers between devices with their start and end apart: 58, of which 26 were waited for; matrix products, arithmetic and copies ran while one was open for 4% of the time, Pallas kernels for 38%

profile of v5, /device:TPU:1, one launch (start us, length us, event | category | flops | bytes accessed | tf_op | source)
XLA Modules:
  0.0 481.3 jit_solution(12724470268630671809)
XLA Ops:
  13.9 4.5 fold_q.1
  24.7 9.7 %collective-permute-done.first_ref = bf16[2,64,2176]{2,1,0:T(8,128)(2,1)} collective-permute-done((bf16[2,64,2176]{2,1,0:T(8,128)(2,1)S(1)}, bf16[2,64,2176]{2,1,0:T(8,128)(2,1)}, u32[]{:S(2)}, u32[]{:S(2)}) %collective-permute-start) | collective-permute-done | bytes 557088 | tf_op jit(solution)/shard_map/ppermute | solution.py:1236
  37.8 4.5 fold_o.1
  45.5 2.4 collective-permute-start.3
  50.9 6.1 %collective-permute-done.3.first_ref = bf16[2,64,2176]{2,1,0:T(8,128)(2,1)S(1)} collective-permute-done((bf16[2,64,2176]{2,1,0:T(8,128)(2,1)S(1)}, bf16[2,64,2176]{2,1,0:T(8,128)(2,1)S(1)}, u32[]{:S(2)}, u32[]{:S(2)}) %collective-permute-start.3) | collective-permute-done | bytes 557088 | tf_op jit(solution)/shard_map/ppermute | solution.py:1239
  57.0 7.6 %collective-permute-start.4 = (bf16[2,64,2176]{2,1,0:T(8,128)(2,1)S(1)}, bf16[2,64,2176]{2,1,0:T(8,128)(2,1)S(1)}, u32[]{:S(2)}, u32[]{:S(2)}) collective-permute-start(bf16[2,64,2176]{2,1,0:T(8,128)(2,1)S(1)} %collective-permute-done.3.first_ref), channel_id=1, source_target_pairs={{0,4},{4,0},{8,12},{12,8},{16,20},{20,16},{24,28},{28,24},{1,5},{5... | collective-permute-start | bytes 1671176 | tf_op jit(solution)/shard_map/ppermute | solution.py:1236
  76.2 3.7 collective-permute-start.7
  82.1 2.7 copy-done.21
  84.8 12.5 %fold_feed.1.own_ref.own_hbm = bf16[2,704,2176]{2,1,0:T(8,128)(2,1)} custom-call(bf16[2,704,2048]{2,1,0:T(8,128)(2,1)S(1)} %bitcast.73, bf16[2,16,2048]{2,1,0:T(8,128)(2,1)S(1)} %bitcast.74, bf16[2,16,704]{2,1,0:T(8,128)(2,1)S(1)} %constant_dynamic-slice_fusion.3.rank_out_ref, f32[2,1,704]{2,1,0:T(1,128)S(1)} %broadcast_in_dim.62.mag_ref), custom_call_target="tpu_custom_call" | custom-call | tf_op jit(solution)/shard_map/fold_feed/pallas_call | solution.py:60
  97.3 3.6 collective-permute-start.8
  104.1 2.8 fold_down.1
  111.4 5.1 %collective-permute-start.9 = (bf16[256,1024]{1,0:T(8,128)(2,1)}, bf16[256,1024]{1,0:T(8,128)(2,1)}, u32[]{:S(2)}, u32[]{:S(2)}) collective-permute-start(bf16[256,1024]{1,0:T(8,128)(2,1)} %collective-permute-done.8.refs_2_.kv_ref), channel_id=1, source_target_pairs={{0,1},{1,2},{2,3},{4,5},{5,6},{6,7},{8,9},{9,10},{10,11},{12,13},{... | collective-permute-start | bytes 1572872 | tf_op jit(solution)/shard_map/ppermute | solution.py:1248
  116.6 6.0 %query_project.1.query_ref = bf16[256,2048]{1,0:T(8,128)(2,1)S(1)} custom-call(bf16[256,2048]{1,0:T(8,128)(2,1)S(1)} %fusion.2.input_ref.normed_ref, f32[256,128]{1,0:T(8,128)S(1)} %copy-done.14, f32[256,128]{1,0:T(8,128)S(1)} %copy-done.16, bf16[8,4,64,2176]{3,2,1,0:T(8,128)(2,1)} %bitcast.105), custom_call_target="tpu_custom_call" | custom-call | tf_op jit(solution)/shard_map/query_project/pallas_call | solution.py:60
  122.6 3.3 collective-permute-done.9.refs_3_.kv_ref
  125.9 5.3 %attend.1 = (bf16[256,2048]{1,0:T(8,128)(2,1)S(1)}, f32[4,1,1024]{2,1,0:T(1,128)S(1)}) custom-call(s32[2]{0:T(128)S(1)} %pad_add_fusion.scalar_ref, bf16[256,2048]{1,0:T(8,128)(2,1)S(1)} %query_project.1.query_ref, bf16[256,1024]{1,0:T(8,128)(2,1)S(1)} %copy-done.23, bf16[256,1024]{1,0:T(8,128)(2,1)} %collective-permute-done.7.refs_1_.kv_ref, ...), custom_call_target="tpu_custom_call" | custom-call | tf_op jit(solution)/shard_map/attend/pallas_call | solution.py:335
  135.4 4.3 collective-permute-start.13
  141.3 5.5 %all-gather.9.cloned.1.call-done = bf16[32,64,2176]{2,1,0:T(8,128)(2,1)} async-done(((bf16[4,64,2176]{2,1,0:T(8,128)(2,1)}), bf16[32,64,2176]{2,1,0:T(8,128)(2,1)}) %all-gather.9.cloned.1.call-update) | async-done | bytes 8912912 | tf_op jit(solution)/shard_map/all_gather | solution.py:1409
  148.1 5.8 %output_project.1 = (f32[256,2048]{1,0:T(8,128)S(1)}, bf16[256,2048]{1,0:T(8,128)(2,1)S(1)}) custom-call(bf16[256,2048]{1,0:T(8,128)(2,1)S(1)} %copy-done.11, bf16[256,2048]{1,0:T(8,128)(2,1)S(1)} %bitcast.68, f32[1,2048]{1,0:T(1,128)S(1)} %bitcast.88, bf16[8,4,64,2176]{3,2,1,0:T(8,128)(2,1)} %bitcast.102), custom_call_target="tpu_custom_call" | custom-call | tf_op jit(solution)/shard_map/output_project/pallas_call | solution.py:60
  157.4 26.3 %collective-permute-done.14.refs_7_.refs_8_ = bf16[1440,256]{1,0:T(8,128)(2,1)} collective-permute-done((bf16[1440,256]{1,0:T(8,128)(2,1)}, bf16[1440,256]{1,0:T(8,128)(2,1)}, u32[]{:S(2)}, u32[]{:S(2)}) %collective-permute-start.14) | collective-permute-done | bytes 737312 | tf_op jit(solution)/shard_map/ppermute | solution.py:1236
  190.1 19.4 %feed_back.4 = (bf16[256,2048]{1,0:T(8,128)(2,1)}, bf16[256,2048]{1,0:T(8,128)(2,1)}, bf16[2,256,704]{2,1,0:T(8,128)(2,1)}, bf16[2,256,704]{2,1,0:T(8,128)(2,1)}...) custom-call(s32[3]{0:T(128)} %pad_add_fusion.1.place_ref, ...), custom_call_target="tpu_custom_call" | custom-call | tf_op jit(solution)/shard_map/feed_back/pallas_call | solution.py:60
  209.5 7.2 %collective-permute-done.18 = bf16[256,2048]{1,0:T(8,128)(2,1)S(1)} collective-permute-done((bf16[256,2048]{1,0:T(8,128)(2,1)S(1)}, bf16[256,2048]{1,0:T(8,128)(2,1)S(1)}, u32[]{:S(2)}, u32[]{:S(2)}) %collective-permute-start.18) | collective-permute-done | bytes 1048608 | tf_op jit(solution)/shard_map/ppermute | solution.py:1236
  217.4 10.7 %feed_forward.1 = (f32[2,512,704]{2,1,0:T(8,128)S(1)}, f32[2,512,704]{2,1,0:T(8,128)S(1)}) custom-call(bf16[512,2048]{1,0:T(8,128)(2,1)S(1)} %pad_maximum_fusion.normed_ref.normed_hbm, bf16[2,704,2176]{2,1,0:T(8,128)(2,1)} %fold_feed.1.own_ref.own_hbm, bf16[2,704,2176]{2,1,0:T(8,128)(2,1)} %collective-permute-done.10.partner_ref.partner_hbm), custom_call_target="tpu_custom_call" | custom-call | tf_op jit(solution)/shard_map/feed_forward/pallas_call | solution.py:60
  229.7 4.6 feed_adapter.4
  236.4 7.2 %collective-permute-done.20.refs_0_.normed_hbm = bf16[256,2048]{1,0:T(8,128)(2,1)S(1)} collective-permute-done((bf16[256,2048]{1,0:T(8,128)(2,1)S(1)}, bf16[256,2048]{1,0:T(8,128)(2,1)S(1)}, u32[]{:S(2)}, u32[]{:S(2)}) %collective-permute-start.20) | collective-permute-done | bytes 1048608 | tf_op jit(solution)/shard_map/ppermute | solution.py:1239
  244.7 19.0 %feed_back.5 = (bf16[256,2048]{1,0:T(8,128)(2,1)}, bf16[256,2048]{1,0:T(8,128)(2,1)}, bf16[2,256,704]{2,1,0:T(8,128)(2,1)}, bf16[2,256,704]{2,1,0:T(8,128)(2,1)}...) custom-call(s32[3]{0:T(128)} %pad_add_fusion.1.place_ref, ...), custom_call_target="tpu_custom_call" | custom-call | tf_op jit(solution)/shard_map/feed_back/pallas_call | solution.py:60
  264.1 17.1 %feed_back.6 = (bf16[256,2048]{1,0:T(8,128)(2,1)}, bf16[256,2048]{1,0:T(8,128)(2,1)}, bf16[2,256,704]{2,1,0:T(8,128)(2,1)}, bf16[2,256,704]{2,1,0:T(8,128)(2,1)}...) custom-call(s32[3]{0:T(128)} %pad_add_fusion.1.place_ref, ...), custom_call_target="tpu_custom_call" | custom-call | tf_op jit(solution)/shard_map/feed_back/pallas_call | solution.py:60
  282.4 17.3 %feed_back.7 = (bf16[256,2048]{1,0:T(8,128)(2,1)}, bf16[256,2048]{1,0:T(8,128)(2,1)}, bf16[2,256,704]{2,1,0:T(8,128)(2,1)}, bf16[2,256,704]{2,1,0:T(8,128)(2,1)}...) custom-call(s32[3]{0:T(128)} %pad_add_fusion.1.place_ref, ...), custom_call_target="tpu_custom_call" | custom-call | tf_op jit(solution)/shard_map/feed_back/pallas_call | solution.py:60
  303.4 4.1 feed_adapter.5
  307.7 4.4 feed_adapter.6
  312.1 3.6 collective-permute-done.25.third_ref
  315.7 6.9 %residual_back.1 = (f32[256,2048]{1,0:T(8,128)S(1)}, bf16[256,2048]{1,0:T(8,128)(2,1)S(1)}, f32[1,2048]{1,0:T(1,128)S(1)}, bf16[256,128]{1,0:T(8,128)(2,1)S(1)},...) custom-call(bf16[256,2048]{1,0:T(8,128)(2,1)S(1)} %copy-done.47, ...), custom_call_target="tpu_custom_call" | custom-call | tf_op jit(solution)/shard_map/residual_back/pallas_call | solution.py:60
  322.7 2.8 attend_back_3.1
  329.4 6.5 %collective-permute-start.30 = (f32[1,2048]{1,0:T(1,128)S(1)}, f32[1,2048]{1,0:T(1,128)S(1)}, u32[]{:S(2)}, u32[]{:S(2)}) collective-permute-start(f32[1,2048]{1,0:T(1,128)S(1)} %add.180), channel_id=1, source_target_pairs={{0,1},{1,0},{2,3},{3,2},{4,5},{5,4},{6,7},{7,6},{8,9},{9,8},{10,11... | collective-permute-start | bytes 24584 | tf_op jit(solution)/shard_map/ppermute | solution.py:1244
  335.9 2.8 attend_back_2.1
  338.7 2.8 attend_back_1.1
  346.2 14.3 %collective-permute-start.31 = (f32[1,2048]{1,0:T(1,128)S(1)}, f32[1,2048]{1,0:T(1,128)S(1)}, u32[]{:S(2)}, u32[]{:S(2)}) collective-permute-start(f32[1,2048]{1,0:T(1,128)S(1)} %add.182), channel_id=1, source_target_pairs={{0,2},{1,3},{2,0},{3,1},{4,6},{5,7},{6,4},{7,5},{8,10},{9,11},{10,... | collective-permute-start | bytes 24584 | tf_op jit(solution)/shard_map/ppermute | solution.py:1244
  360.6 4.9 %attend_back_0.1 = (f32[256,2048]{1,0:T(8,128)S(1)}, f32[256,1024]{1,0:T(8,128)S(1)}) custom-call(s32[2]{0:T(128)S(1)} %copy-done.84, bf16[256,2048]{1,0:T(8,128)(2,1)S(1)} %query_project.1.query_ref, bf16[256,2048]{1,0:T(8,128)(2,1)S(1)} %get-tuple-element.348.grad_ref, f32[4,1,1024]{2,1,0:T(1,128)S(1)} %copy-done.54, ...), custom_call_target="tpu_custom_call", output_to_operand_aliasing={{0}: (6, {})} | custom-call | tf_op jit(solution)/shard_map/attend_back_0/pallas_call | solution.py:412
  365.6 4.7 feed_adapter.7
  370.4 7.2 %feed_pack.1 = (bf16[256,1024]{1,0:T(8,128)(2,1)S(1)}, bf16[256,1024]{1,0:T(8,128)(2,1)S(1)}, f32[1,2048]{1,0:T(1,128)}) custom-call(s32[3]{0:T(128)S(1)} %copy-done.62, bf16[2,704,2176]{2,1,0:T(8,128)(2,1)} %fold_feed.1.own_ref.own_hbm, bf16[2,704,2176]{2,1,0:T(8,128)(2,1)} %collective-permute-done.10.partner_ref.partner_hbm, ...), custom_call_target="tpu_custom_call" | custom-call | tf_op jit(solution)/shard_map/feed_pack/pallas_call | solution.py:60
  377.6 8.3 %collective-permute-start.32 = (bf16[256,1024]{1,0:T(8,128)(2,1)S(1)}, bf16[256,1024]{1,0:T(8,128)(2,1)S(1)}, u32[]{:S(2)}, u32[]{:S(2)}) collective-permute-start(bf16[256,1024]{1,0:T(8,128)(2,1)S(1)} %get-tuple-element.384), channel_id=1, source_target_pairs={{0,4},{4,0},{8,12},{12,8},{16,20},{20,16},{24,28},{28,24},{1,5},{5... | collective-permute-start | bytes 1572872 | tf_op jit(solution)/shard_map/ppermute | solution.py:1236
  386.9 5.8 %output_adapter.1 = (f32[1,2048]{1,0:T(1,128)S(1)}, f32[16,2048]{1,0:T(8,128)S(1)}, f32[16,2048]{1,0:T(8,128)S(1)}) custom-call(bf16[256,2048]{1,0:T(8,128)(2,1)S(1)} %get-tuple-element.389.grad_ref, f32[1,2048]{1,0:T(1,128)S(1)} %get-tuple-element.390.mag_raw_ref, f32[4,512]{1,0:T(4,128)S(1)} %copy-done.85, bf16[256,2048]{1,0:T(8,128)(2,1)S(1)} %copy-done.12, ...), custom_call_target="tpu_custom_call" | custom-call | tf_op jit(solution)/shard_map/output_adapter/pallas_call | solution.py:60
  402.7 2.5 collective-permute-start.38
  405.4 7.5 %query_back.1 = (f32[256,2176]{1,0:T(8,128)S(1)}, f32[16,2048]{1,0:T(8,128)S(1)}, f32[16,2048]{1,0:T(8,128)S(1)}, f32[1,2048]{1,0:T(1,128)S(1)}) custom-call(f32[256,2048]{1,0:T(8,128)S(1)} %copy-done.4, bf16[256,2048]{1,0:T(8,128)(2,1)S(1)} %query_project.1.query_ref, f32[256,128]{1,0:T(8,128)S(1)} %copy-done.14, f32[256,128]{1,0:T(8,128)S(1)} %copy-done.16, ...), custom_call_target="tpu_custom_call" | custom-call | tf_op jit(solution)/shard_map/query_back/pallas_call | solution.py:60
  414.3 3.4 collective-permute-done.36
  420.3 7.7 %key_back.1 = (bf16[256,2048]{1,0:T(8,128)(2,1)}, bf16[64,2304]{1,0:T(8,128)(2,1)S(1)}, bf16[64,2304]{1,0:T(8,128)(2,1)S(1)}) custom-call(s32[4]{0:T(128)S(1)} %iota_xor_fusion.heads_ref, bf16[256,1024]{1,0:T(8,128)(2,1)S(1)} %collective-permute-done.35.sent_ref, f32[256,1024]{1,0:T(8,128)S(1)} %copy-done.45, bf16[256,1024]{1,0:T(8,128)(2,1)S(1)} %copy-done.25, ...), custom_call_target="tpu_custom_call" | custom-call | tf_op jit(solution)/shard_map/key_back/pallas_call | solution.py:60
  429.8 2.8 add_convert_fusion
  442.5 4.5 collective-permute-done.45
  451.5 4.1 collective-permute-done.48.refs_2_
  (401 shorter events, 129.5 us)
Async XLA Ops:
  7.2 109.4 %all-gather.7.cloned.1.call-start = ((), (), s32[]{:S(2)}) async-start(), calls=%async_computation | async-start | bytes 10027008 | tf_op jit(solution)/shard_map/all_gather | solution.py:1409
  18.5 128.4 %all-gather.9.cloned.1.call-start = ((), (), s32[]{:S(2)}) async-start(), calls=%async_computation.1 | async-start | bytes 10027008 | tf_op jit(solution)/shard_map/all_gather | solution.py:1409
  18.5 15.9 %collective-permute-start = (bf16[2,64,2176]{2,1,0:T(8,128)(2,1)S(1)}, bf16[2,64,2176]{2,1,0:T(8,128)(2,1)}, u32[]{:S(2)}, u32[]{:S(2)}) collective-permute-start(bf16[2,64,2176]{2,1,0:T(8,128)(2,1)S(1)} %fold_kv.1.first_ref), channel_id=1, source_target_pairs={{0,8},{4,12},{8,0},{12,4},{16,24},{20,28},{24,16},{28,20},{1,9},{5... | collective-permute-start | bytes 1671176 | tf_op jit(solution)/shard_map/ppermute | solution.py:1236
  20.6 15.1 %collective-permute-start.1 = (bf16[2,64,2176]{2,1,0:T(8,128)(2,1)S(1)}, bf16[2,64,2176]{2,1,0:T(8,128)(2,1)S(1)}, u32[]{:S(2)}, u32[]{:S(2)}) collective-permute-start(bf16[2,64,2176]{2,1,0:T(8,128)(2,1)S(1)} %fold_kv.1.first_ref), channel_id=1, source_target_pairs={{0,16},{4,20},{8,24},{12,28},{16,0},{20,4},{24,8},{28,12},{1,17},{... | collective-permute-start | bytes 1671176 | tf_op jit(solution)/shard_map/ppermute | solution.py:1236
  21.9 13.8 %collective-permute-start.2 = (bf16[2,64,2176]{2,1,0:T(8,128)(2,1)S(1)}, bf16[2,64,2176]{2,1,0:T(8,128)(2,1)S(1)}, u32[]{:S(2)}, u32[]{:S(2)}) collective-permute-start(bf16[2,64,2176]{2,1,0:T(8,128)(2,1)S(1)} %fold_kv.1.first_ref), channel_id=1, source_target_pairs={{0,4},{4,0},{8,12},{12,8},{16,20},{20,16},{24,28},{28,24},{1,5},{5... | collective-permute-start | bytes 1671176 | tf_op jit(solution)/shard_map/ppermute | solution.py:1236
  42.3 202.4 %all-gather.11.cloned.1.call-start = ((), (), s32[]{:S(2)}) async-start(), calls=%async_computation.2 | async-start | bytes 5242880 | tf_op jit(solution)/shard_map/all_gather | solution.py:1446
  45.5 11.5 %collective-permute-start.3 = (bf16[2,64,2176]{2,1,0:T(8,128)(2,1)S(1)}, bf16[2,64,2176]{2,1,0:T(8,128)(2,1)S(1)}, u32[]{:S(2)}, u32[]{:S(2)}) collective-permute-start(bf16[2,64,2176]{2,1,0:T(8,128)(2,1)S(1)} %broadcast_select_fusion.2), channel_id=1, source_target_pairs={{0,8},{4,20},{8,0},{12,28},{16,24},{20,4},{24,16},{28,12},{1,9},{5... | collective-permute-start | bytes 1671176 | tf_op jit(solution)/shard_map/ppermute | solution.py:1239
  49.1 18.5 %collective-permute-start.5 = (bf16[2,64,2176]{2,1,0:T(8,128)(2,1)}, bf16[2,64,2176]{2,1,0:T(8,128)(2,1)S(1)}, u32[]{:S(2)}, u32[]{:S(2)}) collective-permute-start(bf16[2,64,2176]{2,1,0:T(8,128)(2,1)} %collective-permute-done.first_ref), channel_id=1, source_target_pairs={{0,4},{4,0},{8,12},{12,8},{16,20},{20,16},{24,28},{28,24},{1,5},{5... | collective-permute-start | bytes 1671176 | tf_op jit(solution)/shard_map/ppermute | solution.py:1236
  50.6 17.0 %collective-permute-start.6 = (bf16[2,64,2176]{2,1,0:T(8,128)(2,1)S(1)}, bf16[2,64,2176]{2,1,0:T(8,128)(2,1)S(1)}, u32[]{:S(2)}, u32[]{:S(2)}) collective-permute-start(bf16[2,64,2176]{2,1,0:T(8,128)(2,1)S(1)} %collective-permute-done.1.first_ref), channel_id=1, source_target_pairs={{0,4},{4,0},{8,12},{12,8},{16,20},{20,16},{24,28},{28,24},{1,5},{5... | collective-permute-start | bytes 1671176 | tf_op jit(solution)/shard_map/ppermute | solution.py:1236
  57.0 16.5 %collective-permute-start.4 = (bf16[2,64,2176]{2,1,0:T(8,128)(2,1)S(1)}, bf16[2,64,2176]{2,1,0:T(8,128)(2,1)S(1)}, u32[]{:S(2)}, u32[]{:S(2)}) collective-permute-start(bf16[2,64,2176]{2,1,0:T(8,128)(2,1)S(1)} %collective-permute-done.3.first_ref), channel_id=1, source_target_pairs={{0,4},{4,0},{8,12},{12,8},{16,20},{20,16},{24,28},{28,24},{1,5},{5... | collective-permute-start | bytes 1671176 | tf_op jit(solution)/shard_map/ppermute | solution.py:1236
  76.2 21.1 %collective-permute-start.7 = (bf16[256,1024]{1,0:T(8,128)(2,1)S(1)}, bf16[256,1024]{1,0:T(8,128)(2,1)}, u32[]{:S(2)}, u32[]{:S(2)}) collective-permute-start(bf16[256,1024]{1,0:T(8,128)(2,1)S(1)} %get-tuple-element.255.refs_0_.kv_ref), channel_id=1, source_target_pairs={{0,1},{1,2},{2,3},{4,5},{5,6},{6,7},{8,9},{9,10},{10,11},{12,13},{... | collective-permute-start | bytes 1572872 | tf_op jit(solution)/shard_map/ppermute | solution.py:1248
  97.3 14.1 %collective-permute-start.8 = (bf16[256,1024]{1,0:T(8,128)(2,1)}, bf16[256,1024]{1,0:T(8,128)(2,1)}, u32[]{:S(2)}, u32[]{:S(2)}) collective-permute-start(bf16[256,1024]{1,0:T(8,128)(2,1)} %collective-permute-done.7.refs_1_.kv_ref), channel_id=1, source_target_pairs={{0,1},{1,2},{2,3},{4,5},{5,6},{6,7},{8,9},{9,10},{10,11},{12,13},{... | collective-permute-start | bytes 1572872 | tf_op jit(solution)/shard_map/ppermute | solution.py:1248
  111.4 14.5 %collective-permute-start.9 = (bf16[256,1024]{1,0:T(8,128)(2,1)}, bf16[256,1024]{1,0:T(8,128)(2,1)}, u32[]{:S(2)}, u32[]{:S(2)}) collective-permute-start(bf16[256,1024]{1,0:T(8,128)(2,1)} %collective-permute-done.8.refs_2_.kv_ref), channel_id=1, source_target_pairs={{0,1},{1,2},{2,3},{4,5},{5,6},{6,7},{8,9},{9,10},{10,11},{12,13},{... | collective-permute-start | bytes 1572872 | tf_op jit(solution)/shard_map/ppermute | solution.py:1248
  132.1 57.1 %collective-permute-start.10 = (bf16[2,704,2176]{2,1,0:T(8,128)(2,1)}, bf16[2,704,2176]{2,1,0:T(8,128)(2,1)}, u32[]{:S(2)}, u32[]{:S(2)}) collective-permute-start(bf16[2,704,2176]{2,1,0:T(8,128)(2,1)} %fold_feed.1.own_ref.own_hbm), channel_id=1, source_target_pairs={{0,4},{4,0},{8,12},{12,8},{16,20},{20,16},{24,28},{28,24},{1,5},{5... | collective-permute-start | bytes 18382856 | tf_op jit(solution)/shard_map/ppermute | solution.py:1236
  135.3 22.1 %collective-permute-start.12 = (bf16[1440,256]{1,0:T(8,128)(2,1)}, bf16[1440,256]{1,0:T(8,128)(2,1)}, u32[]{:S(2)}, u32[]{:S(2)}) collective-permute-start(bf16[1440,256]{1,0:T(8,128)(2,1)} %get-tuple-element.273), channel_id=1, source_target_pairs={{0,8},{4,12},{8,0},{12,4},{16,24},{20,28},{24,16},{28,20},{1,9},{5... | collective-permute-start | bytes 2211848 | tf_op jit(solution)/shard_map/ppermute | solution.py:1236
  135.4 22.0 %collective-permute-start.13 = (bf16[1440,256]{1,0:T(8,128)(2,1)}, bf16[1440,256]{1,0:T(8,128)(2,1)}, u32[]{:S(2)}, u32[]{:S(2)}) collective-permute-start(bf16[1440,256]{1,0:T(8,128)(2,1)} %get-tuple-element.274), channel_id=1, source_target_pairs={{0,16},{4,20},{8,24},{12,28},{16,0},{20,4},{24,8},{28,12},{1,17},{... | collective-permute-start | bytes 2211848 | tf_op jit(solution)/shard_map/ppermute | solution.py:1236
  139.7 44.1 %collective-permute-start.14 = (bf16[1440,256]{1,0:T(8,128)(2,1)}, bf16[1440,256]{1,0:T(8,128)(2,1)}, u32[]{:S(2)}, u32[]{:S(2)}) collective-permute-start(bf16[1440,256]{1,0:T(8,128)(2,1)} %get-tuple-element.275), channel_id=1, source_target_pairs={{0,24},{4,28},{8,16},{12,20},{16,8},{20,12},{24,0},{28,4},{1,25},{... | collective-permute-start | bytes 2211848 | tf_op jit(solution)/shard_map/ppermute | solution.py:1236
  140.8 44.3 %collective-permute-start.11 = (bf16[1440,256]{1,0:T(8,128)(2,1)}, bf16[1440,256]{1,0:T(8,128)(2,1)}, u32[]{:S(2)}, u32[]{:S(2)}) collective-permute-start(bf16[1440,256]{1,0:T(8,128)(2,1)} %get-tuple-element.279.refs_1_.refs_2_), channel_id=1, source_target_pairs={{0,4},{4,0},{8,12},{12,8},{16,20},{20,16},{24,28},{28,24},{1,5},{5... | collective-permute-start | bytes 2211848 | tf_op jit(solution)/shard_map/ppermute | solution.py:1236
  184.7 32.0 %collective-permute-start.18 = (bf16[256,2048]{1,0:T(8,128)(2,1)S(1)}, bf16[256,2048]{1,0:T(8,128)(2,1)S(1)}, u32[]{:S(2)}, u32[]{:S(2)}) collective-permute-start(bf16[256,2048]{1,0:T(8,128)(2,1)S(1)} %get-tuple-element.298.refs_0_.normed_hbm), channel_id=1, source_target_pairs={{0,8},{4,12},{8,0},{12,4},{16,24},{20,28},{24,16},{28,20},{1,9},{5... | collective-permute-start | bytes 3145736 | tf_op jit(solution)/shard_map/ppermute | solution.py:1236
  184.9 31.9 %collective-permute-start.19 = (bf16[256,2048]{1,0:T(8,128)(2,1)S(1)}, bf16[256,2048]{1,0:T(8,128)(2,1)S(1)}, u32[]{:S(2)}, u32[]{:S(2)}) collective-permute-start(bf16[256,2048]{1,0:T(8,128)(2,1)S(1)} %get-tuple-element.298.refs_0_.normed_hbm), channel_id=1, source_target_pairs={{0,16},{4,20},{8,24},{12,28},{16,0},{20,4},{24,8},{28,12},{1,17},{... | collective-permute-start | bytes 3145736 | tf_op jit(solution)/shard_map/ppermute | solution.py:1236
  216.9 26.8 %collective-permute-start.20 = (bf16[256,2048]{1,0:T(8,128)(2,1)S(1)}, bf16[256,2048]{1,0:T(8,128)(2,1)S(1)}, u32[]{:S(2)}, u32[]{:S(2)}) collective-permute-start(bf16[256,2048]{1,0:T(8,128)(2,1)S(1)} %broadcast_select_fusion.1), channel_id=1, source_target_pairs={{0,8},{4,20},{8,0},{12,28},{16,24},{20,4},{24,16},{28,12},{1,9},{5... | collective-permute-start | bytes 3145736 | tf_op jit(solution)/shard_map/ppermute | solution.py:1239
  263.7 36.2 %collective-permute-start.22 = (bf16[256,2048]{1,0:T(8,128)(2,1)}, bf16[256,2048]{1,0:T(8,128)(2,1)S(1)}, u32[]{:S(2)}, u32[]{:S(2)}) collective-permute-start(bf16[256,2048]{1,0:T(8,128)(2,1)} %get-tuple-element.310), channel_id=1, source_target_pairs={{0,8},{4,20},{8,0},{12,28},{16,24},{20,4},{24,16},{28,12},{1,9},{5... | collective-permute-start | bytes 3145736 | tf_op jit(solution)/shard_map/ppermute | solution.py:1239
  281.2 30.9 %collective-permute-start.24 = (bf16[256,2048]{1,0:T(8,128)(2,1)}, bf16[256,2048]{1,0:T(8,128)(2,1)S(1)}, u32[]{:S(2)}, u32[]{:S(2)}) collective-permute-start(bf16[256,2048]{1,0:T(8,128)(2,1)} %get-tuple-element.314), channel_id=1, source_target_pairs={{0,8},{4,20},{8,0},{12,28},{16,24},{20,4},{24,16},{28,12},{1,9},{5... | collective-permute-start | bytes 3145736 | tf_op jit(solution)/shard_map/ppermute | solution.py:1239
  301.6 14.1 %collective-permute-start.25 = (bf16[256,2048]{1,0:T(8,128)(2,1)S(1)}, bf16[256,2048]{1,0:T(8,128)(2,1)S(1)}, u32[]{:S(2)}, u32[]{:S(2)}) collective-permute-start(bf16[256,2048]{1,0:T(8,128)(2,1)S(1)} %add_convert_fusion.2), channel_id=1, source_target_pairs={{0,16},{4,12},{8,24},{12,4},{16,0},{20,28},{24,8},{28,20},{1,17},{... | collective-permute-start | bytes 3145736 | tf_op jit(solution)/shard_map/ppermute | solution.py:1239
  302.9 4.7 collective-permute-start.21
  307.6 15.1 %collective-permute-start.23 = (f32[1,2048]{1,0:T(1,128)S(1)}, f32[1,2048]{1,0:T(1,128)S(1)}, u32[]{:S(2)}, u32[]{:S(2)}) collective-permute-start(f32[1,2048]{1,0:T(1,128)S(1)} %add.178), channel_id=1, source_target_pairs={{0,8},{4,12},{8,0},{12,4},{16,24},{20,28},{24,16},{28,20},{1,9},{5... | collective-permute-start | bytes 24584 | tf_op jit(solution)/shard_map/ppermute | solution.py:1236
  325.5 17.6 %collective-permute-start.26 = (bf16[256,1024]{1,0:T(8,128)(2,1)S(1)}, bf16[256,1024]{1,0:T(8,128)(2,1)S(1)}, u32[]{:S(2)}, u32[]{:S(2)}) collective-permute-start(bf16[256,1024]{1,0:T(8,128)(2,1)S(1)} %get-tuple-element.349), channel_id=1, source_target_pairs={{1,0},{2,1},{3,2},{5,4},{6,5},{7,6},{9,8},{10,9},{11,10},{13,12},{... | collective-permute-start | bytes 1572872 | tf_op jit(solution)/shard_map/ppermute | solution.py:1248
  329.4 16.8 %collective-permute-start.30 = (f32[1,2048]{1,0:T(1,128)S(1)}, f32[1,2048]{1,0:T(1,128)S(1)}, u32[]{:S(2)}, u32[]{:S(2)}) collective-permute-start(f32[1,2048]{1,0:T(1,128)S(1)} %add.180), channel_id=1, source_target_pairs={{0,1},{1,0},{2,3},{3,2},{4,5},{5,4},{6,7},{7,6},{8,9},{9,8},{10,11... | collective-permute-start | bytes 24584 | tf_op jit(solution)/shard_map/ppermute | solution.py:1244
  343.4 53.8 %collective-permute-start.28 = (bf16[256,2048]{1,0:T(8,128)(2,1)}, bf16[256,2048]{1,0:T(8,128)(2,1)}, u32[]{:S(2)}, u32[]{:S(2)}) collective-permute-start(bf16[256,2048]{1,0:T(8,128)(2,1)} %get-tuple-element.359), channel_id=1, source_target_pairs={{0,8},{4,20},{8,0},{12,28},{16,24},{20,4},{24,16},{28,12},{1,9},{5... | collective-permute-start | bytes 3145736 | tf_op jit(solution)/shard_map/ppermute | solution.py:1239
  343.7 53.4 %collective-permute-start.29 = (bf16[256,2048]{1,0:T(8,128)(2,1)}, bf16[256,2048]{1,0:T(8,128)(2,1)}, u32[]{:S(2)}, u32[]{:S(2)}) collective-permute-start(bf16[256,2048]{1,0:T(8,128)(2,1)} %get-tuple-element.361), channel_id=1, source_target_pairs={{0,8},{4,20},{8,0},{12,28},{16,24},{20,4},{24,16},{28,12},{1,9},{5... | collective-permute-start | bytes 3145736 | tf_op jit(solution)/shard_map/ppermute | solution.py:1239
  344.9 41.0 %collective-permute-start.33 = (bf16[256,1024]{1,0:T(8,128)(2,1)S(1)}, bf16[256,1024]{1,0:T(8,128)(2,1)S(1)}, u32[]{:S(2)}, u32[]{:S(2)}) collective-permute-start(bf16[256,1024]{1,0:T(8,128)(2,1)S(1)} %add_convert_fusion.4), channel_id=1, source_target_pairs={{1,0},{2,1},{3,2},{5,4},{6,5},{7,6},{9,8},{10,9},{11,10},{13,12},{... | collective-permute-start | bytes 1572872 | tf_op jit(solution)/shard_map/ppermute | solution.py:1248
  346.2 24.1 %collective-permute-start.31 = (f32[1,2048]{1,0:T(1,128)S(1)}, f32[1,2048]{1,0:T(1,128)S(1)}, u32[]{:S(2)}, u32[]{:S(2)}) collective-permute-start(f32[1,2048]{1,0:T(1,128)S(1)} %add.182), channel_id=1, source_target_pairs={{0,2},{1,3},{2,0},{3,1},{4,6},{5,7},{6,4},{7,5},{8,10},{9,11},{10,... | collective-permute-start | bytes 24584 | tf_op jit(solution)/shard_map/ppermute | solution.py:1244
  377.6 16.4 %collective-permute-start.32 = (bf16[256,1024]{1,0:T(8,128)(2,1)S(1)}, bf16[256,1024]{1,0:T(8,128)(2,1)S(1)}, u32[]{:S(2)}, u32[]{:S(2)}) collective-permute-start(bf16[256,1024]{1,0:T(8,128)(2,1)S(1)} %get-tuple-element.384), channel_id=1, source_target_pairs={{0,4},{4,0},{8,12},{12,8},{16,20},{20,16},{24,28},{28,24},{1,5},{5... | collective-permute-start | bytes 1572872 | tf_op jit(solution)/shard_map/ppermute | solution.py:1236
  399.3 30.6 %collective-permute-start.34 = (bf16[256,2048]{1,0:T(8,128)(2,1)S(1)}, bf16[256,2048]{1,0:T(8,128)(2,1)S(1)}, u32[]{:S(2)}, u32[]{:S(2)}) collective-permute-start(bf16[256,2048]{1,0:T(8,128)(2,1)S(1)} %add_convert_fusion.1), channel_id=1, source_target_pairs={{0,16},{4,12},{8,24},{12,4},{16,0},{20,28},{24,8},{28,20},{1,17},{... | collective-permute-start | bytes 3145736 | tf_op jit(solution)/shard_map/ppermute | solution.py:1239
  401.0 19.3 %collective-permute-start.35 = (bf16[256,1024]{1,0:T(8,128)(2,1)S(1)}, bf16[256,1024]{1,0:T(8,128)(2,1)S(1)}, u32[]{:S(2)}, u32[]{:S(2)}) collective-permute-start(bf16[256,1024]{1,0:T(8,128)(2,1)S(1)} %copy-done.94), channel_id=1, source_target_pairs={{1,0},{2,1},{3,2},{5,4},{6,5},{7,6},{9,8},{10,9},{11,10},{13,12},{... | collective-permute-start | bytes 1572872 | tf_op jit(solution)/shard_map/ppermute | solution.py:1248
  402.5 15.2 %collective-permute-start.36 = (bf16[64,1024]{1,0:T(8,128)(2,1)}, bf16[64,1024]{1,0:T(8,128)(2,1)S(1)}, u32[]{:S(2)}, u32[]{:S(2)}) collective-permute-start(bf16[64,1024]{1,0:T(8,128)(2,1)} %get-tuple-element.399), channel_id=1, source_target_pairs={{0,8},{4,12},{8,0},{12,4},{16,24},{20,28},{24,16},{28,20},{1,9},{5... | collective-permute-start | bytes 393224 | tf_op jit(solution)/shard_map/ppermute | solution.py:1236
  402.6 15.1 %collective-permute-start.37 = (bf16[64,1024]{1,0:T(8,128)(2,1)S(1)}, bf16[64,1024]{1,0:T(8,128)(2,1)S(1)}, u32[]{:S(2)}, u32[]{:S(2)}) collective-permute-start(bf16[64,1024]{1,0:T(8,128)(2,1)S(1)} %copy-done.116), channel_id=1, source_target_pairs={{0,16},{4,20},{8,24},{12,28},{16,0},{20,4},{24,8},{28,12},{1,17},{... | collective-permute-start | bytes 393224 | tf_op jit(solution)/shard_map/ppermute | solution.py:1236
  402.7 15.7 %collective-permute-start.38 = (bf16[64,1024]{1,0:T(8,128)(2,1)S(1)}, bf16[64,1024]{1,0:T(8,128)(2,1)S(1)}, u32[]{:S(2)}, u32[]{:S(2)}) collective-permute-start(bf16[64,1024]{1,0:T(8,128)(2,1)S(1)} %copy-done.115), channel_id=1, source_target_pairs={{0,24},{4,28},{8,16},{12,20},{16,8},{20,12},{24,0},{28,4},{1,25},{... | collective-permute-start | bytes 393224 | tf_op jit(solution)/shard_map/ppermute | solution.py:1236
  418.4 19.8 %collective-permute-start.43 = (bf16[64,1024]{1,0:T(8,128)(2,1)S(1)}, bf16[64,1024]{1,0:T(8,128)(2,1)S(1)}, u32[]{:S(2)}, u32[]{:S(2)}) collective-permute-start(bf16[64,1024]{1,0:T(8,128)(2,1)S(1)} %add_convert_fusion.7), channel_id=1, source_target_pairs={{0,1},{1,0},{2,3},{3,2},{4,5},{5,4},{6,7},{7,6},{8,9},{9,8},{10,11... | collective-permute-start | bytes 393224 | tf_op jit(solution)/shard_map/ppermute | solution.py:1244
  428.1 4.6 collective-permute-start.39
  438.3 8.7 %collective-permute-start.45 = (bf16[64,1024]{1,0:T(8,128)(2,1)S(1)}, bf16[64,1024]{1,0:T(8,128)(2,1)S(1)}, u32[]{:S(2)}, u32[]{:S(2)}) collective-permute-start(bf16[64,1024]{1,0:T(8,128)(2,1)S(1)} %add_convert_fusion.6), channel_id=1, source_target_pairs={{0,2},{1,3},{2,0},{3,1},{4,6},{5,7},{6,4},{7,5},{8,10},{9,11},{10,... | collective-permute-start | bytes 393224 | tf_op jit(solution)/shard_map/ppermute | solution.py:1244
  442.4 7.4 %collective-permute-start.44 = (bf16[16,2304]{1,0:T(8,128)(2,1)S(1)}, bf16[16,2304]{1,0:T(8,128)(2,1)S(1)}, u32[]{:S(2)}, u32[]{:S(2)}) collective-permute-start(bf16[16,2304]{1,0:T(8,128)(2,1)S(1)} %add_convert_fusion.10), channel_id=1, source_target_pairs={{0,1},{1,0},{2,3},{3,2},{4,5},{5,4},{6,7},{7,6},{8,9},{9,8},{10,11... | collective-permute-start | bytes 221192 | tf_op jit(solution)/shard_map/ppermute | solution.py:1244
  447.0 4.6 collective-permute-start.47
  448.5 7.2 %collective-permute-start.48 = (bf16[64,1024]{1,0:T(8,128)(2,1)S(1)}, bf16[64,1024]{1,0:T(8,128)(2,1)S(1)}, u32[]{:S(2)}, u32[]{:S(2)}) collective-permute-start(bf16[64,1024]{1,0:T(8,128)(2,1)S(1)} %add_convert_fusion.5.refs_0_), channel_id=1, source_target_pairs={{0,16},{4,20},{8,24},{12,28},{16,0},{20,4},{24,8},{28,12},{1,17},{... | collective-permute-start | bytes 393224 | tf_op jit(solution)/shard_map/ppermute | solution.py:1236
  448.5 7.2 %collective-permute-start.49 = (bf16[64,1024]{1,0:T(8,128)(2,1)S(1)}, bf16[64,1024]{1,0:T(8,128)(2,1)S(1)}, u32[]{:S(2)}, u32[]{:S(2)}) collective-permute-start(bf16[64,1024]{1,0:T(8,128)(2,1)S(1)} %add_convert_fusion.5.refs_0_), channel_id=1, source_target_pairs={{0,24},{4,28},{8,16},{12,20},{16,8},{20,12},{24,0},{28,4},{1,25},{... | collective-permute-start | bytes 393224 | tf_op jit(solution)/shard_map/ppermute | solution.py:1236
  449.8 10.7 %collective-permute-start.46 = (bf16[16,2304]{1,0:T(8,128)(2,1)S(1)}, bf16[16,2304]{1,0:T(8,128)(2,1)S(1)}, u32[]{:S(2)}, u32[]{:S(2)}) collective-permute-start(bf16[16,2304]{1,0:T(8,128)(2,1)S(1)} %add_convert_fusion.9), channel_id=1, source_target_pairs={{0,2},{1,3},{2,0},{3,1},{4,6},{5,7},{6,4},{7,5},{8,10},{9,11},{10,... | collective-permute-start | bytes 221192 | tf_op jit(solution)/shard_map/ppermute | solution.py:1244
  458.9 10.4 %collective-permute-start.54 = (bf16[256,1024]{1,0:T(8,128)(2,1)}, bf16[256,1024]{1,0:T(8,128)(2,1)S(1)}, u32[]{:S(2)}, u32[]{:S(2)}) collective-permute-start(bf16[256,1024]{1,0:T(8,128)(2,1)} %join_rows.2.mine_ref), channel_id=1, source_target_pairs={{0,4},{4,0},{8,12},{12,8},{16,20},{20,16},{24,28},{28,24},{1,5},{5... | collective-permute-start | bytes 1572872 | tf_op jit(solution)/shard_map/ppermute | solution.py:1236
  467.7 4.4 collective-permute-start.53
  (127 other events, 1055.5 us)
Sparse Core Ops, SparseCore 0:
  18.6 65.2 all-gather.6
  85.8 60.9 all-gather.8
  149.3 89.9 all-gather.10

commit v6 on v5

--- a/solution.py
+++ b/solution.py
@@ -1670,6 +1670,7 @@
     out_parts = settle(*out_parts)
     late = early = None
     next(late_steps)
+    out_parts = settle(*out_parts)
     block_out = settle((residual + sum(part.astype(f32) for part in out_parts)).astype(bf16))[None]
     while early is None:
         early = next(early_steps)

time: 490 us -> 492 us (level)
  waiting for transfers between devices: 99.7 us -> 93.4 us
    ppermute x35, starting transfers between devices: 49.2 us -> 56.9 us  [swap(): lax.ppermute(value, 'dp', [(i, i ^ bits) for i in range(self.devices)])]
    ppermute x35, waiting for transfers between devices: 66.6 us -> 58.9 us  [swap(): lax.ppermute(value, 'dp', [(i, i ^ bits) for i in range(self.devices)])]
    unnamed x234 -> x236, local copies, waits for them, and re-layouts: 32.1 us -> 33.1 us
  transfers between devices with their start and end apart: 58 -> 58, of which waited for: 26 -> 23; matrix products, arithmetic and copies ran while one was open for 4% -> 5% of each run, Pallas kernels for 38% -> 38%
where the time goes in v6:
time: 492 us; the launch traced here: 483 us
  Pallas kernels  212 us (43%)
  starting transfers between devices  102 us (21%)
  waiting for transfers between devices  93.4 us (19%)
  local copies, waits for them, and re-layouts  42.8 us (9%)
  other arithmetic  16.4 us (3%)
  between operations  16.2 us (3%)
    pallas_call x30, Pallas kernels, kernel_call(): call(*[keep(value, spec) for value, spec in zip(operands, in_specs)])  191 us
    ppermute x35, waiting for transfers between devices, swap(): lax.ppermute(value, 'dp', [(i, i ^ bits) for i in range(self.devices)])  58.9 us
    ppermute x35, starting transfers between devices, swap(): lax.ppermute(value, 'dp', [(i, i ^ bits) for i in range(self.devices)])  56.9 us
    unnamed x236, local copies, waits for them, and re-layouts  33.1 us
    ppermute x6, starting transfers between devices, row_swap(): lax.ppermute(value, 'blk', [(i, i ^ bits) for i in range(self.blocks)])  20.9 us
    ppermute x8, waiting for transfers between devices, split_swap(): lax.ppermute(value, 'dp', [(i, i ^ (odd_bits if i % 2 else even_bits)) fo...  16.9 us
    ppermute x6, starting transfers between devices, row_shift(): return lax.ppermute(value, 'blk', pairs)  16.4 us
    pallas_call x4, Pallas kernels, attend_back(): kernel_call(functools.partial(attend_back_kernel, distance=distance, chai...  13.3 us
  transfers between devices with their start and end apart: 58, of which 23 were waited for; matrix products, arithmetic and copies ran while one was open for 5% of the time, Pallas kernels for 38%

profile of v6, /device:TPU:1, one launch (start us, length us, event | category | flops | bytes accessed | tf_op | source)
XLA Modules:
  0.0 482.6 jit_solution(1311282788550424097)
XLA Ops:
  13.9 4.5 fold_q.1
  24.7 9.7 %collective-permute-done.first_ref = bf16[2,64,2176]{2,1,0:T(8,128)(2,1)} collective-permute-done((bf16[2,64,2176]{2,1,0:T(8,128)(2,1)S(1)}, bf16[2,64,2176]{2,1,0:T(8,128)(2,1)}, u32[]{:S(2)}, u32[]{:S(2)}) %collective-permute-start) | collective-permute-done | bytes 557088 | tf_op jit(solution)/shard_map/ppermute | solution.py:1236
  37.7 4.5 fold_o.1
  45.5 2.4 collective-permute-start.3
  50.9 6.0 %collective-permute-done.3.first_ref = bf16[2,64,2176]{2,1,0:T(8,128)(2,1)S(1)} collective-permute-done((bf16[2,64,2176]{2,1,0:T(8,128)(2,1)S(1)}, bf16[2,64,2176]{2,1,0:T(8,128)(2,1)S(1)}, u32[]{:S(2)}, u32[]{:S(2)}) %collective-permute-start.3) | collective-permute-done | bytes 557088 | tf_op jit(solution)/shard_map/ppermute | solution.py:1239
  56.9 7.7 %collective-permute-start.4 = (bf16[2,64,2176]{2,1,0:T(8,128)(2,1)S(1)}, bf16[2,64,2176]{2,1,0:T(8,128)(2,1)S(1)}, u32[]{:S(2)}, u32[]{:S(2)}) collective-permute-start(bf16[2,64,2176]{2,1,0:T(8,128)(2,1)S(1)} %collective-permute-done.3.first_ref), channel_id=1, source_target_pairs={{0,4},{4,0},{8,12},{12,8},{16,20},{20,16},{24,28},{28,24},{1,5},{5... | collective-permute-start | bytes 1671176 | tf_op jit(solution)/shard_map/ppermute | solution.py:1236
  76.3 3.7 collective-permute-start.7
  82.2 2.7 copy-done.20
  84.9 12.5 %fold_feed.1.own_ref.own_hbm = bf16[2,704,2176]{2,1,0:T(8,128)(2,1)} custom-call(bf16[2,704,2048]{2,1,0:T(8,128)(2,1)S(1)} %bitcast.73, bf16[2,16,2048]{2,1,0:T(8,128)(2,1)S(1)} %bitcast.74, bf16[2,16,704]{2,1,0:T(8,128)(2,1)S(1)} %constant_dynamic-slice_fusion.3.rank_out_ref, f32[2,1,704]{2,1,0:T(1,128)S(1)} %broadcast_in_dim.62.mag_ref), custom_call_target="tpu_custom_call" | custom-call | tf_op jit(solution)/shard_map/fold_feed/pallas_call | solution.py:60
  97.3 3.6 collective-permute-start.8
  104.2 2.8 fold_down.1
  111.5 5.1 %collective-permute-start.9 = (bf16[256,1024]{1,0:T(8,128)(2,1)}, bf16[256,1024]{1,0:T(8,128)(2,1)}, u32[]{:S(2)}, u32[]{:S(2)}) collective-permute-start(bf16[256,1024]{1,0:T(8,128)(2,1)} %collective-permute-done.8.refs_2_.kv_ref), channel_id=1, source_target_pairs={{0,1},{1,2},{2,3},{4,5},{5,6},{6,7},{8,9},{9,10},{10,11},{12,13},{... | collective-permute-start | bytes 1572872 | tf_op jit(solution)/shard_map/ppermute | solution.py:1248
  116.6 6.0 %query_project.1.query_ref = bf16[256,2048]{1,0:T(8,128)(2,1)S(1)} custom-call(bf16[256,2048]{1,0:T(8,128)(2,1)S(1)} %fusion.2.input_ref.normed_ref, f32[256,128]{1,0:T(8,128)S(1)} %copy-done.14, f32[256,128]{1,0:T(8,128)S(1)} %copy-done.16, bf16[8,4,64,2176]{3,2,1,0:T(8,128)(2,1)} %bitcast.105), custom_call_target="tpu_custom_call" | custom-call | tf_op jit(solution)/shard_map/query_project/pallas_call | solution.py:60
  122.6 3.3 collective-permute-done.9.refs_3_.kv_ref
  126.0 5.3 %attend.1 = (bf16[256,2048]{1,0:T(8,128)(2,1)S(1)}, f32[4,1,1024]{2,1,0:T(1,128)S(1)}) custom-call(s32[2]{0:T(128)S(1)} %pad_add_fusion.scalar_ref, bf16[256,2048]{1,0:T(8,128)(2,1)S(1)} %query_project.1.query_ref, bf16[256,1024]{1,0:T(8,128)(2,1)S(1)} %copy-done.22, bf16[256,1024]{1,0:T(8,128)(2,1)} %collective-permute-done.7.refs_1_.kv_ref, ...), custom_call_target="tpu_custom_call" | custom-call | tf_op jit(solution)/shard_map/attend/pallas_call | solution.py:335
  135.5 4.3 collective-permute-start.13
  141.4 5.5 %all-gather.9.cloned.1.call-done = bf16[32,64,2176]{2,1,0:T(8,128)(2,1)} async-done(((bf16[4,64,2176]{2,1,0:T(8,128)(2,1)}), bf16[32,64,2176]{2,1,0:T(8,128)(2,1)}) %all-gather.9.cloned.1.call-update) | async-done | bytes 8912912 | tf_op jit(solution)/shard_map/all_gather | solution.py:1409
  148.1 5.8 %output_project.1 = (f32[256,2048]{1,0:T(8,128)S(1)}, bf16[256,2048]{1,0:T(8,128)(2,1)S(1)}) custom-call(bf16[256,2048]{1,0:T(8,128)(2,1)S(1)} %copy-done.11, bf16[256,2048]{1,0:T(8,128)(2,1)S(1)} %bitcast.68, f32[1,2048]{1,0:T(1,128)S(1)} %bitcast.88, bf16[8,4,64,2176]{3,2,1,0:T(8,128)(2,1)} %bitcast.102), custom_call_target="tpu_custom_call" | custom-call | tf_op jit(solution)/shard_map/output_project/pallas_call | solution.py:60
  157.5 26.3 %collective-permute-done.14.refs_7_.refs_8_ = bf16[1440,256]{1,0:T(8,128)(2,1)} collective-permute-done((bf16[1440,256]{1,0:T(8,128)(2,1)}, bf16[1440,256]{1,0:T(8,128)(2,1)}, u32[]{:S(2)}, u32[]{:S(2)}) %collective-permute-start.14) | collective-permute-done | bytes 737312 | tf_op jit(solution)/shard_map/ppermute | solution.py:1236
  190.1 19.4 %feed_back.4 = (bf16[256,2048]{1,0:T(8,128)(2,1)}, bf16[256,2048]{1,0:T(8,128)(2,1)}, bf16[2,256,704]{2,1,0:T(8,128)(2,1)}, bf16[2,256,704]{2,1,0:T(8,128)(2,1)}...) custom-call(s32[3]{0:T(128)} %pad_add_fusion.1.place_ref, ...), custom_call_target="tpu_custom_call" | custom-call | tf_op jit(solution)/shard_map/feed_back/pallas_call | solution.py:60
  209.5 7.3 %collective-permute-done.18 = bf16[256,2048]{1,0:T(8,128)(2,1)S(1)} collective-permute-done((bf16[256,2048]{1,0:T(8,128)(2,1)S(1)}, bf16[256,2048]{1,0:T(8,128)(2,1)S(1)}, u32[]{:S(2)}, u32[]{:S(2)}) %collective-permute-start.18) | collective-permute-done | bytes 1048608 | tf_op jit(solution)/shard_map/ppermute | solution.py:1236
  217.3 10.7 %feed_forward.1 = (f32[2,512,704]{2,1,0:T(8,128)S(1)}, f32[2,512,704]{2,1,0:T(8,128)S(1)}) custom-call(bf16[512,2048]{1,0:T(8,128)(2,1)S(1)} %pad_maximum_fusion.normed_ref.normed_hbm, bf16[2,704,2176]{2,1,0:T(8,128)(2,1)} %fold_feed.1.own_ref.own_hbm, bf16[2,704,2176]{2,1,0:T(8,128)(2,1)} %collective-permute-done.10.partner_ref.partner_hbm), custom_call_target="tpu_custom_call" | custom-call | tf_op jit(solution)/shard_map/feed_forward/pallas_call | solution.py:60
  229.7 4.6 feed_adapter.4
  236.4 7.3 %collective-permute-done.20.refs_0_.normed_hbm = bf16[256,2048]{1,0:T(8,128)(2,1)S(1)} collective-permute-done((bf16[256,2048]{1,0:T(8,128)(2,1)S(1)}, bf16[256,2048]{1,0:T(8,128)(2,1)S(1)}, u32[]{:S(2)}, u32[]{:S(2)}) %collective-permute-start.20) | collective-permute-done | bytes 1048608 | tf_op jit(solution)/shard_map/ppermute | solution.py:1239
  244.7 19.0 %feed_back.5 = (bf16[256,2048]{1,0:T(8,128)(2,1)}, bf16[256,2048]{1,0:T(8,128)(2,1)}, bf16[2,256,704]{2,1,0:T(8,128)(2,1)}, bf16[2,256,704]{2,1,0:T(8,128)(2,1)}...) custom-call(s32[3]{0:T(128)} %pad_add_fusion.1.place_ref, ...), custom_call_target="tpu_custom_call" | custom-call | tf_op jit(solution)/shard_map/feed_back/pallas_call | solution.py:60
  264.1 17.1 %feed_back.6 = (bf16[256,2048]{1,0:T(8,128)(2,1)}, bf16[256,2048]{1,0:T(8,128)(2,1)}, bf16[2,256,704]{2,1,0:T(8,128)(2,1)}, bf16[2,256,704]{2,1,0:T(8,128)(2,1)}...) custom-call(s32[3]{0:T(128)} %pad_add_fusion.1.place_ref, ...), custom_call_target="tpu_custom_call" | custom-call | tf_op jit(solution)/shard_map/feed_back/pallas_call | solution.py:60
  282.4 17.3 %feed_back.7 = (bf16[256,2048]{1,0:T(8,128)(2,1)}, bf16[256,2048]{1,0:T(8,128)(2,1)}, bf16[2,256,704]{2,1,0:T(8,128)(2,1)}, bf16[2,256,704]{2,1,0:T(8,128)(2,1)}...) custom-call(s32[3]{0:T(128)} %pad_add_fusion.1.place_ref, ...), custom_call_target="tpu_custom_call" | custom-call | tf_op jit(solution)/shard_map/feed_back/pallas_call | solution.py:60
  303.4 4.1 feed_adapter.5
  307.7 4.4 feed_adapter.6
  312.1 3.6 collective-permute-done.25.third_ref
  315.8 6.9 %residual_back.1 = (f32[256,2048]{1,0:T(8,128)S(1)}, bf16[256,2048]{1,0:T(8,128)(2,1)S(1)}, f32[1,2048]{1,0:T(1,128)S(1)}, bf16[256,128]{1,0:T(8,128)(2,1)S(1)},...) custom-call(bf16[256,2048]{1,0:T(8,128)(2,1)S(1)} %copy-done.46, ...), custom_call_target="tpu_custom_call" | custom-call | tf_op jit(solution)/shard_map/residual_back/pallas_call | solution.py:60
  322.7 2.8 attend_back_3.1
  329.5 6.5 %collective-permute-start.30 = (f32[1,2048]{1,0:T(1,128)S(1)}, f32[1,2048]{1,0:T(1,128)S(1)}, u32[]{:S(2)}, u32[]{:S(2)}) collective-permute-start(f32[1,2048]{1,0:T(1,128)S(1)} %add.180), channel_id=1, source_target_pairs={{0,1},{1,0},{2,3},{3,2},{4,5},{5,4},{6,7},{7,6},{8,9},{9,8},{10,11... | collective-permute-start | bytes 24584 | tf_op jit(solution)/shard_map/ppermute | solution.py:1244
  335.9 2.8 attend_back_2.1
  338.7 2.8 attend_back_1.1
  346.3 8.9 %collective-permute-start.31 = (f32[1,2048]{1,0:T(1,128)S(1)}, f32[1,2048]{1,0:T(1,128)S(1)}, u32[]{:S(2)}, u32[]{:S(2)}) collective-permute-start(f32[1,2048]{1,0:T(1,128)S(1)} %add.182), channel_id=1, source_target_pairs={{0,2},{1,3},{2,0},{3,1},{4,6},{5,7},{6,4},{7,5},{8,10},{9,11},{10,... | collective-permute-start | bytes 24584 | tf_op jit(solution)/shard_map/ppermute | solution.py:1244
  355.2 4.9 %attend_back_0.1 = (f32[256,2048]{1,0:T(8,128)S(1)}, f32[256,1024]{1,0:T(8,128)S(1)}) custom-call(s32[2]{0:T(128)S(1)} %copy-done.83, bf16[256,2048]{1,0:T(8,128)(2,1)S(1)} %query_project.1.query_ref, bf16[256,2048]{1,0:T(8,128)(2,1)S(1)} %get-tuple-element.351.grad_ref, f32[4,1,1024]{2,1,0:T(1,128)S(1)} %copy-done.53, ...), custom_call_target="tpu_custom_call", output_to_operand_aliasing={{0}: (6, {})} | custom-call | tf_op jit(solution)/shard_map/attend_back_0/pallas_call | solution.py:412
  360.2 4.7 feed_adapter.7
  365.0 7.2 %feed_pack.1 = (bf16[256,1024]{1,0:T(8,128)(2,1)S(1)}, bf16[256,1024]{1,0:T(8,128)(2,1)S(1)}, f32[1,2048]{1,0:T(1,128)}) custom-call(s32[3]{0:T(128)S(1)} %copy-done.61, bf16[2,704,2176]{2,1,0:T(8,128)(2,1)} %fold_feed.1.own_ref.own_hbm, bf16[2,704,2176]{2,1,0:T(8,128)(2,1)} %collective-permute-done.10.partner_ref.partner_hbm, ...), custom_call_target="tpu_custom_call" | custom-call | tf_op jit(solution)/shard_map/feed_pack/pallas_call | solution.py:60
  372.2 11.1 %collective-permute-start.32 = (bf16[256,1024]{1,0:T(8,128)(2,1)S(1)}, bf16[256,1024]{1,0:T(8,128)(2,1)S(1)}, u32[]{:S(2)}, u32[]{:S(2)}) collective-permute-start(bf16[256,1024]{1,0:T(8,128)(2,1)S(1)} %get-tuple-element.387), channel_id=1, source_target_pairs={{0,4},{4,0},{8,12},{12,8},{16,20},{20,16},{24,28},{28,24},{1,5},{5... | collective-permute-start | bytes 1572872 | tf_op jit(solution)/shard_map/ppermute | solution.py:1236
  385.8 5.8 %output_adapter.1 = (f32[1,2048]{1,0:T(1,128)S(1)}, f32[16,2048]{1,0:T(8,128)S(1)}, f32[16,2048]{1,0:T(8,128)S(1)}) custom-call(bf16[256,2048]{1,0:T(8,128)(2,1)S(1)} %get-tuple-element.392.grad_ref, f32[1,2048]{1,0:T(1,128)S(1)} %get-tuple-element.393.mag_raw_ref, f32[4,512]{1,0:T(4,128)S(1)} %copy-done.84, bf16[256,2048]{1,0:T(8,128)(2,1)S(1)} %copy-done.12, ...), custom_call_target="tpu_custom_call" | custom-call | tf_op jit(solution)/shard_map/output_adapter/pallas_call | solution.py:60
  397.8 2.6 collective-permute-start.37
  403.9 7.5 %query_back.1 = (f32[256,2176]{1,0:T(8,128)S(1)}, f32[16,2048]{1,0:T(8,128)S(1)}, f32[16,2048]{1,0:T(8,128)S(1)}, f32[1,2048]{1,0:T(1,128)S(1)}) custom-call(f32[256,2048]{1,0:T(8,128)S(1)} %copy-done.4, bf16[256,2048]{1,0:T(8,128)(2,1)S(1)} %query_project.1.query_ref, f32[256,128]{1,0:T(8,128)S(1)} %copy-done.14, f32[256,128]{1,0:T(8,128)S(1)} %copy-done.16, ...), custom_call_target="tpu_custom_call" | custom-call | tf_op jit(solution)/shard_map/query_back/pallas_call | solution.py:60
  413.6 8.6 %key_back.1 = (bf16[256,2048]{1,0:T(8,128)(2,1)}, bf16[64,2304]{1,0:T(8,128)(2,1)S(1)}, bf16[64,2304]{1,0:T(8,128)(2,1)S(1)}) custom-call(s32[4]{0:T(128)S(1)} %iota_xor_fusion.heads_ref, bf16[256,1024]{1,0:T(8,128)(2,1)} %collective-permute-done.35.sent_ref, f32[256,1024]{1,0:T(8,128)S(1)} %copy-done.44, bf16[256,1024]{1,0:T(8,128)(2,1)S(1)} %copy-done.24, ...), custom_call_target="tpu_custom_call" | custom-call | tf_op jit(solution)/shard_map/key_back/pallas_call | solution.py:60
  425.3 2.4 collective-permute-start.43
  431.3 3.8 add_convert_fusion
  441.9 5.7 %collective-permute-done.45 = bf16[64,1024]{1,0:T(8,128)(2,1)S(1)} collective-permute-done((bf16[64,1024]{1,0:T(8,128)(2,1)S(1)}, bf16[64,1024]{1,0:T(8,128)(2,1)S(1)}, u32[]{:S(2)}, u32[]{:S(2)}) %collective-permute-start.45) | collective-permute-done | bytes 131104 | tf_op jit(solution)/shard_map/ppermute | solution.py:1244
  457.1 2.7 collective-permute-start.54
  (403 shorter events, 132.5 us)
Async XLA Ops:
  7.2 109.4 %all-gather.7.cloned.1.call-start = ((), (), s32[]{:S(2)}) async-start(), calls=%async_computation | async-start | bytes 10027008 | tf_op jit(solution)/shard_map/all_gather | solution.py:1409
  18.5 128.4 %all-gather.9.cloned.1.call-start = ((), (), s32[]{:S(2)}) async-start(), calls=%async_computation.1 | async-start | bytes 10027008 | tf_op jit(solution)/shard_map/all_gather | solution.py:1409
  18.5 15.8 %collective-permute-start = (bf16[2,64,2176]{2,1,0:T(8,128)(2,1)S(1)}, bf16[2,64,2176]{2,1,0:T(8,128)(2,1)}, u32[]{:S(2)}, u32[]{:S(2)}) collective-permute-start(bf16[2,64,2176]{2,1,0:T(8,128)(2,1)S(1)} %fold_kv.1.first_ref), channel_id=1, source_target_pairs={{0,8},{4,12},{8,0},{12,4},{16,24},{20,28},{24,16},{28,20},{1,9},{5... | collective-permute-start | bytes 1671176 | tf_op jit(solution)/shard_map/ppermute | solution.py:1236
  20.6 15.1 %collective-permute-start.1 = (bf16[2,64,2176]{2,1,0:T(8,128)(2,1)S(1)}, bf16[2,64,2176]{2,1,0:T(8,128)(2,1)S(1)}, u32[]{:S(2)}, u32[]{:S(2)}) collective-permute-start(bf16[2,64,2176]{2,1,0:T(8,128)(2,1)S(1)} %fold_kv.1.first_ref), channel_id=1, source_target_pairs={{0,16},{4,20},{8,24},{12,28},{16,0},{20,4},{24,8},{28,12},{1,17},{... | collective-permute-start | bytes 1671176 | tf_op jit(solution)/shard_map/ppermute | solution.py:1236
  21.9 13.8 %collective-permute-start.2 = (bf16[2,64,2176]{2,1,0:T(8,128)(2,1)S(1)}, bf16[2,64,2176]{2,1,0:T(8,128)(2,1)S(1)}, u32[]{:S(2)}, u32[]{:S(2)}) collective-permute-start(bf16[2,64,2176]{2,1,0:T(8,128)(2,1)S(1)} %fold_kv.1.first_ref), channel_id=1, source_target_pairs={{0,4},{4,0},{8,12},{12,8},{16,20},{20,16},{24,28},{28,24},{1,5},{5... | collective-permute-start | bytes 1671176 | tf_op jit(solution)/shard_map/ppermute | solution.py:1236
  42.2 202.4 %all-gather.11.cloned.1.call-start = ((), (), s32[]{:S(2)}) async-start(), calls=%async_computation.2 | async-start | bytes 5242880 | tf_op jit(solution)/shard_map/all_gather | solution.py:1446
  45.5 11.4 %collective-permute-start.3 = (bf16[2,64,2176]{2,1,0:T(8,128)(2,1)S(1)}, bf16[2,64,2176]{2,1,0:T(8,128)(2,1)S(1)}, u32[]{:S(2)}, u32[]{:S(2)}) collective-permute-start(bf16[2,64,2176]{2,1,0:T(8,128)(2,1)S(1)} %broadcast_select_fusion.2), channel_id=1, source_target_pairs={{0,8},{4,20},{8,0},{12,28},{16,24},{20,4},{24,16},{28,12},{1,9},{5... | collective-permute-start | bytes 1671176 | tf_op jit(solution)/shard_map/ppermute | solution.py:1239
  49.0 18.6 %collective-permute-start.5 = (bf16[2,64,2176]{2,1,0:T(8,128)(2,1)}, bf16[2,64,2176]{2,1,0:T(8,128)(2,1)S(1)}, u32[]{:S(2)}, u32[]{:S(2)}) collective-permute-start(bf16[2,64,2176]{2,1,0:T(8,128)(2,1)} %collective-permute-done.first_ref), channel_id=1, source_target_pairs={{0,4},{4,0},{8,12},{12,8},{16,20},{20,16},{24,28},{28,24},{1,5},{5... | collective-permute-start | bytes 1671176 | tf_op jit(solution)/shard_map/ppermute | solution.py:1236
  50.6 17.1 %collective-permute-start.6 = (bf16[2,64,2176]{2,1,0:T(8,128)(2,1)S(1)}, bf16[2,64,2176]{2,1,0:T(8,128)(2,1)S(1)}, u32[]{:S(2)}, u32[]{:S(2)}) collective-permute-start(bf16[2,64,2176]{2,1,0:T(8,128)(2,1)S(1)} %collective-permute-done.1.first_ref), channel_id=1, source_target_pairs={{0,4},{4,0},{8,12},{12,8},{16,20},{20,16},{24,28},{28,24},{1,5},{5... | collective-permute-start | bytes 1671176 | tf_op jit(solution)/shard_map/ppermute | solution.py:1236
  56.9 16.7 %collective-permute-start.4 = (bf16[2,64,2176]{2,1,0:T(8,128)(2,1)S(1)}, bf16[2,64,2176]{2,1,0:T(8,128)(2,1)S(1)}, u32[]{:S(2)}, u32[]{:S(2)}) collective-permute-start(bf16[2,64,2176]{2,1,0:T(8,128)(2,1)S(1)} %collective-permute-done.3.first_ref), channel_id=1, source_target_pairs={{0,4},{4,0},{8,12},{12,8},{16,20},{20,16},{24,28},{28,24},{1,5},{5... | collective-permute-start | bytes 1671176 | tf_op jit(solution)/shard_map/ppermute | solution.py:1236
  76.3 21.0 %collective-permute-start.7 = (bf16[256,1024]{1,0:T(8,128)(2,1)S(1)}, bf16[256,1024]{1,0:T(8,128)(2,1)}, u32[]{:S(2)}, u32[]{:S(2)}) collective-permute-start(bf16[256,1024]{1,0:T(8,128)(2,1)S(1)} %get-tuple-element.258.refs_0_.kv_ref), channel_id=1, source_target_pairs={{0,1},{1,2},{2,3},{4,5},{5,6},{6,7},{8,9},{9,10},{10,11},{12,13},{... | collective-permute-start | bytes 1572872 | tf_op jit(solution)/shard_map/ppermute | solution.py:1248
  97.3 14.1 %collective-permute-start.8 = (bf16[256,1024]{1,0:T(8,128)(2,1)}, bf16[256,1024]{1,0:T(8,128)(2,1)}, u32[]{:S(2)}, u32[]{:S(2)}) collective-permute-start(bf16[256,1024]{1,0:T(8,128)(2,1)} %collective-permute-done.7.refs_1_.kv_ref), channel_id=1, source_target_pairs={{0,1},{1,2},{2,3},{4,5},{5,6},{6,7},{8,9},{9,10},{10,11},{12,13},{... | collective-permute-start | bytes 1572872 | tf_op jit(solution)/shard_map/ppermute | solution.py:1248
  111.5 14.5 %collective-permute-start.9 = (bf16[256,1024]{1,0:T(8,128)(2,1)}, bf16[256,1024]{1,0:T(8,128)(2,1)}, u32[]{:S(2)}, u32[]{:S(2)}) collective-permute-start(bf16[256,1024]{1,0:T(8,128)(2,1)} %collective-permute-done.8.refs_2_.kv_ref), channel_id=1, source_target_pairs={{0,1},{1,2},{2,3},{4,5},{5,6},{6,7},{8,9},{9,10},{10,11},{12,13},{... | collective-permute-start | bytes 1572872 | tf_op jit(solution)/shard_map/ppermute | solution.py:1248
  132.2 57.1 %collective-permute-start.10 = (bf16[2,704,2176]{2,1,0:T(8,128)(2,1)}, bf16[2,704,2176]{2,1,0:T(8,128)(2,1)}, u32[]{:S(2)}, u32[]{:S(2)}) collective-permute-start(bf16[2,704,2176]{2,1,0:T(8,128)(2,1)} %fold_feed.1.own_ref.own_hbm), channel_id=1, source_target_pairs={{0,4},{4,0},{8,12},{12,8},{16,20},{20,16},{24,28},{28,24},{1,5},{5... | collective-permute-start | bytes 18382856 | tf_op jit(solution)/shard_map/ppermute | solution.py:1236
  135.4 22.1 %collective-permute-start.12 = (bf16[1440,256]{1,0:T(8,128)(2,1)}, bf16[1440,256]{1,0:T(8,128)(2,1)}, u32[]{:S(2)}, u32[]{:S(2)}) collective-permute-start(bf16[1440,256]{1,0:T(8,128)(2,1)} %get-tuple-element.276), channel_id=1, source_target_pairs={{0,8},{4,12},{8,0},{12,4},{16,24},{20,28},{24,16},{28,20},{1,9},{5... | collective-permute-start | bytes 2211848 | tf_op jit(solution)/shard_map/ppermute | solution.py:1236
  135.5 22.0 %collective-permute-start.13 = (bf16[1440,256]{1,0:T(8,128)(2,1)}, bf16[1440,256]{1,0:T(8,128)(2,1)}, u32[]{:S(2)}, u32[]{:S(2)}) collective-permute-start(bf16[1440,256]{1,0:T(8,128)(2,1)} %get-tuple-element.277), channel_id=1, source_target_pairs={{0,16},{4,20},{8,24},{12,28},{16,0},{20,4},{24,8},{28,12},{1,17},{... | collective-permute-start | bytes 2211848 | tf_op jit(solution)/shard_map/ppermute | solution.py:1236
  139.7 44.0 %collective-permute-start.14 = (bf16[1440,256]{1,0:T(8,128)(2,1)}, bf16[1440,256]{1,0:T(8,128)(2,1)}, u32[]{:S(2)}, u32[]{:S(2)}) collective-permute-start(bf16[1440,256]{1,0:T(8,128)(2,1)} %get-tuple-element.278), channel_id=1, source_target_pairs={{0,24},{4,28},{8,16},{12,20},{16,8},{20,12},{24,0},{28,4},{1,25},{... | collective-permute-start | bytes 2211848 | tf_op jit(solution)/shard_map/ppermute | solution.py:1236
  140.8 44.3 %collective-permute-start.11 = (bf16[1440,256]{1,0:T(8,128)(2,1)}, bf16[1440,256]{1,0:T(8,128)(2,1)}, u32[]{:S(2)}, u32[]{:S(2)}) collective-permute-start(bf16[1440,256]{1,0:T(8,128)(2,1)} %get-tuple-element.282.refs_1_.refs_2_), channel_id=1, source_target_pairs={{0,4},{4,0},{8,12},{12,8},{16,20},{20,16},{24,28},{28,24},{1,5},{5... | collective-permute-start | bytes 2211848 | tf_op jit(solution)/shard_map/ppermute | solution.py:1236
  184.8 32.0 %collective-permute-start.18 = (bf16[256,2048]{1,0:T(8,128)(2,1)S(1)}, bf16[256,2048]{1,0:T(8,128)(2,1)S(1)}, u32[]{:S(2)}, u32[]{:S(2)}) collective-permute-start(bf16[256,2048]{1,0:T(8,128)(2,1)S(1)} %get-tuple-element.301.refs_0_.normed_hbm), channel_id=1, source_target_pairs={{0,8},{4,12},{8,0},{12,4},{16,24},{20,28},{24,16},{28,20},{1,9},{5... | collective-permute-start | bytes 3145736 | tf_op jit(solution)/shard_map/ppermute | solution.py:1236
  184.9 31.9 %collective-permute-start.19 = (bf16[256,2048]{1,0:T(8,128)(2,1)S(1)}, bf16[256,2048]{1,0:T(8,128)(2,1)S(1)}, u32[]{:S(2)}, u32[]{:S(2)}) collective-permute-start(bf16[256,2048]{1,0:T(8,128)(2,1)S(1)} %get-tuple-element.301.refs_0_.normed_hbm), channel_id=1, source_target_pairs={{0,16},{4,20},{8,24},{12,28},{16,0},{20,4},{24,8},{28,12},{1,17},{... | collective-permute-start | bytes 3145736 | tf_op jit(solution)/shard_map/ppermute | solution.py:1236
  216.9 26.7 %collective-permute-start.20 = (bf16[256,2048]{1,0:T(8,128)(2,1)S(1)}, bf16[256,2048]{1,0:T(8,128)(2,1)S(1)}, u32[]{:S(2)}, u32[]{:S(2)}) collective-permute-start(bf16[256,2048]{1,0:T(8,128)(2,1)S(1)} %broadcast_select_fusion.1), channel_id=1, source_target_pairs={{0,8},{4,20},{8,0},{12,28},{16,24},{20,4},{24,16},{28,12},{1,9},{5... | collective-permute-start | bytes 3145736 | tf_op jit(solution)/shard_map/ppermute | solution.py:1239
  263.7 36.2 %collective-permute-start.22 = (bf16[256,2048]{1,0:T(8,128)(2,1)}, bf16[256,2048]{1,0:T(8,128)(2,1)S(1)}, u32[]{:S(2)}, u32[]{:S(2)}) collective-permute-start(bf16[256,2048]{1,0:T(8,128)(2,1)} %get-tuple-element.313), channel_id=1, source_target_pairs={{0,8},{4,20},{8,0},{12,28},{16,24},{20,4},{24,16},{28,12},{1,9},{5... | collective-permute-start | bytes 3145736 | tf_op jit(solution)/shard_map/ppermute | solution.py:1239
  281.2 30.9 %collective-permute-start.24 = (bf16[256,2048]{1,0:T(8,128)(2,1)}, bf16[256,2048]{1,0:T(8,128)(2,1)S(1)}, u32[]{:S(2)}, u32[]{:S(2)}) collective-permute-start(bf16[256,2048]{1,0:T(8,128)(2,1)} %get-tuple-element.317), channel_id=1, source_target_pairs={{0,8},{4,20},{8,0},{12,28},{16,24},{20,4},{24,16},{28,12},{1,9},{5... | collective-permute-start | bytes 3145736 | tf_op jit(solution)/shard_map/ppermute | solution.py:1239
  301.6 14.1 %collective-permute-start.25 = (bf16[256,2048]{1,0:T(8,128)(2,1)S(1)}, bf16[256,2048]{1,0:T(8,128)(2,1)S(1)}, u32[]{:S(2)}, u32[]{:S(2)}) collective-permute-start(bf16[256,2048]{1,0:T(8,128)(2,1)S(1)} %add_convert_fusion.2), channel_id=1, source_target_pairs={{0,16},{4,12},{8,24},{12,4},{16,0},{20,28},{24,8},{28,20},{1,17},{... | collective-permute-start | bytes 3145736 | tf_op jit(solution)/shard_map/ppermute | solution.py:1239
  307.6 15.1 %collective-permute-start.23 = (f32[1,2048]{1,0:T(1,128)S(1)}, f32[1,2048]{1,0:T(1,128)S(1)}, u32[]{:S(2)}, u32[]{:S(2)}) collective-permute-start(f32[1,2048]{1,0:T(1,128)S(1)} %add.178), channel_id=1, source_target_pairs={{0,8},{4,12},{8,0},{12,4},{16,24},{20,28},{24,16},{28,20},{1,9},{5... | collective-permute-start | bytes 24584 | tf_op jit(solution)/shard_map/ppermute | solution.py:1236
  325.6 17.6 %collective-permute-start.26 = (bf16[256,1024]{1,0:T(8,128)(2,1)S(1)}, bf16[256,1024]{1,0:T(8,128)(2,1)S(1)}, u32[]{:S(2)}, u32[]{:S(2)}) collective-permute-start(bf16[256,1024]{1,0:T(8,128)(2,1)S(1)} %get-tuple-element.352), channel_id=1, source_target_pairs={{1,0},{2,1},{3,2},{5,4},{6,5},{7,6},{9,8},{10,9},{11,10},{13,12},{... | collective-permute-start | bytes 1572872 | tf_op jit(solution)/shard_map/ppermute | solution.py:1248
  329.5 16.8 %collective-permute-start.30 = (f32[1,2048]{1,0:T(1,128)S(1)}, f32[1,2048]{1,0:T(1,128)S(1)}, u32[]{:S(2)}, u32[]{:S(2)}) collective-permute-start(f32[1,2048]{1,0:T(1,128)S(1)} %add.180), channel_id=1, source_target_pairs={{0,1},{1,0},{2,3},{3,2},{4,5},{5,4},{6,7},{7,6},{8,9},{9,8},{10,11... | collective-permute-start | bytes 24584 | tf_op jit(solution)/shard_map/ppermute | solution.py:1244
  343.4 57.0 %collective-permute-start.28 = (bf16[256,2048]{1,0:T(8,128)(2,1)}, bf16[256,2048]{1,0:T(8,128)(2,1)}, u32[]{:S(2)}, u32[]{:S(2)}) collective-permute-start(bf16[256,2048]{1,0:T(8,128)(2,1)} %get-tuple-element.362), channel_id=1, source_target_pairs={{0,8},{4,20},{8,0},{12,28},{16,24},{20,4},{24,16},{28,12},{1,9},{5... | collective-permute-start | bytes 3145736 | tf_op jit(solution)/shard_map/ppermute | solution.py:1239
  343.8 57.7 %collective-permute-start.29 = (bf16[256,2048]{1,0:T(8,128)(2,1)}, bf16[256,2048]{1,0:T(8,128)(2,1)}, u32[]{:S(2)}, u32[]{:S(2)}) collective-permute-start(bf16[256,2048]{1,0:T(8,128)(2,1)} %get-tuple-element.364), channel_id=1, source_target_pairs={{0,8},{4,20},{8,0},{12,28},{16,24},{20,4},{24,16},{28,12},{1,9},{5... | collective-permute-start | bytes 3145736 | tf_op jit(solution)/shard_map/ppermute | solution.py:1239
  344.9 38.3 %collective-permute-start.33 = (bf16[256,1024]{1,0:T(8,128)(2,1)S(1)}, bf16[256,1024]{1,0:T(8,128)(2,1)S(1)}, u32[]{:S(2)}, u32[]{:S(2)}) collective-permute-start(bf16[256,1024]{1,0:T(8,128)(2,1)S(1)} %add_convert_fusion.4), channel_id=1, source_target_pairs={{1,0},{2,1},{3,2},{5,4},{6,5},{7,6},{9,8},{10,9},{11,10},{13,12},{... | collective-permute-start | bytes 1572872 | tf_op jit(solution)/shard_map/ppermute | solution.py:1248
  346.3 18.7 %collective-permute-start.31 = (f32[1,2048]{1,0:T(1,128)S(1)}, f32[1,2048]{1,0:T(1,128)S(1)}, u32[]{:S(2)}, u32[]{:S(2)}) collective-permute-start(f32[1,2048]{1,0:T(1,128)S(1)} %add.182), channel_id=1, source_target_pairs={{0,2},{1,3},{2,0},{3,1},{4,6},{5,7},{6,4},{7,5},{8,10},{9,11},{10,... | collective-permute-start | bytes 24584 | tf_op jit(solution)/shard_map/ppermute | solution.py:1244
  372.2 20.7 %collective-permute-start.32 = (bf16[256,1024]{1,0:T(8,128)(2,1)S(1)}, bf16[256,1024]{1,0:T(8,128)(2,1)S(1)}, u32[]{:S(2)}, u32[]{:S(2)}) collective-permute-start(bf16[256,1024]{1,0:T(8,128)(2,1)S(1)} %get-tuple-element.387), channel_id=1, source_target_pairs={{0,4},{4,0},{8,12},{12,8},{16,20},{20,16},{24,28},{28,24},{1,5},{5... | collective-permute-start | bytes 1572872 | tf_op jit(solution)/shard_map/ppermute | solution.py:1236
  384.3 29.3 %collective-permute-start.35 = (bf16[256,1024]{1,0:T(8,128)(2,1)}, bf16[256,1024]{1,0:T(8,128)(2,1)}, u32[]{:S(2)}, u32[]{:S(2)}) collective-permute-start(bf16[256,1024]{1,0:T(8,128)(2,1)} %add_convert_fusion.3), channel_id=1, source_target_pairs={{1,0},{2,1},{3,2},{5,4},{6,5},{7,6},{9,8},{10,9},{11,10},{13,12},{... | collective-permute-start | bytes 1572872 | tf_op jit(solution)/shard_map/ppermute | solution.py:1248
  396.0 16.8 %collective-permute-start.36 = (bf16[64,1024]{1,0:T(8,128)(2,1)}, bf16[64,1024]{1,0:T(8,128)(2,1)S(1)}, u32[]{:S(2)}, u32[]{:S(2)}) collective-permute-start(bf16[64,1024]{1,0:T(8,128)(2,1)} %get-tuple-element.402), channel_id=1, source_target_pairs={{0,8},{4,12},{8,0},{12,4},{16,24},{20,28},{24,16},{28,20},{1,9},{5... | collective-permute-start | bytes 393224 | tf_op jit(solution)/shard_map/ppermute | solution.py:1236
  397.8 15.1 %collective-permute-start.37 = (bf16[64,1024]{1,0:T(8,128)(2,1)}, bf16[64,1024]{1,0:T(8,128)(2,1)S(1)}, u32[]{:S(2)}, u32[]{:S(2)}) collective-permute-start(bf16[64,1024]{1,0:T(8,128)(2,1)} %get-tuple-element.403), channel_id=1, source_target_pairs={{0,16},{4,20},{8,24},{12,28},{16,0},{20,4},{24,8},{28,12},{1,17},{... | collective-permute-start | bytes 393224 | tf_op jit(solution)/shard_map/ppermute | solution.py:1236
  400.4 12.5 %collective-permute-start.38 = (bf16[64,1024]{1,0:T(8,128)(2,1)}, bf16[64,1024]{1,0:T(8,128)(2,1)S(1)}, u32[]{:S(2)}, u32[]{:S(2)}) collective-permute-start(bf16[64,1024]{1,0:T(8,128)(2,1)} %get-tuple-element.404), channel_id=1, source_target_pairs={{0,24},{4,28},{8,16},{12,20},{16,8},{20,12},{24,0},{28,4},{1,25},{... | collective-permute-start | bytes 393224 | tf_op jit(solution)/shard_map/ppermute | solution.py:1236
  403.4 24.3 %collective-permute-start.34 = (bf16[256,2048]{1,0:T(8,128)(2,1)S(1)}, bf16[256,2048]{1,0:T(8,128)(2,1)S(1)}, u32[]{:S(2)}, u32[]{:S(2)}) collective-permute-start(bf16[256,2048]{1,0:T(8,128)(2,1)S(1)} %add_convert_fusion.1), channel_id=1, source_target_pairs={{0,16},{4,12},{8,24},{12,4},{16,0},{20,28},{24,8},{28,20},{1,17},{... | collective-permute-start | bytes 3145736 | tf_op jit(solution)/shard_map/ppermute | solution.py:1239
  423.0 5.7 %collective-permute-start.39 = (bf16[64,2304]{1,0:T(8,128)(2,1)S(1)}, bf16[64,2304]{1,0:T(8,128)(2,1)S(1)}, u32[]{:S(2)}, u32[]{:S(2)}) collective-permute-start(bf16[64,2304]{1,0:T(8,128)(2,1)S(1)} %get-tuple-element.426), channel_id=1, source_target_pairs={{0,4},{4,0},{8,12},{12,8},{16,20},{20,16},{24,28},{28,24},{1,5},{5... | collective-permute-start | bytes 884744 | tf_op jit(solution)/shard_map/ppermute | solution.py:1236
  425.3 12.5 %collective-permute-start.43 = (bf16[64,1024]{1,0:T(8,128)(2,1)}, bf16[64,1024]{1,0:T(8,128)(2,1)S(1)}, u32[]{:S(2)}, u32[]{:S(2)}) collective-permute-start(bf16[64,1024]{1,0:T(8,128)(2,1)} %add_convert_fusion.7), channel_id=1, source_target_pairs={{0,1},{1,0},{2,3},{3,2},{4,5},{5,4},{6,7},{7,6},{8,9},{9,8},{10,11... | collective-permute-start | bytes 393224 | tf_op jit(solution)/shard_map/ppermute | solution.py:1244
  435.1 5.3 %collective-permute-start.40 = (bf16[16,2304]{1,0:T(8,128)(2,1)S(1)}, bf16[16,2304]{1,0:T(8,128)(2,1)S(1)}, u32[]{:S(2)}, u32[]{:S(2)}) collective-permute-start(bf16[16,2304]{1,0:T(8,128)(2,1)S(1)} %copy-done.117), channel_id=1, source_target_pairs={{0,8},{4,12},{8,0},{12,4},{16,24},{20,28},{24,16},{28,20},{1,9},{5... | collective-permute-start | bytes 221192 | tf_op jit(solution)/shard_map/ppermute | solution.py:1236
  435.2 5.3 %collective-permute-start.41 = (bf16[16,2304]{1,0:T(8,128)(2,1)S(1)}, bf16[16,2304]{1,0:T(8,128)(2,1)S(1)}, u32[]{:S(2)}, u32[]{:S(2)}) collective-permute-start(bf16[16,2304]{1,0:T(8,128)(2,1)S(1)} %copy-done.116), channel_id=1, source_target_pairs={{0,16},{4,20},{8,24},{12,28},{16,0},{20,4},{24,8},{28,12},{1,17},{... | collective-permute-start | bytes 221192 | tf_op jit(solution)/shard_map/ppermute | solution.py:1236
  435.5 5.0 %collective-permute-start.42 = (bf16[16,2304]{1,0:T(8,128)(2,1)S(1)}, bf16[16,2304]{1,0:T(8,128)(2,1)S(1)}, u32[]{:S(2)}, u32[]{:S(2)}) collective-permute-start(bf16[16,2304]{1,0:T(8,128)(2,1)S(1)} %copy-done.115), channel_id=1, source_target_pairs={{0,24},{4,28},{8,16},{12,20},{16,8},{20,12},{24,0},{28,4},{1,25},{... | collective-permute-start | bytes 221192 | tf_op jit(solution)/shard_map/ppermute | solution.py:1236
  438.7 8.9 %collective-permute-start.45 = (bf16[64,1024]{1,0:T(8,128)(2,1)S(1)}, bf16[64,1024]{1,0:T(8,128)(2,1)S(1)}, u32[]{:S(2)}, u32[]{:S(2)}) collective-permute-start(bf16[64,1024]{1,0:T(8,128)(2,1)S(1)} %add_convert_fusion.6), channel_id=1, source_target_pairs={{0,2},{1,3},{2,0},{3,1},{4,6},{5,7},{6,4},{7,5},{8,10},{9,11},{10,... | collective-permute-start | bytes 393224 | tf_op jit(solution)/shard_map/ppermute | solution.py:1244
  440.6 9.8 %collective-permute-start.44 = (bf16[16,2304]{1,0:T(8,128)(2,1)S(1)}, bf16[16,2304]{1,0:T(8,128)(2,1)S(1)}, u32[]{:S(2)}, u32[]{:S(2)}) collective-permute-start(bf16[16,2304]{1,0:T(8,128)(2,1)S(1)} %add_convert_fusion.10), channel_id=1, source_target_pairs={{0,1},{1,0},{2,3},{3,2},{4,5},{5,4},{6,7},{7,6},{8,9},{9,8},{10,11... | collective-permute-start | bytes 221192 | tf_op jit(solution)/shard_map/ppermute | solution.py:1244
  448.0 6.5 %collective-permute-start.49 = (bf16[64,1024]{1,0:T(8,128)(2,1)S(1)}, bf16[64,1024]{1,0:T(8,128)(2,1)S(1)}, u32[]{:S(2)}, u32[]{:S(2)}) collective-permute-start(bf16[64,1024]{1,0:T(8,128)(2,1)S(1)} %add_convert_fusion.5.refs_0_), channel_id=1, source_target_pairs={{0,24},{4,28},{8,16},{12,20},{16,8},{20,12},{24,0},{28,4},{1,25},{... | collective-permute-start | bytes 393224 | tf_op jit(solution)/shard_map/ppermute | solution.py:1236
  450.4 9.4 %collective-permute-start.46 = (bf16[16,2304]{1,0:T(8,128)(2,1)S(1)}, bf16[16,2304]{1,0:T(8,128)(2,1)S(1)}, u32[]{:S(2)}, u32[]{:S(2)}) collective-permute-start(bf16[16,2304]{1,0:T(8,128)(2,1)S(1)} %add_convert_fusion.9), channel_id=1, source_target_pairs={{0,2},{1,3},{2,0},{3,1},{4,6},{5,7},{6,4},{7,5},{8,10},{9,11},{10,... | collective-permute-start | bytes 221192 | tf_op jit(solution)/shard_map/ppermute | solution.py:1244
  457.1 13.4 %collective-permute-start.54 = (bf16[256,1024]{1,0:T(8,128)(2,1)}, bf16[256,1024]{1,0:T(8,128)(2,1)S(1)}, u32[]{:S(2)}, u32[]{:S(2)}) collective-permute-start(bf16[256,1024]{1,0:T(8,128)(2,1)} %join_rows.2.mine_ref), channel_id=1, source_target_pairs={{0,4},{4,0},{8,12},{12,8},{16,20},{20,16},{24,28},{28,24},{1,5},{5... | collective-permute-start | bytes 1572872 | tf_op jit(solution)/shard_map/ppermute | solution.py:1236
  468.2 5.1 %collective-permute-start.53 = (bf16[64,2304]{1,0:T(8,128)(2,1)}, bf16[64,2304]{1,0:T(8,128)(2,1)S(1)}, u32[]{:S(2)}, u32[]{:S(2)}) collective-permute-start(bf16[64,2304]{1,0:T(8,128)(2,1)} %join_rows.3.mine_ref), channel_id=1, source_target_pairs={{0,4},{4,0},{8,12},{12,8},{16,20},{20,16},{24,28},{28,24},{1,5},{5... | collective-permute-start | bytes 884744 | tf_op jit(solution)/shard_map/ppermute | solution.py:1236
  (128 other events, 1030.4 us)
Sparse Core Ops, SparseCore 0:
  18.6 65.2 all-gather.6
  85.8 60.9 all-gather.8
  149.3 89.9 all-gather.10
